TPU v7x, 32 devices: a whole 2x2x4 slice. The times are simulated.
32 devices in a mesh: tower: 2 (over x), dp: 16 (over z, y, core).
Axes of the slice: x: 2, y: 2, z: 4, core: 2. Of those that a mesh axis runs over, the one named last changes fastest.
Arguments:
- states: bfloat16 [2, 2, 8192, 768], P('tower', None, 'dp'), may hold values from -6 to 6
- segment_ids: int32 [2, 2, 8192], P('tower', None, 'dp'), may hold values from 0 to 8, as said below
- lengths: int32 [2, 2, 128], P('tower', None, 'dp'), may hold values from 16 to 96, as said below
- positives: int32 [2, 128], replicated, may hold values from 0 to 127
- w_query: bfloat16 [768, 768], replicated, may hold values from -0.078125 to 0.078125
- w_key: bfloat16 [768, 768], replicated, may hold values from -0.078125 to 0.078125
- w_value: bfloat16 [768, 768], replicated, may hold values from -0.21875 to 0.21875
- w_out: bfloat16 [768, 768], replicated, may hold values from -1.25 to 1.25
- w_in: bfloat16 [768, 3072], replicated, may hold values from -0.21875 to 0.21875
- w_ffout: bfloat16 [3072, 768], replicated, may hold values from -0.15625 to 0.15625
- w_proj: bfloat16 [768, 768], replicated, may hold values from -0.21875 to 0.21875
- gain_attn: float32 [768], replicated, may hold values from 0.5 to 1.5
- gain_ffn: float32 [768], replicated, may hold values from 0.5 to 1.5
- gain_final: float32 [768], replicated, may hold values from 0.5 to 1.5
- rel_bias: float32 [32, 12], replicated, may hold values from -6 to 6
Outputs:
- loss: float32 [], replicated
- embeddings: float32 [2, 2, 128, 768], P('tower', None, 'dp')
- d_states: float32 [2, 2, 8192, 768], P('tower', None, 'dp')
- grad_query: float32 [768, 768], replicated
- grad_key: float32 [768, 768], replicated
- grad_value: float32 [768, 768], replicated
- grad_out: float32 [768, 768], replicated
- grad_in: float32 [768, 3072], replicated
- grad_ffout: float32 [3072, 768], replicated
- grad_proj: float32 [768, 768], replicated
- grad_gain_attn: float32 [768], replicated
- grad_gain_ffn: float32 [768], replicated
- grad_gain_final: float32 [768], replicated
- grad_rel_bias: float32 [32, 12], replicated
Inputs may be any that keep to these rules, and one draw needn't show every extreme that they name: `segment_ids`: in each device's row of 512 tokens: on tower index 0, query c (c < 8) holds the first lengths-many positions of slot c * 64 to (c + 1) * 64 - 1 and the rest of the slot has id 8; on tower index 1 passages 0 to 7 lie end to end in order and fill the row. Every item's count of positions equals its lengths entry. `lengths`: queries hold 16 to 64 tokens, query 0 of every row exactly 64; passages hold 32 to 96 tokens and sum to 512 in each row, passage 0 of every row exactly 96.
All inputs are finite; a program needn't handle non-finite values.
Results may differ from a plain program's by a relative error of at most 0.034.
The roundings to bfloat16 on the way count: a program that leaves them out, or rounds other values in their place, can miss the bound.
Values sent between devices are 32-bit elements; how exact they have to be, the bound alone decides.
No kernel may reach another device: no remote copies, remote signals or barrier semaphores. Data moves between devices by JAX's collectives and lax.ppermute only.
A program may use at most 256 MiB of HBM per device.

v0:
```python
import jax
import jax.numpy as jnp
from jax import lax
from jax.sharding import PartitionSpec as P

highest = lax.Precision.HIGHEST
norm_epsilon = 1e-06
logit_scale = 50.0
bucket_edges = (12, 16, 23, 32, 46, 64, 91)


def bucket_table(length):
    where_at = jnp.arange(length, dtype=jnp.int32)
    offset = where_at[None, :] - where_at[:, None]
    distance = jnp.abs(offset)
    far_bucket = jnp.full_like(distance, 8)
    for edge_value in bucket_edges:
        far_bucket = far_bucket + (distance >= edge_value).astype(jnp.int32)
    near_far = jnp.where(distance < 8, distance, far_bucket)
    return near_far + jnp.where(offset > 0, 16, 0)


def rms_scale(values, gain_vec):
    return (
        values
        * lax.rsqrt(jnp.mean(values * values, axis=-1, keepdims=True) + norm_epsilon)
        * gain_vec
    )


def unit_rows(values):
    return values * lax.rsqrt(jnp.sum(values * values, axis=-1, keepdims=True) + norm_epsilon)


def softmax_terms(logits, target_hot):
    maxima = jnp.max(logits, axis=1, keepdims=True)
    log_total = maxima + jnp.log(jnp.sum(jnp.exp(logits - maxima), axis=1, keepdims=True))
    loss_part = jnp.sum(log_total[:, 0] - jnp.sum(logits * target_hot, axis=1))
    return (loss_part, jnp.exp(logits - log_total) - target_hot)


def local(
    states,
    segment_ids,
    lengths,
    positives,
    w_query,
    w_key,
    w_value,
    w_out,
    w_in,
    w_ffout,
    w_proj,
    gain_attn,
    gain_ffn,
    gain_final,
    rel_bias,
):
    length = states.shape[2]
    model_width = states.shape[3]
    item_count = lengths.shape[2]
    bucket_count = rel_bias.shape[0]
    head_count = rel_bias.shape[1]
    head_dim = model_width // head_count
    ff_width = w_in.shape[1]
    tower_index = lax.axis_index("tower")
    dp_index = lax.axis_index("dp")
    dp_count = lax.axis_size("dp")
    row_count = item_count * dp_count
    bucket = bucket_table(length)
    code_full = (
        bucket[:, :, None] == jnp.arange(bucket_count, dtype=jnp.int32)[None, None, :]
    ).astype(jnp.float32)
    bias_map = jnp.einsum("qkb,bh->hqk", code_full, rel_bias, precision=highest)
    code_low = code_full.astype(jnp.bfloat16)
    flat_sizes = (
        model_width * model_width,
        model_width * model_width,
        model_width * model_width,
        model_width * model_width,
        model_width * ff_width,
        ff_width * model_width,
        model_width * model_width,
        4 * model_width,
    )

    def scores_of(query_h, key_h, same_seg):
        raw_scores = (
            jnp.einsum("qhd,khd->hqk", query_h, key_h, preferred_element_type=jnp.float32)
            + bias_map
        )
        return jnp.where(same_seg[None], raw_scores, -1000000000.0)

    def micro_batch(carry, micro_inputs):
        loss_acc, grad_acc = carry
        states_mb, segment, counts, targets = micro_inputs
        states_f = states_mb.astype(jnp.float32)
        normed, back_attn = jax.vjp(rms_scale, states_f, gain_attn)
        normed_low = normed.astype(jnp.bfloat16)
        query_h = (
            jnp.dot(normed_low, w_query, preferred_element_type=jnp.float32)
            .astype(jnp.bfloat16)
            .reshape(length, head_count, head_dim)
        )
        key_h = (
            jnp.dot(normed_low, w_key, preferred_element_type=jnp.float32)
            .astype(jnp.bfloat16)
            .reshape(length, head_count, head_dim)
        )
        value_h = (
            jnp.dot(normed_low, w_value, preferred_element_type=jnp.float32)
            .astype(jnp.bfloat16)
            .reshape(length, head_count, head_dim)
        )
        same_seg = segment[:, None] == segment[None, :]
        scores = scores_of(query_h, key_h, same_seg)
        maxima = jnp.max(scores, axis=-1, keepdims=True)
        expo_vals = jnp.exp(scores - maxima)
        row_total = jnp.sum(expo_vals, axis=-1, keepdims=True)
        log_norm = maxima + jnp.log(row_total)
        probs_low = (expo_vals / row_total).astype(jnp.bfloat16)
        mixed_low = (
            jnp.einsum("hqk,khd->qhd", probs_low, value_h, preferred_element_type=jnp.float32)
            .reshape(length, model_width)
            .astype(jnp.bfloat16)
        )
        hidden = states_f + jnp.dot(mixed_low, w_out, preferred_element_type=jnp.float32)
        normed_two, back_ffn = jax.vjp(rms_scale, hidden, gain_ffn)
        normed_two_low = normed_two.astype(jnp.bfloat16)
        inner = jnp.dot(normed_two_low, w_in, preferred_element_type=jnp.float32)
        activ_low = jnp.maximum(inner, 0.0).astype(jnp.bfloat16)
        output = hidden + jnp.dot(activ_low, w_ffout, preferred_element_type=jnp.float32)
        final_norm, back_final = jax.vjp(rms_scale, output, gain_final)
        member = (segment[:, None] == jnp.arange(item_count, dtype=jnp.int32)[None, :]).astype(
            jnp.float32
        )
        count_f = counts.astype(jnp.float32)[:, None]
        pooled_low = (jnp.dot(member.T, final_norm, precision=highest) / count_f).astype(
            jnp.bfloat16
        )
        embed = jnp.dot(pooled_low, w_proj, preferred_element_type=jnp.float32)
        unit_embed, back_unit = jax.vjp(unit_rows, embed)
        gathered = lax.all_gather(unit_embed, ("tower", "dp"), axis=0, tiled=True)
        queries_all = gathered[:row_count]
        passages_all = gathered[row_count:]
        columns = jnp.arange(row_count, dtype=jnp.int32)[None, :]
        logits = logit_scale * jnp.dot(queries_all, passages_all.T, precision=highest)
        target_hot = (columns == targets[:, None]).astype(jnp.float32)
        loss_part, grad_logits = softmax_terms(logits, target_hot)
        own_rows = lax.dynamic_slice_in_dim(grad_logits, dp_index * item_count, item_count, 0)
        own_cols = lax.dynamic_slice_in_dim(grad_logits, dp_index * item_count, item_count, 1)
        as_query = logit_scale * jnp.dot(own_rows, passages_all, precision=highest)
        as_passage = logit_scale * jnp.dot(own_cols.T, queries_all, precision=highest)
        grad_embed = jnp.where(tower_index == 0, as_query, as_passage)
        (grad_e,) = back_unit(grad_embed)
        grad_e_low = grad_e.astype(jnp.bfloat16)
        grad_proj = jnp.dot(pooled_low.T, grad_e_low, preferred_element_type=jnp.float32)
        grad_pooled = jnp.dot(grad_e_low, w_proj.T, preferred_element_type=jnp.float32)
        grad_final_norm = jnp.dot(member, grad_pooled / count_f, precision=highest)
        grad_output, grad_gain_final = back_final(grad_final_norm)
        grad_output_low = grad_output.astype(jnp.bfloat16)
        grad_ffout = jnp.dot(activ_low.T, grad_output_low, preferred_element_type=jnp.float32)
        grad_activ = jnp.dot(grad_output_low, w_ffout.T, preferred_element_type=jnp.float32)
        grad_inner_low = jnp.where(inner > 0, grad_activ, 0.0).astype(jnp.bfloat16)
        grad_in = jnp.dot(normed_two_low.T, grad_inner_low, preferred_element_type=jnp.float32)
        grad_normed_two = jnp.dot(grad_inner_low, w_in.T, preferred_element_type=jnp.float32)
        grad_hidden_norm, grad_gain_ffn = back_ffn(grad_normed_two)
        grad_hidden = grad_output + grad_hidden_norm
        grad_hidden_low = grad_hidden.astype(jnp.bfloat16)
        grad_out = jnp.dot(mixed_low.T, grad_hidden_low, preferred_element_type=jnp.float32)
        grad_mixed = (
            jnp.dot(grad_hidden_low, w_out.T, preferred_element_type=jnp.float32)
            .astype(jnp.bfloat16)
            .reshape(length, head_count, head_dim)
        )
        probs_full = jnp.exp(scores_of(query_h, key_h, same_seg) - log_norm)
        grad_probs = jnp.einsum(
            "qhd,khd->hqk", grad_mixed, value_h, preferred_element_type=jnp.float32
        )
        grad_scores = (
            probs_full * (grad_probs - jnp.sum(probs_full * grad_probs, axis=-1, keepdims=True))
        ).astype(jnp.bfloat16)
        grad_query_h = (
            jnp.einsum("hqk,khd->qhd", grad_scores, key_h, preferred_element_type=jnp.float32)
            .reshape(length, model_width)
            .astype(jnp.bfloat16)
        )
        grad_key_h = (
            jnp.einsum("hqk,qhd->khd", grad_scores, query_h, preferred_element_type=jnp.float32)
            .reshape(length, model_width)
            .astype(jnp.bfloat16)
        )
        grad_value_h = (
            jnp.einsum(
                "hqk,qhd->khd",
                probs_full.astype(jnp.bfloat16),
                grad_mixed,
                preferred_element_type=jnp.float32,
            )
            .reshape(length, model_width)
            .astype(jnp.bfloat16)
        )
        grad_bias = jnp.einsum(
            "hqk,qkb->bh", grad_scores, code_low, preferred_element_type=jnp.float32
        )
        grad_query = jnp.dot(normed_low.T, grad_query_h, preferred_element_type=jnp.float32)
        grad_key = jnp.dot(normed_low.T, grad_key_h, preferred_element_type=jnp.float32)
        grad_value = jnp.dot(normed_low.T, grad_value_h, preferred_element_type=jnp.float32)
        grad_normed = (
            jnp.dot(grad_query_h, w_query.T, preferred_element_type=jnp.float32)
            + jnp.dot(grad_key_h, w_key.T, preferred_element_type=jnp.float32)
            + jnp.dot(grad_value_h, w_value.T, preferred_element_type=jnp.float32)
        )
        grad_states_norm, grad_gain_attn = back_attn(grad_normed)
        grad_states = grad_hidden + grad_states_norm
        small_grads = jnp.concatenate(
            [
                grad_gain_attn,
                grad_gain_ffn,
                grad_gain_final,
                grad_bias.reshape(-1),
                jnp.zeros((model_width - bucket_count * head_count,), jnp.float32),
            ]
        )
        grad_flat = (
            grad_query.reshape(-1),
            grad_key.reshape(-1),
            grad_value.reshape(-1),
            grad_out.reshape(-1),
            grad_in.reshape(-1),
            grad_ffout.reshape(-1),
            grad_proj.reshape(-1),
            small_grads,
        )
        grad_next = tuple((older + newer for older, newer in zip(grad_acc, grad_flat)))
        return ((loss_acc + loss_part, grad_next), (unit_embed, grad_states))

    grad_start = tuple((jnp.zeros((flat_size,), jnp.float32) for flat_size in flat_sizes))
    (loss_sum, grad_acc), (embed_stack, grad_stack) = lax.scan(
        micro_batch,
        (jnp.zeros((), jnp.float32), grad_start),
        (states[0], segment_ids[0], lengths[0], positives),
    )
    grad_acc = (
        lax.psum_scatter(grad_acc[0], ("tower", "dp"), scatter_dimension=0, tiled=True),
        lax.psum_scatter(grad_acc[1], ("tower", "dp"), scatter_dimension=0, tiled=True),
        lax.psum_scatter(grad_acc[2], ("tower", "dp"), scatter_dimension=0, tiled=True),
        lax.psum_scatter(grad_acc[3], ("tower", "dp"), scatter_dimension=0, tiled=True),
        lax.psum_scatter(grad_acc[4], ("tower", "dp"), scatter_dimension=0, tiled=True),
        lax.psum_scatter(grad_acc[5], ("tower", "dp"), scatter_dimension=0, tiled=True),
        lax.psum_scatter(grad_acc[6], ("tower", "dp"), scatter_dimension=0, tiled=True),
        lax.psum_scatter(grad_acc[7], ("tower", "dp"), scatter_dimension=0, tiled=True),
    )
    whole = (
        lax.all_gather(grad_acc[0], ("tower", "dp"), axis=0, tiled=True),
        lax.all_gather(grad_acc[1], ("tower", "dp"), axis=0, tiled=True),
        lax.all_gather(grad_acc[2], ("tower", "dp"), axis=0, tiled=True),
        lax.all_gather(grad_acc[3], ("tower", "dp"), axis=0, tiled=True),
        lax.all_gather(grad_acc[4], ("tower", "dp"), axis=0, tiled=True),
        lax.all_gather(grad_acc[5], ("tower", "dp"), axis=0, tiled=True),
        lax.all_gather(grad_acc[6], ("tower", "dp"), axis=0, tiled=True),
        lax.all_gather(grad_acc[7], ("tower", "dp"), axis=0, tiled=True),
    )
    micro_count = states.shape[1]
    loss = loss_sum / (micro_count * row_count)
    small_whole = whole[7]
    grad_gain_attn = small_whole[:model_width]
    grad_gain_ffn = small_whole[model_width : 2 * model_width]
    grad_gain_final = small_whole[2 * model_width : 3 * model_width]
    grad_rel_bias = small_whole[
        3 * model_width : 3 * model_width + bucket_count * head_count
    ].reshape(bucket_count, head_count)
    return (
        loss,
        embed_stack[None],
        grad_stack[None],
        whole[0].reshape(model_width, model_width),
        whole[1].reshape(model_width, model_width),
        whole[2].reshape(model_width, model_width),
        whole[3].reshape(model_width, model_width),
        whole[4].reshape(model_width, ff_width),
        whole[5].reshape(ff_width, model_width),
        whole[6].reshape(model_width, model_width),
        grad_gain_attn,
        grad_gain_ffn,
        grad_gain_final,
        grad_rel_bias,
    )


def solution(mesh):
    return jax.shard_map(
        local,
        mesh=mesh,
        in_specs=(
            P("tower", None, "dp", None),
            P("tower", None, "dp"),
            P("tower", None, "dp"),
            P(),
            P(),
            P(),
            P(),
            P(),
            P(),
            P(),
            P(),
            P(),
            P(),
            P(),
            P(),
        ),
        out_specs=(
            P(),
            P("tower", None, "dp", None),
            P("tower", None, "dp", None),
            P(),
            P(),
            P(),
            P(),
            P(),
            P(),
            P(),
            P(),
            P(),
            P(),
            P(),
        ),
        check_vma=False,
    )
```

profile of v0, /device:TPU:0, one launch (start us, length us, event | category | flops | bytes accessed | tf_op | source)
XLA Modules:
  0.0 1491.8 jit_solution(15431839114174384854)
XLA Ops:
  10.4 13.7 fusion.86
  24.0 17.7 %copy.68 = f32[12,512,512]{1,2,0:T(8,128)} copy(f32[12,512,512]{2,0,1:T(8,128)} %fusion.86) | data formatting | bytes 25165824
  41.8 505.2 %while.33 = (s32[]{:T(128)}, f32[]{:T(128)}, f32[589824]{0:T(1024)}, f32[589824]{0:T(1024)}, f32[589824]{0:T(1024)}, /*index=5*/f32[589824]{0:T(1024)}, f32[2359...) while((s32[]{:T(128)}, f32[]{:T(128)}, ...), condition=%wide.region_19.20_spmd.clone, body=%wide.region_0.19_spmd.clone.sunk | while | flops 24776302592 | bytes 825582592 | solution.py:239
  49.5 3.5 convolution_convert_fusion.14
  55.4 6.4 fusion.279
  71.3 5.2 fusion.283
  83.2 46.0 %all_gather.39 = f32[256,768]{1,0:T(8,128)S(1)} all-gather(f32[8,768]{1,0:T(8,128)S(1)} %get-tuple-element.919), channel_id=1, replica_groups=mesh['tower'=2,'dp'=16] {'tower','dp'}, dimensions={0}, use_global_device_ids=true | all-gather | bytes 811008 | tf_op jit(solution)/shard_map/while/body/eval_jaxpr/all_gather | solution.py:143
  140.7 5.9 select_convert_fusion.2
  146.6 3.4 multiply_reduce_fusion.21
  155.3 12.2 multiply_reduce_fusion.22
  167.5 6.9 multiply_convert_fusion.9
  178.0 3.5 fusion.291
  181.4 3.4 reshape.408
  184.8 3.4 select_add_fusion.13
  188.2 6.6 fusion.292
  195.7 3.5 fusion.293
  202.6 4.8 convolution_convert_fusion.17
  208.3 3.5 fusion.294
  215.0 5.0 select_add_fusion.14
  227.5 3.4 reshape.412
  230.9 5.2 select_add_fusion.15
  236.1 5.2 fusion.297
  241.3 11.0 reshape.413
  252.3 4.8 convolution_bitcast_fusion.2
  257.1 5.8 copy.91
  262.9 10.2 select_add_fusion.16
  279.6 7.6 fusion.301
  298.1 3.5 convolution_convert_fusion.14
  303.9 6.6 fusion.279
  320.1 5.2 fusion.283
  332.0 38.9 %all_gather.39 = f32[256,768]{1,0:T(8,128)S(1)} all-gather(f32[8,768]{1,0:T(8,128)S(1)} %get-tuple-element.919), channel_id=1, replica_groups=mesh['tower'=2,'dp'=16] {'tower','dp'}, dimensions={0}, use_global_device_ids=true | all-gather | bytes 811008 | tf_op jit(solution)/shard_map/while/body/eval_jaxpr/all_gather | solution.py:143
  382.4 5.9 select_convert_fusion.2
  388.3 3.4 multiply_reduce_fusion.21
  397.0 12.2 multiply_reduce_fusion.22
  409.2 6.9 multiply_convert_fusion.9
  419.7 3.5 fusion.291
  423.2 3.4 reshape.408
  426.6 4.1 select_add_fusion.13
  430.7 6.6 fusion.292
  438.2 3.5 fusion.293
  445.1 4.8 convolution_convert_fusion.17
  450.8 3.5 fusion.294
  457.5 6.4 select_add_fusion.14
  471.4 3.4 reshape.412
  474.8 6.6 select_add_fusion.15
  481.4 5.2 fusion.297
  486.5 11.1 reshape.413
  497.6 4.8 convolution_bitcast_fusion.2
  502.4 5.8 copy.91
  508.2 17.6 %select_add_fusion.16 = (f32[2359296]{0:T(1024)}, f32[2359296]{0:T(1024)}) fusion(f32[2359296]{0:T(1024)S(1)} %bitcast.254, f32[2359296]{0:T(1024)} %get-tuple-element.985, pred[]{:T(512)S(6)} %compare.3, f32[2359296]{0:T(1024)} %bitcast.255, f32[2359296]{0:T(1024)} %get-tuple-element.984), kind=kLoop, calls=%fused_computation.13.clone.1 | loop fusion | flops 9437184 | bytes 56623104 | tf_op jit(solution)/shard_map/while/body/eval_jaxpr/add | solution.py:235
  532.3 7.6 fusion.301
  547.1 461.2 %all-reduce.12.cloned.1.call-done = (f32[589824]{0:T(1024)}, f32[589824]{0:T(1024)}, f32[589824]{0:T(1024)}, f32[589824]{0:T(1024)}, f32[2359296]{0:T(1024)}, /*index=5*/f32[2359296]{0:T(1024)}, f32[589824]{0:T(1024)}) async-done(((f32[589824]{0:T(1024)}, f32[589824]{0:T(1024)}, f32[589824]{0:T(1024)}, f32[589824]{0:T(1024)}, f32[2359296]{0:T(1024)}, /*index=5*/f32[2359296]{0:T(1024)}, f32[589824]{0:T(1024)}), ...) | async-done | bytes 30670864
  1019.8 40.7 %all-reduce.8 = f32[3072]{0:T(1024)S(1)} all-reduce(f32[3072]{0:T(1024)S(1)} %copy-done.34), channel_id=9, replica_groups=mesh['tower'=2,'dp'=16] {'tower','dp'}, use_global_device_ids=true, to_apply=%region_27.28.clone | all-reduce | flops 3072 | bytes 24576
  1060.7 39.3 %all-reduce = f32[3072]{0:T(1024)S(1)} all-reduce(f32[3072]{0:T(1024)S(1)} %dynamic-slice_dynamic-update-slice_fusion), channel_id=1, replica_groups=mesh['tower'=2,'dp'=16] {'tower','dp'}, use_global_device_ids=true, to_apply=%add | all-reduce | flops 3072 | bytes 24576
  1101.3 3.4 reshape.376
  1104.7 24.2 %all-gather.10.cloned.1.call-done = f32[589824]{0:T(1024)} async-done(((f32[18432]{0:T(1024)}), f32[589824]{0:T(1024)}) %all-gather.10.cloned.1.call-update) | async-done | bytes 2359312 | tf_op jit(solution)/shard_map/all_gather | solution.py:256
  1128.8 3.4 reshape.377
  1132.2 55.8 %all-gather.12.cloned.1.call-done = f32[589824]{0:T(1024)} async-done(((f32[18432]{0:T(1024)}), f32[589824]{0:T(1024)}) %all-gather.12.cloned.1.call-update) | async-done | bytes 2359312 | tf_op jit(solution)/shard_map/all_gather | solution.py:257
  1191.4 55.8 %all-gather.14.cloned.1.call-done = f32[589824]{0:T(1024)} async-done(((f32[18432]{0:T(1024)}), f32[589824]{0:T(1024)}) %all-gather.14.cloned.1.call-update) | async-done | bytes 2359312 | tf_op jit(solution)/shard_map/all_gather | solution.py:258
  1250.5 55.2 %all-gather.20.cloned.1.call-done = f32[589824]{0:T(1024)} async-done(((f32[18432]{0:T(1024)}), f32[589824]{0:T(1024)}) %all-gather.20.cloned.1.call-update) | async-done | bytes 2359312 | tf_op jit(solution)/shard_map/all_gather | solution.py:261
  1309.1 80.4 %all-gather.16.cloned.1.call-done = f32[2359296]{0:T(1024)} async-done(((f32[73728]{0:T(1024)}), f32[2359296]{0:T(1024)}) %all-gather.16.cloned.1.call-update) | async-done | bytes 9437200 | tf_op jit(solution)/shard_map/all_gather | solution.py:259
  1389.5 10.9 reshape.380
  1400.4 72.0 %all-gather.18.cloned.1.call-done = f32[2359296]{0:T(1024)} async-done(((f32[73728]{0:T(1024)}), f32[2359296]{0:T(1024)}) %all-gather.18.cloned.1.call-update) | async-done | bytes 9437200 | tf_op jit(solution)/shard_map/all_gather | solution.py:260
  1472.3 11.3 reshape.381
  (373 shorter events, 167.5 us)
Async XLA Ops:
  7.2 1001.1 %all-reduce.12.cloned.1.call-start = ((), (), s32[]{:S(2)}) async-start(), calls=%async_computation.7 | async-start | bytes 61341696
  24.0 17.7 %copy-start.27 = (f32[768]{0:T(1024)S(1)}, f32[768]{0:T(1024)}, u32[]{:S(2)}) copy-start(f32[768]{0:T(1024)} %param.29) | copy-start | bytes 9220
  24.0 17.7 %copy-start.28 = (f32[768]{0:T(1024)S(1)}, f32[768]{0:T(1024)}, u32[]{:S(2)}) copy-start(f32[768]{0:T(1024)} %param.28) | copy-start | bytes 9220
  24.0 17.7 %copy-start.29 = (f32[768]{0:T(1024)S(1)}, f32[768]{0:T(1024)}, u32[]{:S(2)}) copy-start(f32[768]{0:T(1024)} %param.30) | copy-start | bytes 9220
  46.6 17.1 %copy-start.21 = (bf16[512,768]{0,1:T(8,128)(2,1)}, bf16[512,768]{0,1:T(8,128)(2,1)S(1)}, u32[]{:S(2)}) copy-start(bf16[512,768]{0,1:T(8,128)(2,1)S(1)} %copy.87) | copy-start | bytes 2359300 | tf_op jit(solution)/shard_map/while
  49.5 5.9 copy-start.15
  61.8 4.6 copy-start.2
  68.9 7.6 slice-start.12
  71.3 5.2 copy-start.7
  71.3 5.2 slice-start.13
  130.1 10.5 slice-start.6
  134.2 6.1 copy-start.6
  140.2 6.3 slice-start.10
  140.6 9.3 copy-start.12
  140.6 5.9 copy-start.8
  140.7 5.9 slice-start.11
  151.3 74.1 %copy-start.10 = (f32[512,768]{1,0:T(8,128)}, f32[512,768]{1,0:T(8,128)S(1)}, u32[]{:S(2)}) copy-start(f32[512,768]{1,0:T(8,128)S(1)} %fusion.290) | copy-start | bytes 4718596 | tf_op jit(solution)/shard_map/while
  155.3 12.2 slice-start
  155.3 12.2 slice-start.1
  155.3 12.2 slice-start.2
  227.5 8.6 slice-start.8
  230.9 5.2 slice-start.9
  230.9 5.2 copy-start.13
  241.3 11.0 copy-start.9
  252.3 10.6 slice-start.3
  252.3 10.6 slice-start.4
  257.1 5.8 slice-start.5
  279.6 7.9 copy-start.32
  279.6 7.9 copy-start.31
  279.6 7.9 copy-start.11
  295.1 17.2 %copy-start.21 = (bf16[512,768]{0,1:T(8,128)(2,1)}, bf16[512,768]{0,1:T(8,128)(2,1)S(1)}, u32[]{:S(2)}) copy-start(bf16[512,768]{0,1:T(8,128)(2,1)S(1)} %copy.87) | copy-start | bytes 2359300 | tf_op jit(solution)/shard_map/while
  298.0 5.9 copy-start.15
  317.6 7.6 slice-start.12
  320.0 5.2 copy-start.7
  320.1 5.2 slice-start.13
  371.8 10.5 slice-start.6
  375.9 6.1 copy-start.6
  382.0 6.3 slice-start.10
  382.4 9.3 copy-start.12
  382.4 5.9 copy-start.8
  382.4 5.9 slice-start.11
  393.0 76.2 %copy-start.10 = (f32[512,768]{1,0:T(8,128)}, f32[512,768]{1,0:T(8,128)S(1)}, u32[]{:S(2)}) copy-start(f32[512,768]{1,0:T(8,128)S(1)} %fusion.290) | copy-start | bytes 4718596 | tf_op jit(solution)/shard_map/while
  397.0 12.2 slice-start
  397.0 12.2 slice-start.1
  397.0 12.2 slice-start.2
  471.4 9.9 slice-start.8
  474.8 6.6 slice-start.9
  474.8 6.6 copy-start.13
  486.5 11.1 copy-start.9
  497.6 10.6 slice-start.3
  497.6 10.6 slice-start.4
  502.4 5.8 slice-start.5
  532.2 7.9 copy-start.32
  532.2 7.9 copy-start.31
  532.3 7.9 copy-start.11
  547.0 472.8 %copy-start.34 = (f32[3072]{0:T(1024)S(1)}, f32[3072]{0:T(1024)}, u32[]{:S(2)}) copy-start(f32[3072]{0:T(1024)} %get-tuple-element.375) | copy-start | bytes 36868
  547.0 554.3 %all-gather.8.cloned.1.call-start = ((), (), s32[]{:S(2)}) async-start(), calls=%async_computation | async-start | bytes 2433024 | tf_op jit(solution)/shard_map/all_gather | solution.py:255
  1009.8 119.0 %all-gather.10.cloned.1.call-start = ((), (), s32[]{:S(2)}) async-start(), calls=%async_computation.1 | async-start | bytes 2433024 | tf_op jit(solution)/shard_map/all_gather | solution.py:256
  1011.4 176.6 %all-gather.12.cloned.1.call-start = ((), (), s32[]{:S(2)}) async-start(), calls=%async_computation.2 | async-start | bytes 2433024 | tf_op jit(solution)/shard_map/all_gather | solution.py:257
  1013.0 234.1 %all-gather.14.cloned.1.call-start = ((), (), s32[]{:S(2)}) async-start(), calls=%async_computation.3 | async-start | bytes 2433024 | tf_op jit(solution)/shard_map/all_gather | solution.py:258
  1014.6 291.1 %all-gather.20.cloned.1.call-start = ((), (), s32[]{:S(2)}) async-start(), calls=%async_computation.6 | async-start | bytes 2433024 | tf_op jit(solution)/shard_map/all_gather | solution.py:261
  1016.2 373.2 %all-gather.16.cloned.1.call-start = ((), (), s32[]{:S(2)}) async-start(), calls=%async_computation.4 | async-start | bytes 9732096 | tf_op jit(solution)/shard_map/all_gather | solution.py:259
  1018.0 454.3 %all-gather.18.cloned.1.call-start = ((), (), s32[]{:S(2)}) async-start(), calls=%async_computation.5 | async-start | bytes 9732096 | tf_op jit(solution)/shard_map/all_gather | solution.py:260
  1472.3 11.3 copy-start.1
  (44 other events, 104.4 us)
Sparse Core Ops, SparseCore 0:
  547.1 461.1 all-reduce.11
  1011.8 57.4 all-gather.7
  1072.8 56.0 all-gather.9
  1132.2 55.7 all-gather.11
  1191.3 55.7 all-gather.13
  1249.9 55.7 all-gather.19
  1309.2 80.1 all-gather.15
  1392.4 79.9 all-gather.17
where the time goes:
time: 1500 us; the launch traced here: 1490 us
  waiting for transfers between devices  805 us (54%)
  matrix products  238 us (16%)
  local copies, waits for them, and re-layouts  169 us (11%)
  blocking collectives  165 us (11%)
  other arithmetic  91.9 us (6%)
  between operations  15.7 us (1%)
    unnamed x9, waiting for transfers between devices  461 us
    all_gather x2, blocking collectives, micro_batch(): gathered = lax.all_gather(unit_embed, ('tower', 'dp'), axis=0, tiled=True)  84.9 us
    all_gather x1, waiting for transfers between devices, local(): lax.all_gather(grad_acc[4], ('tower', 'dp'), axis=0, tiled=True)  80.4 us
    unnamed x2, blocking collectives  79.9 us
    all_gather x1, waiting for transfers between devices, local(): lax.all_gather(grad_acc[5], ('tower', 'dp'), axis=0, tiled=True)  72 us
    add x10, other arithmetic, micro_batch(): older + newer  58.5 us
    all_gather x1, waiting for transfers between devices, local(): lax.all_gather(grad_acc[2], ('tower', 'dp'), axis=0, tiled=True)  55.8 us
    all_gather x1, waiting for transfers between devices, local(): lax.all_gather(grad_acc[3], ('tower', 'dp'), axis=0, tiled=True)  55.8 us
  transfers between devices with their start and end apart: 8, of which 7 were waited for; matrix products, arithmetic and copies ran while one was open for 3% of the time, Pallas kernels for 0%

commit v1 on v0

v1 whole, which is shorter than its diff:
```python
import jax
import jax.numpy as jnp
from jax import lax
from jax.sharding import PartitionSpec as P

highest = lax.Precision.HIGHEST
norm_epsilon = 1e-06
logit_scale = 50.0
bucket_edges = (12, 16, 23, 32, 46, 64, 91)
AXES = ("tower", "dp")


def bucket_table(length):
    where_at = jnp.arange(length, dtype=jnp.int32)
    offset = where_at[None, :] - where_at[:, None]
    distance = jnp.abs(offset)
    far_bucket = jnp.full_like(distance, 8)
    for edge_value in bucket_edges:
        far_bucket = far_bucket + (distance >= edge_value).astype(jnp.int32)
    near_far = jnp.where(distance < 8, distance, far_bucket)
    return near_far + jnp.where(offset > 0, 16, 0)


def rms_scale(values, gain_vec):
    return (
        values
        * lax.rsqrt(jnp.mean(values * values, axis=-1, keepdims=True) + norm_epsilon)
        * gain_vec
    )


def unit_rows(values):
    return values * lax.rsqrt(jnp.sum(values * values, axis=-1, keepdims=True) + norm_epsilon)


def softmax_terms(logits, target_hot):
    maxima = jnp.max(logits, axis=1, keepdims=True)
    log_total = maxima + jnp.log(jnp.sum(jnp.exp(logits - maxima), axis=1, keepdims=True))
    loss_part = jnp.sum(log_total[:, 0] - jnp.sum(logits * target_hot, axis=1))
    return (loss_part, jnp.exp(logits - log_total) - target_hot)


def mm(a, b):
    return jnp.dot(a, b, preferred_element_type=jnp.float32)


def mm_t(a, b):
    return lax.dot_general(a, b, (((1,), (1,)), ((), ())), preferred_element_type=jnp.float32)


def t_mm(a, b):
    return lax.dot_general(a, b, (((0,), (0,)), ((), ())), preferred_element_type=jnp.float32)


class Net:
    def __init__(self):
        self.dp = lax.axis_size("dp")
        self.size = self.dp * lax.axis_size("tower")
        self.index = lax.axis_index("tower") * self.dp + lax.axis_index("dp")

    def bit(self, b):
        return (self.index >> b) & 1

    def swap(self, value, b):
        return lax.ppermute(value, AXES, [(i, i ^ (1 << b)) for i in range(self.size)])


def join(own, other, bit):
    first = jnp.where(bit == 0, own, other)
    second = jnp.where(bit == 0, other, own)
    return jnp.concatenate([first, second], axis=0)


def half_of(value, which):
    rows = value.shape[0] // 2
    return lax.dynamic_slice_in_dim(value, which * rows, rows, 0)


def scatter_sum(net, sent, kept, order):
    got = net.swap(sent, order[0])
    for b in order[1:]:
        bit = net.bit(b)
        sent = half_of(kept, 1 - bit) + half_of(got, 1 - bit)
        kept = half_of(kept, bit) + half_of(got, bit)
        got = net.swap(sent, b)
    return kept + got


def gather_all(net, piece, order):
    for b in reversed(order):
        piece = join(piece, net.swap(piece, b), net.bit(b))
    return piece


def sum_small(net, value, order):
    for b in order:
        value = value + net.swap(value, b)
    return value


def local(
    states,
    segment_ids,
    lengths,
    positives,
    w_query,
    w_key,
    w_value,
    w_out,
    w_in,
    w_ffout,
    w_proj,
    gain_attn,
    gain_ffn,
    gain_final,
    rel_bias,
):
    micro_count = states.shape[1]
    length = states.shape[2]
    model_width = states.shape[3]
    item_count = lengths.shape[2]
    bucket_count, head_count = rel_bias.shape
    head_dim = model_width // head_count
    ff_width = w_in.shape[1]
    tower_index = lax.axis_index("tower")
    dp_index = lax.axis_index("dp")
    dp_count = lax.axis_size("dp")
    row_count = item_count * dp_count
    rows = micro_count * length
    net = Net()
    bits = net.size.bit_length() - 1
    core = 0
    chips = tuple(range(1, bits))
    gather_order = (0, 4, 1, 2, 3) if bits == 5 else tuple(range(bits))

    bucket = bucket_table(length)
    code_full = (
        bucket[:, :, None] == jnp.arange(bucket_count, dtype=jnp.int32)[None, None, :]
    ).astype(jnp.float32)
    bias_map = jnp.einsum("qkb,bh->hqk", code_full, rel_bias, precision=highest)
    code_low = code_full.astype(jnp.bfloat16)

    segment = segment_ids[0]
    same_seg = segment[:, :, None] == segment[:, None, :]

    def heads(value):
        return value.reshape(micro_count, length, head_count, head_dim)

    states_f = states[0].reshape(rows, model_width).astype(jnp.float32)
    normed, back_attn = jax.vjp(rms_scale, states_f, gain_attn)
    normed_low = normed.astype(jnp.bfloat16)
    query_h = heads(mm(normed_low, w_query).astype(jnp.bfloat16))
    key_h = heads(mm(normed_low, w_key).astype(jnp.bfloat16))
    value_h = heads(mm(normed_low, w_value).astype(jnp.bfloat16))

    def scores_of():
        raw = (
            jnp.einsum("bqhd,bkhd->bhqk", query_h, key_h, preferred_element_type=jnp.float32)
            + bias_map[None]
        )
        return jnp.where(same_seg[:, None], raw, -1000000000.0)

    scores = scores_of()
    maxima = jnp.max(scores, axis=-1, keepdims=True)
    expo_vals = jnp.exp(scores - maxima)
    row_total = jnp.sum(expo_vals, axis=-1, keepdims=True)
    log_norm = maxima + jnp.log(row_total)
    probs_low = (expo_vals / row_total).astype(jnp.bfloat16)
    mixed_low = (
        jnp.einsum("bhqk,bkhd->bqhd", probs_low, value_h, preferred_element_type=jnp.float32)
        .reshape(rows, model_width)
        .astype(jnp.bfloat16)
    )
    hidden = states_f + mm(mixed_low, w_out)
    normed_two, back_ffn = jax.vjp(rms_scale, hidden, gain_ffn)
    normed_two_low = normed_two.astype(jnp.bfloat16)
    inner = mm(normed_two_low, w_in)
    activ_low = jnp.maximum(inner, 0.0).astype(jnp.bfloat16)
    output = hidden + mm(activ_low, w_ffout)
    final_norm, back_final = jax.vjp(rms_scale, output, gain_final)
    member = (segment[:, :, None] == jnp.arange(item_count, dtype=jnp.int32)).astype(jnp.float32)
    count_f = lengths[0].astype(jnp.float32)[:, :, None]
    pooled_low = (
        jnp.einsum(
            "btc,btf->bcf",
            member,
            final_norm.reshape(micro_count, length, model_width),
            precision=highest,
        )
        / count_f
    ).astype(jnp.bfloat16)
    pooled_flat = pooled_low.reshape(micro_count * item_count, model_width)
    embed = mm(pooled_flat, w_proj)
    unit_embed, back_unit = jax.vjp(unit_rows, embed)

    every = unit_embed[None]
    for b in reversed(gather_order):
        every = join(every, net.swap(every, b), net.bit(b))
    every = every.reshape((2,) * bits + (micro_count, item_count, model_width))
    place = [bits - 1 - b for b in gather_order]
    every = jnp.transpose(
        every,
        [bits]
        + [gather_order.index(b) for b in reversed(range(bits))]
        + [bits + 1, bits + 2],
    ).reshape(micro_count, 2, row_count, model_width)
    queries_all = every[:, 0]
    passages_all = every[:, 1]
    columns = jnp.arange(row_count, dtype=jnp.int32)[None, :]
    loss_sum = jnp.zeros((), jnp.float32)
    grad_embed = []
    for m in range(micro_count):
        logits = logit_scale * jnp.dot(queries_all[m], passages_all[m].T, precision=highest)
        target_hot = (columns == positives[m][:, None]).astype(jnp.float32)
        loss_part, grad_logits = softmax_terms(logits, target_hot)
        loss_sum = loss_sum + loss_part
        own_rows = lax.dynamic_slice_in_dim(grad_logits, dp_index * item_count, item_count, 0)
        own_cols = lax.dynamic_slice_in_dim(grad_logits, dp_index * item_count, item_count, 1)
        own = jnp.where(tower_index == 0, own_rows, own_cols.T)
        others = jnp.where(tower_index == 0, passages_all[m], queries_all[m])
        grad_embed.append(logit_scale * jnp.dot(own, others, precision=highest))
    grad_embed = jnp.concatenate(grad_embed, axis=0)
    (grad_e,) = back_unit(grad_embed)
    grad_e_low = grad_e.astype(jnp.bfloat16)
    grad_pooled = mm_t(grad_e_low, w_proj).reshape(micro_count, item_count, model_width)
    grad_final_norm = jnp.einsum(
        "btc,bcf->btf", member, grad_pooled / count_f, precision=highest
    ).reshape(rows, model_width)
    grad_output, grad_gain_final = back_final(grad_final_norm)
    grad_output_low = grad_output.astype(jnp.bfloat16)

    def halves(left, right, core_bit):
        wide = left.shape[1] // 2
        other = t_mm(
            lax.dynamic_slice_in_dim(left, (1 - core_bit) * wide, wide, 1), right
        )
        own = t_mm(lax.dynamic_slice_in_dim(left, core_bit * wide, wide, 1), right)
        return other, own

    core_bit = net.bit(core)
    if bits == 5:
        orders = (((0, 4, 1, 2, 3), (0, 1, 4, 2, 3)), ((0, 4, 2, 3, 1), (0, 1, 2, 3, 4)))
    else:
        orders = ((tuple(range(bits)),) * 2,) * 2

    def total(left, right, order):
        sent, kept = halves(left, right, core_bit)
        return gather_all(net, scatter_sum(net, sent, kept, order), order)

    ff_half = ff_width // 2
    whole_ffout = jnp.concatenate(
        [
            total(activ_low[:, :ff_half], grad_output_low, orders[0][0]),
            total(activ_low[:, ff_half:], grad_output_low, orders[0][1]),
        ],
        axis=0,
    )
    grad_activ = mm_t(grad_output_low, w_ffout)
    grad_inner_low = jnp.where(inner > 0, grad_activ, 0.0).astype(jnp.bfloat16)
    whole_in = jnp.concatenate(
        [
            total(normed_two_low, grad_inner_low[:, :ff_half], orders[1][0]),
            total(normed_two_low, grad_inner_low[:, ff_half:], orders[1][1]),
        ],
        axis=1,
    )
    grad_normed_two = mm_t(grad_inner_low, w_in)
    grad_hidden_norm, grad_gain_ffn = back_ffn(grad_normed_two)
    grad_hidden = grad_output + grad_hidden_norm
    grad_hidden_low = grad_hidden.astype(jnp.bfloat16)
    grad_mixed = heads(mm_t(grad_hidden_low, w_out).astype(jnp.bfloat16))
    probs_full = jnp.exp(scores_of() - log_norm)
    grad_probs = jnp.einsum(
        "bqhd,bkhd->bhqk", grad_mixed, value_h, preferred_element_type=jnp.float32
    )
    grad_scores = (
        probs_full * (grad_probs - jnp.sum(probs_full * grad_probs, axis=-1, keepdims=True))
    ).astype(jnp.bfloat16)

    def flat(value):
        return value.reshape(rows, model_width).astype(jnp.bfloat16)

    grad_query_h = flat(
        jnp.einsum("bhqk,bkhd->bqhd", grad_scores, key_h, preferred_element_type=jnp.float32)
    )
    grad_key_h = flat(
        jnp.einsum("bhqk,bqhd->bkhd", grad_scores, query_h, preferred_element_type=jnp.float32)
    )
    grad_value_h = flat(
        jnp.einsum(
            "bhqk,bqhd->bkhd",
            probs_full.astype(jnp.bfloat16),
            grad_mixed,
            preferred_element_type=jnp.float32,
        )
    )
    grad_bias = jnp.einsum(
        "hqk,qkn->nh", jnp.sum(grad_scores.astype(jnp.float32), axis=0), code_full,
    )
    grad_qkv = jnp.concatenate([grad_query_h, grad_key_h, grad_value_h], axis=1)
    grad_normed = (
        mm_t(grad_query_h, w_query) + mm_t(grad_key_h, w_key) + mm_t(grad_value_h, w_value)
    )
    cut = model_width // 2
    first_sent, first_kept = halves(normed_low, grad_qkv[:, : 5 * cut], core_bit)
    rest = [
        halves(normed_low, grad_qkv[:, 5 * cut :], core_bit),
        halves(mixed_low, grad_hidden_low, core_bit),
        halves(pooled_flat, grad_e_low, core_bit),
    ]
    last_sent = jnp.concatenate([r[0] for r in rest], axis=1)
    last_kept = jnp.concatenate([r[1] for r in rest], axis=1)
    order = orders[0][0]
    whole_first = gather_all(net, scatter_sum(net, first_sent, first_kept, order), order)
    order = orders[0][1]
    whole_last = gather_all(net, scatter_sum(net, last_sent, last_kept, order), order)

    grad_states_norm, grad_gain_attn = back_attn(grad_normed)
    grad_states = grad_hidden + grad_states_norm
    small = jnp.concatenate(
        [
            grad_gain_attn,
            grad_gain_ffn,
            grad_gain_final,
            grad_bias.reshape(-1),
            jnp.zeros((model_width - bucket_count * head_count,), jnp.float32),
        ]
    ).reshape(-1, 128)
    small = sum_small(net, small, tuple(range(bits))).reshape(-1)
    loss = loss_sum / (micro_count * row_count)
    width = model_width
    return (
        loss,
        unit_embed.reshape(1, micro_count, item_count, model_width),
        grad_states.reshape(1, micro_count, length, model_width),
        whole_first[:, :width],
        whole_first[:, width : 2 * width],
        jnp.concatenate([whole_first[:, 2 * width :], whole_last[:, :cut]], axis=1),
        whole_last[:, cut : cut + width],
        whole_in,
        whole_ffout,
        whole_last[:, cut + width :],
        small[:width],
        small[width : 2 * width],
        small[2 * width : 3 * width],
        small[3 * width : 3 * width + bucket_count * head_count].reshape(
            bucket_count, head_count
        ),
    )


def solution(mesh):
    return jax.shard_map(
        local,
        mesh=mesh,
        in_specs=(
            P("tower", None, "dp", None),
            P("tower", None, "dp"),
            P("tower", None, "dp"),
        )
        + (P(),) * 12,
        out_specs=(P(), P("tower", None, "dp", None), P("tower", None, "dp", None)) + (P(),) * 11,
        check_vma=False,
    )
```

time: 1500 us -> 789 us (0.53)
  waiting for transfers between devices: 805 us -> 293 us
  blocking collectives: 165 us -> 0 us
  starting transfers between devices: 0.33 us -> 57.9 us
  matrix products: 238 us -> 185 us
  local copies, waits for them, and re-layouts: 169 us -> 122 us
  other arithmetic: 91.9 us -> 120 us
    unnamed x9 -> x0, waiting for transfers between devices: 461 us -> none
    all_gather x7 -> x0, waiting for transfers between devices: 343 us -> none  [the longest x1 80.4 us: local(): lax.all_gather(grad_acc[4], ('tower', 'dp'), axis=0, tiled=True)]
    ppermute x0 -> x70, waiting for transfers between devices: none -> 293 us  [swap(): lax.ppermute(value, AXES, [(i, i ^ 1 << b) for i in range(self.size)])]
    all_gather x2 -> x0, blocking collectives: 84.9 us -> none  [micro_batch(): gathered = lax.all_gather(unit_embed, ('tower', 'dp'), axis=0, tiled=True)]
    unnamed x2 -> x0, blocking collectives: 79.9 us -> none
    reshape x21 -> x7, local copies, waits for them, and re-layouts: 94.6 us -> 15.8 us  [the longest x4 14.8 us: heads(): return value.reshape(micro_count, length, head_count, head_dim)]
    ppermute x0 -> x70, starting transfers between devices: none -> 57.9 us  [swap(): lax.ppermute(value, AXES, [(i, i ^ 1 << b) for i in range(self.size)])]
    dot_general x66 -> x43, matrix products: 224 us -> 173 us  [the longest x7 35.2 us: mm_t(): lax.dot_general(a, b, (((1,), (1,)), ((), ())), preferred_element_type=jn...]
  transfers between devices with their start and end apart: 8 -> 70, of which waited for: 7 -> 36; matrix products, arithmetic and copies ran while one was open for 3% -> 11% of each run, Pallas kernels for 0% -> 0%
where the time goes in v1:
time: 789 us; the launch traced here: 783 us
  waiting for transfers between devices  293 us (37%)
  matrix products  185 us (23%)
  local copies, waits for them, and re-layouts  122 us (15%)
  other arithmetic  120 us (15%)
  starting transfers between devices  57.9 us (7%)
    ppermute x70, waiting for transfers between devices, swap(): lax.ppermute(value, AXES, [(i, i ^ 1 << b) for i in range(self.size)])  293 us
    ppermute x70, starting transfers between devices, swap(): lax.ppermute(value, AXES, [(i, i ^ 1 << b) for i in range(self.size)])  57.9 us
    eq x1, local copies, waits for them, and re-layouts, local(): bucket[:, :, None]  45.2 us
    dot_general x7, matrix products, mm_t(): lax.dot_general(a, b, (((1,), (1,)), ((), ())), preferred_element_type=jn...  35.2 us
    dot_general x16, matrix products, t_mm(): lax.dot_general(a, b, (((0,), (0,)), ((), ())), preferred_element_type=jn...  33.6 us
    dot_general x7, matrix products, mm(): return jnp.dot(a, b, preferred_element_type=jnp.float32)  26.2 us
    reduce_sum x1, other arithmetic, local(): jnp.sum(grad_scores.astype(jnp.float32), axis=0)  21.8 us
    unnamed x157, local copies, waits for them, and re-layouts  19.6 us
  transfers between devices with their start and end apart: 70, of which 36 were waited for; matrix products, arithmetic and copies ran while one was open for 11% of the time, Pallas kernels for 0%

profile of v1, /device:TPU:0, one launch (start us, length us, event | category | flops | bytes accessed | tf_op | source)
XLA Modules:
  0.0 783.2 jit_solution(9390637897839568059)
XLA Ops:
  1.1 8.8 %iota_compare_fusion = pred[512,512,32]{0,2,1:T(32,128)(4,1)} fusion(s32[512,512]{0,1:T(8,128)S(1)} %fusion.63), kind=kLoop, calls=%fused_computation | loop fusion | flops 8388608 | bytes 9437184 | tf_op jit(solution)/shard_map/eq | solution.py:138
  9.9 45.2 %copy.81 = pred[512,512,32]{1,2,0:T(32,128)(4,1)S(1)} copy(pred[512,512,32]{0,2,1:T(32,128)(4,1)} %iota_compare_fusion) | data formatting | bytes 16777216 | tf_op jit(solution)/shard_map/eq | solution.py:138
  55.1 12.2 %convolution_bitcast_fusion = f32[12,512,512]{2,0,1:T(8,128)} fusion(pred[512,512,32]{1,2,0:T(32,128)(4,1)S(1)} %copy.81, f32[32,12]{0,1:T(8,128)S(1)} %copy-done.53), kind=kOutput, calls=%fused_computation.19 | convolution fusion | flops 1207959552 | bytes 20973056 | tf_op jit(solution)/shard_map/qkb,bh->hqk/dot_general | solution.py:140
  67.4 17.8 %copy.82 = f32[12,512,512]{1,2,0:T(8,128)} copy(f32[12,512,512]{2,0,1:T(8,128)} %convolution_bitcast_fusion) | data formatting | bytes 25165824 | tf_op jit(solution)/shard_map/qkb,bh->hqk/dot_general | solution.py:140
  93.6 4.2 reshape.260
  97.8 4.3 convolution_convert_fusion.4
  104.6 3.9 reshape.259
  108.9 3.9 convolution_convert_fusion.5
  115.4 3.8 reshape.258
  119.2 14.4 %fusion.131 = (f32[2,12,512]{2,1,0:T(8,128)S(1)}, f32[2,12,512,512]{2,3,1,0:T(8,128)}) fusion(f32[12,512,512]{1,2,0:T(8,128)} %copy.82, bf16[2,512,12,64]{1,0,3,2:T(2,128)(2,1)} %reshape.260, bf16[2,512,12,64]{1,0,3,2:T(2,128)(2,1)} %reshape.259, pred[2,512,512]{1,2,0:T(8,128)(4,1)S(1)} %broadcast_compare_fusion), kind=kOutput, calls=%fused_computation.378 | convolution fusion | flops 824168448 | bytes 41467904 | tf_op jit(solution)/shard_map/bqhd,bkhd->bhqk/dot_general | solution.py:158
  133.7 10.2 %fusion = f32[2,12,512]{2,1,0:T(8,128)S(1)} fusion(f32[2,12,512,512]{2,3,1,0:T(8,128)} %get-tuple-element.179, f32[2,12,512]{2,1,0:T(8,128)S(1)} %get-tuple-element.178), kind=kLoop, calls=%fused_computation.8 | loop fusion | flops 12570624 | bytes 25264128 | tf_op jit(solution)/shard_map/reduce_sum | solution.py:166
  143.9 10.6 %fusion.45 = bf16[2,512,12,64]{1,3,2,0:T(8,128)(2,1)S(1)} fusion(f32[2,12,512,512]{2,3,1,0:T(8,128)} %get-tuple-element.179, f32[2,12,512]{2,1,0:T(8,128)S(1)} %fusion, f32[2,12,512]{2,1,0:T(8,128)S(1)} %get-tuple-element.178, bf16[2,512,12,64]{1,0,3,2:T(2,128)(2,1)S(1)} %copy-done.18), kind=kOutput, calls=%fused_computation.98 | convolution fusion | flops 824967168 | bytes 28409856 | tf_op jit(solution)/shard_map/bhqk,bkhd->bqhd/dot_general | solution.py:170
  159.7 8.1 %maximum_convert_fusion = (bf16[1024,3072]{1,0:T(8,128)(2,1)S(1)}, f32[1024,3072]{1,0:T(8,128)}) fusion(bf16[1024,768]{1,0:T(8,128)(2,1)S(1)} %multiply_convert_fusion.1, bf16[768,3072]{1,0:T(8,128)(2,1)S(1)} %bitcast.229), kind=kOutput, calls=%fused_computation.15 | convolution fusion | flops 4838129664 | bytes 25165824 | tf_op jit(solution)/shard_map/dot_general | solution.py:44
  167.9 5.2 multiply_reduce_fusion.4
  176.6 4.1 collective-permute-start
  184.8 3.2 collective-permute-done.1
  189.9 3.9 collective-permute-done.2
  195.6 6.1 collective-permute-done.3
  202.0 5.9 fusion.130
  219.4 10.4 %select_convert_fusion = bf16[1024,3072]{1,0:T(8,128)(2,1)} fusion(f32[1024,3072]{1,0:T(8,128)} %get-tuple-element.183, bf16[1024,768]{1,0:T(8,128)(2,1)S(1)} %fusion.129, bf16[3072,768]{1,0:T(8,128)(2,1)S(1)} %bitcast.227), kind=kOutput, calls=%fused_computation.14 | convolution fusion | flops 4841275392 | bytes 25165824 | tf_op jit(solution)/shard_map/dot_general | solution.py:48
  229.9 9.0 %multiply_reduce_fusion.1 = (f32[768]{0:T(1024)S(1)}, f32[1024]{0:T(1024)S(1)}, f32[1024,768]{1,0:T(8,128)S(1)}) fusion(f32[1024,768]{1,0:T(8,128)S(1)} %copy-done.15, f32[1024]{0:T(1024)S(1)} %fusion.120, f32[768]{0:T(1024)S(1)} %copy-done.51, bf16[1024,3072]{1,0:T(8,128)(2,1)} %select_convert_fusion, bf16[768,3072]{1,0:T(8,128)(2,1)} %param.23), kind=kOutput, calls=%fused_computation.45 | convolution fusion | flops 4836554752 | bytes 17315840 | tf_op jit(solution)/shard_map/dot_general | solution.py:48
  245.3 2.9 reshape.268
  248.2 11.5 %fusion.40 = bf16[2,512,12,64]{1,3,2,0:T(8,128)(2,1)} fusion(f32[2,12,512,512]{2,3,1,0:T(8,128)} %get-tuple-element.179, f32[2,12,512]{2,1,0:T(8,128)S(1)} %log_add_fusion, bf16[2,512,12,64]{1,0,3,2:T(2,128)(2,1)S(1)} %reshape.268), kind=kOutput, calls=%fused_computation.95 | convolution fusion | flops 818675712 | bytes 28360704 | tf_op jit(solution)/shard_map/bhqk,bqhd->bkhd/dot_general | solution.py:290
  259.7 16.0 %multiply_reduce_fusion = (f32[2,12,512]{2,1,0:T(8,128)S(1)}, f32[2,12,512,512]{2,3,1,0:T(8,128)}) fusion(f32[2,12,512,512]{2,3,1,0:T(8,128)} %get-tuple-element.179, f32[2,12,512]{2,1,0:T(8,128)S(1)} %log_add_fusion, bf16[2,512,12,64]{1,0,3,2:T(2,128)(2,1)} %reshape.258, bf16[2,512,12,64]{1,0,3,2:T(2,128)(2,1)S(1)} %reshape.268), kind=kOutput, calls=%fused_computation.3 | convolution fusion | flops 824168448 | bytes 53575680 | tf_op jit(solution)/shard_map/bqhd,bkhd->bhqk/dot_general | solution.py:273
  275.7 21.8 %convert_reduce_fusion = (bf16[12,512,512]{1,2,0:T(8,128)(2,1)}, bf16[2,12,512,512]{2,3,1,0:T(8,128)(2,1)S(1)}) fusion(f32[2,12,512,512]{2,3,1,0:T(8,128)} %get-tuple-element.194, f32[2,12,512]{2,1,0:T(8,128)S(1)} %get-tuple-element.193, f32[2,12,512,512]{2,3,1,0:T(8,128)} %get-tuple-element.179, f32[2,12,512]{2,1,0:T(8,128)S(1)} %log_add_fusion), kind=kLoop, calls=%fused_computation.1 | loop fusion | flops 34603008 | bytes 69304320 | tf_op jit(solution)/shard_map/reduce_sum | solution.py:298
  297.5 4.6 copy-done.1
  302.1 4.5 fusion.43
  306.6 9.1 %fusion.44 = bf16[2,512,12,64]{1,3,2,0:T(8,128)(2,1)S(1)} fusion(bf16[2,12,512,512]{2,3,1,0:T(8,128)(2,1)} %copy-done.1, bf16[2,512,12,64]{1,0,3,2:T(2,128)(2,1)} %reshape.259), kind=kOutput, calls=%fused_computation.97 | convolution fusion | flops 806092800 | bytes 15728640 | tf_op jit(solution)/shard_map/bhqk,bqhd->bkhd/dot_general | solution.py:287
  321.7 3.2 fusion.134
  327.7 3.6 fusion.135
  334.2 3.5 fusion.56
  337.7 3.5 fusion.55
  349.7 2.9 fusion.32
  355.4 3.1 fusion.36
  358.5 2.9 fusion.38
  361.8 7.6 fusion.60
  369.6 5.8 fusion.14
  397.7 3.2 dynamic-slice_add_fusion.9
  421.7 8.3 %collective-permute-done.36 = f32[192,1536]{1,0:T(8,128)} collective-permute-done((f32[192,1536]{1,0:T(8,128)}, f32[192,1536]{1,0:T(8,128)}, u32[]{:S(2)}, u32[]{:S(2)}) %collective-permute-start.36) | collective-permute-done | bytes 1179680 | tf_op jit(solution)/shard_map/ppermute | solution.py:65
  438.8 16.3 %collective-permute-done.56 = f32[384,768]{1,0:T(8,128)S(1)} collective-permute-done((f32[384,768]{1,0:T(8,128)S(1)}, f32[384,768]{1,0:T(8,128)S(1)}, u32[]{:S(2)}, u32[]{:S(2)}) %collective-permute-start.56) | collective-permute-done | bytes 1179680 | tf_op jit(solution)/shard_map/ppermute | solution.py:65
  462.3 39.1 %collective-permute-done.57 = f32[192,768]{1,0:T(8,128)S(1)} collective-permute-done((f32[192,768]{1,0:T(8,128)S(1)}, f32[192,768]{1,0:T(8,128)S(1)}, u32[]{:S(2)}, u32[]{:S(2)}) %collective-permute-start.57) | collective-permute-done | bytes 589856 | tf_op jit(solution)/shard_map/ppermute | solution.py:65
  506.0 10.0 %collective-permute-done.28 = f32[48,1536]{1,0:T(8,128)S(1)} collective-permute-done((f32[48,1536]{1,0:T(8,128)S(1)}, f32[48,1536]{1,0:T(8,128)S(1)}, u32[]{:S(2)}, u32[]{:S(2)}) %collective-permute-start.28) | collective-permute-done | bytes 294944 | tf_op jit(solution)/shard_map/ppermute | solution.py:65
  519.2 3.4 collective-permute-done.48
  528.5 5.1 collective-permute-done.59
  535.9 8.3 %collective-permute-done.40 = f32[24,1536]{1,0:T(8,128)S(1)} collective-permute-done((f32[24,1536]{1,0:T(8,128)S(1)}, f32[24,1536]{1,0:T(8,128)S(1)}, u32[]{:S(2)}, u32[]{:S(2)}) %collective-permute-start.40) | collective-permute-done | bytes 147488 | tf_op jit(solution)/shard_map/ppermute | solution.py:65
  547.3 14.1 %collective-permute-done.60 = f32[48,768]{1,0:T(8,128)S(1)} collective-permute-done((f32[48,768]{1,0:T(8,128)S(1)}, f32[48,768]{1,0:T(8,128)S(1)}, u32[]{:S(2)}, u32[]{:S(2)}) %collective-permute-start.60) | collective-permute-done | bytes 147488 | tf_op jit(solution)/shard_map/ppermute | solution.py:65
  561.5 3.1 collective-permute-done.50
  564.7 6.4 collective-permute-done.41
  571.1 5.6 collective-permute-done.31
  576.8 6.2 collective-permute-done.61
  589.4 33.1 %collective-permute-done.18 = f32[48,1920]{1,0:T(8,128)S(1)} collective-permute-done((f32[48,1920]{1,0:T(8,128)S(1)}, f32[48,1920]{1,0:T(8,128)S(1)}, u32[]{:S(2)}, u32[]{:S(2)}) %collective-permute-start.18) | collective-permute-done | bytes 368672 | tf_op jit(solution)/shard_map/ppermute | solution.py:65
  622.5 7.8 collective-permute-done.8
  630.3 3.0 collective-permute-start.9
  635.1 3.6 collective-permute-done.52
  638.9 5.9 collective-permute-done.19
  648.6 8.4 %collective-permute-done.20 = f32[24,1920]{1,0:T(8,128)S(1)} collective-permute-done((f32[24,1920]{1,0:T(8,128)S(1)}, f32[24,1920]{1,0:T(8,128)S(1)}, u32[]{:S(2)}, u32[]{:S(2)}) %collective-permute-start.20) | collective-permute-done | bytes 184352 | tf_op jit(solution)/shard_map/ppermute | solution.py:65
  657.1 9.9 %collective-permute-done.10 = f32[24,1920]{1,0:T(8,128)S(1)} collective-permute-done((f32[24,1920]{1,0:T(8,128)S(1)}, f32[24,1920]{1,0:T(8,128)S(1)}, u32[]{:S(2)}, u32[]{:S(2)}) %collective-permute-start.10) | collective-permute-done | bytes 184352 | tf_op jit(solution)/shard_map/ppermute | solution.py:65
  667.1 10.4 %collective-permute-done.21 = f32[48,1920]{1,0:T(8,128)S(1)} collective-permute-done((f32[48,1920]{1,0:T(8,128)S(1)}, f32[48,1920]{1,0:T(8,128)S(1)}, u32[]{:S(2)}, u32[]{:S(2)}) %collective-permute-start.21) | collective-permute-done | bytes 368672 | tf_op jit(solution)/shard_map/ppermute | solution.py:65
  678.0 9.2 %collective-permute-done.11 = f32[48,1920]{1,0:T(8,128)S(1)} collective-permute-done((f32[48,1920]{1,0:T(8,128)S(1)}, f32[48,1920]{1,0:T(8,128)S(1)}, u32[]{:S(2)}, u32[]{:S(2)}) %collective-permute-start.11) | collective-permute-done | bytes 368672 | tf_op jit(solution)/shard_map/ppermute | solution.py:65
  689.4 14.5 %collective-permute-done.22 = f32[96,1920]{1,0:T(8,128)S(1)} collective-permute-done((f32[96,1920]{1,0:T(8,128)S(1)}, f32[96,1920]{1,0:T(8,128)S(1)}, u32[]{:S(2)}, u32[]{:S(2)}) %collective-permute-start.22) | collective-permute-done | bytes 737312 | tf_op jit(solution)/shard_map/ppermute | solution.py:65
  706.6 32.2 %collective-permute-done.23 = f32[192,1920]{1,0:T(8,128)S(1)} collective-permute-done((f32[192,1920]{1,0:T(8,128)S(1)}, f32[192,1920]{1,0:T(8,128)S(1)}, u32[]{:S(2)}, u32[]{:S(2)}) %collective-permute-start.23) | collective-permute-done | bytes 1474592 | tf_op jit(solution)/shard_map/ppermute | solution.py:65
  754.8 8.5 %maximum_maximum_fusion = f32[768,3072]{1,0:T(8,128)} fusion(f32[384,1536]{1,0:T(8,128)} %get-tuple-element.86, f32[384,1536]{1,0:T(8,128)} %get-tuple-element.85, f32[384,1536]{1,0:T(8,128)} %get-tuple-element.82, f32[384,1536]{1,0:T(8,128)} %get-tuple-element.81), kind=kLoop, calls=%fused_computation.17 | loop fusion | flops 7077888 | bytes 18874368 | tf_op jit(solution)/shard_map/concatenate | solution.py:260
  763.3 8.4 %pad_maximum_fusion = f32[3072,768]{1,0:T(8,128)} fusion(f32[768,768]{1,0:T(8,128)} %get-tuple-element.78, f32[768,768]{1,0:T(8,128)} %get-tuple-element.77, f32[768,768]{1,0:T(8,128)} %get-tuple-element.74, f32[768,768]{1,0:T(8,128)} %get-tuple-element.73), kind=kLoop, calls=%fused_computation.18 | loop fusion | flops 7077888 | bytes 18874368 | tf_op jit(solution)/shard_map/concatenate | solution.py:251
  776.6 5.2 pad_maximum_fusion.7
  (444 shorter events, 187.2 us)
Async XLA Ops:
  176.6 6.7 collective-permute-start
  188.1 5.7 collective-permute-start.2
  193.9 7.8 %collective-permute-start.3 = (f32[8,16,768]{2,1,0:T(8,128)S(1)}, f32[8,16,768]{2,1,0:T(8,128)S(1)}, u32[]{:S(2)}, u32[]{:S(2)}) collective-permute-start(f32[8,16,768]{2,1,0:T(8,128)S(1)} %pad_maximum_fusion.31), channel_id=1, source_target_pairs={{0,16},{1,17},{2,18},{3,19},{4,20},{5,21},{6,22},{7,23},{8,24},{9,... | collective-permute-start | bytes 1179656 | tf_op jit(solution)/shard_map/ppermute | solution.py:65
  201.8 6.1 collective-permute-start.4
  361.4 33.2 %collective-permute-start.35 = (f32[384,1536]{1,0:T(8,128)}, f32[384,1536]{1,0:T(8,128)}, u32[]{:S(2)}, u32[]{:S(2)}) collective-permute-start(f32[384,1536]{1,0:T(8,128)} %fusion.17), channel_id=1, source_target_pairs={{0,1},{1,0},{2,3},{3,2},{4,5},{5,4},{6,7},{7,6},{8,9},{9,8},{10,11... | collective-permute-start | bytes 7077896 | tf_op jit(solution)/shard_map/ppermute | solution.py:65
  380.1 20.7 %collective-permute-start.25 = (f32[384,1536]{1,0:T(8,128)S(1)}, f32[384,1536]{1,0:T(8,128)S(1)}, u32[]{:S(2)}, u32[]{:S(2)}) collective-permute-start(f32[384,1536]{1,0:T(8,128)S(1)} %copy-done.57), channel_id=1, source_target_pairs={{0,1},{1,0},{2,3},{3,2},{4,5},{5,4},{6,7},{7,6},{8,9},{9,8},{10,11... | collective-permute-start | bytes 7077896 | tf_op jit(solution)/shard_map/ppermute | solution.py:65
  380.2 23.7 %collective-permute-start.55 = (f32[768,768]{1,0:T(8,128)S(1)}, f32[768,768]{1,0:T(8,128)S(1)}, u32[]{:S(2)}, u32[]{:S(2)}) collective-permute-start(f32[768,768]{1,0:T(8,128)S(1)} %copy-done.56), channel_id=1, source_target_pairs={{0,1},{1,0},{2,3},{3,2},{4,5},{5,4},{6,7},{7,6},{8,9},{9,8},{10,11... | collective-permute-start | bytes 7077896 | tf_op jit(solution)/shard_map/ppermute | solution.py:65
  384.9 34.0 %collective-permute-start.15 = (f32[384,1920]{1,0:T(8,128)}, f32[384,1920]{1,0:T(8,128)}, u32[]{:S(2)}, u32[]{:S(2)}) collective-permute-start(f32[384,1920]{1,0:T(8,128)} %pad_maximum_fusion.5), channel_id=1, source_target_pairs={{0,1},{1,0},{2,3},{3,2},{4,5},{5,4},{6,7},{7,6},{8,9},{9,8},{10,11... | collective-permute-start | bytes 8847368 | tf_op jit(solution)/shard_map/ppermute | solution.py:65
  393.7 22.3 %collective-permute-start.45 = (f32[768,768]{1,0:T(8,128)}, f32[768,768]{1,0:T(8,128)}, u32[]{:S(2)}, u32[]{:S(2)}) collective-permute-start(f32[768,768]{1,0:T(8,128)} %fusion.36), channel_id=1, source_target_pairs={{0,1},{1,0},{2,3},{3,2},{4,5},{5,4},{6,7},{7,6},{8,9},{9,8},{10,11... | collective-permute-start | bytes 7077896 | tf_op jit(solution)/shard_map/ppermute | solution.py:65
  394.6 41.2 %collective-permute-start.5 = (f32[384,1920]{1,0:T(8,128)}, f32[384,1920]{1,0:T(8,128)}, u32[]{:S(2)}, u32[]{:S(2)}) collective-permute-start(f32[384,1920]{1,0:T(8,128)} %fusion.56), channel_id=1, source_target_pairs={{0,1},{1,0},{2,3},{3,2},{4,5},{5,4},{6,7},{7,6},{8,9},{9,8},{10,11... | collective-permute-start | bytes 8847368 | tf_op jit(solution)/shard_map/ppermute | solution.py:65
  400.8 29.2 %collective-permute-start.36 = (f32[192,1536]{1,0:T(8,128)}, f32[192,1536]{1,0:T(8,128)}, u32[]{:S(2)}, u32[]{:S(2)}) collective-permute-start(f32[192,1536]{1,0:T(8,128)} %get-tuple-element.88), channel_id=1, source_target_pairs={{0,2},{1,3},{2,0},{3,1},{4,6},{5,7},{6,4},{7,5},{8,10},{9,11},{10,... | collective-permute-start | bytes 3538952 | tf_op jit(solution)/shard_map/ppermute | solution.py:65
  404.0 29.2 %collective-permute-start.26 = (f32[192,1536]{1,0:T(8,128)}, f32[192,1536]{1,0:T(8,128)}, u32[]{:S(2)}, u32[]{:S(2)}) collective-permute-start(f32[192,1536]{1,0:T(8,128)} %get-tuple-element.84), channel_id=1, source_target_pairs={{0,16},{1,17},{2,18},{3,19},{4,20},{5,21},{6,22},{7,23},{8,24},{9,... | collective-permute-start | bytes 3538952 | tf_op jit(solution)/shard_map/ppermute | solution.py:65
  416.1 39.1 %collective-permute-start.56 = (f32[384,768]{1,0:T(8,128)S(1)}, f32[384,768]{1,0:T(8,128)S(1)}, u32[]{:S(2)}, u32[]{:S(2)}) collective-permute-start(f32[384,768]{1,0:T(8,128)S(1)} %get-tuple-element.80), channel_id=1, source_target_pairs={{0,2},{1,3},{2,0},{3,1},{4,6},{5,7},{6,4},{7,5},{8,10},{9,11},{10,... | collective-permute-start | bytes 3538952 | tf_op jit(solution)/shard_map/ppermute | solution.py:65
  418.9 39.3 %collective-permute-start.46 = (f32[384,768]{1,0:T(8,128)S(1)}, f32[384,768]{1,0:T(8,128)S(1)}, u32[]{:S(2)}, u32[]{:S(2)}) collective-permute-start(f32[384,768]{1,0:T(8,128)S(1)} %get-tuple-element.76), channel_id=1, source_target_pairs={{0,16},{1,17},{2,18},{3,19},{4,20},{5,21},{6,22},{7,23},{8,24},{9,... | collective-permute-start | bytes 3538952 | tf_op jit(solution)/shard_map/ppermute | solution.py:65
  430.0 93.6 %collective-permute-start.16 = (f32[192,1920]{1,0:T(8,128)S(1)}, f32[192,1920]{1,0:T(8,128)S(1)}, u32[]{:S(2)}, u32[]{:S(2)}) collective-permute-start(f32[192,1920]{1,0:T(8,128)S(1)} %get-tuple-element.68), channel_id=1, source_target_pairs={{0,2},{1,3},{2,0},{3,1},{4,6},{5,7},{6,4},{7,5},{8,10},{9,11},{10,... | collective-permute-start | bytes 4423688 | tf_op jit(solution)/shard_map/ppermute | solution.py:65
  433.1 26.5 %collective-permute-start.37 = (f32[96,1536]{1,0:T(8,128)S(1)}, f32[96,1536]{1,0:T(8,128)S(1)}, u32[]{:S(2)}, u32[]{:S(2)}) collective-permute-start(f32[96,1536]{1,0:T(8,128)S(1)} %get-tuple-element.112), channel_id=1, source_target_pairs={{0,4},{1,5},{2,6},{3,7},{4,0},{5,1},{6,2},{7,3},{8,12},{9,13},{10,... | collective-permute-start | bytes 1769480 | tf_op jit(solution)/shard_map/ppermute | solution.py:65
  435.8 23.9 %collective-permute-start.27 = (f32[96,1536]{1,0:T(8,128)S(1)}, f32[96,1536]{1,0:T(8,128)S(1)}, u32[]{:S(2)}, u32[]{:S(2)}) collective-permute-start(f32[96,1536]{1,0:T(8,128)S(1)} %get-tuple-element.108), channel_id=1, source_target_pairs={{0,4},{1,5},{2,6},{3,7},{4,0},{5,1},{6,2},{7,3},{8,12},{9,13},{10,... | collective-permute-start | bytes 1769480 | tf_op jit(solution)/shard_map/ppermute | solution.py:65
  455.2 70.8 %collective-permute-start.6 = (f32[192,1920]{1,0:T(8,128)S(1)}, f32[192,1920]{1,0:T(8,128)S(1)}, u32[]{:S(2)}, u32[]{:S(2)}) collective-permute-start(f32[192,1920]{1,0:T(8,128)S(1)} %get-tuple-element.72), channel_id=1, source_target_pairs={{0,16},{1,17},{2,18},{3,19},{4,20},{5,21},{6,22},{7,23},{8,24},{9,... | collective-permute-start | bytes 4423688 | tf_op jit(solution)/shard_map/ppermute | solution.py:65
  458.2 43.2 %collective-permute-start.57 = (f32[192,768]{1,0:T(8,128)S(1)}, f32[192,768]{1,0:T(8,128)S(1)}, u32[]{:S(2)}, u32[]{:S(2)}) collective-permute-start(f32[192,768]{1,0:T(8,128)S(1)} %get-tuple-element.104), channel_id=1, source_target_pairs={{0,16},{1,17},{2,18},{3,19},{4,20},{5,21},{6,22},{7,23},{8,24},{9,... | collective-permute-start | bytes 1769480 | tf_op jit(solution)/shard_map/ppermute | solution.py:65
  459.6 44.2 %collective-permute-start.47 = (f32[192,768]{1,0:T(8,128)S(1)}, f32[192,768]{1,0:T(8,128)S(1)}, u32[]{:S(2)}, u32[]{:S(2)}) collective-permute-start(f32[192,768]{1,0:T(8,128)S(1)} %get-tuple-element.100), channel_id=1, source_target_pairs={{0,2},{1,3},{2,0},{3,1},{4,6},{5,7},{6,4},{7,5},{8,10},{9,11},{10,... | collective-permute-start | bytes 1769480 | tf_op jit(solution)/shard_map/ppermute | solution.py:65
  459.8 46.0 %collective-permute-start.38 = (f32[48,1536]{1,0:T(8,128)S(1)}, f32[48,1536]{1,0:T(8,128)S(1)}, u32[]{:S(2)}, u32[]{:S(2)}) collective-permute-start(f32[48,1536]{1,0:T(8,128)S(1)} %get-tuple-element.138), channel_id=1, source_target_pairs={{0,8},{1,9},{2,10},{3,11},{4,12},{5,13},{6,14},{7,15},{8,0},{9,1},... | collective-permute-start | bytes 884744 | tf_op jit(solution)/shard_map/ppermute | solution.py:65
  501.3 14.7 %collective-permute-start.28 = (f32[48,1536]{1,0:T(8,128)S(1)}, f32[48,1536]{1,0:T(8,128)S(1)}, u32[]{:S(2)}, u32[]{:S(2)}) collective-permute-start(f32[48,1536]{1,0:T(8,128)S(1)} %get-tuple-element.134), channel_id=1, source_target_pairs={{0,8},{1,9},{2,10},{3,11},{4,12},{5,13},{6,14},{7,15},{8,0},{9,1},... | collective-permute-start | bytes 884744 | tf_op jit(solution)/shard_map/ppermute | solution.py:65
  503.8 15.4 %collective-permute-start.58 = (f32[96,768]{1,0:T(8,128)S(1)}, f32[96,768]{1,0:T(8,128)S(1)}, u32[]{:S(2)}, u32[]{:S(2)}) collective-permute-start(f32[96,768]{1,0:T(8,128)S(1)} %get-tuple-element.130), channel_id=1, source_target_pairs={{0,4},{1,5},{2,6},{3,7},{4,0},{5,1},{6,2},{7,3},{8,12},{9,13},{10,... | collective-permute-start | bytes 884744 | tf_op jit(solution)/shard_map/ppermute | solution.py:65
  505.8 16.8 %collective-permute-start.48 = (f32[96,768]{1,0:T(8,128)S(1)}, f32[96,768]{1,0:T(8,128)S(1)}, u32[]{:S(2)}, u32[]{:S(2)}) collective-permute-start(f32[96,768]{1,0:T(8,128)S(1)} %get-tuple-element.126), channel_id=1, source_target_pairs={{0,4},{1,5},{2,6},{3,7},{4,0},{5,1},{6,2},{7,3},{8,12},{9,13},{10,... | collective-permute-start | bytes 884744 | tf_op jit(solution)/shard_map/ppermute | solution.py:65
  516.0 11.5 %collective-permute-start.39 = (f32[24,1536]{1,0:T(8,128)S(1)}, f32[24,1536]{1,0:T(8,128)S(1)}, u32[]{:S(2)}, u32[]{:S(2)}) collective-permute-start(f32[24,1536]{1,0:T(8,128)S(1)} %dynamic-slice_add_fusion.40), channel_id=1, source_target_pairs={{0,16},{1,17},{2,18},{3,19},{4,20},{5,21},{6,22},{7,23},{8,24},{9,... | collective-permute-start | bytes 442376 | tf_op jit(solution)/shard_map/ppermute | solution.py:65
  519.2 8.4 %collective-permute-start.29 = (f32[24,1536]{1,0:T(8,128)S(1)}, f32[24,1536]{1,0:T(8,128)S(1)}, u32[]{:S(2)}, u32[]{:S(2)}) collective-permute-start(f32[24,1536]{1,0:T(8,128)S(1)} %dynamic-slice_add_fusion.41), channel_id=1, source_target_pairs={{0,2},{1,3},{2,0},{3,1},{4,6},{5,7},{6,4},{7,5},{8,10},{9,11},{10,... | collective-permute-start | bytes 442376 | tf_op jit(solution)/shard_map/ppermute | solution.py:65
  522.6 11.0 %collective-permute-start.59 = (f32[48,768]{1,0:T(8,128)S(1)}, f32[48,768]{1,0:T(8,128)S(1)}, u32[]{:S(2)}, u32[]{:S(2)}) collective-permute-start(f32[48,768]{1,0:T(8,128)S(1)} %dynamic-slice_add_fusion.38), channel_id=1, source_target_pairs={{0,8},{1,9},{2,10},{3,11},{4,12},{5,13},{6,14},{7,15},{8,0},{9,1},... | collective-permute-start | bytes 442376 | tf_op jit(solution)/shard_map/ppermute | solution.py:65
  523.6 12.3 %collective-permute-start.49 = (f32[48,768]{1,0:T(8,128)S(1)}, f32[48,768]{1,0:T(8,128)S(1)}, u32[]{:S(2)}, u32[]{:S(2)}) collective-permute-start(f32[48,768]{1,0:T(8,128)S(1)} %dynamic-slice_add_fusion.39), channel_id=1, source_target_pairs={{0,8},{1,9},{2,10},{3,11},{4,12},{5,13},{6,14},{7,15},{8,0},{9,1},... | collective-permute-start | bytes 442376 | tf_op jit(solution)/shard_map/ppermute | solution.py:65
  526.0 57.2 %collective-permute-start.17 = (f32[96,1920]{1,0:T(8,128)S(1)}, f32[96,1920]{1,0:T(8,128)S(1)}, u32[]{:S(2)}, u32[]{:S(2)}) collective-permute-start(f32[96,1920]{1,0:T(8,128)S(1)} %get-tuple-element.92), channel_id=1, source_target_pairs={{0,16},{1,17},{2,18},{3,19},{4,20},{5,21},{6,22},{7,23},{8,24},{9,... | collective-permute-start | bytes 2211848 | tf_op jit(solution)/shard_map/ppermute | solution.py:65
  527.5 56.9 %collective-permute-start.7 = (f32[96,1920]{1,0:T(8,128)S(1)}, f32[96,1920]{1,0:T(8,128)S(1)}, u32[]{:S(2)}, u32[]{:S(2)}) collective-permute-start(f32[96,1920]{1,0:T(8,128)S(1)} %get-tuple-element.96), channel_id=1, source_target_pairs={{0,2},{1,3},{2,0},{3,1},{4,6},{5,7},{6,4},{7,5},{8,10},{9,11},{10,... | collective-permute-start | bytes 2211848 | tf_op jit(solution)/shard_map/ppermute | solution.py:65
  527.6 16.6 %collective-permute-start.40 = (f32[24,1536]{1,0:T(8,128)S(1)}, f32[24,1536]{1,0:T(8,128)S(1)}, u32[]{:S(2)}, u32[]{:S(2)}) collective-permute-start(f32[24,1536]{1,0:T(8,128)S(1)} %add_add_fusion.8), channel_id=1, source_target_pairs={{0,16},{1,17},{2,18},{3,19},{4,20},{5,21},{6,22},{7,23},{8,24},{9,... | collective-permute-start | bytes 442376 | tf_op jit(solution)/shard_map/ppermute | solution.py:65
  533.6 12.2 %collective-permute-start.30 = (f32[24,1536]{1,0:T(8,128)S(1)}, f32[24,1536]{1,0:T(8,128)S(1)}, u32[]{:S(2)}, u32[]{:S(2)}) collective-permute-start(f32[24,1536]{1,0:T(8,128)S(1)} %add_add_fusion.9), channel_id=1, source_target_pairs={{0,2},{1,3},{2,0},{3,1},{4,6},{5,7},{6,4},{7,5},{8,10},{9,11},{10,... | collective-permute-start | bytes 442376 | tf_op jit(solution)/shard_map/ppermute | solution.py:65
  535.9 25.5 %collective-permute-start.60 = (f32[48,768]{1,0:T(8,128)S(1)}, f32[48,768]{1,0:T(8,128)S(1)}, u32[]{:S(2)}, u32[]{:S(2)}) collective-permute-start(f32[48,768]{1,0:T(8,128)S(1)} %add_add_fusion.6), channel_id=1, source_target_pairs={{0,8},{1,9},{2,10},{3,11},{4,12},{5,13},{6,14},{7,15},{8,0},{9,1},... | collective-permute-start | bytes 442376 | tf_op jit(solution)/shard_map/ppermute | solution.py:65
  544.2 20.4 %collective-permute-start.50 = (f32[48,768]{1,0:T(8,128)S(1)}, f32[48,768]{1,0:T(8,128)S(1)}, u32[]{:S(2)}, u32[]{:S(2)}) collective-permute-start(f32[48,768]{1,0:T(8,128)S(1)} %add_add_fusion.7), channel_id=1, source_target_pairs={{0,8},{1,9},{2,10},{3,11},{4,12},{5,13},{6,14},{7,15},{8,0},{9,1},... | collective-permute-start | bytes 442376 | tf_op jit(solution)/shard_map/ppermute | solution.py:65
  545.8 25.2 %collective-permute-start.41 = (f32[48,1536]{1,0:T(8,128)S(1)}, f32[48,1536]{1,0:T(8,128)S(1)}, u32[]{:S(2)}, u32[]{:S(2)}) collective-permute-start(f32[48,1536]{1,0:T(8,128)S(1)} %pad_maximum_fusion.35), channel_id=1, source_target_pairs={{0,8},{1,9},{2,10},{3,11},{4,12},{5,13},{6,14},{7,15},{8,0},{9,1},... | collective-permute-start | bytes 884744 | tf_op jit(solution)/shard_map/ppermute | solution.py:65
  561.4 15.2 %collective-permute-start.31 = (f32[48,1536]{1,0:T(8,128)S(1)}, f32[48,1536]{1,0:T(8,128)S(1)}, u32[]{:S(2)}, u32[]{:S(2)}) collective-permute-start(f32[48,1536]{1,0:T(8,128)S(1)} %pad_maximum_fusion.34), channel_id=1, source_target_pairs={{0,8},{1,9},{2,10},{3,11},{4,12},{5,13},{6,14},{7,15},{8,0},{9,1},... | collective-permute-start | bytes 884744 | tf_op jit(solution)/shard_map/ppermute | solution.py:65
  564.6 18.4 %collective-permute-start.61 = (f32[96,768]{1,0:T(8,128)S(1)}, f32[96,768]{1,0:T(8,128)S(1)}, u32[]{:S(2)}, u32[]{:S(2)}) collective-permute-start(f32[96,768]{1,0:T(8,128)S(1)} %pad_maximum_fusion.37), channel_id=1, source_target_pairs={{0,4},{1,5},{2,6},{3,7},{4,0},{5,1},{6,2},{7,3},{8,12},{9,13},{10,... | collective-permute-start | bytes 884744 | tf_op jit(solution)/shard_map/ppermute | solution.py:65
  571.0 18.3 %collective-permute-start.51 = (f32[96,768]{1,0:T(8,128)S(1)}, f32[96,768]{1,0:T(8,128)S(1)}, u32[]{:S(2)}, u32[]{:S(2)}) collective-permute-start(f32[96,768]{1,0:T(8,128)S(1)} %pad_maximum_fusion.36), channel_id=1, source_target_pairs={{0,4},{1,5},{2,6},{3,7},{4,0},{5,1},{6,2},{7,3},{8,12},{9,13},{10,... | collective-permute-start | bytes 884744 | tf_op jit(solution)/shard_map/ppermute | solution.py:65
  576.7 53.7 %collective-permute-start.42 = (f32[96,1536]{1,0:T(8,128)S(1)}, f32[96,1536]{1,0:T(8,128)S(1)}, u32[]{:S(2)}, u32[]{:S(2)}) collective-permute-start(f32[96,1536]{1,0:T(8,128)S(1)} %pad_maximum_fusion.28), channel_id=1, source_target_pairs={{0,4},{1,5},{2,6},{3,7},{4,0},{5,1},{6,2},{7,3},{8,12},{9,13},{10,... | collective-permute-start | bytes 1769480 | tf_op jit(solution)/shard_map/ppermute | solution.py:65
  583.0 50.5 %collective-permute-start.32 = (f32[96,1536]{1,0:T(8,128)S(1)}, f32[96,1536]{1,0:T(8,128)S(1)}, u32[]{:S(2)}, u32[]{:S(2)}) collective-permute-start(f32[96,1536]{1,0:T(8,128)S(1)} %pad_maximum_fusion.27), channel_id=1, source_target_pairs={{0,4},{1,5},{2,6},{3,7},{4,0},{5,1},{6,2},{7,3},{8,12},{9,13},{10,... | collective-permute-start | bytes 1769480 | tf_op jit(solution)/shard_map/ppermute | solution.py:65
  583.1 50.7 %collective-permute-start.62 = (f32[192,768]{1,0:T(8,128)S(1)}, f32[192,768]{1,0:T(8,128)S(1)}, u32[]{:S(2)}, u32[]{:S(2)}) collective-permute-start(f32[192,768]{1,0:T(8,128)S(1)} %pad_maximum_fusion.30), channel_id=1, source_target_pairs={{0,16},{1,17},{2,18},{3,19},{4,20},{5,21},{6,22},{7,23},{8,24},{9,... | collective-permute-start | bytes 1769480 | tf_op jit(solution)/shard_map/ppermute | solution.py:65
  584.4 38.1 %collective-permute-start.18 = (f32[48,1920]{1,0:T(8,128)S(1)}, f32[48,1920]{1,0:T(8,128)S(1)}, u32[]{:S(2)}, u32[]{:S(2)}) collective-permute-start(f32[48,1920]{1,0:T(8,128)S(1)} %get-tuple-element.118), channel_id=1, source_target_pairs={{0,4},{1,5},{2,6},{3,7},{4,0},{5,1},{6,2},{7,3},{8,12},{9,13},{10,... | collective-permute-start | bytes 1105928 | tf_op jit(solution)/shard_map/ppermute | solution.py:65
  589.3 41.0 %collective-permute-start.8 = (f32[48,1920]{1,0:T(8,128)S(1)}, f32[48,1920]{1,0:T(8,128)S(1)}, u32[]{:S(2)}, u32[]{:S(2)}) collective-permute-start(f32[48,1920]{1,0:T(8,128)S(1)} %get-tuple-element.122), channel_id=1, source_target_pairs={{0,4},{1,5},{2,6},{3,7},{4,0},{5,1},{6,2},{7,3},{8,12},{9,13},{10,... | collective-permute-start | bytes 1105928 | tf_op jit(solution)/shard_map/ppermute | solution.py:65
  622.5 16.2 %collective-permute-start.52 = (f32[192,768]{1,0:T(8,128)S(1)}, f32[192,768]{1,0:T(8,128)S(1)}, u32[]{:S(2)}, u32[]{:S(2)}) collective-permute-start(f32[192,768]{1,0:T(8,128)S(1)} %pad_maximum_fusion.29), channel_id=1, source_target_pairs={{0,2},{1,3},{2,0},{3,1},{4,6},{5,7},{6,4},{7,5},{8,10},{9,11},{10,... | collective-permute-start | bytes 1769480 | tf_op jit(solution)/shard_map/ppermute | solution.py:65
  630.3 14.4 %collective-permute-start.19 = (f32[24,1920]{1,0:T(8,128)S(1)}, f32[24,1920]{1,0:T(8,128)S(1)}, u32[]{:S(2)}, u32[]{:S(2)}) collective-permute-start(f32[24,1920]{1,0:T(8,128)S(1)} %dynamic-slice_add_fusion.36), channel_id=1, source_target_pairs={{0,8},{1,9},{2,10},{3,11},{4,12},{5,13},{6,14},{7,15},{8,0},{9,1},... | collective-permute-start | bytes 552968 | tf_op jit(solution)/shard_map/ppermute | solution.py:65
  630.3 18.3 %collective-permute-start.9 = (f32[24,1920]{1,0:T(8,128)S(1)}, f32[24,1920]{1,0:T(8,128)S(1)}, u32[]{:S(2)}, u32[]{:S(2)}) collective-permute-start(f32[24,1920]{1,0:T(8,128)S(1)} %dynamic-slice_add_fusion.37), channel_id=1, source_target_pairs={{0,8},{1,9},{2,10},{3,11},{4,12},{5,13},{6,14},{7,15},{8,0},{9,1},... | collective-permute-start | bytes 552968 | tf_op jit(solution)/shard_map/ppermute | solution.py:65
  633.5 54.8 %collective-permute-start.43 = (f32[192,1536]{1,0:T(8,128)S(1)}, f32[192,1536]{1,0:T(8,128)S(1)}, u32[]{:S(2)}, u32[]{:S(2)}) collective-permute-start(f32[192,1536]{1,0:T(8,128)S(1)} %pad_maximum_fusion.21), channel_id=1, source_target_pairs={{0,2},{1,3},{2,0},{3,1},{4,6},{5,7},{6,4},{7,5},{8,10},{9,11},{10,... | collective-permute-start | bytes 3538952 | tf_op jit(solution)/shard_map/ppermute | solution.py:65
  633.8 55.1 %collective-permute-start.33 = (f32[192,1536]{1,0:T(8,128)S(1)}, f32[192,1536]{1,0:T(8,128)S(1)}, u32[]{:S(2)}, u32[]{:S(2)}) collective-permute-start(f32[192,1536]{1,0:T(8,128)S(1)} %pad_maximum_fusion.20), channel_id=1, source_target_pairs={{0,16},{1,17},{2,18},{3,19},{4,20},{5,21},{6,22},{7,23},{8,24},{9,... | collective-permute-start | bytes 3538952 | tf_op jit(solution)/shard_map/ppermute | solution.py:65
  638.7 65.4 %collective-permute-start.63 = (f32[384,768]{1,0:T(8,128)S(1)}, f32[384,768]{1,0:T(8,128)S(1)}, u32[]{:S(2)}, u32[]{:S(2)}) collective-permute-start(f32[384,768]{1,0:T(8,128)S(1)} %pad_maximum_fusion.23), channel_id=1, source_target_pairs={{0,2},{1,3},{2,0},{3,1},{4,6},{5,7},{6,4},{7,5},{8,10},{9,11},{10,... | collective-permute-start | bytes 3538952 | tf_op jit(solution)/shard_map/ppermute | solution.py:65
  644.7 61.5 %collective-permute-start.53 = (f32[384,768]{1,0:T(8,128)S(1)}, f32[384,768]{1,0:T(8,128)S(1)}, u32[]{:S(2)}, u32[]{:S(2)}) collective-permute-start(f32[384,768]{1,0:T(8,128)S(1)} %pad_maximum_fusion.22), channel_id=1, source_target_pairs={{0,16},{1,17},{2,18},{3,19},{4,20},{5,21},{6,22},{7,23},{8,24},{9,... | collective-permute-start | bytes 3538952 | tf_op jit(solution)/shard_map/ppermute | solution.py:65
  648.6 8.5 %collective-permute-start.20 = (f32[24,1920]{1,0:T(8,128)S(1)}, f32[24,1920]{1,0:T(8,128)S(1)}, u32[]{:S(2)}, u32[]{:S(2)}) collective-permute-start(f32[24,1920]{1,0:T(8,128)S(1)} %add_add_fusion.4), channel_id=1, source_target_pairs={{0,8},{1,9},{2,10},{3,11},{4,12},{5,13},{6,14},{7,15},{8,0},{9,1},... | collective-permute-start | bytes 552968 | tf_op jit(solution)/shard_map/ppermute | solution.py:65
  657.1 10.0 %collective-permute-start.10 = (f32[24,1920]{1,0:T(8,128)S(1)}, f32[24,1920]{1,0:T(8,128)S(1)}, u32[]{:S(2)}, u32[]{:S(2)}) collective-permute-start(f32[24,1920]{1,0:T(8,128)S(1)} %add_add_fusion.5), channel_id=1, source_target_pairs={{0,8},{1,9},{2,10},{3,11},{4,12},{5,13},{6,14},{7,15},{8,0},{9,1},... | collective-permute-start | bytes 552968 | tf_op jit(solution)/shard_map/ppermute | solution.py:65
  667.1 10.5 %collective-permute-start.21 = (f32[48,1920]{1,0:T(8,128)S(1)}, f32[48,1920]{1,0:T(8,128)S(1)}, u32[]{:S(2)}, u32[]{:S(2)}) collective-permute-start(f32[48,1920]{1,0:T(8,128)S(1)} %pad_maximum_fusion.33), channel_id=1, source_target_pairs={{0,4},{1,5},{2,6},{3,7},{4,0},{5,1},{6,2},{7,3},{8,12},{9,13},{10,... | collective-permute-start | bytes 1105928 | tf_op jit(solution)/shard_map/ppermute | solution.py:65
  677.5 9.6 %collective-permute-start.11 = (f32[48,1920]{1,0:T(8,128)S(1)}, f32[48,1920]{1,0:T(8,128)S(1)}, u32[]{:S(2)}, u32[]{:S(2)}) collective-permute-start(f32[48,1920]{1,0:T(8,128)S(1)} %pad_maximum_fusion.32), channel_id=1, source_target_pairs={{0,4},{1,5},{2,6},{3,7},{4,0},{5,1},{6,2},{7,3},{8,12},{9,13},{10,... | collective-permute-start | bytes 1105928 | tf_op jit(solution)/shard_map/ppermute | solution.py:65
  687.2 16.7 %collective-permute-start.22 = (f32[96,1920]{1,0:T(8,128)S(1)}, f32[96,1920]{1,0:T(8,128)S(1)}, u32[]{:S(2)}, u32[]{:S(2)}) collective-permute-start(f32[96,1920]{1,0:T(8,128)S(1)} %pad_maximum_fusion.26), channel_id=1, source_target_pairs={{0,16},{1,17},{2,18},{3,19},{4,20},{5,21},{6,22},{7,23},{8,24},{9,... | collective-permute-start | bytes 2211848 | tf_op jit(solution)/shard_map/ppermute | solution.py:65
  688.4 16.5 %collective-permute-start.12 = (f32[96,1920]{1,0:T(8,128)S(1)}, f32[96,1920]{1,0:T(8,128)S(1)}, u32[]{:S(2)}, u32[]{:S(2)}) collective-permute-start(f32[96,1920]{1,0:T(8,128)S(1)} %pad_maximum_fusion.25), channel_id=1, source_target_pairs={{0,2},{1,3},{2,0},{3,1},{4,6},{5,7},{6,4},{7,5},{8,10},{9,11},{10,... | collective-permute-start | bytes 2211848 | tf_op jit(solution)/shard_map/ppermute | solution.py:65
  688.9 55.6 %collective-permute-start.44 = (f32[384,1536]{1,0:T(8,128)S(1)}, f32[384,1536]{1,0:T(8,128)S(1)}, u32[]{:S(2)}, u32[]{:S(2)}) collective-permute-start(f32[384,1536]{1,0:T(8,128)S(1)} %pad_maximum_fusion.12), channel_id=1, source_target_pairs={{0,1},{1,0},{2,3},{3,2},{4,5},{5,4},{6,7},{7,6},{8,9},{9,8},{10,11... | collective-permute-start | bytes 7077896 | tf_op jit(solution)/shard_map/ppermute | solution.py:65
  703.9 48.2 %collective-permute-start.34 = (f32[384,1536]{1,0:T(8,128)S(1)}, f32[384,1536]{1,0:T(8,128)S(1)}, u32[]{:S(2)}, u32[]{:S(2)}) collective-permute-start(f32[384,1536]{1,0:T(8,128)S(1)} %pad_maximum_fusion.11), channel_id=1, source_target_pairs={{0,1},{1,0},{2,3},{3,2},{4,5},{5,4},{6,7},{7,6},{8,9},{9,8},{10,11... | collective-permute-start | bytes 7077896 | tf_op jit(solution)/shard_map/ppermute | solution.py:65
  704.1 34.8 %collective-permute-start.23 = (f32[192,1920]{1,0:T(8,128)S(1)}, f32[192,1920]{1,0:T(8,128)S(1)}, u32[]{:S(2)}, u32[]{:S(2)}) collective-permute-start(f32[192,1920]{1,0:T(8,128)S(1)} %pad_maximum_fusion.17), channel_id=1, source_target_pairs={{0,2},{1,3},{2,0},{3,1},{4,6},{5,7},{6,4},{7,5},{8,10},{9,11},{10,... | collective-permute-start | bytes 4423688 | tf_op jit(solution)/shard_map/ppermute | solution.py:65
  705.1 36.2 %collective-permute-start.13 = (f32[192,1920]{1,0:T(8,128)S(1)}, f32[192,1920]{1,0:T(8,128)S(1)}, u32[]{:S(2)}, u32[]{:S(2)}) collective-permute-start(f32[192,1920]{1,0:T(8,128)S(1)} %pad_maximum_fusion.16), channel_id=1, source_target_pairs={{0,16},{1,17},{2,18},{3,19},{4,20},{5,21},{6,22},{7,23},{8,24},{9,... | collective-permute-start | bytes 4423688 | tf_op jit(solution)/shard_map/ppermute | solution.py:65
  706.2 40.9 %collective-permute-start.64 = (f32[768,768]{1,0:T(8,128)S(1)}, f32[768,768]{1,0:T(8,128)S(1)}, u32[]{:S(2)}, u32[]{:S(2)}) collective-permute-start(f32[768,768]{1,0:T(8,128)S(1)} %pad_maximum_fusion.14), channel_id=1, source_target_pairs={{0,1},{1,0},{2,3},{3,2},{4,5},{5,4},{6,7},{7,6},{8,9},{9,8},{10,11... | collective-permute-start | bytes 7077896 | tf_op jit(solution)/shard_map/ppermute | solution.py:65
  738.9 10.8 %collective-permute-start.54 = (f32[768,768]{1,0:T(8,128)S(1)}, f32[768,768]{1,0:T(8,128)S(1)}, u32[]{:S(2)}, u32[]{:S(2)}) collective-permute-start(f32[768,768]{1,0:T(8,128)S(1)} %pad_maximum_fusion.13), channel_id=1, source_target_pairs={{0,1},{1,0},{2,3},{3,2},{4,5},{5,4},{6,7},{7,6},{8,9},{9,8},{10,11... | collective-permute-start | bytes 7077896 | tf_op jit(solution)/shard_map/ppermute | solution.py:65
  741.2 30.5 %collective-permute-start.24 = (f32[384,1920]{1,0:T(8,128)}, f32[384,1920]{1,0:T(8,128)}, u32[]{:S(2)}, u32[]{:S(2)}) collective-permute-start(f32[384,1920]{1,0:T(8,128)} %pad_maximum_fusion.6), channel_id=1, source_target_pairs={{0,1},{1,0},{2,3},{3,2},{4,5},{5,4},{6,7},{7,6},{8,9},{9,8},{10,11... | collective-permute-start | bytes 8847368 | tf_op jit(solution)/shard_map/ppermute | solution.py:65
  744.5 29.6 %collective-permute-start.14 = (f32[384,1920]{1,0:T(8,128)}, f32[384,1920]{1,0:T(8,128)}, u32[]{:S(2)}, u32[]{:S(2)}) collective-permute-start(f32[384,1920]{1,0:T(8,128)} %pad_maximum_fusion.3), channel_id=1, source_target_pairs={{0,1},{1,0},{2,3},{3,2},{4,5},{5,4},{6,7},{7,6},{8,9},{9,8},{10,11... | collective-permute-start | bytes 8847368 | tf_op jit(solution)/shard_map/ppermute | solution.py:65
  (79 other events, 525.1 us)

commit v2 on v1

--- a/solution.py
+++ b/solution.py
@@ -1,6 +1,8 @@
 import jax
 import jax.numpy as jnp
 from jax import lax
+from jax.experimental import pallas as pl
+from jax.experimental.pallas import tpu as pltpu
 from jax.sharding import PartitionSpec as P
 
 highest = lax.Precision.HIGHEST
@@ -8,17 +10,16 @@
 logit_scale = 50.0
 bucket_edges = (12, 16, 23, 32, 46, 64, 91)
 AXES = ("tower", "dp")
-
-
-def bucket_table(length):
-    where_at = jnp.arange(length, dtype=jnp.int32)
-    offset = where_at[None, :] - where_at[:, None]
+LANES = 128
+
+
+def bucket_code(offset, bucket_count):
     distance = jnp.abs(offset)
     far_bucket = jnp.full_like(distance, 8)
     for edge_value in bucket_edges:
         far_bucket = far_bucket + (distance >= edge_value).astype(jnp.int32)
-    near_far = jnp.where(distance < 8, distance, far_bucket)
-    return near_far + jnp.where(offset > 0, 16, 0)
+    bucket = jnp.where(distance < 8, distance, far_bucket) + jnp.where(offset > 0, 16, 0)
+    return (bucket[:, None] == jnp.arange(bucket_count, dtype=jnp.int32)[None, :]).astype(jnp.float32)
 
 
 def rms_scale(values, gain_vec):
@@ -50,6 +51,175 @@
 
 def t_mm(a, b):
     return lax.dot_general(a, b, (((0,), (0,)), ((), ())), preferred_element_type=jnp.float32)
+
+
+def dot_nt(a, b):
+    return lax.dot_general(a, b, (((1,), (1,)), ((), ())), preferred_element_type=jnp.float32)
+
+def dot_tn(a, b):
+    return lax.dot_general(a, b, (((0,), (0,)), ((), ())), preferred_element_type=jnp.float32)
+
+def dot_nn(a, b):
+    return lax.dot_general(a, b, (((1,), (0,)), ((), ())), preferred_element_type=jnp.float32)
+
+
+def head_parts(value, head_dim):
+    lane = lax.broadcasted_iota(jnp.int32, value.shape, 1)
+    zero = jnp.zeros_like(value)
+    return [
+        jnp.where((lane >= a * head_dim) & (lane < (a + 1) * head_dim), value, zero)
+        for a in range(value.shape[1] // head_dim)
+    ]
+
+
+def diagonals(row):
+    wide = jnp.broadcast_to(row, (LANES, row.shape[1]))
+    return pltpu.roll(wide, 0, 1, stride=1, stride_axis=0)
+
+
+def forward_kernel(head_dim, q_ref, k_ref, v_ref, segc_ref, segr_ref, rows_ref, o_ref, diag_ref):
+    length, width = q_ref.shape
+    group = width // head_dim
+    tiles = length // LANES
+
+    @pl.when(pl.program_id(1) == 0)
+    def _():
+        for a in range(group):
+            diag_ref[a] = diagonals(rows_ref[a])
+
+    keys = head_parts(k_ref[...], head_dim)
+    values = head_parts(v_ref[...], head_dim)
+    segr = segr_ref[...]
+    for t in range(tiles):
+        here = slice(t * LANES, (t + 1) * LANES)
+        query = q_ref[here, :]
+        same = segc_ref[here, :] == segr
+        total = None
+        for a in range(group):
+            s = dot_nt(query, keys[a])
+            s = s + diag_ref[a, :, LANES * (tiles - t) : LANES * (tiles - t) + length]
+            s = jnp.where(same, s, -1000000000.0)
+            e = jnp.exp(s - jnp.max(s, axis=1, keepdims=True))
+            p = e * (1.0 / jnp.sum(e, axis=1, keepdims=True))
+            part = dot_nn(p.astype(jnp.bfloat16), values[a])
+            total = part if total is None else total + part
+        o_ref[here, :] = total.astype(o_ref.dtype)
+
+
+def fold_diagonals(value):
+    n = value.shape[1]
+    rows = value.shape[0]
+    while rows > 1:
+        rows //= 2
+        value = value[:rows] + pltpu.roll(value[rows:], n - rows, 1)
+    return value
+
+
+def backward_kernel(head_dim, q_ref, k_ref, v_ref, g_ref, segc_ref, segr_ref, rows_ref,
+                    gq_ref, gk_ref, gv_ref, gb_ref, diag_ref, fold_ref):
+    length, width = q_ref.shape
+    group = width // head_dim
+    tiles = length // LANES
+    micro = pl.program_id(1)
+
+    @pl.when(micro == 0)
+    def _():
+        for a in range(group):
+            diag_ref[a] = diagonals(rows_ref[a])
+        fold_ref[...] = jnp.zeros_like(fold_ref)
+
+    keys = head_parts(k_ref[...], head_dim)
+    values = head_parts(v_ref[...], head_dim)
+    segc = segc_ref[...]
+    chunk = 2 * LANES
+    gk = [None]
+    gv = [None]
+    for c in range(length // chunk):
+        here = slice(c * chunk, (c + 1) * chunk)
+        query = q_ref[here, :]
+        grad = g_ref[here, :]
+        query_parts = head_parts(query, head_dim)
+        grad_parts = head_parts(grad, head_dim)
+        same = segc == segr_ref[:, here]
+        gq = None
+        for a in range(group):
+            s = dot_nt(keys[a], query)
+            bias = jnp.concatenate(
+                [
+                    diag_ref[a, :, LANES * (tiles - t) + c * chunk : LANES * (tiles - t) + (c + 1) * chunk]
+                    for t in range(tiles)
+                ],
+                axis=0,
+            )
+            s = jnp.where(same, s + bias, -1000000000.0)
+            e = jnp.exp(s - jnp.max(s, axis=0, keepdims=True))
+            p = e * (1.0 / jnp.sum(e, axis=0, keepdims=True))
+            gp = dot_nt(values[a], grad)
+            gs = p * (gp - jnp.sum(p * gp, axis=0, keepdims=True))
+            gs = gs.astype(jnp.bfloat16)
+            p = p.astype(jnp.bfloat16)
+            gs_f = gs.astype(jnp.float32)
+            for t in range(tiles):
+                at = LANES * (tiles - t) + c * chunk
+                fold_ref[a, :, at : at + chunk] += gs_f[t * LANES : (t + 1) * LANES]
+            part = dot_nn(gs, query_parts[a])
+            gk[0] = part if gk[0] is None else gk[0] + part
+            part = dot_nn(p, grad_parts[a])
+            gv[0] = part if gv[0] is None else gv[0] + part
+            part = dot_tn(gs, keys[a])
+            gq = part if gq is None else gq + part
+        gq_ref[here, :] = gq.astype(gq_ref.dtype)
+    gk_ref[...] = gk[0].astype(gk_ref.dtype)
+    gv_ref[...] = gv[0].astype(gv_ref.dtype)
+
+    @pl.when(micro == pl.num_programs(1) - 1)
+    def _():
+        for a in range(group):
+            gb_ref[a] = fold_diagonals(fold_ref[a])
+
+
+def attention_specs(length, width, group, span):
+    return (
+        pl.BlockSpec((length, width), lambda h, m: (m, h)),
+        pl.BlockSpec((length, 1), lambda h, m: (m, 0)),
+        pl.BlockSpec((None, 1, length), lambda h, m: (m, 0, 0)),
+        pl.BlockSpec((group, 1, span), lambda h, m: (h, 0, 0)),
+    )
+
+
+def attention(query, key, value, segment, rows, head_dim):
+    micro_count, length = segment.shape
+    model_width = query.shape[1]
+    width = max(LANES, head_dim)
+    group = width // head_dim
+    block, segc, segr, line = attention_specs(length, width, group, rows.shape[2])
+    return pl.pallas_call(
+        lambda *refs: forward_kernel(head_dim, *refs),
+        name="attention_forward",
+        grid=(model_width // width, micro_count),
+        in_specs=[block, block, block, segc, segr, line],
+        out_specs=block,
+        out_shape=jax.ShapeDtypeStruct(query.shape, jnp.bfloat16),
+        scratch_shapes=[pltpu.VMEM((group, LANES, rows.shape[2]), jnp.float32)],
+    )(query, key, value, segment.reshape(-1, 1), segment[:, None, :], rows)
+
+
+def attention_grads(query, key, value, grad, segment, rows, head_dim):
+    micro_count, length = segment.shape
+    model_width = query.shape[1]
+    width = max(LANES, head_dim)
+    group = width // head_dim
+    block, segc, segr, line = attention_specs(length, width, group, rows.shape[2])
+    flat = jax.ShapeDtypeStruct(query.shape, jnp.bfloat16)
+    return pl.pallas_call(
+        lambda *refs: backward_kernel(head_dim, *refs),
+        name="attention_backward",
+        grid=(model_width // width, micro_count),
+        in_specs=[block, block, block, block, segc, segr, line],
+        out_specs=[block, block, block, line],
+        out_shape=[flat, flat, flat, jax.ShapeDtypeStruct(rows.shape, jnp.float32)],
+        scratch_shapes=[pltpu.VMEM((group, LANES, rows.shape[2]), jnp.float32)] * 2,
+    )(query, key, value, grad, segment.reshape(-1, 1), segment[:, None, :], rows)
 
 
 class Net:
@@ -133,49 +303,26 @@
     chips = tuple(range(1, bits))
     gather_order = (0, 4, 1, 2, 3) if bits == 5 else tuple(range(bits))
 
-    bucket = bucket_table(length)
-    code_full = (
-        bucket[:, :, None] == jnp.arange(bucket_count, dtype=jnp.int32)[None, None, :]
-    ).astype(jnp.float32)
-    bias_map = jnp.einsum("qkb,bh->hqk", code_full, rel_bias, precision=highest)
-    code_low = code_full.astype(jnp.bfloat16)
+    offset = jnp.arange(2 * length, dtype=jnp.int32) - length
+    code = bucket_code(offset, bucket_count)
+    code_back = bucket_code(-offset, bucket_count)
+
+    def bias_rows(which):
+        return jnp.dot(which, rel_bias, precision=highest).T[:, None, :]
 
     segment = segment_ids[0]
-    same_seg = segment[:, :, None] == segment[:, None, :]
-
-    def heads(value):
-        return value.reshape(micro_count, length, head_count, head_dim)
 
     states_f = states[0].reshape(rows, model_width).astype(jnp.float32)
     normed, back_attn = jax.vjp(rms_scale, states_f, gain_attn)
     normed_low = normed.astype(jnp.bfloat16)
-    query_h = heads(mm(normed_low, w_query).astype(jnp.bfloat16))
-    key_h = heads(mm(normed_low, w_key).astype(jnp.bfloat16))
-    value_h = heads(mm(normed_low, w_value).astype(jnp.bfloat16))
-
-    def scores_of():
-        raw = (
-            jnp.einsum("bqhd,bkhd->bhqk", query_h, key_h, preferred_element_type=jnp.float32)
-            + bias_map[None]
-        )
-        return jnp.where(same_seg[:, None], raw, -1000000000.0)
-
-    scores = scores_of()
-    maxima = jnp.max(scores, axis=-1, keepdims=True)
-    expo_vals = jnp.exp(scores - maxima)
-    row_total = jnp.sum(expo_vals, axis=-1, keepdims=True)
-    log_norm = maxima + jnp.log(row_total)
-    probs_low = (expo_vals / row_total).astype(jnp.bfloat16)
-    mixed_low = (
-        jnp.einsum("bhqk,bkhd->bqhd", probs_low, value_h, preferred_element_type=jnp.float32)
-        .reshape(rows, model_width)
-        .astype(jnp.bfloat16)
-    )
+    query_low = mm(normed_low, w_query).astype(jnp.bfloat16)
+    key_low = mm(normed_low, w_key).astype(jnp.bfloat16)
+    value_low = mm(normed_low, w_value).astype(jnp.bfloat16)
+    mixed_low = attention(query_low, key_low, value_low, segment, bias_rows(code), head_dim)
     hidden = states_f + mm(mixed_low, w_out)
     normed_two, back_ffn = jax.vjp(rms_scale, hidden, gain_ffn)
     normed_two_low = normed_two.astype(jnp.bfloat16)
-    inner = mm(normed_two_low, w_in)
-    activ_low = jnp.maximum(inner, 0.0).astype(jnp.bfloat16)
+    activ_low = jnp.maximum(mm(normed_two_low, w_in), 0.0).astype(jnp.bfloat16)
     output = hidden + mm(activ_low, w_ffout)
     final_norm, back_final = jax.vjp(rms_scale, output, gain_final)
     member = (segment[:, :, None] == jnp.arange(item_count, dtype=jnp.int32)).astype(jnp.float32)
@@ -256,7 +403,7 @@
         axis=0,
     )
     grad_activ = mm_t(grad_output_low, w_ffout)
-    grad_inner_low = jnp.where(inner > 0, grad_activ, 0.0).astype(jnp.bfloat16)
+    grad_inner_low = jnp.where(activ_low > 0, grad_activ, 0.0).astype(jnp.bfloat16)
     whole_in = jnp.concatenate(
         [
             total(normed_two_low, grad_inner_low[:, :ff_half], orders[1][0]),
@@ -268,35 +415,11 @@
     grad_hidden_norm, grad_gain_ffn = back_ffn(grad_normed_two)
     grad_hidden = grad_output + grad_hidden_norm
     grad_hidden_low = grad_hidden.astype(jnp.bfloat16)
-    grad_mixed = heads(mm_t(grad_hidden_low, w_out).astype(jnp.bfloat16))
-    probs_full = jnp.exp(scores_of() - log_norm)
-    grad_probs = jnp.einsum(
-        "bqhd,bkhd->bhqk", grad_mixed, value_h, preferred_element_type=jnp.float32
-    )
-    grad_scores = (
-        probs_full * (grad_probs - jnp.sum(probs_full * grad_probs, axis=-1, keepdims=True))
-    ).astype(jnp.bfloat16)
-
-    def flat(value):
-        return value.reshape(rows, model_width).astype(jnp.bfloat16)
-
-    grad_query_h = flat(
-        jnp.einsum("bhqk,bkhd->bqhd", grad_scores, key_h, preferred_element_type=jnp.float32)
-    )
-    grad_key_h = flat(
-        jnp.einsum("bhqk,bqhd->bkhd", grad_scores, query_h, preferred_element_type=jnp.float32)
-    )
-    grad_value_h = flat(
-        jnp.einsum(
-            "bhqk,bqhd->bkhd",
-            probs_full.astype(jnp.bfloat16),
-            grad_mixed,
-            preferred_element_type=jnp.float32,
-        )
-    )
-    grad_bias = jnp.einsum(
-        "hqk,qkn->nh", jnp.sum(grad_scores.astype(jnp.float32), axis=0), code_full,
-    )
+    grad_mixed = mm_t(grad_hidden_low, w_out).astype(jnp.bfloat16)
+    grad_query_h, grad_key_h, grad_value_h, grad_rows = attention_grads(
+        query_low, key_low, value_low, grad_mixed, segment, bias_rows(code_back), head_dim
+    )
+    grad_bias = jnp.einsum("hx,xb->bh", grad_rows[:, 0], code_back, precision=highest)
     grad_qkv = jnp.concatenate([grad_query_h, grad_key_h, grad_value_h], axis=1)
     grad_normed = (
         mm_t(grad_query_h, w_query) + mm_t(grad_key_h, w_key) + mm_t(grad_value_h, w_value)

time: 789 us -> 650 us (0.82)
  local copies, waits for them, and re-layouts: 122 us -> 23.9 us
  matrix products: 185 us -> 106 us
  Pallas kernels: 0 us -> 71.7 us
  other arithmetic: 120 us -> 80.3 us
    dot_general x8 -> x3, matrix products: 86 us -> 2.12 us  [the longest x2 1.53 us: bias_rows(): return jnp.dot(which, rel_bias, precision=highest).T[:, None, :]]
    pallas_call x0 -> x2, Pallas kernels: none -> 71.7 us  [the longest x1 43.1 us: attention_grads(): pl.pallas_call(lambda *refs: backward_kernel(head_dim, *refs), name='atte...]
    eq x1 -> x0, local copies, waits for them, and re-layouts: 45.2 us -> none  [local(): bucket[:, :, None]]
    reduce_sum x2 -> x0, other arithmetic: 32.1 us -> none  [the longest x1 21.8 us: local(): jnp.sum(grad_scores.astype(jnp.float32), axis=0)]
    dot_general x1 -> x0, local copies, waits for them, and re-layouts: 17.8 us -> none  [local(): bias_map = jnp.einsum('qkb,bh->hqk', code_full, rel_bias, precision=highest)]
    convert_element_type x8 -> x0, local copies, waits for them, and re-layouts: 15.8 us -> none  [the longest x3 4.86 us: flat(): return value.reshape(rows, model_width).astype(jnp.bfloat16)]
    reshape x4 -> x0, local copies, waits for them, and re-layouts: 14.8 us -> none  [heads(): return value.reshape(micro_count, length, head_count, head_dim)]
    eq x2 -> x0, other arithmetic: 9.14 us -> none  [the longest x1 8.78 us: local(): bucket[:, :, None]]
  transfers between devices with their start and end apart: 70 -> 70, of which waited for: 36 -> 35; matrix products, arithmetic and copies ran while one was open for 11% -> 13% of each run, Pallas kernels for 0% -> 0%
where the time goes in v2:
time: 650 us; the launch traced here: 642 us
  waiting for transfers between devices  295 us (45%)
  matrix products  106 us (16%)
  other arithmetic  80.3 us (12%)
  Pallas kernels  71.7 us (11%)
  starting transfers between devices  60.1 us (9%)
  local copies, waits for them, and re-layouts  23.9 us (4%)
    ppermute x70, waiting for transfers between devices, swap(): lax.ppermute(value, AXES, [(i, i ^ 1 << b) for i in range(self.size)])  295 us
    ppermute x70, starting transfers between devices, swap(): lax.ppermute(value, AXES, [(i, i ^ 1 << b) for i in range(self.size)])  60.1 us
    pallas_call x1, Pallas kernels, attention_grads(): pl.pallas_call(lambda *refs: backward_kernel(head_dim, *refs), name='atte...  43.1 us
    dot_general x7, matrix products, mm_t(): lax.dot_general(a, b, (((1,), (1,)), ((), ())), preferred_element_type=jn...  36 us
    dot_general x16, matrix products, t_mm(): lax.dot_general(a, b, (((0,), (0,)), ((), ())), preferred_element_type=jn...  33.6 us
    pallas_call x1, Pallas kernels, attention(): pl.pallas_call(lambda *refs: forward_kernel(head_dim, *refs), name='atten...  28.7 us
    dot_general x7, matrix products, mm(): return jnp.dot(a, b, preferred_element_type=jnp.float32)  25.5 us
    add x18, other arithmetic, scatter_sum(): kept = half_of(kept, bit) + half_of(got, bit)  18.1 us
  transfers between devices with their start and end apart: 70, of which 35 were waited for; matrix products, arithmetic and copies ran while one was open for 13% of the time, Pallas kernels for 0%

profile of v2, /device:TPU:0, one launch (start us, length us, event | category | flops | bytes accessed | tf_op | source)
XLA Modules:
  0.0 642.3 jit_solution(798673420928579395)
XLA Ops:
  3.9 2.5 convolution_convert_fusion.3.refs_0_
  6.4 2.5 convolution_convert_fusion.2.refs_1_
  9.0 2.5 convolution_convert_fusion.1.refs_2_
  14.3 28.7 %attention_forward.1 = bf16[1024,768]{1,0:T(8,128)(2,1)} custom-call(bf16[1024,768]{1,0:T(8,128)(2,1)} %convolution_convert_fusion.3.refs_0_, bf16[1024,768]{1,0:T(8,128)(2,1)} %convolution_convert_fusion.2.refs_1_, bf16[1024,768]{1,0:T(8,128)(2,1)} %convolution_convert_fusion.1.refs_2_, s32[1024,1]{1,0:T(8,128)} %bitcast.161, ...), custom_call_target="tpu_custom_call" | custom-call | tf_op jit(solution)/shard_map/attention_forward/pallas_call | solution.py:196
  42.9 3.3 multiply_reduce_fusion.4
  48.2 8.9 %maximum_convert_fusion = bf16[1024,3072]{1,0:T(8,128)(2,1)S(1)} fusion(bf16[1024,768]{1,0:T(8,128)(2,1)S(1)} %multiply_convert_fusion, bf16[768,3072]{1,0:T(8,128)(2,1)} %param.23), kind=kOutput, calls=%fused_computation.1 | convolution fusion | flops 4838129664 | bytes 12582912 | tf_op jit(solution)/shard_map/dot_general | solution.py:45
  57.2 5.2 multiply_reduce_fusion.3
  66.6 4.1 collective-permute-start
  70.7 2.6 collective-permute-done
  74.8 3.2 collective-permute-done.1
  79.9 3.9 collective-permute-done.2
  87.4 5.1 collective-permute-done.3
  97.4 5.9 fusion.118
  121.1 10.6 %select_convert_fusion = bf16[1024,3072]{1,0:T(8,128)(2,1)} fusion(bf16[1024,3072]{1,0:T(8,128)(2,1)S(1)} %bitcast.159, bf16[1024,768]{1,0:T(8,128)(2,1)S(1)} %fusion.117, bf16[3072,768]{1,0:T(8,128)(2,1)} %param.24), kind=kOutput, calls=%fused_computation | convolution fusion | flops 4841275392 | bytes 18874368 | tf_op jit(solution)/shard_map/dot_general | solution.py:49
  131.8 7.5 %multiply_reduce_fusion = (f32[768]{0:T(1024)S(1)}, f32[1024]{0:T(1024)S(1)}, f32[1024,768]{1,0:T(8,128)S(1)}) fusion(f32[1024,768]{1,0:T(8,128)S(1)} %copy-done.12, f32[1024]{0:T(1024)S(1)} %copy-done.47, f32[768]{0:T(1024)S(1)} %copy-done.53, bf16[1024,3072]{1,0:T(8,128)(2,1)} %select_convert_fusion, bf16[768,3072]{1,0:T(8,128)(2,1)S(1)} %bitcast.174), kind=kOutput, calls=%fused_computation.29 | convolution fusion | flops 4836554752 | bytes 17315840 | tf_op jit(solution)/shard_map/dot_general | solution.py:49
  142.7 2.6 convolution_convert_fusion.refs_3_
  145.3 43.1 %attention_backward.1 = (bf16[1024,768]{1,0:T(8,128)(2,1)}, bf16[1024,768]{1,0:T(8,128)(2,1)}, bf16[1024,768]{1,0:T(8,128)(2,1)}, f32[12,1,1024]{2,1,0:T(1,128)}) custom-call(bf16[1024,768]{1,0:T(8,128)(2,1)} %convolution_convert_fusion.3.refs_0_, bf16[1024,768]{1,0:T(8,128)(2,1)} %convolution_convert_fusion.2.refs_1_, ...), custom_call_target="tpu_custom_call" | custom-call | tf_op jit(solution)/shard_map/attention_backward/pallas_call | solution.py:214
  188.4 5.0 fusion.121
  193.4 3.1 fusion.122
  196.5 2.8 fusion.9
  199.4 3.5 fusion.29
  202.9 3.4 fusion.28
  206.3 2.8 fusion.11
  209.1 2.8 fusion.13
  212.0 2.8 fusion.15
  214.8 2.9 fusion.20
  217.7 2.9 fusion.22
  220.6 3.1 fusion.24
  223.7 2.9 fusion.26
  227.9 5.5 fusion.6
  243.4 2.5 collective-permute-start.68
  253.1 2.5 fusion.1
  255.6 3.6 dynamic-slice_add_fusion.9
  267.1 2.8 dynamic-slice_add_fusion.5
  275.8 12.5 %collective-permute-done.36 = f32[192,1536]{1,0:T(8,128)} collective-permute-done((f32[192,1536]{1,0:T(8,128)}, f32[192,1536]{1,0:T(8,128)}, u32[]{:S(2)}, u32[]{:S(2)}) %collective-permute-start.36) | collective-permute-done | bytes 1179680 | tf_op jit(solution)/shard_map/ppermute | solution.py:235
  297.6 15.9 %collective-permute-done.56 = f32[384,768]{1,0:T(8,128)S(1)} collective-permute-done((f32[384,768]{1,0:T(8,128)S(1)}, f32[384,768]{1,0:T(8,128)S(1)}, u32[]{:S(2)}, u32[]{:S(2)}) %collective-permute-start.56) | collective-permute-done | bytes 1179680 | tf_op jit(solution)/shard_map/ppermute | solution.py:235
  321.3 38.7 %collective-permute-done.57 = f32[192,768]{1,0:T(8,128)S(1)} collective-permute-done((f32[192,768]{1,0:T(8,128)S(1)}, f32[192,768]{1,0:T(8,128)S(1)}, u32[]{:S(2)}, u32[]{:S(2)}) %collective-permute-start.57) | collective-permute-done | bytes 589856 | tf_op jit(solution)/shard_map/ppermute | solution.py:235
  364.7 10.4 %collective-permute-done.28 = f32[48,1536]{1,0:T(8,128)S(1)} collective-permute-done((f32[48,1536]{1,0:T(8,128)S(1)}, f32[48,1536]{1,0:T(8,128)S(1)}, u32[]{:S(2)}, u32[]{:S(2)}) %collective-permute-start.28) | collective-permute-done | bytes 294944 | tf_op jit(solution)/shard_map/ppermute | solution.py:235
  377.9 3.8 collective-permute-done.48
  387.3 5.8 collective-permute-done.59
  395.4 8.1 %collective-permute-done.40 = f32[24,1536]{1,0:T(8,128)S(1)} collective-permute-done((f32[24,1536]{1,0:T(8,128)S(1)}, f32[24,1536]{1,0:T(8,128)S(1)}, u32[]{:S(2)}, u32[]{:S(2)}) %collective-permute-start.40) | collective-permute-done | bytes 147488 | tf_op jit(solution)/shard_map/ppermute | solution.py:235
  406.6 14.3 %collective-permute-done.60 = f32[48,768]{1,0:T(8,128)S(1)} collective-permute-done((f32[48,768]{1,0:T(8,128)S(1)}, f32[48,768]{1,0:T(8,128)S(1)}, u32[]{:S(2)}, u32[]{:S(2)}) %collective-permute-start.60) | collective-permute-done | bytes 147488 | tf_op jit(solution)/shard_map/ppermute | solution.py:235
  421.0 3.1 collective-permute-done.50
  424.1 6.4 collective-permute-done.41
  430.6 5.5 collective-permute-done.31
  436.2 6.2 collective-permute-done.61
  446.0 2.8 collective-permute-done.51
  448.9 33.1 %collective-permute-done.18 = f32[48,1920]{1,0:T(8,128)S(1)} collective-permute-done((f32[48,1920]{1,0:T(8,128)S(1)}, f32[48,1920]{1,0:T(8,128)S(1)}, u32[]{:S(2)}, u32[]{:S(2)}) %collective-permute-start.18) | collective-permute-done | bytes 368672 | tf_op jit(solution)/shard_map/ppermute | solution.py:235
  482.0 7.8 %collective-permute-done.8 = f32[48,1920]{1,0:T(8,128)S(1)} collective-permute-done((f32[48,1920]{1,0:T(8,128)S(1)}, f32[48,1920]{1,0:T(8,128)S(1)}, u32[]{:S(2)}, u32[]{:S(2)}) %collective-permute-start.8) | collective-permute-done | bytes 368672 | tf_op jit(solution)/shard_map/ppermute | solution.py:235
  489.8 3.0 collective-permute-start.9
  494.5 3.6 collective-permute-done.52
  498.3 5.9 collective-permute-done.19
  505.3 2.7 collective-permute-done.9
  508.1 8.4 %collective-permute-done.20 = f32[24,1920]{1,0:T(8,128)S(1)} collective-permute-done((f32[24,1920]{1,0:T(8,128)S(1)}, f32[24,1920]{1,0:T(8,128)S(1)}, u32[]{:S(2)}, u32[]{:S(2)}) %collective-permute-start.20) | collective-permute-done | bytes 184352 | tf_op jit(solution)/shard_map/ppermute | solution.py:235
  516.6 9.9 %collective-permute-done.10 = f32[24,1920]{1,0:T(8,128)S(1)} collective-permute-done((f32[24,1920]{1,0:T(8,128)S(1)}, f32[24,1920]{1,0:T(8,128)S(1)}, u32[]{:S(2)}, u32[]{:S(2)}) %collective-permute-start.10) | collective-permute-done | bytes 184352 | tf_op jit(solution)/shard_map/ppermute | solution.py:235
  526.6 10.4 %collective-permute-done.21 = f32[48,1920]{1,0:T(8,128)S(1)} collective-permute-done((f32[48,1920]{1,0:T(8,128)S(1)}, f32[48,1920]{1,0:T(8,128)S(1)}, u32[]{:S(2)}, u32[]{:S(2)}) %collective-permute-start.21) | collective-permute-done | bytes 368672 | tf_op jit(solution)/shard_map/ppermute | solution.py:235
  537.4 9.2 %collective-permute-done.11 = f32[48,1920]{1,0:T(8,128)S(1)} collective-permute-done((f32[48,1920]{1,0:T(8,128)S(1)}, f32[48,1920]{1,0:T(8,128)S(1)}, u32[]{:S(2)}, u32[]{:S(2)}) %collective-permute-start.11) | collective-permute-done | bytes 368672 | tf_op jit(solution)/shard_map/ppermute | solution.py:235
  549.4 13.9 %collective-permute-done.22 = f32[96,1920]{1,0:T(8,128)S(1)} collective-permute-done((f32[96,1920]{1,0:T(8,128)S(1)}, f32[96,1920]{1,0:T(8,128)S(1)}, u32[]{:S(2)}, u32[]{:S(2)}) %collective-permute-start.22) | collective-permute-done | bytes 737312 | tf_op jit(solution)/shard_map/ppermute | solution.py:235
  566.6 31.7 %collective-permute-done.23 = f32[192,1920]{1,0:T(8,128)S(1)} collective-permute-done((f32[192,1920]{1,0:T(8,128)S(1)}, f32[192,1920]{1,0:T(8,128)S(1)}, u32[]{:S(2)}, u32[]{:S(2)}) %collective-permute-start.23) | collective-permute-done | bytes 1474592 | tf_op jit(solution)/shard_map/ppermute | solution.py:235
  603.6 2.7 broadcast_select_fusion.9
  611.2 2.7 broadcast_select_fusion.11
  613.9 8.7 %maximum_maximum_fusion = f32[768,3072]{1,0:T(8,128)} fusion(f32[384,1536]{1,0:T(8,128)} %get-tuple-element.78, f32[384,1536]{1,0:T(8,128)} %get-tuple-element.77, f32[384,1536]{1,0:T(8,128)} %get-tuple-element.74, f32[384,1536]{1,0:T(8,128)} %get-tuple-element.73), kind=kLoop, calls=%fused_computation.2 | loop fusion | flops 7077888 | bytes 18874368 | tf_op jit(solution)/shard_map/concatenate | solution.py:407
  622.6 8.3 %pad_maximum_fusion = f32[3072,768]{1,0:T(8,128)} fusion(f32[768,768]{1,0:T(8,128)} %get-tuple-element.70, f32[768,768]{1,0:T(8,128)} %get-tuple-element.69, f32[768,768]{1,0:T(8,128)} %get-tuple-element.66, f32[768,768]{1,0:T(8,128)} %get-tuple-element.65), kind=kLoop, calls=%fused_computation.3 | loop fusion | flops 7077888 | bytes 18874368 | tf_op jit(solution)/shard_map/concatenate | solution.py:398
  635.8 5.2 pad_maximum_fusion.7
  (443 shorter events, 139.2 us)
Async XLA Ops:
  66.6 6.7 %collective-permute-start = (f32[1,16,768]{2,1,0:T(8,128)S(1)}, f32[1,16,768]{2,1,0:T(8,128)S(1)}, u32[]{:S(2)}, u32[]{:S(2)}) collective-permute-start(f32[1,16,768]{2,1,0:T(8,128)S(1)} %multiply_bitcast_fusion.1), channel_id=1, source_target_pairs={{0,8},{1,9},{2,10},{3,11},{4,12},{5,13},{6,14},{7,15},{8,0},{9,1},... | collective-permute-start | bytes 147464 | tf_op jit(solution)/shard_map/ppermute | solution.py:235
  78.1 5.7 collective-permute-start.2
  84.6 7.9 %collective-permute-start.3 = (f32[8,16,768]{2,1,0:T(8,128)S(1)}, f32[8,16,768]{2,1,0:T(8,128)}, u32[]{:S(2)}, u32[]{:S(2)}) collective-permute-start(f32[8,16,768]{2,1,0:T(8,128)S(1)} %pad_maximum_fusion.31), channel_id=1, source_target_pairs={{0,16},{1,17},{2,18},{3,19},{4,20},{5,21},{6,22},{7,23},{8,24},{9,... | collective-permute-start | bytes 1179656 | tf_op jit(solution)/shard_map/ppermute | solution.py:235
  94.6 8.6 %collective-permute-start.4 = (f32[16,16,768]{2,1,0:T(8,128)}, f32[16,16,768]{2,1,0:T(8,128)}, u32[]{:S(2)}, u32[]{:S(2)}) collective-permute-start(f32[16,16,768]{2,1,0:T(8,128)} %pad_maximum_fusion.24), channel_id=1, source_target_pairs={{0,1},{1,0},{2,3},{3,2},{4,5},{5,4},{6,7},{7,6},{8,9},{9,8},{10,11... | collective-permute-start | bytes 2359304 | tf_op jit(solution)/shard_map/ppermute | solution.py:235
  226.6 25.9 %collective-permute-start.35 = (f32[384,1536]{1,0:T(8,128)}, f32[384,1536]{1,0:T(8,128)}, u32[]{:S(2)}, u32[]{:S(2)}) collective-permute-start(f32[384,1536]{1,0:T(8,128)} %fusion.9), channel_id=1, source_target_pairs={{0,1},{1,0},{2,3},{3,2},{4,5},{5,4},{6,7},{7,6},{8,9},{9,8},{10,11... | collective-permute-start | bytes 7077896 | tf_op jit(solution)/shard_map/ppermute | solution.py:235
  238.1 21.1 %collective-permute-start.25 = (f32[384,1536]{1,0:T(8,128)S(1)}, f32[384,1536]{1,0:T(8,128)S(1)}, u32[]{:S(2)}, u32[]{:S(2)}) collective-permute-start(f32[384,1536]{1,0:T(8,128)S(1)} %copy-done.66), channel_id=1, source_target_pairs={{0,1},{1,0},{2,3},{3,2},{4,5},{5,4},{6,7},{7,6},{8,9},{9,8},{10,11... | collective-permute-start | bytes 7077896 | tf_op jit(solution)/shard_map/ppermute | solution.py:235
  238.2 24.5 %collective-permute-start.55 = (f32[768,768]{1,0:T(8,128)S(1)}, f32[768,768]{1,0:T(8,128)S(1)}, u32[]{:S(2)}, u32[]{:S(2)}) collective-permute-start(f32[768,768]{1,0:T(8,128)S(1)} %copy-done.65), channel_id=1, source_target_pairs={{0,1},{1,0},{2,3},{3,2},{4,5},{5,4},{6,7},{7,6},{8,9},{9,8},{10,11... | collective-permute-start | bytes 7077896 | tf_op jit(solution)/shard_map/ppermute | solution.py:235
  242.8 29.5 %collective-permute-start.15 = (f32[384,1920]{1,0:T(8,128)}, f32[384,1920]{1,0:T(8,128)}, u32[]{:S(2)}, u32[]{:S(2)}) collective-permute-start(f32[384,1920]{1,0:T(8,128)} %pad_maximum_fusion.5), channel_id=1, source_target_pairs={{0,1},{1,0},{2,3},{3,2},{4,5},{5,4},{6,7},{7,6},{8,9},{9,8},{10,11... | collective-permute-start | bytes 8847368 | tf_op jit(solution)/shard_map/ppermute | solution.py:235
  251.7 18.2 %collective-permute-start.45 = (f32[768,768]{1,0:T(8,128)}, f32[768,768]{1,0:T(8,128)}, u32[]{:S(2)}, u32[]{:S(2)}) collective-permute-start(f32[768,768]{1,0:T(8,128)} %fusion.24), channel_id=1, source_target_pairs={{0,1},{1,0},{2,3},{3,2},{4,5},{5,4},{6,7},{7,6},{8,9},{9,8},{10,11... | collective-permute-start | bytes 7077896 | tf_op jit(solution)/shard_map/ppermute | solution.py:235
  252.5 42.1 %collective-permute-start.5 = (f32[384,1920]{1,0:T(8,128)}, f32[384,1920]{1,0:T(8,128)}, u32[]{:S(2)}, u32[]{:S(2)}) collective-permute-start(f32[384,1920]{1,0:T(8,128)} %fusion.29), channel_id=1, source_target_pairs={{0,1},{1,0},{2,3},{3,2},{4,5},{5,4},{6,7},{7,6},{8,9},{9,8},{10,11... | collective-permute-start | bytes 8847368 | tf_op jit(solution)/shard_map/ppermute | solution.py:235
  259.2 29.2 %collective-permute-start.36 = (f32[192,1536]{1,0:T(8,128)}, f32[192,1536]{1,0:T(8,128)}, u32[]{:S(2)}, u32[]{:S(2)}) collective-permute-start(f32[192,1536]{1,0:T(8,128)} %get-tuple-element.80), channel_id=1, source_target_pairs={{0,2},{1,3},{2,0},{3,1},{4,6},{5,7},{6,4},{7,5},{8,10},{9,11},{10,... | collective-permute-start | bytes 3538952 | tf_op jit(solution)/shard_map/ppermute | solution.py:235
  262.7 29.2 %collective-permute-start.26 = (f32[192,1536]{1,0:T(8,128)}, f32[192,1536]{1,0:T(8,128)}, u32[]{:S(2)}, u32[]{:S(2)}) collective-permute-start(f32[192,1536]{1,0:T(8,128)} %get-tuple-element.76), channel_id=1, source_target_pairs={{0,16},{1,17},{2,18},{3,19},{4,20},{5,21},{6,22},{7,23},{8,24},{9,... | collective-permute-start | bytes 3538952 | tf_op jit(solution)/shard_map/ppermute | solution.py:235
  269.9 43.6 %collective-permute-start.56 = (f32[384,768]{1,0:T(8,128)S(1)}, f32[384,768]{1,0:T(8,128)S(1)}, u32[]{:S(2)}, u32[]{:S(2)}) collective-permute-start(f32[384,768]{1,0:T(8,128)S(1)} %get-tuple-element.72), channel_id=1, source_target_pairs={{0,2},{1,3},{2,0},{3,1},{4,6},{5,7},{6,4},{7,5},{8,10},{9,11},{10,... | collective-permute-start | bytes 3538952 | tf_op jit(solution)/shard_map/ppermute | solution.py:235
  272.4 44.6 %collective-permute-start.46 = (f32[384,768]{1,0:T(8,128)S(1)}, f32[384,768]{1,0:T(8,128)S(1)}, u32[]{:S(2)}, u32[]{:S(2)}) collective-permute-start(f32[384,768]{1,0:T(8,128)S(1)} %get-tuple-element.68), channel_id=1, source_target_pairs={{0,16},{1,17},{2,18},{3,19},{4,20},{5,21},{6,22},{7,23},{8,24},{9,... | collective-permute-start | bytes 3538952 | tf_op jit(solution)/shard_map/ppermute | solution.py:235
  288.3 94.4 %collective-permute-start.16 = (f32[192,1920]{1,0:T(8,128)S(1)}, f32[192,1920]{1,0:T(8,128)S(1)}, u32[]{:S(2)}, u32[]{:S(2)}) collective-permute-start(f32[192,1920]{1,0:T(8,128)S(1)} %get-tuple-element.60), channel_id=1, source_target_pairs={{0,2},{1,3},{2,0},{3,1},{4,6},{5,7},{6,4},{7,5},{8,10},{9,11},{10,... | collective-permute-start | bytes 4423688 | tf_op jit(solution)/shard_map/ppermute | solution.py:235
  291.8 26.8 %collective-permute-start.37 = (f32[96,1536]{1,0:T(8,128)S(1)}, f32[96,1536]{1,0:T(8,128)S(1)}, u32[]{:S(2)}, u32[]{:S(2)}) collective-permute-start(f32[96,1536]{1,0:T(8,128)S(1)} %get-tuple-element.104), channel_id=1, source_target_pairs={{0,4},{1,5},{2,6},{3,7},{4,0},{5,1},{6,2},{7,3},{8,12},{9,13},{10,... | collective-permute-start | bytes 1769480 | tf_op jit(solution)/shard_map/ppermute | solution.py:235
  294.6 24.2 %collective-permute-start.27 = (f32[96,1536]{1,0:T(8,128)S(1)}, f32[96,1536]{1,0:T(8,128)S(1)}, u32[]{:S(2)}, u32[]{:S(2)}) collective-permute-start(f32[96,1536]{1,0:T(8,128)S(1)} %get-tuple-element.100), channel_id=1, source_target_pairs={{0,4},{1,5},{2,6},{3,7},{4,0},{5,1},{6,2},{7,3},{8,12},{9,13},{10,... | collective-permute-start | bytes 1769480 | tf_op jit(solution)/shard_map/ppermute | solution.py:235
  313.5 71.3 %collective-permute-start.6 = (f32[192,1920]{1,0:T(8,128)S(1)}, f32[192,1920]{1,0:T(8,128)S(1)}, u32[]{:S(2)}, u32[]{:S(2)}) collective-permute-start(f32[192,1920]{1,0:T(8,128)S(1)} %get-tuple-element.64), channel_id=1, source_target_pairs={{0,16},{1,17},{2,18},{3,19},{4,20},{5,21},{6,22},{7,23},{8,24},{9,... | collective-permute-start | bytes 4423688 | tf_op jit(solution)/shard_map/ppermute | solution.py:235
  317.0 43.0 %collective-permute-start.57 = (f32[192,768]{1,0:T(8,128)S(1)}, f32[192,768]{1,0:T(8,128)S(1)}, u32[]{:S(2)}, u32[]{:S(2)}) collective-permute-start(f32[192,768]{1,0:T(8,128)S(1)} %get-tuple-element.96), channel_id=1, source_target_pairs={{0,16},{1,17},{2,18},{3,19},{4,20},{5,21},{6,22},{7,23},{8,24},{9,... | collective-permute-start | bytes 1769480 | tf_op jit(solution)/shard_map/ppermute | solution.py:235
  318.7 43.8 %collective-permute-start.47 = (f32[192,768]{1,0:T(8,128)S(1)}, f32[192,768]{1,0:T(8,128)S(1)}, u32[]{:S(2)}, u32[]{:S(2)}) collective-permute-start(f32[192,768]{1,0:T(8,128)S(1)} %get-tuple-element.92), channel_id=1, source_target_pairs={{0,2},{1,3},{2,0},{3,1},{4,6},{5,7},{6,4},{7,5},{8,10},{9,11},{10,... | collective-permute-start | bytes 1769480 | tf_op jit(solution)/shard_map/ppermute | solution.py:235
  318.8 45.6 %collective-permute-start.38 = (f32[48,1536]{1,0:T(8,128)S(1)}, f32[48,1536]{1,0:T(8,128)S(1)}, u32[]{:S(2)}, u32[]{:S(2)}) collective-permute-start(f32[48,1536]{1,0:T(8,128)S(1)} %get-tuple-element.130), channel_id=1, source_target_pairs={{0,8},{1,9},{2,10},{3,11},{4,12},{5,13},{6,14},{7,15},{8,0},{9,1},... | collective-permute-start | bytes 884744 | tf_op jit(solution)/shard_map/ppermute | solution.py:235
  360.0 15.1 %collective-permute-start.28 = (f32[48,1536]{1,0:T(8,128)S(1)}, f32[48,1536]{1,0:T(8,128)S(1)}, u32[]{:S(2)}, u32[]{:S(2)}) collective-permute-start(f32[48,1536]{1,0:T(8,128)S(1)} %get-tuple-element.126), channel_id=1, source_target_pairs={{0,8},{1,9},{2,10},{3,11},{4,12},{5,13},{6,14},{7,15},{8,0},{9,1},... | collective-permute-start | bytes 884744 | tf_op jit(solution)/shard_map/ppermute | solution.py:235
  362.5 15.4 %collective-permute-start.58 = (f32[96,768]{1,0:T(8,128)S(1)}, f32[96,768]{1,0:T(8,128)S(1)}, u32[]{:S(2)}, u32[]{:S(2)}) collective-permute-start(f32[96,768]{1,0:T(8,128)S(1)} %get-tuple-element.122), channel_id=1, source_target_pairs={{0,4},{1,5},{2,6},{3,7},{4,0},{5,1},{6,2},{7,3},{8,12},{9,13},{10,... | collective-permute-start | bytes 884744 | tf_op jit(solution)/shard_map/ppermute | solution.py:235
  364.4 17.2 %collective-permute-start.48 = (f32[96,768]{1,0:T(8,128)S(1)}, f32[96,768]{1,0:T(8,128)S(1)}, u32[]{:S(2)}, u32[]{:S(2)}) collective-permute-start(f32[96,768]{1,0:T(8,128)S(1)} %get-tuple-element.118), channel_id=1, source_target_pairs={{0,4},{1,5},{2,6},{3,7},{4,0},{5,1},{6,2},{7,3},{8,12},{9,13},{10,... | collective-permute-start | bytes 884744 | tf_op jit(solution)/shard_map/ppermute | solution.py:235
  375.1 11.2 %collective-permute-start.39 = (f32[24,1536]{1,0:T(8,128)S(1)}, f32[24,1536]{1,0:T(8,128)S(1)}, u32[]{:S(2)}, u32[]{:S(2)}) collective-permute-start(f32[24,1536]{1,0:T(8,128)S(1)} %dynamic-slice_add_fusion.40), channel_id=1, source_target_pairs={{0,16},{1,17},{2,18},{3,19},{4,20},{5,21},{6,22},{7,23},{8,24},{9,... | collective-permute-start | bytes 442376 | tf_op jit(solution)/shard_map/ppermute | solution.py:235
  377.8 8.6 %collective-permute-start.29 = (f32[24,1536]{1,0:T(8,128)S(1)}, f32[24,1536]{1,0:T(8,128)S(1)}, u32[]{:S(2)}, u32[]{:S(2)}) collective-permute-start(f32[24,1536]{1,0:T(8,128)S(1)} %dynamic-slice_add_fusion.41), channel_id=1, source_target_pairs={{0,2},{1,3},{2,0},{3,1},{4,6},{5,7},{6,4},{7,5},{8,10},{9,11},{10,... | collective-permute-start | bytes 442376 | tf_op jit(solution)/shard_map/ppermute | solution.py:235
  381.6 11.4 %collective-permute-start.59 = (f32[48,768]{1,0:T(8,128)S(1)}, f32[48,768]{1,0:T(8,128)S(1)}, u32[]{:S(2)}, u32[]{:S(2)}) collective-permute-start(f32[48,768]{1,0:T(8,128)S(1)} %dynamic-slice_add_fusion.38), channel_id=1, source_target_pairs={{0,8},{1,9},{2,10},{3,11},{4,12},{5,13},{6,14},{7,15},{8,0},{9,1},... | collective-permute-start | bytes 442376 | tf_op jit(solution)/shard_map/ppermute | solution.py:235
  382.7 12.6 %collective-permute-start.49 = (f32[48,768]{1,0:T(8,128)S(1)}, f32[48,768]{1,0:T(8,128)S(1)}, u32[]{:S(2)}, u32[]{:S(2)}) collective-permute-start(f32[48,768]{1,0:T(8,128)S(1)} %dynamic-slice_add_fusion.39), channel_id=1, source_target_pairs={{0,8},{1,9},{2,10},{3,11},{4,12},{5,13},{6,14},{7,15},{8,0},{9,1},... | collective-permute-start | bytes 442376 | tf_op jit(solution)/shard_map/ppermute | solution.py:235
  384.8 57.7 %collective-permute-start.17 = (f32[96,1920]{1,0:T(8,128)S(1)}, f32[96,1920]{1,0:T(8,128)S(1)}, u32[]{:S(2)}, u32[]{:S(2)}) collective-permute-start(f32[96,1920]{1,0:T(8,128)S(1)} %get-tuple-element.84), channel_id=1, source_target_pairs={{0,16},{1,17},{2,18},{3,19},{4,20},{5,21},{6,22},{7,23},{8,24},{9,... | collective-permute-start | bytes 2211848 | tf_op jit(solution)/shard_map/ppermute | solution.py:235
  386.3 57.5 %collective-permute-start.7 = (f32[96,1920]{1,0:T(8,128)S(1)}, f32[96,1920]{1,0:T(8,128)S(1)}, u32[]{:S(2)}, u32[]{:S(2)}) collective-permute-start(f32[96,1920]{1,0:T(8,128)S(1)} %get-tuple-element.88), channel_id=1, source_target_pairs={{0,2},{1,3},{2,0},{3,1},{4,6},{5,7},{6,4},{7,5},{8,10},{9,11},{10,... | collective-permute-start | bytes 2211848 | tf_op jit(solution)/shard_map/ppermute | solution.py:235
  386.5 17.0 %collective-permute-start.40 = (f32[24,1536]{1,0:T(8,128)S(1)}, f32[24,1536]{1,0:T(8,128)S(1)}, u32[]{:S(2)}, u32[]{:S(2)}) collective-permute-start(f32[24,1536]{1,0:T(8,128)S(1)} %add_add_fusion.8), channel_id=1, source_target_pairs={{0,16},{1,17},{2,18},{3,19},{4,20},{5,21},{6,22},{7,23},{8,24},{9,... | collective-permute-start | bytes 442376 | tf_op jit(solution)/shard_map/ppermute | solution.py:235
  393.1 12.0 %collective-permute-start.30 = (f32[24,1536]{1,0:T(8,128)S(1)}, f32[24,1536]{1,0:T(8,128)S(1)}, u32[]{:S(2)}, u32[]{:S(2)}) collective-permute-start(f32[24,1536]{1,0:T(8,128)S(1)} %add_add_fusion.9), channel_id=1, source_target_pairs={{0,2},{1,3},{2,0},{3,1},{4,6},{5,7},{6,4},{7,5},{8,10},{9,11},{10,... | collective-permute-start | bytes 442376 | tf_op jit(solution)/shard_map/ppermute | solution.py:235
  395.4 25.6 %collective-permute-start.60 = (f32[48,768]{1,0:T(8,128)S(1)}, f32[48,768]{1,0:T(8,128)S(1)}, u32[]{:S(2)}, u32[]{:S(2)}) collective-permute-start(f32[48,768]{1,0:T(8,128)S(1)} %add_add_fusion.6), channel_id=1, source_target_pairs={{0,8},{1,9},{2,10},{3,11},{4,12},{5,13},{6,14},{7,15},{8,0},{9,1},... | collective-permute-start | bytes 442376 | tf_op jit(solution)/shard_map/ppermute | solution.py:235
  403.5 20.6 %collective-permute-start.50 = (f32[48,768]{1,0:T(8,128)S(1)}, f32[48,768]{1,0:T(8,128)S(1)}, u32[]{:S(2)}, u32[]{:S(2)}) collective-permute-start(f32[48,768]{1,0:T(8,128)S(1)} %add_add_fusion.7), channel_id=1, source_target_pairs={{0,8},{1,9},{2,10},{3,11},{4,12},{5,13},{6,14},{7,15},{8,0},{9,1},... | collective-permute-start | bytes 442376 | tf_op jit(solution)/shard_map/ppermute | solution.py:235
  405.1 25.4 %collective-permute-start.41 = (f32[48,1536]{1,0:T(8,128)S(1)}, f32[48,1536]{1,0:T(8,128)S(1)}, u32[]{:S(2)}, u32[]{:S(2)}) collective-permute-start(f32[48,1536]{1,0:T(8,128)S(1)} %pad_maximum_fusion.35), channel_id=1, source_target_pairs={{0,8},{1,9},{2,10},{3,11},{4,12},{5,13},{6,14},{7,15},{8,0},{9,1},... | collective-permute-start | bytes 884744 | tf_op jit(solution)/shard_map/ppermute | solution.py:235
  420.9 15.2 %collective-permute-start.31 = (f32[48,1536]{1,0:T(8,128)S(1)}, f32[48,1536]{1,0:T(8,128)S(1)}, u32[]{:S(2)}, u32[]{:S(2)}) collective-permute-start(f32[48,1536]{1,0:T(8,128)S(1)} %pad_maximum_fusion.34), channel_id=1, source_target_pairs={{0,8},{1,9},{2,10},{3,11},{4,12},{5,13},{6,14},{7,15},{8,0},{9,1},... | collective-permute-start | bytes 884744 | tf_op jit(solution)/shard_map/ppermute | solution.py:235
  424.1 18.4 %collective-permute-start.61 = (f32[96,768]{1,0:T(8,128)S(1)}, f32[96,768]{1,0:T(8,128)S(1)}, u32[]{:S(2)}, u32[]{:S(2)}) collective-permute-start(f32[96,768]{1,0:T(8,128)S(1)} %pad_maximum_fusion.37), channel_id=1, source_target_pairs={{0,4},{1,5},{2,6},{3,7},{4,0},{5,1},{6,2},{7,3},{8,12},{9,13},{10,... | collective-permute-start | bytes 884744 | tf_op jit(solution)/shard_map/ppermute | solution.py:235
  430.5 18.3 %collective-permute-start.51 = (f32[96,768]{1,0:T(8,128)S(1)}, f32[96,768]{1,0:T(8,128)S(1)}, u32[]{:S(2)}, u32[]{:S(2)}) collective-permute-start(f32[96,768]{1,0:T(8,128)S(1)} %pad_maximum_fusion.36), channel_id=1, source_target_pairs={{0,4},{1,5},{2,6},{3,7},{4,0},{5,1},{6,2},{7,3},{8,12},{9,13},{10,... | collective-permute-start | bytes 884744 | tf_op jit(solution)/shard_map/ppermute | solution.py:235
  436.1 53.7 %collective-permute-start.42 = (f32[96,1536]{1,0:T(8,128)S(1)}, f32[96,1536]{1,0:T(8,128)S(1)}, u32[]{:S(2)}, u32[]{:S(2)}) collective-permute-start(f32[96,1536]{1,0:T(8,128)S(1)} %pad_maximum_fusion.28), channel_id=1, source_target_pairs={{0,4},{1,5},{2,6},{3,7},{4,0},{5,1},{6,2},{7,3},{8,12},{9,13},{10,... | collective-permute-start | bytes 1769480 | tf_op jit(solution)/shard_map/ppermute | solution.py:235
  442.4 50.5 %collective-permute-start.32 = (f32[96,1536]{1,0:T(8,128)S(1)}, f32[96,1536]{1,0:T(8,128)S(1)}, u32[]{:S(2)}, u32[]{:S(2)}) collective-permute-start(f32[96,1536]{1,0:T(8,128)S(1)} %pad_maximum_fusion.27), channel_id=1, source_target_pairs={{0,4},{1,5},{2,6},{3,7},{4,0},{5,1},{6,2},{7,3},{8,12},{9,13},{10,... | collective-permute-start | bytes 1769480 | tf_op jit(solution)/shard_map/ppermute | solution.py:235
  442.6 50.7 %collective-permute-start.62 = (f32[192,768]{1,0:T(8,128)S(1)}, f32[192,768]{1,0:T(8,128)S(1)}, u32[]{:S(2)}, u32[]{:S(2)}) collective-permute-start(f32[192,768]{1,0:T(8,128)S(1)} %pad_maximum_fusion.30), channel_id=1, source_target_pairs={{0,16},{1,17},{2,18},{3,19},{4,20},{5,21},{6,22},{7,23},{8,24},{9,... | collective-permute-start | bytes 1769480 | tf_op jit(solution)/shard_map/ppermute | solution.py:235
  443.8 38.1 %collective-permute-start.18 = (f32[48,1920]{1,0:T(8,128)S(1)}, f32[48,1920]{1,0:T(8,128)S(1)}, u32[]{:S(2)}, u32[]{:S(2)}) collective-permute-start(f32[48,1920]{1,0:T(8,128)S(1)} %get-tuple-element.110), channel_id=1, source_target_pairs={{0,4},{1,5},{2,6},{3,7},{4,0},{5,1},{6,2},{7,3},{8,12},{9,13},{10,... | collective-permute-start | bytes 1105928 | tf_op jit(solution)/shard_map/ppermute | solution.py:235
  448.8 41.0 %collective-permute-start.8 = (f32[48,1920]{1,0:T(8,128)S(1)}, f32[48,1920]{1,0:T(8,128)S(1)}, u32[]{:S(2)}, u32[]{:S(2)}) collective-permute-start(f32[48,1920]{1,0:T(8,128)S(1)} %get-tuple-element.114), channel_id=1, source_target_pairs={{0,4},{1,5},{2,6},{3,7},{4,0},{5,1},{6,2},{7,3},{8,12},{9,13},{10,... | collective-permute-start | bytes 1105928 | tf_op jit(solution)/shard_map/ppermute | solution.py:235
  481.9 16.2 %collective-permute-start.52 = (f32[192,768]{1,0:T(8,128)S(1)}, f32[192,768]{1,0:T(8,128)S(1)}, u32[]{:S(2)}, u32[]{:S(2)}) collective-permute-start(f32[192,768]{1,0:T(8,128)S(1)} %pad_maximum_fusion.29), channel_id=1, source_target_pairs={{0,2},{1,3},{2,0},{3,1},{4,6},{5,7},{6,4},{7,5},{8,10},{9,11},{10,... | collective-permute-start | bytes 1769480 | tf_op jit(solution)/shard_map/ppermute | solution.py:235
  489.7 14.4 %collective-permute-start.19 = (f32[24,1920]{1,0:T(8,128)S(1)}, f32[24,1920]{1,0:T(8,128)S(1)}, u32[]{:S(2)}, u32[]{:S(2)}) collective-permute-start(f32[24,1920]{1,0:T(8,128)S(1)} %dynamic-slice_add_fusion.36), channel_id=1, source_target_pairs={{0,8},{1,9},{2,10},{3,11},{4,12},{5,13},{6,14},{7,15},{8,0},{9,1},... | collective-permute-start | bytes 552968 | tf_op jit(solution)/shard_map/ppermute | solution.py:235
  489.8 18.3 %collective-permute-start.9 = (f32[24,1920]{1,0:T(8,128)S(1)}, f32[24,1920]{1,0:T(8,128)S(1)}, u32[]{:S(2)}, u32[]{:S(2)}) collective-permute-start(f32[24,1920]{1,0:T(8,128)S(1)} %dynamic-slice_add_fusion.37), channel_id=1, source_target_pairs={{0,8},{1,9},{2,10},{3,11},{4,12},{5,13},{6,14},{7,15},{8,0},{9,1},... | collective-permute-start | bytes 552968 | tf_op jit(solution)/shard_map/ppermute | solution.py:235
  493.0 54.8 %collective-permute-start.43 = (f32[192,1536]{1,0:T(8,128)S(1)}, f32[192,1536]{1,0:T(8,128)S(1)}, u32[]{:S(2)}, u32[]{:S(2)}) collective-permute-start(f32[192,1536]{1,0:T(8,128)S(1)} %pad_maximum_fusion.21), channel_id=1, source_target_pairs={{0,2},{1,3},{2,0},{3,1},{4,6},{5,7},{6,4},{7,5},{8,10},{9,11},{10,... | collective-permute-start | bytes 3538952 | tf_op jit(solution)/shard_map/ppermute | solution.py:235
  493.2 55.7 %collective-permute-start.33 = (f32[192,1536]{1,0:T(8,128)S(1)}, f32[192,1536]{1,0:T(8,128)S(1)}, u32[]{:S(2)}, u32[]{:S(2)}) collective-permute-start(f32[192,1536]{1,0:T(8,128)S(1)} %pad_maximum_fusion.20), channel_id=1, source_target_pairs={{0,16},{1,17},{2,18},{3,19},{4,20},{5,21},{6,22},{7,23},{8,24},{9,... | collective-permute-start | bytes 3538952 | tf_op jit(solution)/shard_map/ppermute | solution.py:235
  498.1 65.4 %collective-permute-start.63 = (f32[384,768]{1,0:T(8,128)S(1)}, f32[384,768]{1,0:T(8,128)S(1)}, u32[]{:S(2)}, u32[]{:S(2)}) collective-permute-start(f32[384,768]{1,0:T(8,128)S(1)} %pad_maximum_fusion.23), channel_id=1, source_target_pairs={{0,2},{1,3},{2,0},{3,1},{4,6},{5,7},{6,4},{7,5},{8,10},{9,11},{10,... | collective-permute-start | bytes 3538952 | tf_op jit(solution)/shard_map/ppermute | solution.py:235
  504.2 62.0 %collective-permute-start.53 = (f32[384,768]{1,0:T(8,128)S(1)}, f32[384,768]{1,0:T(8,128)S(1)}, u32[]{:S(2)}, u32[]{:S(2)}) collective-permute-start(f32[384,768]{1,0:T(8,128)S(1)} %pad_maximum_fusion.22), channel_id=1, source_target_pairs={{0,16},{1,17},{2,18},{3,19},{4,20},{5,21},{6,22},{7,23},{8,24},{9,... | collective-permute-start | bytes 3538952 | tf_op jit(solution)/shard_map/ppermute | solution.py:235
  508.0 8.5 %collective-permute-start.20 = (f32[24,1920]{1,0:T(8,128)S(1)}, f32[24,1920]{1,0:T(8,128)S(1)}, u32[]{:S(2)}, u32[]{:S(2)}) collective-permute-start(f32[24,1920]{1,0:T(8,128)S(1)} %add_add_fusion.4), channel_id=1, source_target_pairs={{0,8},{1,9},{2,10},{3,11},{4,12},{5,13},{6,14},{7,15},{8,0},{9,1},... | collective-permute-start | bytes 552968 | tf_op jit(solution)/shard_map/ppermute | solution.py:235
  516.5 10.0 %collective-permute-start.10 = (f32[24,1920]{1,0:T(8,128)S(1)}, f32[24,1920]{1,0:T(8,128)S(1)}, u32[]{:S(2)}, u32[]{:S(2)}) collective-permute-start(f32[24,1920]{1,0:T(8,128)S(1)} %add_add_fusion.5), channel_id=1, source_target_pairs={{0,8},{1,9},{2,10},{3,11},{4,12},{5,13},{6,14},{7,15},{8,0},{9,1},... | collective-permute-start | bytes 552968 | tf_op jit(solution)/shard_map/ppermute | solution.py:235
  526.5 10.5 %collective-permute-start.21 = (f32[48,1920]{1,0:T(8,128)S(1)}, f32[48,1920]{1,0:T(8,128)S(1)}, u32[]{:S(2)}, u32[]{:S(2)}) collective-permute-start(f32[48,1920]{1,0:T(8,128)S(1)} %pad_maximum_fusion.33), channel_id=1, source_target_pairs={{0,4},{1,5},{2,6},{3,7},{4,0},{5,1},{6,2},{7,3},{8,12},{9,13},{10,... | collective-permute-start | bytes 1105928 | tf_op jit(solution)/shard_map/ppermute | solution.py:235
  537.0 9.6 %collective-permute-start.11 = (f32[48,1920]{1,0:T(8,128)S(1)}, f32[48,1920]{1,0:T(8,128)S(1)}, u32[]{:S(2)}, u32[]{:S(2)}) collective-permute-start(f32[48,1920]{1,0:T(8,128)S(1)} %pad_maximum_fusion.32), channel_id=1, source_target_pairs={{0,4},{1,5},{2,6},{3,7},{4,0},{5,1},{6,2},{7,3},{8,12},{9,13},{10,... | collective-permute-start | bytes 1105928 | tf_op jit(solution)/shard_map/ppermute | solution.py:235
  546.6 16.7 %collective-permute-start.22 = (f32[96,1920]{1,0:T(8,128)S(1)}, f32[96,1920]{1,0:T(8,128)S(1)}, u32[]{:S(2)}, u32[]{:S(2)}) collective-permute-start(f32[96,1920]{1,0:T(8,128)S(1)} %pad_maximum_fusion.26), channel_id=1, source_target_pairs={{0,16},{1,17},{2,18},{3,19},{4,20},{5,21},{6,22},{7,23},{8,24},{9,... | collective-permute-start | bytes 2211848 | tf_op jit(solution)/shard_map/ppermute | solution.py:235
  547.8 17.6 %collective-permute-start.12 = (f32[96,1920]{1,0:T(8,128)S(1)}, f32[96,1920]{1,0:T(8,128)S(1)}, u32[]{:S(2)}, u32[]{:S(2)}) collective-permute-start(f32[96,1920]{1,0:T(8,128)S(1)} %pad_maximum_fusion.25), channel_id=1, source_target_pairs={{0,2},{1,3},{2,0},{3,1},{4,6},{5,7},{6,4},{7,5},{8,10},{9,11},{10,... | collective-permute-start | bytes 2211848 | tf_op jit(solution)/shard_map/ppermute | solution.py:235
  548.9 54.7 %collective-permute-start.44 = (f32[384,1536]{1,0:T(8,128)S(1)}, f32[384,1536]{1,0:T(8,128)S(1)}, u32[]{:S(2)}, u32[]{:S(2)}) collective-permute-start(f32[384,1536]{1,0:T(8,128)S(1)} %pad_maximum_fusion.12), channel_id=1, source_target_pairs={{0,1},{1,0},{2,3},{3,2},{4,5},{5,4},{6,7},{7,6},{8,9},{9,8},{10,11... | collective-permute-start | bytes 7077896 | tf_op jit(solution)/shard_map/ppermute | solution.py:235
  563.3 47.9 %collective-permute-start.34 = (f32[384,1536]{1,0:T(8,128)S(1)}, f32[384,1536]{1,0:T(8,128)S(1)}, u32[]{:S(2)}, u32[]{:S(2)}) collective-permute-start(f32[384,1536]{1,0:T(8,128)S(1)} %pad_maximum_fusion.11), channel_id=1, source_target_pairs={{0,1},{1,0},{2,3},{3,2},{4,5},{5,4},{6,7},{7,6},{8,9},{9,8},{10,11... | collective-permute-start | bytes 7077896 | tf_op jit(solution)/shard_map/ppermute | solution.py:235
  563.5 34.8 %collective-permute-start.23 = (f32[192,1920]{1,0:T(8,128)S(1)}, f32[192,1920]{1,0:T(8,128)S(1)}, u32[]{:S(2)}, u32[]{:S(2)}) collective-permute-start(f32[192,1920]{1,0:T(8,128)S(1)} %pad_maximum_fusion.17), channel_id=1, source_target_pairs={{0,2},{1,3},{2,0},{3,1},{4,6},{5,7},{6,4},{7,5},{8,10},{9,11},{10,... | collective-permute-start | bytes 4423688 | tf_op jit(solution)/shard_map/ppermute | solution.py:235
  565.7 34.6 %collective-permute-start.13 = (f32[192,1920]{1,0:T(8,128)S(1)}, f32[192,1920]{1,0:T(8,128)S(1)}, u32[]{:S(2)}, u32[]{:S(2)}) collective-permute-start(f32[192,1920]{1,0:T(8,128)S(1)} %pad_maximum_fusion.16), channel_id=1, source_target_pairs={{0,16},{1,17},{2,18},{3,19},{4,20},{5,21},{6,22},{7,23},{8,24},{9,... | collective-permute-start | bytes 4423688 | tf_op jit(solution)/shard_map/ppermute | solution.py:235
  566.2 40.1 %collective-permute-start.64 = (f32[768,768]{1,0:T(8,128)S(1)}, f32[768,768]{1,0:T(8,128)S(1)}, u32[]{:S(2)}, u32[]{:S(2)}) collective-permute-start(f32[768,768]{1,0:T(8,128)S(1)} %pad_maximum_fusion.14), channel_id=1, source_target_pairs={{0,1},{1,0},{2,3},{3,2},{4,5},{5,4},{6,7},{7,6},{8,9},{9,8},{10,11... | collective-permute-start | bytes 7077896 | tf_op jit(solution)/shard_map/ppermute | solution.py:235
  598.3 10.5 %collective-permute-start.54 = (f32[768,768]{1,0:T(8,128)S(1)}, f32[768,768]{1,0:T(8,128)S(1)}, u32[]{:S(2)}, u32[]{:S(2)}) collective-permute-start(f32[768,768]{1,0:T(8,128)S(1)} %pad_maximum_fusion.13), channel_id=1, source_target_pairs={{0,1},{1,0},{2,3},{3,2},{4,5},{5,4},{6,7},{7,6},{8,9},{9,8},{10,11... | collective-permute-start | bytes 7077896 | tf_op jit(solution)/shard_map/ppermute | solution.py:235
  600.3 30.5 %collective-permute-start.24 = (f32[384,1920]{1,0:T(8,128)}, f32[384,1920]{1,0:T(8,128)}, u32[]{:S(2)}, u32[]{:S(2)}) collective-permute-start(f32[384,1920]{1,0:T(8,128)} %pad_maximum_fusion.6), channel_id=1, source_target_pairs={{0,1},{1,0},{2,3},{3,2},{4,5},{5,4},{6,7},{7,6},{8,9},{9,8},{10,11... | collective-permute-start | bytes 8847368 | tf_op jit(solution)/shard_map/ppermute | solution.py:235
  603.6 29.6 %collective-permute-start.14 = (f32[384,1920]{1,0:T(8,128)}, f32[384,1920]{1,0:T(8,128)}, u32[]{:S(2)}, u32[]{:S(2)}) collective-permute-start(f32[384,1920]{1,0:T(8,128)} %pad_maximum_fusion.3), channel_id=1, source_target_pairs={{0,1},{1,0},{2,3},{3,2},{4,5},{5,4},{6,7},{7,6},{8,9},{9,8},{10,11... | collective-permute-start | bytes 8847368 | tf_op jit(solution)/shard_map/ppermute | solution.py:235
  (89 other events, 513.9 us)

commit v3 on v2

--- a/solution.py
+++ b/solution.py
@@ -47,10 +47,6 @@
 
 def mm_t(a, b):
     return lax.dot_general(a, b, (((1,), (1,)), ((), ())), preferred_element_type=jnp.float32)
-
-
-def t_mm(a, b):
-    return lax.dot_general(a, b, (((0,), (0,)), ((), ())), preferred_element_type=jnp.float32)
 
 
 def dot_nt(a, b):
@@ -178,12 +174,12 @@
             gb_ref[a] = fold_diagonals(fold_ref[a])
 
 
-def attention_specs(length, width, group, span):
+def attention_specs(length, width, group, span, first):
     return (
-        pl.BlockSpec((length, width), lambda h, m: (m, h)),
+        pl.BlockSpec((length, width), lambda h, m: (m, first + h)),
         pl.BlockSpec((length, 1), lambda h, m: (m, 0)),
         pl.BlockSpec((None, 1, length), lambda h, m: (m, 0, 0)),
-        pl.BlockSpec((group, 1, span), lambda h, m: (h, 0, 0)),
+        pl.BlockSpec((group, 1, span), lambda h, m: (first + h, 0, 0)),
     )
 
 
@@ -192,7 +188,7 @@
     model_width = query.shape[1]
     width = max(LANES, head_dim)
     group = width // head_dim
-    block, segc, segr, line = attention_specs(length, width, group, rows.shape[2])
+    block, segc, segr, line = attention_specs(length, width, group, rows.shape[2], 0)
     return pl.pallas_call(
         lambda *refs: forward_kernel(head_dim, *refs),
         name="attention_forward",
@@ -204,22 +200,31 @@
     )(query, key, value, segment.reshape(-1, 1), segment[:, None, :], rows)
 
 
-def attention_grads(query, key, value, grad, segment, rows, head_dim):
+def attention_grads(query, key, value, grad, segment, rows, head_dim, part, parts, before):
     micro_count, length = segment.shape
     model_width = query.shape[1]
     width = max(LANES, head_dim)
     group = width // head_dim
-    block, segc, segr, line = attention_specs(length, width, group, rows.shape[2])
+    count = model_width // width // parts
+    first = part * count
+    block, segc, segr, line = attention_specs(length, width, group, rows.shape[2], first)
     flat = jax.ShapeDtypeStruct(query.shape, jnp.bfloat16)
+    kept = len(before)
+
+    def kernel(*refs):
+        backward_kernel(head_dim, *refs[:7], *refs[7 + kept :])
+
     return pl.pallas_call(
-        lambda *refs: backward_kernel(head_dim, *refs),
+        kernel,
         name="attention_backward",
-        grid=(model_width // width, micro_count),
-        in_specs=[block, block, block, block, segc, segr, line],
+        grid=(count, micro_count),
+        in_specs=[block, block, block, block, segc, segr, line]
+        + [pl.BlockSpec(memory_space=pl.ANY)] * kept,
         out_specs=[block, block, block, line],
         out_shape=[flat, flat, flat, jax.ShapeDtypeStruct(rows.shape, jnp.float32)],
+        input_output_aliases={7 + n: n for n in range(kept)},
         scratch_shapes=[pltpu.VMEM((group, LANES, rows.shape[2]), jnp.float32)] * 2,
-    )(query, key, value, grad, segment.reshape(-1, 1), segment[:, None, :], rows)
+    )(query, key, value, grad, segment.reshape(-1, 1), segment[:, None, :], rows, *before)
 
 
 class Net:
@@ -227,18 +232,34 @@
         self.dp = lax.axis_size("dp")
         self.size = self.dp * lax.axis_size("tower")
         self.index = lax.axis_index("tower") * self.dp + lax.axis_index("dp")
+        count = self.size.bit_length() - 1
+        if count == 5:
+            self.steps = ((0, 0), (4, 1), (1, 4), (2, 2), (3, 3))
+        else:
+            self.steps = tuple((b, b) for b in range(count))
+        self.bits = [self.bit_of(k) for k in range(count)]
 
     def bit(self, b):
         return (self.index >> b) & 1
 
+    def bit_of(self, k):
+        first, second = self.steps[k]
+        if first == second:
+            return self.bit(first)
+        return jnp.where(self.bit(0) == 0, self.bit(first), self.bit(second))
+
     def swap(self, value, b):
         return lax.ppermute(value, AXES, [(i, i ^ (1 << b)) for i in range(self.size)])
 
+    def swap_step(self, value, k):
+        pairs = [(i, i ^ (1 << self.steps[k][i & 1])) for i in range(self.size)]
+        return lax.ppermute(value, AXES, pairs)
+
 
 def join(own, other, bit):
-    first = jnp.where(bit == 0, own, other)
-    second = jnp.where(bit == 0, other, own)
-    return jnp.concatenate([first, second], axis=0)
+    rows, width = own.shape
+    side = lax.broadcasted_iota(jnp.int32, (2, rows, width), 0)
+    return jnp.where(side == bit, own[None], other[None]).reshape(2 * rows, width)
 
 
 def half_of(value, which):
@@ -246,26 +267,226 @@
     return lax.dynamic_slice_in_dim(value, which * rows, rows, 0)
 
 
-def scatter_sum(net, sent, kept, order):
-    got = net.swap(sent, order[0])
-    for b in order[1:]:
-        bit = net.bit(b)
-        sent = half_of(kept, 1 - bit) + half_of(got, 1 - bit)
-        kept = half_of(kept, bit) + half_of(got, bit)
-        got = net.swap(sent, b)
-    return kept + got
-
-
-def gather_all(net, piece, order):
-    for b in reversed(order):
-        piece = join(piece, net.swap(piece, b), net.bit(b))
-    return piece
-
-
-def sum_small(net, value, order):
-    for b in order:
-        value = value + net.swap(value, b)
-    return value
+def weight_grads(bit, lefts, rights):
+    height = lefts[0].shape[1] // 2
+    width = min(r.shape[1] for r in rights)
+    rows = max(r for r in range(LANES, min(height, 512) + 1, LANES) if height % r == 0)
+    stacks = height // rows
+    ends = [sum(r.shape[1] for r in rights[: n + 1]) // width for n in range(len(rights))]
+    starts = [end - r.shape[1] // width for end, r in zip(ends, rights)]
+    columns = ends[-1]
+    count = len(lefts)
+
+    def kernel(bit_ref, *refs):
+        left_refs, right_refs, (sent_ref, kept_ref) = refs[:count], refs[count:-2], refs[-2:]
+        side, column = pl.program_id(0), pl.program_id(2)
+
+        def one(left_ref, right_ref):
+            value = dot_tn(left_ref[...], right_ref[...])
+
+            @pl.when(side == 0)
+            def _():
+                sent_ref[...] = value
+
+            @pl.when(side == 1)
+            def _():
+                kept_ref[...] = value
+
+        for left_ref, right_ref, start, end in zip(left_refs, right_refs, starts, ends):
+            inside = (column >= start) & (column < end)
+            pl.when(inside)(lambda left_ref=left_ref, right_ref=right_ref: one(left_ref, right_ref))
+
+    def left_place(side, stack, column, bit_ref):
+        half = jnp.where(side == 0, 1 - bit_ref[0], bit_ref[0])
+        return (0, half * stacks + stack)
+
+    def right_place(start, end):
+        return lambda side, stack, column, bit_ref: (0, jnp.clip(column - start, 0, end - start - 1))
+
+    def sent_place(side, stack, column, bit_ref):
+        return (jnp.where(side == 0, stack, stacks - 1), jnp.where(side == 0, column, columns - 1))
+
+    def kept_place(side, stack, column, bit_ref):
+        return (jnp.where(side == 1, stack, 0), jnp.where(side == 1, column, 0))
+
+    return pl.pallas_call(
+        kernel,
+        name="weight_grads",
+        grid_spec=pltpu.PrefetchScalarGridSpec(
+            num_scalar_prefetch=1,
+            grid=(2, stacks, columns),
+            in_specs=[pl.BlockSpec((v.shape[0], rows), left_place) for v in lefts]
+            + [
+                pl.BlockSpec((v.shape[0], width), right_place(start, end))
+                for v, start, end in zip(rights, starts, ends)
+            ],
+            out_specs=[
+                pl.BlockSpec((rows, width), sent_place),
+                pl.BlockSpec((rows, width), kept_place),
+            ],
+        ),
+        out_shape=[jax.ShapeDtypeStruct((height, columns * width), jnp.float32)] * 2,
+    )(bit.reshape(1), *lefts, *rights)
+
+
+def feed_backward_kernel(
+    go_ref, act_ref, hid_ref, gain_ref, wff_ref, win_ref, wout_ref,
+    gu_ref, gh_ref, ghl_ref, gm_ref, gg_ref,
+):
+    grad_output = go_ref[...]
+    grad_activ = dot_nt(grad_output.astype(jnp.bfloat16), wff_ref[...])
+    grad_inner = jnp.where(act_ref[...] > 0, grad_activ, 0.0).astype(jnp.bfloat16)
+    gu_ref[...] = grad_inner
+    grad_normed = dot_nt(grad_inner, win_ref[...])
+    hidden = hid_ref[...]
+    scale = lax.rsqrt(jnp.mean(hidden * hidden, axis=1, keepdims=True) + norm_epsilon)
+    unit = hidden * scale
+
+    @pl.when(pl.program_id(0) == 0)
+    def _():
+        gg_ref[...] = jnp.zeros_like(gg_ref)
+
+    gg_ref[...] += jnp.sum(grad_normed * unit, axis=0, keepdims=True)
+    scaled = grad_normed * gain_ref[...]
+    grad_hidden = grad_output + scale * (
+        scaled - unit * jnp.mean(unit * scaled, axis=1, keepdims=True)
+    )
+    gh_ref[...] = grad_hidden
+    low = grad_hidden.astype(jnp.bfloat16)
+    ghl_ref[...] = low
+    gm_ref[...] = dot_nt(low, wout_ref[...]).astype(jnp.bfloat16)
+
+
+def feed_backward(grad_output, activ, hidden, gain, w_ffout, w_in, w_out):
+    rows, width = grad_output.shape
+    inner = activ.shape[1]
+    tile = 256
+
+    def lines(n):
+        return pl.BlockSpec((tile, n), lambda t: (t, 0))
+
+    def whole(*shape):
+        return pl.BlockSpec(shape, lambda t: (0, 0))
+
+    return pl.pallas_call(
+        feed_backward_kernel,
+        name="feed_backward",
+        grid=(rows // tile,),
+        in_specs=[
+            lines(width),
+            lines(inner),
+            lines(width),
+            whole(1, width),
+            whole(inner, width),
+            whole(width, inner),
+            whole(width, width),
+        ],
+        out_specs=[lines(inner), lines(width), lines(width), lines(width), whole(1, width)],
+        out_shape=[
+            jax.ShapeDtypeStruct((rows, inner), jnp.bfloat16),
+            jax.ShapeDtypeStruct((rows, width), jnp.float32),
+            jax.ShapeDtypeStruct((rows, width), jnp.bfloat16),
+            jax.ShapeDtypeStruct((rows, width), jnp.bfloat16),
+            jax.ShapeDtypeStruct((1, width), jnp.float32),
+        ],
+    )(grad_output, activ, hidden, gain[None], w_ffout, w_in, w_out)
+
+
+def put_together(own, other, bit, widths):
+    half = 4
+    rows, wide = own.shape
+    block = rows // half
+
+    def kernel(bit_ref, own_ref, other_ref, *out_refs):
+        is_own = pl.program_id(0) // half == bit_ref[0]
+
+        def copy(source):
+            at = 0
+            for out, width in zip(out_refs, widths):
+                out[...] = source[:, at : at + width]
+                at += width
+
+        pl.when(is_own)(lambda: copy(own_ref))
+        pl.when(jnp.logical_not(is_own))(lambda: copy(other_ref))
+
+    def place(side):
+        def index(step, bit_ref):
+            first = jnp.where(side == 0, bit_ref[0], 1 - bit_ref[0]) * half
+            return (jnp.clip(step - first, 0, half - 1), 0)
+
+        return index
+
+    return pl.pallas_call(
+        kernel,
+        name="put_together",
+        grid_spec=pltpu.PrefetchScalarGridSpec(
+            num_scalar_prefetch=1,
+            grid=(2 * half,),
+            in_specs=[pl.BlockSpec((block, wide), place(side)) for side in (0, 1)],
+            out_specs=[pl.BlockSpec((block, w), lambda step, bit_ref: (step, 0)) for w in widths],
+        ),
+        out_shape=[jax.ShapeDtypeStruct((2 * rows, w), own.dtype) for w in widths],
+        cost_estimate=pl.CostEstimate(
+            flops=0, transcendentals=0, bytes_accessed=16 * rows * wide
+        ),
+    )(bit.reshape(1), own, other)
+
+
+def tie(*values):
+    return lax.optimization_barrier(values)
+
+
+class Sum:
+    def __init__(self, net, lefts, rights):
+        self.net = net
+        self.widths = [r.shape[1] for r in rights]
+        self.step = 0
+        self.back = False
+        self.done = False
+        self.held = weight_grads(net.bits[0], lefts, rights)
+
+    def go(self):
+        if self.back:
+            self.got = self.net.swap_step(self.held[0], self.step - 1)
+        else:
+            self.got = self.net.swap_step(self.held[0], self.step)
+
+    def end(self):
+        bits = self.net.bits
+        if self.back:
+            self.step -= 1
+            self.done = self.step == 0
+            if self.done:
+                self.held = put_together(self.held[0], self.got, bits[0], self.widths)
+            else:
+                self.held = [join(self.held[0], self.got, bits[self.step])]
+            return
+        self.step += 1
+        self.back = self.step == len(bits)
+        kept, got = self.held[1], self.got
+        if self.back:
+            self.held = [kept + got]
+        else:
+            bit = bits[self.step]
+            self.held = [
+                half_of(kept, 1 - bit) + half_of(got, 1 - bit),
+                half_of(kept, bit) + half_of(got, bit),
+            ]
+
+
+def tie_all(sums, *values):
+    values, held = tie(values, [s.held for s in sums])
+    for s, h in zip(sums, held):
+        s.held = h
+    return values
+
+
+def advance(sums, steps):
+    for s, count in zip(sums, steps):
+        for _ in range(count):
+            if not s.done:
+                s.go()
+                s.end()
 
 
 def local(
@@ -298,9 +519,7 @@
     row_count = item_count * dp_count
     rows = micro_count * length
     net = Net()
-    bits = net.size.bit_length() - 1
-    core = 0
-    chips = tuple(range(1, bits))
+    bits = len(net.steps)
     gather_order = (0, 4, 1, 2, 3) if bits == 5 else tuple(range(bits))
 
     offset = jnp.arange(2 * length, dtype=jnp.int32) - length
@@ -320,7 +539,7 @@
     value_low = mm(normed_low, w_value).astype(jnp.bfloat16)
     mixed_low = attention(query_low, key_low, value_low, segment, bias_rows(code), head_dim)
     hidden = states_f + mm(mixed_low, w_out)
-    normed_two, back_ffn = jax.vjp(rms_scale, hidden, gain_ffn)
+    normed_two = rms_scale(hidden, gain_ffn)
     normed_two_low = normed_two.astype(jnp.bfloat16)
     activ_low = jnp.maximum(mm(normed_two_low, w_in), 0.0).astype(jnp.bfloat16)
     output = hidden + mm(activ_low, w_ffout)
@@ -340,7 +559,7 @@
     embed = mm(pooled_flat, w_proj)
     unit_embed, back_unit = jax.vjp(unit_rows, embed)
 
-    every = unit_embed[None]
+    every = unit_embed
     for b in reversed(gather_order):
         every = join(every, net.swap(every, b), net.bit(b))
     every = every.reshape((2,) * bits + (micro_count, item_count, model_width))
@@ -376,93 +595,93 @@
     grad_output, grad_gain_final = back_final(grad_final_norm)
     grad_output_low = grad_output.astype(jnp.bfloat16)
 
-    def halves(left, right, core_bit):
-        wide = left.shape[1] // 2
-        other = t_mm(
-            lax.dynamic_slice_in_dim(left, (1 - core_bit) * wide, wide, 1), right
+    first = Sum(net, [activ_low], [grad_output_low])
+    (grad_output,) = tie_all([first], grad_output)
+    first.go()
+    grad_inner_low, grad_hidden, grad_hidden_low, grad_mixed, grad_gain_ffn = feed_backward(
+        grad_output, activ_low, hidden, gain_ffn, w_ffout, w_in, w_out
+    )
+    first.end()
+    grad_inner_low, grad_hidden_low, grad_mixed = tie_all(
+        [first], grad_inner_low, grad_hidden_low, grad_mixed
+    )
+    first.go()
+    parts = 3
+    rows_back = bias_rows(code_back)
+
+    def attention_part(part, query, before):
+        return attention_grads(
+            query, key_low, value_low, grad_mixed, segment, rows_back, head_dim, part, parts, before
         )
-        own = t_mm(lax.dynamic_slice_in_dim(left, core_bit * wide, wide, 1), right)
-        return other, own
-
-    core_bit = net.bit(core)
-    if bits == 5:
-        orders = (((0, 4, 1, 2, 3), (0, 1, 4, 2, 3)), ((0, 4, 2, 3, 1), (0, 1, 2, 3, 4)))
-    else:
-        orders = ((tuple(range(bits)),) * 2,) * 2
-
-    def total(left, right, order):
-        sent, kept = halves(left, right, core_bit)
-        return gather_all(net, scatter_sum(net, sent, kept, order), order)
-
-    ff_half = ff_width // 2
-    whole_ffout = jnp.concatenate(
-        [
-            total(activ_low[:, :ff_half], grad_output_low, orders[0][0]),
-            total(activ_low[:, ff_half:], grad_output_low, orders[0][1]),
-        ],
-        axis=0,
-    )
-    grad_activ = mm_t(grad_output_low, w_ffout)
-    grad_inner_low = jnp.where(activ_low > 0, grad_activ, 0.0).astype(jnp.bfloat16)
-    whole_in = jnp.concatenate(
-        [
-            total(normed_two_low, grad_inner_low[:, :ff_half], orders[1][0]),
-            total(normed_two_low, grad_inner_low[:, ff_half:], orders[1][1]),
-        ],
-        axis=1,
-    )
-    grad_normed_two = mm_t(grad_inner_low, w_in)
-    grad_hidden_norm, grad_gain_ffn = back_ffn(grad_normed_two)
-    grad_hidden = grad_output + grad_hidden_norm
-    grad_hidden_low = grad_hidden.astype(jnp.bfloat16)
-    grad_mixed = mm_t(grad_hidden_low, w_out).astype(jnp.bfloat16)
-    grad_query_h, grad_key_h, grad_value_h, grad_rows = attention_grads(
-        query_low, key_low, value_low, grad_mixed, segment, bias_rows(code_back), head_dim
-    )
+
+    grads = attention_part(0, query_low, ())
+    second = Sum(net, [normed_two_low], [grad_inner_low])
+    first.end()
+    query_low, grads = tie_all([first, second], query_low, grads)
+    first.go()
+    second.go()
+    grads = attention_part(1, query_low, grads)
+    first.end()
+    second.end()
+    query_low, grads = tie_all([first, second], query_low, grads)
+    first.go()
+    second.go()
+    grads = attention_part(2, query_low, grads)
+    first.end()
+    (grads,) = tie_all([first], grads)
+    grad_query_h, grad_key_h, grad_value_h, grad_rows = grads
+    first.go()
+    third = Sum(
+        net,
+        [normed_low] * 3 + [mixed_low, pooled_flat],
+        [grad_query_h, grad_key_h, grad_value_h, grad_hidden_low, grad_e_low],
+    )
+    first.end()
+    second.end()
+    grad_query_h, grad_key_h, grad_value_h = tie_all(
+        [first, second, third], grad_query_h, grad_key_h, grad_value_h
+    )
+    sums = [first, second, third]
+    advance(sums, (1, 1, 1))
     grad_bias = jnp.einsum("hx,xb->bh", grad_rows[:, 0], code_back, precision=highest)
-    grad_qkv = jnp.concatenate([grad_query_h, grad_key_h, grad_value_h], axis=1)
     grad_normed = (
         mm_t(grad_query_h, w_query) + mm_t(grad_key_h, w_key) + mm_t(grad_value_h, w_value)
     )
-    cut = model_width // 2
-    first_sent, first_kept = halves(normed_low, grad_qkv[:, : 5 * cut], core_bit)
-    rest = [
-        halves(normed_low, grad_qkv[:, 5 * cut :], core_bit),
-        halves(mixed_low, grad_hidden_low, core_bit),
-        halves(pooled_flat, grad_e_low, core_bit),
-    ]
-    last_sent = jnp.concatenate([r[0] for r in rest], axis=1)
-    last_kept = jnp.concatenate([r[1] for r in rest], axis=1)
-    order = orders[0][0]
-    whole_first = gather_all(net, scatter_sum(net, first_sent, first_kept, order), order)
-    order = orders[0][1]
-    whole_last = gather_all(net, scatter_sum(net, last_sent, last_kept, order), order)
-
     grad_states_norm, grad_gain_attn = back_attn(grad_normed)
     grad_states = grad_hidden + grad_states_norm
     small = jnp.concatenate(
-        [
-            grad_gain_attn,
-            grad_gain_ffn,
-            grad_gain_final,
-            grad_bias.reshape(-1),
-            jnp.zeros((model_width - bucket_count * head_count,), jnp.float32),
-        ]
-    ).reshape(-1, 128)
-    small = sum_small(net, small, tuple(range(bits))).reshape(-1)
+        [grad_gain_attn, grad_gain_ffn[0], grad_gain_final, grad_bias.reshape(-1)]
+    )
+    lines = -(-small.shape[0] // (8 * LANES)) * 8
+    small = jnp.pad(small, (0, lines * LANES - small.shape[0])).reshape(lines, LANES)
+    (grad_states,) = tie_all(sums, grad_states)
+    if bits == 5:
+        plan = ((1, 1, 1), (1, 2, 1), (1, 1, 1), (1, 1, 1), (0, 1, 2), (0, 1, 1), (0, 0, 1), (0, 0, 1))
+    else:
+        plan = ((1, 1, 1),) * (2 * bits)
+    for turn, steps in enumerate(plan):
+        advance(sums, steps)
+        if turn < bits:
+            small = small + net.swap(small, turn)
+        if turn + 1 < len(plan):
+            (small,) = tie_all(sums, small)
+    (whole_ffout,) = first.held
+    (whole_in,) = second.held
+    whole_query, whole_key, whole_value, whole_out, whole_proj = third.held
+    small = small.reshape(-1)
     loss = loss_sum / (micro_count * row_count)
     width = model_width
     return (
         loss,
         unit_embed.reshape(1, micro_count, item_count, model_width),
         grad_states.reshape(1, micro_count, length, model_width),
-        whole_first[:, :width],
-        whole_first[:, width : 2 * width],
-        jnp.concatenate([whole_first[:, 2 * width :], whole_last[:, :cut]], axis=1),
-        whole_last[:, cut : cut + width],
+        whole_query,
+        whole_key,
+        whole_value,
+        whole_out,
         whole_in,
         whole_ffout,
-        whole_last[:, cut + width :],
+        whole_proj,
         small[:width],
         small[width : 2 * width],
         small[2 * width : 3 * width],

time: 650 us -> 580 us (0.89)
  Pallas kernels: 71.7 us -> 171 us
  waiting for transfers between devices: 295 us -> 214 us
  matrix products: 106 us -> 39 us
  starting transfers between devices: 60.1 us -> 39.6 us
  other arithmetic: 80.3 us -> 89.3 us
  local copies, waits for them, and re-layouts: 23.9 us -> 14.9 us
    ppermute x70 -> x10, waiting for transfers between devices: 295 us -> 79.4 us  [swap(): lax.ppermute(value, AXES, [(i, i ^ 1 << b) for i in range(self.size)])]
    ppermute x0 -> x30, waiting for transfers between devices: none -> 135 us  [swap_step(): return lax.ppermute(value, AXES, pairs)]
    pallas_call x1 -> x10, Pallas kernels: 43.1 us -> 142 us  [the longest x3 47.1 us: attention_grads(): pl.pallas_call(kernel, name='attention_backward', grid=(count, micro_coun...]
    ppermute x70 -> x10, starting transfers between devices: 60.1 us -> 13.4 us  [swap(): lax.ppermute(value, AXES, [(i, i ^ 1 << b) for i in range(self.size)])]
    dot_general x16 -> x0, matrix products: 33.6 us -> none  [t_mm(): lax.dot_general(a, b, (((0,), (0,)), ((), ())), preferred_element_type=jn...]
    concatenate x34 -> x0, other arithmetic: 30.5 us -> none  [the longest x30 11.5 us: join(): return jnp.concatenate([first, second], axis=0)]
    dot_general x7 -> x4, matrix products: 36 us -> 8.57 us  [mm_t(): lax.dot_general(a, b, (((1,), (1,)), ((), ())), preferred_element_type=jn...]
    ppermute x0 -> x30, starting transfers between devices: none -> 26.2 us  [swap_step(): return lax.ppermute(value, AXES, pairs)]
  transfers between devices with their start and end apart: 70 -> 40, of which waited for: 35 -> 20; matrix products, arithmetic and copies ran while one was open for 13% -> 8% of each run, Pallas kernels for 0% -> 17%
where the time goes in v3:
time: 580 us; the launch traced here: 572 us
  waiting for transfers between devices  214 us (37%)
  Pallas kernels  171 us (29%)
  other arithmetic  89.3 us (15%)
  starting transfers between devices  39.6 us (7%)
  matrix products  39 us (7%)
  local copies, waits for them, and re-layouts  14.9 us (3%)
    ppermute x30, waiting for transfers between devices, swap_step(): return lax.ppermute(value, AXES, pairs)  135 us
    ppermute x10, waiting for transfers between devices, swap(): lax.ppermute(value, AXES, [(i, i ^ 1 << b) for i in range(self.size)])  79.4 us
    pallas_call x3, Pallas kernels, attention_grads(): pl.pallas_call(kernel, name='attention_backward', grid=(count, micro_coun...  47.1 us
    pallas_call x3, Pallas kernels, weight_grads(): pl.pallas_call(kernel, name='weight_grads', grid_spec=pltpu.PrefetchScala...  41.4 us
    add x12, other arithmetic, end(): half_of(kept, bit) + half_of(got, bit)  40.7 us
    select_n x19, other arithmetic, join(): jnp.where(side == bit, own[None], other[None]).reshape(2 * rows, width)  33.5 us
    pallas_call x3, Pallas kernels, put_together(): pl.pallas_call(kernel, name='put_together', grid_spec=pltpu.PrefetchScala...  31.7 us
    pallas_call x1, Pallas kernels, attention(): pl.pallas_call(lambda *refs: forward_kernel(head_dim, *refs), name='atten...  28.8 us
  transfers between devices with their start and end apart: 40, of which 20 were waited for; matrix products, arithmetic and copies ran while one was open for 8% of the time, Pallas kernels for 17%

profile of v3, /device:TPU:0, one launch (start us, length us, event | category | flops | bytes accessed | tf_op | source)
XLA Modules:
  0.0 572.1 jit_solution(7310394400484994789)
XLA Ops:
  1.3 1.9 fusion.6
  4.4 2.5 convolution_convert_fusion.2.refs_0_
  6.9 2.5 convolution_convert_fusion.1.refs_1_
  9.5 2.5 convolution_convert_fusion.refs_2_
  14.9 28.8 %attention_forward.1.refs_3_ = bf16[1024,768]{1,0:T(8,128)(2,1)} custom-call(bf16[1024,768]{1,0:T(8,128)(2,1)} %convolution_convert_fusion.2.refs_0_, bf16[1024,768]{1,0:T(8,128)(2,1)} %convolution_convert_fusion.1.refs_1_, bf16[1024,768]{1,0:T(8,128)(2,1)} %convolution_convert_fusion.refs_2_, s32[1024,1]{1,0:T(8,128)} %bitcast.219, ...), custom_call_target="tpu_custom_call" | custom-call | tf_op jit(solution)/shard_map/attention_forward/pallas_call | solution.py:192
  43.7 3.4 multiply_reduce_fusion.2
  48.7 5.8 %maximum_convert_fusion.refs_0_.act_ref = bf16[1024,3072]{1,0:T(8,128)(2,1)S(1)} fusion(bf16[1024,768]{1,0:T(8,128)(2,1)S(1)} %multiply_convert_fusion.refs_0_, bf16[768,3072]{1,0:T(8,128)(2,1)S(1)} %bitcast.227), kind=kOutput, calls=%fused_computation | convolution fusion | flops 4838129664 | bytes 12582912 | tf_op jit(solution)/shard_map/dot_general | solution.py:45
  54.6 5.2 multiply_reduce_fusion.1
  63.8 4.1 collective-permute-start
  68.5 1.9 collective-permute-done
  72.4 2.7 collective-permute-done.1
  75.9 1.8 collective-permute-start.2
  77.8 3.8 collective-permute-done.2
  82.4 1.8 collective-permute-start.3
  84.8 5.4 collective-permute-done.3
  102.7 1.8 fusion.8
  106.9 2.9 fusion.58
  109.8 11.9 %weight_grads.3 = (f32[1536,768]{1,0:T(8,128)}, f32[1536,768]{1,0:T(8,128)}) custom-call(s32[1]{0:T(128)} %bitcast.37.bit_ref, bf16[1024,3072]{1,0:T(8,128)(2,1)} %copy-done.4, bf16[1024,768]{1,0:T(8,128)(2,1)} %get-tuple-element.248.refs_1_), custom_call_target="tpu_custom_call" | custom-call | tf_op jit(solution)/shard_map/weight_grads/pallas_call | solution.py:312
  122.8 22.2 %feed_backward.1 = (bf16[1024,3072]{1,0:T(8,128)(2,1)}, f32[1024,768]{1,0:T(8,128)}, bf16[1024,768]{1,0:T(8,128)(2,1)}, bf16[1024,768]{1,0:T(8,128)(2,1)}, f32[1,768]{1,0:T(1,128)}) custom-call(f32[1024,768]{1,0:T(8,128)} %get-tuple-element.122.go_ref, bf16[1024,3072]{1,0:T(8,128)(2,1)} %copy-done.4, f32[1024,768]{1,0:T(8,128)} %copy-done.10, ...), custom_call_target="tpu_custom_call" | custom-call | tf_op jit(solution)/shard_map/feed_backward/pallas_call | solution.py:371
  145.0 6.6 %dynamic-slice_add_fusion.4 = (f32[768,768]{1,0:T(8,128)}, f32[768,768]{1,0:T(8,128)}) fusion(f32[1536,768]{1,0:T(8,128)} %collective-permute-done.5, s32[]{:T(128)S(6)} %select_n.287, f32[1536,768]{1,0:T(8,128)} %get-tuple-element.127, s32[]{:T(128)S(6)} %select_n.286), kind=kLoop, calls=%fused_computation.34 | loop fusion | flops 1179648 | bytes 14155784 | tf_op jit(solution)/shard_map/add | solution.py:473
  154.4 12.7 %weight_grads.4 = (f32[384,3072]{1,0:T(8,128)}, f32[384,3072]{1,0:T(8,128)}) custom-call(s32[1]{0:T(128)} %bitcast.37.bit_ref, bf16[1024,768]{1,0:T(8,128)(2,1)} %copy-done.13, bf16[1024,3072]{1,0:T(8,128)(2,1)} %get-tuple-element.136.refs_1_), custom_call_target="tpu_custom_call" | custom-call | tf_op jit(solution)/shard_map/weight_grads/pallas_call | solution.py:312
  167.1 15.6 %attention_backward.3 = (bf16[1024,768]{1,0:T(8,128)(2,1)}, bf16[1024,768]{1,0:T(8,128)(2,1)}, bf16[1024,768]{1,0:T(8,128)(2,1)}, f32[12,1,1024]{2,1,0:T(1,128)}) custom-call(bf16[1024,768]{1,0:T(8,128)(2,1)} %convolution_convert_fusion.2.refs_0_, bf16[1024,768]{1,0:T(8,128)(2,1)} %convolution_convert_fusion.1.refs_1_, ...), custom_call_target="tpu_custom_call" | custom-call | tf_op jit(solution)/shard_map/attention_backward/pallas_call | solution.py:217
  182.7 4.0 dynamic-slice_add_fusion.10
  188.3 15.8 %attention_backward.4 = (bf16[1024,768]{1,0:T(8,128)(2,1)}, bf16[1024,768]{1,0:T(8,128)(2,1)}, bf16[1024,768]{1,0:T(8,128)(2,1)}, f32[12,1,1024]{2,1,0:T(1,128)}) custom-call(bf16[1024,768]{1,0:T(8,128)(2,1)} %convolution_convert_fusion.2.refs_0_, ...), custom_call_target="tpu_custom_call", output_to_operand_aliasing={{0}: (7, {}), {1}: (8, {}), {2}: (9, {}), {3}: (10, {})} | custom-call | tf_op jit(solution)/shard_map/attention_backward/pallas_call | solution.py:217
  204.1 2.6 dynamic-slice_add_fusion.16
  206.7 7.0 %dynamic-slice_add_fusion.2 = (f32[192,3072]{1,0:T(8,128)}, f32[192,3072]{1,0:T(8,128)}) fusion(f32[384,3072]{1,0:T(8,128)} %collective-permute-done.8, s32[]{:T(128)S(6)} %select_n.296, f32[384,3072]{1,0:T(8,128)} %get-tuple-element.150, s32[]{:T(128)S(6)} %select_n.295), kind=kLoop, calls=%fused_computation.32 | loop fusion | flops 1179648 | bytes 14155784 | tf_op jit(solution)/shard_map/add | solution.py:473
  215.3 15.6 %attention_backward.5 = (bf16[1024,768]{1,0:T(8,128)(2,1)}, bf16[1024,768]{1,0:T(8,128)(2,1)}, bf16[1024,768]{1,0:T(8,128)(2,1)}, f32[12,1,1024]{2,1,0:T(1,128)}) custom-call(bf16[1024,768]{1,0:T(8,128)(2,1)} %convolution_convert_fusion.2.refs_0_, ...), custom_call_target="tpu_custom_call", output_to_operand_aliasing={{0}: (7, {}), {1}: (8, {}), {2}: (9, {}), {3}: (10, {})} | custom-call | tf_op jit(solution)/shard_map/attention_backward/pallas_call | solution.py:217
  231.0 1.9 dynamic-slice_add_fusion.22
  232.9 3.0 collective-permute-start.10
  236.0 16.9 %weight_grads.5 = (f32[384,3840]{1,0:T(8,128)}, f32[384,3840]{1,0:T(8,128)}) custom-call(s32[1]{0:T(128)} %bitcast.37.bit_ref, bf16[1024,768]{1,0:T(8,128)(2,1)} %copy-done.3, bf16[1024,768]{1,0:T(8,128)(2,1)} %copy-done.3, bf16[1024,768]{1,0:T(8,128)(2,1)} %copy-done.3, bf16[1024,768]{1,0:T(8,128)(2,1)} %attention_forward.1.refs_3_, ...), custom_call_target="tpu_custom_call" | custom-call | tf_op jit(solution)/shard_map/weight_grads/pallas_call | solution.py:312
  253.9 4.1 dynamic-slice_add_fusion.8
  259.4 3.2 fusion.61
  264.1 2.1 fusion.5
  266.3 2.5 fusion
  268.8 5.5 collective-permute-done.12
  275.6 6.0 %dynamic-slice_add_fusion = (f32[192,3840]{1,0:T(8,128)}, f32[192,3840]{1,0:T(8,128)}) fusion(f32[384,3840]{1,0:T(8,128)} %collective-permute-done.14, s32[]{:T(128)S(6)} %select_n.296, f32[384,3840]{1,0:T(8,128)S(1)} %bitcast.225, s32[]{:T(128)S(6)} %select_n.295), kind=kLoop, calls=%fused_computation.28 | loop fusion | flops 1474560 | bytes 17694728 | tf_op jit(solution)/shard_map/add | solution.py:473
  287.1 12.3 %collective-permute-done.16 = f32[192,768]{1,0:T(8,128)} collective-permute-done((f32[192,768]{1,0:T(8,128)S(1)}, f32[192,768]{1,0:T(8,128)}, u32[]{:S(2)}, u32[]{:S(2)}) %collective-permute-start.16) | collective-permute-done | bytes 589856 | tf_op jit(solution)/shard_map/ppermute | solution.py:256
  299.4 2.3 bitcast_select_fusion.9
  301.7 8.6 %collective-permute-done.17 = f32[48,3072]{1,0:T(8,128)S(1)} collective-permute-done((f32[48,3072]{1,0:T(8,128)}, f32[48,3072]{1,0:T(8,128)S(1)}, u32[]{:S(2)}, u32[]{:S(2)}) %collective-permute-start.17) | collective-permute-done | bytes 589856 | tf_op jit(solution)/shard_map/ppermute | solution.py:256
  310.4 6.7 %collective-permute-done.18 = f32[192,3840]{1,0:T(8,128)} collective-permute-done((f32[192,3840]{1,0:T(8,128)}, f32[192,3840]{1,0:T(8,128)}, u32[]{:S(2)}, u32[]{:S(2)}) %collective-permute-start.18) | collective-permute-done | bytes 2949152 | tf_op jit(solution)/shard_map/ppermute | solution.py:256
  317.1 3.2 dynamic-slice_add_fusion.6
  322.3 2.8 collective-permute-start.21
  325.2 11.4 %collective-permute-done.21 = f32[24,3072]{1,0:T(8,128)S(1)} collective-permute-done((f32[24,3072]{1,0:T(8,128)S(1)}, f32[24,3072]{1,0:T(8,128)S(1)}, u32[]{:S(2)}, u32[]{:S(2)}) %collective-permute-start.21) | collective-permute-done | bytes 294944 | tf_op jit(solution)/shard_map/ppermute | solution.py:256
  338.2 14.6 %collective-permute-done.19 = f32[24,128]{1,0:T(8,128)S(1)} collective-permute-done((f32[24,128]{1,0:T(8,128)S(1)}, f32[24,128]{1,0:T(8,128)S(1)}, u32[]{:S(2)}, u32[]{:S(2)}) %collective-permute-start.19) | collective-permute-done | bytes 12320 | tf_op jit(solution)/shard_map/ppermute | solution.py:252
  353.7 3.3 bitcast_select_fusion.5
  357.0 2.4 dynamic-slice_add_fusion.12
  364.3 25.8 %collective-permute-done.24 = f32[24,128]{1,0:T(8,128)S(1)} collective-permute-done((f32[24,128]{1,0:T(8,128)S(1)}, f32[24,128]{1,0:T(8,128)S(1)}, u32[]{:S(2)}, u32[]{:S(2)}) %collective-permute-start.24) | collective-permute-done | bytes 12320 | tf_op jit(solution)/shard_map/ppermute | solution.py:252
  391.5 1.9 dynamic-slice_add_fusion.18
  393.5 5.1 bitcast_select_fusion.2.own_ref
  400.5 1.8 collective-permute-start.28
  402.5 17.0 %collective-permute-done.28 = f32[24,128]{1,0:T(8,128)S(1)} collective-permute-done((f32[24,128]{1,0:T(8,128)S(1)}, f32[24,128]{1,0:T(8,128)S(1)}, u32[]{:S(2)}, u32[]{:S(2)}) %collective-permute-start.28) | collective-permute-done | bytes 12320 | tf_op jit(solution)/shard_map/ppermute | solution.py:252
  419.6 3.1 bitcast_select_fusion.4
  422.7 10.2 %put_together.3 = f32[3072,768]{1,0:T(8,128)} custom-call(s32[1]{0:T(128)} %bitcast.37.bit_ref, f32[1536,768]{1,0:T(8,128)} %bitcast_select_fusion.2.own_ref, f32[1536,768]{1,0:T(8,128)} %collective-permute-done.29.other_ref), custom_call_target="tpu_custom_call" | custom-call | bytes 18874368 | tf_op jit(solution)/shard_map/put_together/pallas_call | solution.py:419
  434.1 19.1 %collective-permute-done.34 = f32[24,3840]{1,0:T(8,128)S(1)} collective-permute-done((f32[24,3840]{1,0:T(8,128)S(1)}, f32[24,3840]{1,0:T(8,128)S(1)}, u32[]{:S(2)}, u32[]{:S(2)}) %collective-permute-start.34) | collective-permute-done | bytes 368672 | tf_op jit(solution)/shard_map/ppermute | solution.py:256
  455.1 7.2 %collective-permute-done.32 = f32[24,128]{1,0:T(8,128)S(1)} collective-permute-done((f32[24,128]{1,0:T(8,128)S(1)}, f32[24,128]{1,0:T(8,128)S(1)}, u32[]{:S(2)}, u32[]{:S(2)}) %collective-permute-start.32) | collective-permute-done | bytes 12320 | tf_op jit(solution)/shard_map/ppermute | solution.py:252
  462.3 10.5 %collective-permute-done.35 = f32[48,3840]{1,0:T(8,128)} collective-permute-done((f32[48,3840]{1,0:T(8,128)S(1)}, f32[48,3840]{1,0:T(8,128)}, u32[]{:S(2)}, u32[]{:S(2)}) %collective-permute-start.35) | collective-permute-done | bytes 737312 | tf_op jit(solution)/shard_map/ppermute | solution.py:256
  474.1 3.2 bitcast_select_fusion.1.own_ref
  478.1 18.7 %collective-permute-done.37 = f32[96,3840]{1,0:T(8,128)S(1)} collective-permute-done((f32[96,3840]{1,0:T(8,128)S(1)}, f32[96,3840]{1,0:T(8,128)S(1)}, u32[]{:S(2)}, u32[]{:S(2)}) %collective-permute-start.37) | collective-permute-done | bytes 1474592 | tf_op jit(solution)/shard_map/ppermute | solution.py:256
  496.8 2.0 bitcast_select_fusion.3
  498.9 10.1 %put_together.4 = f32[768,3072]{1,0:T(8,128)} custom-call(s32[1]{0:T(128)} %bitcast.37.bit_ref, f32[384,3072]{1,0:T(8,128)} %copy-done.8, f32[384,3072]{1,0:T(8,128)} %collective-permute-done.36.other_ref), custom_call_target="tpu_custom_call" | custom-call | bytes 18874368 | tf_op jit(solution)/shard_map/put_together/pallas_call | solution.py:419
  509.4 34.9 %collective-permute-done.38 = f32[192,3840]{1,0:T(8,128)S(1)} collective-permute-done((f32[192,3840]{1,0:T(8,128)}, f32[192,3840]{1,0:T(8,128)S(1)}, u32[]{:S(2)}, u32[]{:S(2)}) %collective-permute-start.38) | collective-permute-done | bytes 2949152 | tf_op jit(solution)/shard_map/ppermute | solution.py:256
  544.3 5.2 bitcast_select_fusion.own_ref
  552.8 6.6 %collective-permute-done.39.other_ref = f32[384,3840]{1,0:T(8,128)} collective-permute-done((f32[384,3840]{1,0:T(8,128)}, f32[384,3840]{1,0:T(8,128)}, u32[]{:S(2)}, u32[]{:S(2)}) %collective-permute-start.39) | collective-permute-done | bytes 5898272 | tf_op jit(solution)/shard_map/ppermute | solution.py:256
  559.4 11.4 %put_together.5 = (f32[768,768]{1,0:T(8,128)}, f32[768,768]{1,0:T(8,128)}, f32[768,768]{1,0:T(8,128)}, f32[768,768]{1,0:T(8,128)}, f32[768,768]{1,0:T(8,128)}) custom-call(s32[1]{0:T(128)} %bitcast.37.bit_ref, f32[384,3840]{1,0:T(8,128)} %bitcast_select_fusion.own_ref, f32[384,3840]{1,0:T(8,128)} %collective-permute-done.39.other_ref), custom_call_target="tpu_custom_call" | custom-call | bytes 23592960 | tf_op jit(solution)/shard_map/put_together/pallas_call | solution.py:419
  (280 shorter events, 68.4 us)
Async XLA Ops:
  0.6 8.9 %copy-start = (bf16[768,768]{1,0:T(8,128)(2,1)S(1)}, bf16[768,768]{1,0:T(8,128)(2,1)}, u32[]{:S(2)}) copy-start(bf16[768,768]{1,0:T(8,128)(2,1)} %param.21) | copy-start | bytes 3538948
  14.9 28.8 %copy-start.6 = (bf16[1,2,512,768]{3,2,1,0:T(8,128)(2,1)S(1)}, bf16[1,2,512,768]{3,2,1,0:T(8,128)(2,1)}, u32[]{:S(2)}) copy-start(bf16[1,2,512,768]{3,2,1,0:T(8,128)(2,1)} %param.15) | copy-start | bytes 4718596
  14.9 33.8 %slice-start.2 = ((s8[4718592]{0:T(1024)(128)(4,1)}), s8[524288]{0:T(1024)(128)(4,1)S(1)}, s32[]{:S(2)}) async-start(s8[4718592]{0:T(1024)(128)(4,1)} %bitcast.226), calls=%async_computation.2 | async-start | bytes 1048576
  47.1 7.4 %copy-start.10 = (f32[1024,768]{1,0:T(8,128)}, f32[1024,768]{1,0:T(8,128)S(1)}, u32[]{:S(2)}) copy-start(f32[1024,768]{1,0:T(8,128)S(1)} %get-tuple-element.284.hid_ref) | copy-start | bytes 9437188
  47.2 7.4 %slice-start.4 = ((s8[4718592]{0:T(1024)(128)(4,1)}), s8[4194304]{0:T(1024)(128)(4,1)S(1)}, s32[]{:S(2)}) async-start(s8[4718592]{0:T(1024)(128)(4,1)} %bitcast.228), calls=%async_computation.4 | async-start | bytes 8388608
  48.7 5.8 %slice-start.5 = ((s8[4718592]{0:T(1024)(128)(4,1)}), s8[524288]{0:T(1024)(128)(4,1)S(1)}, s32[]{:S(2)}) async-start(s8[4718592]{0:T(1024)(128)(4,1)} %bitcast.228), calls=%async_computation.5 | async-start | bytes 1048576
  54.6 5.3 copy-start.25
  61.5 22.7 %copy-start.34 = (s32[2,128]{1,0:T(2,128)S(1)}, s32[2,128]{1,0:T(2,128)}, u32[]{:S(2)}) copy-start(s32[2,128]{1,0:T(2,128)} %param.18) | copy-start | bytes 3076
  62.8 30.2 %copy-start.21 = (bf16[16,768]{1,0:T(8,128)(2,1)}, bf16[16,768]{1,0:T(8,128)(2,1)S(1)}, u32[]{:S(2)}) copy-start(bf16[16,768]{1,0:T(8,128)(2,1)S(1)} %fusion.10.refs_4_) | copy-start | bytes 73732
  63.8 6.7 %collective-permute-start = (f32[16,768]{1,0:T(8,128)S(1)}, f32[16,768]{1,0:T(8,128)S(1)}, u32[]{:S(2)}, u32[]{:S(2)}) collective-permute-start(f32[16,768]{1,0:T(8,128)S(1)} %broadcast_multiply_fusion), channel_id=1, source_target_pairs={{0,8},{1,9},{2,10},{3,11},{4,12},{5,13},{6,14},{7,15},{8,0},{9,1},... | collective-permute-start | bytes 147464 | tf_op jit(solution)/shard_map/ppermute | solution.py:252
  70.5 4.6 collective-permute-start.1
  75.9 5.7 %collective-permute-start.2 = (f32[64,768]{1,0:T(8,128)S(1)}, f32[64,768]{1,0:T(8,128)S(1)}, u32[]{:S(2)}, u32[]{:S(2)}) collective-permute-start(f32[64,768]{1,0:T(8,128)S(1)} %bitcast_select_fusion.15), channel_id=1, source_target_pairs={{0,2},{1,3},{2,0},{3,1},{4,6},{5,7},{6,4},{7,5},{8,10},{9,11},{10,... | collective-permute-start | bytes 589832 | tf_op jit(solution)/shard_map/ppermute | solution.py:252
  77.8 7.0 %copy-start.39 = (pred[2]{0:T(512)(128)(4,1)}, pred[2]{0:T(512)(128)(4,1)S(1)}, u32[]{:S(2)}) copy-start(pred[2]{0:T(512)(128)(4,1)S(1)} %iota_compare_fusion.15) | copy-start | bytes 10
  82.4 7.8 %collective-permute-start.3 = (f32[128,768]{1,0:T(8,128)S(1)}, f32[128,768]{1,0:T(8,128)S(1)}, u32[]{:S(2)}, u32[]{:S(2)}) collective-permute-start(f32[128,768]{1,0:T(8,128)S(1)} %bitcast_select_fusion.14), channel_id=1, source_target_pairs={{0,16},{1,17},{2,18},{3,19},{4,20},{5,21},{6,22},{7,23},{8,24},{9,... | collective-permute-start | bytes 1179656 | tf_op jit(solution)/shard_map/ppermute | solution.py:252
  91.3 3.6 collective-permute-start.4
  96.2 6.4 %copy-start.38 = (f32[16]{0:T(128)S(1)}, f32[16]{0:T(128)}, u32[]{:S(2)}) copy-start(f32[16]{0:T(128)} %copy-done.37) | copy-start | bytes 196
  121.7 23.3 %collective-permute-start.5 = (f32[1536,768]{1,0:T(8,128)}, f32[1536,768]{1,0:T(8,128)}, u32[]{:S(2)}, u32[]{:S(2)}) collective-permute-start(f32[1536,768]{1,0:T(8,128)} %get-tuple-element.128), channel_id=1, source_target_pairs={{0,1},{1,0},{2,3},{3,2},{4,5},{5,4},{6,7},{7,6},{8,9},{9,8},{10,11... | collective-permute-start | bytes 14155784 | tf_op jit(solution)/shard_map/ppermute | solution.py:256
  145.0 8.3 %copy-start.30 = (s32[1024]{0:T(1024)S(1)}, s32[1024]{0:T(1024)}, u32[]{:S(2)}) copy-start(s32[1024]{0:T(1024)} %get-tuple-element.295) | copy-start | bytes 12292
  145.0 8.3 %copy-start.47 = (f32[32,12]{0,1:T(8,128)S(1)}, f32[32,12]{0,1:T(8,128)}, u32[]{:S(2)}) copy-start(f32[32,12]{0,1:T(8,128)} %param.29) | copy-start | bytes 4612
  151.6 31.1 %collective-permute-start.6 = (f32[768,768]{1,0:T(8,128)}, f32[768,768]{1,0:T(8,128)}, u32[]{:S(2)}, u32[]{:S(2)}) collective-permute-start(f32[768,768]{1,0:T(8,128)} %get-tuple-element.135), channel_id=1, source_target_pairs={{0,16},{1,3},{2,18},{3,1},{4,20},{5,7},{6,22},{7,5},{8,24},{9,11},... | collective-permute-start | bytes 7077896 | tf_op jit(solution)/shard_map/ppermute | solution.py:256
  186.7 19.9 %collective-permute-start.8 = (f32[384,3072]{1,0:T(8,128)}, f32[384,3072]{1,0:T(8,128)}, u32[]{:S(2)}, u32[]{:S(2)}) collective-permute-start(f32[384,3072]{1,0:T(8,128)} %get-tuple-element.151), channel_id=1, source_target_pairs={{0,1},{1,0},{2,3},{3,2},{4,5},{5,4},{6,7},{7,6},{8,9},{9,8},{10,11... | collective-permute-start | bytes 14155784 | tf_op jit(solution)/shard_map/ppermute | solution.py:256
  186.7 17.4 %collective-permute-start.7 = (f32[384,768]{1,0:T(8,128)}, f32[384,768]{1,0:T(8,128)}, u32[]{:S(2)}, u32[]{:S(2)}) collective-permute-start(f32[384,768]{1,0:T(8,128)} %get-tuple-element.149), channel_id=1, source_target_pairs={{0,2},{1,17},{2,0},{3,19},{4,6},{5,21},{6,4},{7,23},{8,10},{9,25},... | collective-permute-start | bytes 3538952 | tf_op jit(solution)/shard_map/ppermute | solution.py:256
  213.6 40.2 %collective-permute-start.11 = (f32[192,3072]{1,0:T(8,128)}, f32[192,3072]{1,0:T(8,128)}, u32[]{:S(2)}, u32[]{:S(2)}) collective-permute-start(f32[192,3072]{1,0:T(8,128)} %get-tuple-element.169), channel_id=1, source_target_pairs={{0,16},{1,3},{2,18},{3,1},{4,20},{5,7},{6,22},{7,5},{8,24},{9,11},... | collective-permute-start | bytes 7077896 | tf_op jit(solution)/shard_map/ppermute | solution.py:256
  214.2 16.8 %collective-permute-start.9 = (f32[192,768]{1,0:T(8,128)}, f32[192,768]{1,0:T(8,128)}, u32[]{:S(2)}, u32[]{:S(2)}) collective-permute-start(f32[192,768]{1,0:T(8,128)} %get-tuple-element.162), channel_id=1, source_target_pairs={{0,4},{1,5},{2,6},{3,7},{4,0},{5,1},{6,2},{7,3},{8,12},{9,13},{10,... | collective-permute-start | bytes 1769480 | tf_op jit(solution)/shard_map/ppermute | solution.py:256
  232.9 19.9 %collective-permute-start.10 = (f32[96,768]{1,0:T(8,128)}, f32[96,768]{1,0:T(8,128)}, u32[]{:S(2)}, u32[]{:S(2)}) collective-permute-start(f32[96,768]{1,0:T(8,128)} %get-tuple-element.167), channel_id=1, source_target_pairs={{0,8},{1,9},{2,10},{3,11},{4,12},{5,13},{6,14},{7,15},{8,0},{9,1},... | collective-permute-start | bytes 884744 | tf_op jit(solution)/shard_map/ppermute | solution.py:256
  235.9 16.9 %copy-start.18 = (f32[96,768]{1,0:T(8,128)S(1)}, f32[96,768]{1,0:T(8,128)}, u32[]{:S(2)}) copy-start(f32[96,768]{1,0:T(8,128)} %get-tuple-element.166) | copy-start | bytes 884740
  257.9 17.6 %collective-permute-start.14 = (f32[384,3840]{1,0:T(8,128)}, f32[384,3840]{1,0:T(8,128)}, u32[]{:S(2)}, u32[]{:S(2)}) collective-permute-start(f32[384,3840]{1,0:T(8,128)} %get-tuple-element.180), channel_id=1, source_target_pairs={{0,1},{1,0},{2,3},{3,2},{4,5},{5,4},{6,7},{7,6},{8,9},{9,8},{10,11... | collective-permute-start | bytes 17694728 | tf_op jit(solution)/shard_map/ppermute | solution.py:256
  258.1 16.2 %collective-permute-start.12 = (f32[96,768]{1,0:T(8,128)S(1)}, f32[96,768]{1,0:T(8,128)S(1)}, u32[]{:S(2)}, u32[]{:S(2)}) collective-permute-start(f32[96,768]{1,0:T(8,128)S(1)} %add.430), channel_id=1, source_target_pairs={{0,8},{1,9},{2,10},{3,11},{4,12},{5,13},{6,14},{7,15},{8,0},{9,1},... | collective-permute-start | bytes 884744 | tf_op jit(solution)/shard_map/ppermute | solution.py:256
  258.1 16.5 %collective-permute-start.13 = (f32[96,3072]{1,0:T(8,128)}, f32[96,3072]{1,0:T(8,128)S(1)}, u32[]{:S(2)}, u32[]{:S(2)}) collective-permute-start(f32[96,3072]{1,0:T(8,128)} %get-tuple-element.178), channel_id=1, source_target_pairs={{0,2},{1,17},{2,0},{3,19},{4,6},{5,21},{6,4},{7,23},{8,10},{9,25},... | collective-permute-start | bytes 3538952 | tf_op jit(solution)/shard_map/ppermute | solution.py:256
  266.2 9.3 %slice-start = ((s8[5898240]{0:T(1024)(128)(4,1)}), s8[4194304]{0:T(1024)(128)(4,1)S(1)}, s32[]{:S(2)}) async-start(s8[5898240]{0:T(1024)(128)(4,1)} %bitcast.224), calls=%async_computation | async-start | bytes 8388608
  266.2 8.4 %copy-start.15 = (f32[96,3072]{1,0:T(8,128)S(1)}, f32[96,3072]{1,0:T(8,128)}, u32[]{:S(2)}) copy-start(f32[96,3072]{1,0:T(8,128)} %get-tuple-element.177) | copy-start | bytes 3538948
  266.3 9.3 %slice-start.1 = ((s8[5898240]{0:T(1024)(128)(4,1)}), s8[1703936]{0:T(1024)(128)(4,1)S(1)}, s32[]{:S(2)}) async-start(s8[5898240]{0:T(1024)(128)(4,1)} %bitcast.224), calls=%async_computation.1 | async-start | bytes 3407872
  275.6 9.6 %copy-start.31 = (f32[1,768]{1,0:T(1,128)S(1)}, f32[1,768]{1,0:T(1,128)}, u32[]{:S(2)}) copy-start(f32[1,768]{1,0:T(1,128)} %get-tuple-element.182) | copy-start | bytes 9220
  275.6 9.6 %copy-start.23 = (f32[12,1,1024]{2,1,0:T(1,128)S(1)}, f32[12,1,1024]{2,1,0:T(1,128)}, u32[]{:S(2)}) copy-start(f32[12,1,1024]{2,1,0:T(1,128)} %get-tuple-element.183) | copy-start | bytes 147460
  275.6 10.4 %copy-start.36 = (pred[2]{0:T(512)(128)(4,1)S(1)}, pred[2]{0:T(512)(128)(4,1)}, u32[]{:S(2)}) copy-start(pred[2]{0:T(512)(128)(4,1)} %copy-done.35) | copy-start | bytes 10
  281.6 35.5 %collective-permute-start.18 = (f32[192,3840]{1,0:T(8,128)}, f32[192,3840]{1,0:T(8,128)}, u32[]{:S(2)}, u32[]{:S(2)}) collective-permute-start(f32[192,3840]{1,0:T(8,128)} %get-tuple-element.188), channel_id=1, source_target_pairs={{0,16},{1,3},{2,18},{3,1},{4,20},{5,7},{6,22},{7,5},{8,24},{9,11},... | collective-permute-start | bytes 8847368 | tf_op jit(solution)/shard_map/ppermute | solution.py:256
  283.1 16.3 %collective-permute-start.16 = (f32[192,768]{1,0:T(8,128)S(1)}, f32[192,768]{1,0:T(8,128)}, u32[]{:S(2)}, u32[]{:S(2)}) collective-permute-start(f32[192,768]{1,0:T(8,128)S(1)} %bitcast_select_fusion.13), channel_id=1, source_target_pairs={{0,4},{1,5},{2,6},{3,7},{4,0},{5,1},{6,2},{7,3},{8,12},{9,13},{10,... | collective-permute-start | bytes 1769480 | tf_op jit(solution)/shard_map/ppermute | solution.py:256
  283.8 26.5 %collective-permute-start.17 = (f32[48,3072]{1,0:T(8,128)}, f32[48,3072]{1,0:T(8,128)S(1)}, u32[]{:S(2)}, u32[]{:S(2)}) collective-permute-start(f32[48,3072]{1,0:T(8,128)} %get-tuple-element.186), channel_id=1, source_target_pairs={{0,4},{1,5},{2,6},{3,7},{4,0},{5,1},{6,2},{7,3},{8,12},{9,13},{10,... | collective-permute-start | bytes 1769480 | tf_op jit(solution)/shard_map/ppermute | solution.py:256
  285.9 1.2 collective-permute-start.15
  286.1 31.0 %copy-start.11 = (f32[192,3840]{1,0:T(8,128)S(1)}, f32[192,3840]{1,0:T(8,128)}, u32[]{:S(2)}) copy-start(f32[192,3840]{1,0:T(8,128)} %get-tuple-element.187) | copy-start | bytes 8847364
  320.3 36.7 %collective-permute-start.23 = (f32[96,3840]{1,0:T(8,128)}, f32[96,3840]{1,0:T(8,128)}, u32[]{:S(2)}, u32[]{:S(2)}) collective-permute-start(f32[96,3840]{1,0:T(8,128)} %get-tuple-element.194), channel_id=1, source_target_pairs={{0,2},{1,17},{2,0},{3,19},{4,6},{5,21},{6,4},{7,23},{8,10},{9,25},... | collective-permute-start | bytes 4423688 | tf_op jit(solution)/shard_map/ppermute | solution.py:256
  321.5 32.2 %collective-permute-start.20 = (f32[384,768]{1,0:T(8,128)}, f32[384,768]{1,0:T(8,128)}, u32[]{:S(2)}, u32[]{:S(2)}) collective-permute-start(f32[384,768]{1,0:T(8,128)} %bitcast_select_fusion.9), channel_id=1, source_target_pairs={{0,2},{1,17},{2,0},{3,19},{4,6},{5,21},{6,4},{7,23},{8,10},{9,25},... | collective-permute-start | bytes 3538952 | tf_op jit(solution)/shard_map/ppermute | solution.py:256
  322.3 14.2 %collective-permute-start.21 = (f32[24,3072]{1,0:T(8,128)S(1)}, f32[24,3072]{1,0:T(8,128)S(1)}, u32[]{:S(2)}, u32[]{:S(2)}) collective-permute-start(f32[24,3072]{1,0:T(8,128)S(1)} %get-tuple-element.192), channel_id=1, source_target_pairs={{0,8},{1,9},{2,10},{3,11},{4,12},{5,13},{6,14},{7,15},{8,0},{9,1},... | collective-permute-start | bytes 884744 | tf_op jit(solution)/shard_map/ppermute | solution.py:256
  336.6 16.2 %collective-permute-start.22 = (f32[24,3072]{1,0:T(8,128)S(1)}, f32[24,3072]{1,0:T(8,128)S(1)}, u32[]{:S(2)}, u32[]{:S(2)}) collective-permute-start(f32[24,3072]{1,0:T(8,128)S(1)} %add.452), channel_id=1, source_target_pairs={{0,8},{1,9},{2,10},{3,11},{4,12},{5,13},{6,14},{7,15},{8,0},{9,1},... | collective-permute-start | bytes 884744 | tf_op jit(solution)/shard_map/ppermute | solution.py:256
  336.7 16.1 %collective-permute-start.19 = (f32[24,128]{1,0:T(8,128)S(1)}, f32[24,128]{1,0:T(8,128)S(1)}, u32[]{:S(2)}, u32[]{:S(2)}) collective-permute-start(f32[24,128]{1,0:T(8,128)S(1)} %fusion.89), channel_id=1, source_target_pairs={{0,2},{1,3},{2,0},{3,1},{4,6},{5,7},{6,4},{7,5},{8,10},{9,11},{10,... | collective-permute-start | bytes 36872 | tf_op jit(solution)/shard_map/ppermute | solution.py:252
  359.4 34.1 %collective-permute-start.25 = (f32[768,768]{1,0:T(8,128)}, f32[768,768]{1,0:T(8,128)}, u32[]{:S(2)}, u32[]{:S(2)}) collective-permute-start(f32[768,768]{1,0:T(8,128)} %bitcast_select_fusion.5), channel_id=1, source_target_pairs={{0,16},{1,3},{2,18},{3,1},{4,20},{5,7},{6,22},{7,5},{8,24},{9,11},... | collective-permute-start | bytes 7077896 | tf_op jit(solution)/shard_map/ppermute | solution.py:256
  360.9 30.6 %collective-permute-start.27 = (f32[48,3840]{1,0:T(8,128)}, f32[48,3840]{1,0:T(8,128)}, u32[]{:S(2)}, u32[]{:S(2)}) collective-permute-start(f32[48,3840]{1,0:T(8,128)} %get-tuple-element.199), channel_id=1, source_target_pairs={{0,4},{1,5},{2,6},{3,7},{4,0},{5,1},{6,2},{7,3},{8,12},{9,13},{10,... | collective-permute-start | bytes 2211848 | tf_op jit(solution)/shard_map/ppermute | solution.py:256
  361.6 28.5 %collective-permute-start.26 = (f32[48,3072]{1,0:T(8,128)}, f32[48,3072]{1,0:T(8,128)}, u32[]{:S(2)}, u32[]{:S(2)}) collective-permute-start(f32[48,3072]{1,0:T(8,128)} %bitcast_select_fusion.12), channel_id=1, source_target_pairs={{0,4},{1,5},{2,6},{3,7},{4,0},{5,1},{6,2},{7,3},{8,12},{9,13},{10,... | collective-permute-start | bytes 1769480 | tf_op jit(solution)/shard_map/ppermute | solution.py:256
  362.9 27.2 %collective-permute-start.24 = (f32[24,128]{1,0:T(8,128)S(1)}, f32[24,128]{1,0:T(8,128)S(1)}, u32[]{:S(2)}, u32[]{:S(2)}) collective-permute-start(f32[24,128]{1,0:T(8,128)S(1)} %add.451), channel_id=1, source_target_pairs={{0,4},{1,5},{2,6},{3,7},{4,0},{5,1},{6,2},{7,3},{8,12},{9,13},{10,... | collective-permute-start | bytes 36872 | tf_op jit(solution)/shard_map/ppermute | solution.py:252
  398.6 24.1 %collective-permute-start.29 = (f32[1536,768]{1,0:T(8,128)}, f32[1536,768]{1,0:T(8,128)}, u32[]{:S(2)}, u32[]{:S(2)}) collective-permute-start(f32[1536,768]{1,0:T(8,128)} %bitcast_select_fusion.2.own_ref), channel_id=1, source_target_pairs={{0,1},{1,0},{2,3},{3,2},{4,5},{5,4},{6,7},{7,6},{8,9},{9,8},{10,11... | collective-permute-start | bytes 14155784 | tf_op jit(solution)/shard_map/ppermute | solution.py:256
  398.6 21.0 %collective-permute-start.30 = (f32[96,3072]{1,0:T(8,128)S(1)}, f32[96,3072]{1,0:T(8,128)}, u32[]{:S(2)}, u32[]{:S(2)}) collective-permute-start(f32[96,3072]{1,0:T(8,128)S(1)} %bitcast_select_fusion.8), channel_id=1, source_target_pairs={{0,2},{1,17},{2,0},{3,19},{4,6},{5,21},{6,4},{7,23},{8,10},{9,25},... | collective-permute-start | bytes 3538952 | tf_op jit(solution)/shard_map/ppermute | solution.py:256
  399.4 20.1 %collective-permute-start.31 = (f32[24,3840]{1,0:T(8,128)}, f32[24,3840]{1,0:T(8,128)S(1)}, u32[]{:S(2)}, u32[]{:S(2)}) collective-permute-start(f32[24,3840]{1,0:T(8,128)} %get-tuple-element.204), channel_id=1, source_target_pairs={{0,8},{1,9},{2,10},{3,11},{4,12},{5,13},{6,14},{7,15},{8,0},{9,1},... | collective-permute-start | bytes 1105928 | tf_op jit(solution)/shard_map/ppermute | solution.py:256
  400.5 18.9 %collective-permute-start.28 = (f32[24,128]{1,0:T(8,128)S(1)}, f32[24,128]{1,0:T(8,128)S(1)}, u32[]{:S(2)}, u32[]{:S(2)}) collective-permute-start(f32[24,128]{1,0:T(8,128)S(1)} %add.455), channel_id=1, source_target_pairs={{0,8},{1,9},{2,10},{3,11},{4,12},{5,13},{6,14},{7,15},{8,0},{9,1},... | collective-permute-start | bytes 36872 | tf_op jit(solution)/shard_map/ppermute | solution.py:252
  419.5 14.5 %copy-start.17 = (f32[24,3840]{1,0:T(8,128)}, f32[24,3840]{1,0:T(8,128)S(1)}, u32[]{:S(2)}) copy-start(f32[24,3840]{1,0:T(8,128)S(1)} %add.459) | copy-start | bytes 1105924
  422.7 32.2 %copy-start.41 = (pred[2]{0:T(512)(128)(4,1)S(1)}, pred[2]{0:T(512)(128)(4,1)}, u32[]{:S(2)}) copy-start(pred[2]{0:T(512)(128)(4,1)} %copy-done.40) | copy-start | bytes 10
  432.9 41.2 %collective-permute-start.33 = (f32[192,3072]{1,0:T(8,128)}, f32[192,3072]{1,0:T(8,128)}, u32[]{:S(2)}, u32[]{:S(2)}) collective-permute-start(f32[192,3072]{1,0:T(8,128)} %bitcast_select_fusion.4), channel_id=1, source_target_pairs={{0,16},{1,3},{2,18},{3,1},{4,20},{5,7},{6,22},{7,5},{8,24},{9,11},... | collective-permute-start | bytes 7077896 | tf_op jit(solution)/shard_map/ppermute | solution.py:256
  434.1 19.1 %collective-permute-start.34 = (f32[24,3840]{1,0:T(8,128)S(1)}, f32[24,3840]{1,0:T(8,128)S(1)}, u32[]{:S(2)}, u32[]{:S(2)}) collective-permute-start(f32[24,3840]{1,0:T(8,128)S(1)} %add.459), channel_id=1, source_target_pairs={{0,8},{1,9},{2,10},{3,11},{4,12},{5,13},{6,14},{7,15},{8,0},{9,1},... | collective-permute-start | bytes 1105928 | tf_op jit(solution)/shard_map/ppermute | solution.py:256
  454.2 18.6 %collective-permute-start.35 = (f32[48,3840]{1,0:T(8,128)S(1)}, f32[48,3840]{1,0:T(8,128)}, u32[]{:S(2)}, u32[]{:S(2)}) collective-permute-start(f32[48,3840]{1,0:T(8,128)S(1)} %bitcast_select_fusion.11), channel_id=1, source_target_pairs={{0,4},{1,5},{2,6},{3,7},{4,0},{5,1},{6,2},{7,3},{8,12},{9,13},{10,... | collective-permute-start | bytes 2211848 | tf_op jit(solution)/shard_map/ppermute | solution.py:256
  454.3 8.0 %collective-permute-start.32 = (f32[24,128]{1,0:T(8,128)S(1)}, f32[24,128]{1,0:T(8,128)S(1)}, u32[]{:S(2)}, u32[]{:S(2)}) collective-permute-start(f32[24,128]{1,0:T(8,128)S(1)} %add.458), channel_id=1, source_target_pairs={{0,16},{1,17},{2,18},{3,19},{4,20},{5,21},{6,22},{7,23},{8,24},{9,... | collective-permute-start | bytes 36872 | tf_op jit(solution)/shard_map/ppermute | solution.py:252
  477.3 21.5 %copy-start.8 = (f32[384,3072]{1,0:T(8,128)}, f32[384,3072]{1,0:T(8,128)S(1)}, u32[]{:S(2)}) copy-start(f32[384,3072]{1,0:T(8,128)S(1)} %bitcast_select_fusion.1.own_ref) | copy-start | bytes 14155780
  477.3 21.5 %collective-permute-start.36 = (f32[384,3072]{1,0:T(8,128)S(1)}, f32[384,3072]{1,0:T(8,128)}, u32[]{:S(2)}, u32[]{:S(2)}) collective-permute-start(f32[384,3072]{1,0:T(8,128)S(1)} %bitcast_select_fusion.1.own_ref), channel_id=1, source_target_pairs={{0,1},{1,0},{2,3},{3,2},{4,5},{5,4},{6,7},{7,6},{8,9},{9,8},{10,11... | collective-permute-start | bytes 14155784 | tf_op jit(solution)/shard_map/ppermute | solution.py:256
  477.4 19.4 %collective-permute-start.37 = (f32[96,3840]{1,0:T(8,128)S(1)}, f32[96,3840]{1,0:T(8,128)S(1)}, u32[]{:S(2)}, u32[]{:S(2)}) collective-permute-start(f32[96,3840]{1,0:T(8,128)S(1)} %bitcast_select_fusion.7), channel_id=1, source_target_pairs={{0,2},{1,17},{2,0},{3,19},{4,6},{5,21},{6,4},{7,23},{8,10},{9,25},... | collective-permute-start | bytes 4423688 | tf_op jit(solution)/shard_map/ppermute | solution.py:256
  508.9 35.4 %collective-permute-start.38 = (f32[192,3840]{1,0:T(8,128)}, f32[192,3840]{1,0:T(8,128)S(1)}, u32[]{:S(2)}, u32[]{:S(2)}) collective-permute-start(f32[192,3840]{1,0:T(8,128)} %bitcast_select_fusion.3), channel_id=1, source_target_pairs={{0,16},{1,3},{2,18},{3,1},{4,20},{5,7},{6,22},{7,5},{8,24},{9,11},... | collective-permute-start | bytes 8847368 | tf_op jit(solution)/shard_map/ppermute | solution.py:256
  549.5 9.9 %collective-permute-start.39 = (f32[384,3840]{1,0:T(8,128)}, f32[384,3840]{1,0:T(8,128)}, u32[]{:S(2)}, u32[]{:S(2)}) collective-permute-start(f32[384,3840]{1,0:T(8,128)} %bitcast_select_fusion.own_ref), channel_id=1, source_target_pairs={{0,1},{1,0},{2,3},{3,2},{4,5},{5,4},{6,7},{7,6},{8,9},{9,8},{10,11... | collective-permute-start | bytes 17694728 | tf_op jit(solution)/shard_map/ppermute | solution.py:256
  (32 other events, 87.5 us)

commit v4 on v3

--- a/solution.py
+++ b/solution.py
@@ -11,6 +11,7 @@
 bucket_edges = (12, 16, 23, 32, 46, 64, 91)
 AXES = ("tower", "dp")
 LANES = 128
+TILE = 256
 
 
 def bucket_code(offset, bucket_count):
@@ -86,14 +87,19 @@
     keys = head_parts(k_ref[...], head_dim)
     values = head_parts(v_ref[...], head_dim)
     segr = segr_ref[...]
-    for t in range(tiles):
-        here = slice(t * LANES, (t + 1) * LANES)
+    deep = 2
+    for c in range(tiles // deep):
+        here = slice(c * deep * LANES, (c + 1) * deep * LANES)
         query = q_ref[here, :]
         same = segc_ref[here, :] == segr
         total = None
         for a in range(group):
             s = dot_nt(query, keys[a])
-            s = s + diag_ref[a, :, LANES * (tiles - t) : LANES * (tiles - t) + length]
+            bias = [
+                diag_ref[a, :, LANES * (tiles - t) : LANES * (tiles - t) + length]
+                for t in range(c * deep, (c + 1) * deep)
+            ]
+            s = s + jnp.concatenate(bias, axis=0)
             s = jnp.where(same, s, -1000000000.0)
             e = jnp.exp(s - jnp.max(s, axis=1, keepdims=True))
             p = e * (1.0 / jnp.sum(e, axis=1, keepdims=True))
@@ -127,7 +133,7 @@
     keys = head_parts(k_ref[...], head_dim)
     values = head_parts(v_ref[...], head_dim)
     segc = segc_ref[...]
-    chunk = 2 * LANES
+    chunk = length
     gk = [None]
     gv = [None]
     for c in range(length // chunk):
@@ -232,38 +238,49 @@
         self.dp = lax.axis_size("dp")
         self.size = self.dp * lax.axis_size("tower")
         self.index = lax.axis_index("tower") * self.dp + lax.axis_index("dp")
-        count = self.size.bit_length() - 1
-        if count == 5:
-            self.steps = ((0, 0), (4, 1), (1, 4), (2, 2), (3, 3))
+        self.count = self.size.bit_length() - 1
+        if self.count == 5:
+            self.stages = (((0,), (0,)), ((4,), (1,)), ((1,), (4,)), ((2, 3), (2, 3)))
         else:
-            self.steps = tuple((b, b) for b in range(count))
-        self.bits = [self.bit_of(k) for k in range(count)]
+            self.stages = tuple(((b,), (b,)) for b in range(self.count))
+        self.digits = [self.digit_of(stage) for stage in self.stages]
 
     def bit(self, b):
         return (self.index >> b) & 1
 
-    def bit_of(self, k):
-        first, second = self.steps[k]
-        if first == second:
-            return self.bit(first)
-        return jnp.where(self.bit(0) == 0, self.bit(first), self.bit(second))
+    def digit_of(self, stage):
+        first, second = (sum(self.bit(b) << n for n, b in enumerate(bits)) for bits in stage)
+        return first if stage[0] == stage[1] else jnp.where(self.bit(0) == 0, first, second)
 
     def swap(self, value, b):
         return lax.ppermute(value, AXES, [(i, i ^ (1 << b)) for i in range(self.size)])
 
-    def swap_step(self, value, k):
-        pairs = [(i, i ^ (1 << self.steps[k][i & 1])) for i in range(self.size)]
-        return lax.ppermute(value, AXES, pairs)
-
-
-def join(own, other, bit):
-    rows, width = own.shape
-    side = lax.broadcasted_iota(jnp.int32, (2, rows, width), 0)
-    return jnp.where(side == bit, own[None], other[None]).reshape(2 * rows, width)
-
-
-def half_of(value, which):
-    rows = value.shape[0] // 2
+    def peers(self, k):
+        return range(1, 1 << len(self.stages[k][0]))
+
+    def send(self, value, k, r):
+        return self.send_by(value, self.stages[k], r)
+
+    def send_by(self, value, stage, r):
+        masks = [sum(((r >> n) & 1) << b for n, b in enumerate(bits)) for bits in stage]
+        return lax.ppermute(value, AXES, [(i, i ^ masks[i & 1]) for i in range(self.size)])
+
+    def collect(self, value, stage):
+        peers = range(1, 1 << len(stage[0]))
+        return place([value, *(self.send_by(value, stage, r) for r in peers)], self.digit_of(stage))
+
+
+def place(pieces, digit):
+    rows, width = pieces[0].shape
+    source = lax.broadcasted_iota(jnp.int32, (len(pieces), rows, width), 0) ^ digit
+    value = pieces[0][None]
+    for r, piece in enumerate(pieces[1:], 1):
+        value = jnp.where(source == r, piece[None], value)
+    return value.reshape(len(pieces) * rows, width)
+
+
+def part_of(value, which, count):
+    rows = value.shape[0] // count
     return lax.dynamic_slice_in_dim(value, which * rows, rows, 0)
 
 
@@ -276,57 +293,112 @@
     starts = [end - r.shape[1] // width for end, r in zip(ends, rights)]
     columns = ends[-1]
     count = len(lefts)
+    fresh = [n == 0 or lefts[n] is not lefts[n - 1] for n in range(count)]
+    owners = [max(m for m in range(n + 1) if fresh[m]) for n in range(count)]
 
     def kernel(bit_ref, *refs):
-        left_refs, right_refs, (sent_ref, kept_ref) = refs[:count], refs[count:-2], refs[-2:]
-        side, column = pl.program_id(0), pl.program_id(2)
-
-        def one(left_ref, right_ref):
-            value = dot_tn(left_ref[...], right_ref[...])
-
-            @pl.when(side == 0)
-            def _():
-                sent_ref[...] = value
-
-            @pl.when(side == 1)
-            def _():
-                kept_ref[...] = value
-
-        for left_ref, right_ref, start, end in zip(left_refs, right_refs, starts, ends):
-            inside = (column >= start) & (column < end)
-            pl.when(inside)(lambda left_ref=left_ref, right_ref=right_ref: one(left_ref, right_ref))
-
-    def left_place(side, stack, column, bit_ref):
-        half = jnp.where(side == 0, 1 - bit_ref[0], bit_ref[0])
-        return (0, half * stacks + stack)
+        other_refs, own_refs, right_refs = (refs[n * count : (n + 1) * count] for n in range(3))
+        sent_ref, kept_ref = refs[3 * count : 3 * count + 2]
+        turned_refs = refs[3 * count + 2 :]
+        column = pl.program_id(1)
+
+        def one(n):
+            if fresh[n]:
+
+                @pl.when(column == starts[n])
+                def _():
+                    turned_refs[n][:rows] = other_refs[n][...].T
+                    turned_refs[n][rows:] = own_refs[n][...].T
+
+            value = dot_nn(turned_refs[owners[n]][...], right_refs[n][...])
+            sent_ref[...] = value[:rows]
+            kept_ref[...] = value[rows:]
+
+        for n in range(count):
+            pl.when((column >= starts[n]) & (column < ends[n]))(lambda n=n: one(n))
+
+    def left_place(side):
+        def index(stack, column, bit_ref):
+            half = jnp.where(side == 0, 1 - bit_ref[0], bit_ref[0])
+            return (0, half * stacks + stack)
+
+        return index
 
     def right_place(start, end):
-        return lambda side, stack, column, bit_ref: (0, jnp.clip(column - start, 0, end - start - 1))
-
-    def sent_place(side, stack, column, bit_ref):
-        return (jnp.where(side == 0, stack, stacks - 1), jnp.where(side == 0, column, columns - 1))
-
-    def kept_place(side, stack, column, bit_ref):
-        return (jnp.where(side == 1, stack, 0), jnp.where(side == 1, column, 0))
+        return lambda stack, column, bit_ref: (0, jnp.clip(column - start, 0, end - start - 1))
 
     return pl.pallas_call(
         kernel,
         name="weight_grads",
         grid_spec=pltpu.PrefetchScalarGridSpec(
             num_scalar_prefetch=1,
-            grid=(2, stacks, columns),
-            in_specs=[pl.BlockSpec((v.shape[0], rows), left_place) for v in lefts]
+            grid=(stacks, columns),
+            in_specs=[
+                pl.BlockSpec((v.shape[0], rows), left_place(side)) for side in (0, 1) for v in lefts
+            ]
             + [
                 pl.BlockSpec((v.shape[0], width), right_place(start, end))
                 for v, start, end in zip(rights, starts, ends)
             ],
-            out_specs=[
-                pl.BlockSpec((rows, width), sent_place),
-                pl.BlockSpec((rows, width), kept_place),
-            ],
+            out_specs=[pl.BlockSpec((rows, width), lambda stack, column, bit_ref: (stack, column))]
+            * 2,
+            scratch_shapes=[pltpu.VMEM((2 * rows, v.shape[0]), v.dtype) for v in lefts],
         ),
         out_shape=[jax.ShapeDtypeStruct((height, columns * width), jnp.float32)] * 2,
-    )(bit.reshape(1), *lefts, *rights)
+    )(bit.reshape(1), *lefts, *lefts, *rights)
+
+
+def row_tiles(rows):
+    tile = min(rows, TILE)
+
+    def lines(n):
+        return pl.BlockSpec((tile, n), lambda t: (t, 0))
+
+    def whole(*shape):
+        return pl.BlockSpec(shape, lambda t: (0, 0))
+
+    return tile, lines, whole
+
+
+def norm_backward(values, grad, gain, sum_ref):
+    scale = lax.rsqrt(jnp.mean(values * values, axis=1, keepdims=True) + norm_epsilon)
+    unit = values * scale
+
+    @pl.when(pl.program_id(0) == 0)
+    def _():
+        sum_ref[...] = jnp.zeros_like(sum_ref)
+
+    sum_ref[...] += jnp.sum(grad * unit, axis=0, keepdims=True)
+    scaled = grad * gain
+    return scale * (scaled - unit * jnp.mean(unit * scaled, axis=1, keepdims=True))
+
+
+def project_backward_kernel(
+    gq_ref, gk_ref, gv_ref, gh_ref, x_ref, gain_ref, wq_ref, wk_ref, wv_ref, gx_ref, gg_ref
+):
+    grad = (
+        dot_nt(gq_ref[...], wq_ref[...])
+        + dot_nt(gk_ref[...], wk_ref[...])
+        + dot_nt(gv_ref[...], wv_ref[...])
+    )
+    values = x_ref[...].astype(jnp.float32)
+    gx_ref[...] = gh_ref[...] + norm_backward(values, grad, gain_ref[...], gg_ref)
+
+
+def project_backward(grads, grad_hidden, states, gain, weights):
+    rows, width = grad_hidden.shape
+    tile, lines, whole = row_tiles(rows)
+    return pl.pallas_call(
+        project_backward_kernel,
+        name="project_backward",
+        grid=(rows // tile,),
+        in_specs=[lines(width)] * 5 + [whole(1, width)] + [whole(width, width)] * 3,
+        out_specs=[lines(width), whole(1, width)],
+        out_shape=[
+            jax.ShapeDtypeStruct((rows, width), jnp.float32),
+            jax.ShapeDtypeStruct((1, width), jnp.float32),
+        ],
+    )(*grads, grad_hidden, states, gain[None], *weights)
 
 
 def feed_backward_kernel(
@@ -338,19 +410,7 @@
     grad_inner = jnp.where(act_ref[...] > 0, grad_activ, 0.0).astype(jnp.bfloat16)
     gu_ref[...] = grad_inner
     grad_normed = dot_nt(grad_inner, win_ref[...])
-    hidden = hid_ref[...]
-    scale = lax.rsqrt(jnp.mean(hidden * hidden, axis=1, keepdims=True) + norm_epsilon)
-    unit = hidden * scale
-
-    @pl.when(pl.program_id(0) == 0)
-    def _():
-        gg_ref[...] = jnp.zeros_like(gg_ref)
-
-    gg_ref[...] += jnp.sum(grad_normed * unit, axis=0, keepdims=True)
-    scaled = grad_normed * gain_ref[...]
-    grad_hidden = grad_output + scale * (
-        scaled - unit * jnp.mean(unit * scaled, axis=1, keepdims=True)
-    )
+    grad_hidden = grad_output + norm_backward(hid_ref[...], grad_normed, gain_ref[...], gg_ref)
     gh_ref[...] = grad_hidden
     low = grad_hidden.astype(jnp.bfloat16)
     ghl_ref[...] = low
@@ -360,14 +420,7 @@
 def feed_backward(grad_output, activ, hidden, gain, w_ffout, w_in, w_out):
     rows, width = grad_output.shape
     inner = activ.shape[1]
-    tile = 256
-
-    def lines(n):
-        return pl.BlockSpec((tile, n), lambda t: (t, 0))
-
-    def whole(*shape):
-        return pl.BlockSpec(shape, lambda t: (0, 0))
-
+    tile, lines, whole = row_tiles(rows)
     return pl.pallas_call(
         feed_backward_kernel,
         name="feed_backward",
@@ -392,13 +445,16 @@
     )(grad_output, activ, hidden, gain[None], w_ffout, w_in, w_out)
 
 
-def put_together(own, other, bit, widths):
-    half = 4
-    rows, wide = own.shape
-    block = rows // half
-
-    def kernel(bit_ref, own_ref, other_ref, *out_refs):
-        is_own = pl.program_id(0) // half == bit_ref[0]
+def put(pieces, places, count, widths, before=()):
+    rows, wide = pieces[0].shape
+    splits = 1
+    while rows % (16 * splits) == 0 and rows // splits * wide > 320 * 1024:
+        splits *= 2
+    block = rows // splits
+    number, kept = len(pieces), len(before)
+
+    def kernel(places_ref, *refs):
+        out_refs = refs[number + kept :]
 
         def copy(source):
             at = 0
@@ -406,30 +462,28 @@
                 out[...] = source[:, at : at + width]
                 at += width
 
-        pl.when(is_own)(lambda: copy(own_ref))
-        pl.when(jnp.logical_not(is_own))(lambda: copy(other_ref))
-
-    def place(side):
-        def index(step, bit_ref):
-            first = jnp.where(side == 0, bit_ref[0], 1 - bit_ref[0]) * half
-            return (jnp.clip(step - first, 0, half - 1), 0)
-
-        return index
+        for n in range(number):
+            pl.when(pl.program_id(0) // splits == n)(lambda n=n: copy(refs[n]))
+
+    def source(n):
+        return lambda step, places_ref: (jnp.clip(step - n * splits, 0, splits - 1), 0)
+
+    def target(step, places_ref):
+        return (places_ref[step // splits] * splits + step % splits, 0)
 
     return pl.pallas_call(
         kernel,
-        name="put_together",
+        name="put",
         grid_spec=pltpu.PrefetchScalarGridSpec(
             num_scalar_prefetch=1,
-            grid=(2 * half,),
-            in_specs=[pl.BlockSpec((block, wide), place(side)) for side in (0, 1)],
-            out_specs=[pl.BlockSpec((block, w), lambda step, bit_ref: (step, 0)) for w in widths],
+            grid=(number * splits,),
+            in_specs=[pl.BlockSpec((block, wide), source(n)) for n in range(number)]
+            + [pl.BlockSpec(memory_space=pl.ANY)] * kept,
+            out_specs=[pl.BlockSpec((block, w), target) for w in widths],
         ),
-        out_shape=[jax.ShapeDtypeStruct((2 * rows, w), own.dtype) for w in widths],
-        cost_estimate=pl.CostEstimate(
-            flops=0, transcendentals=0, bytes_accessed=16 * rows * wide
-        ),
-    )(bit.reshape(1), own, other)
+        out_shape=[jax.ShapeDtypeStruct((count * rows, w), pieces[0].dtype) for w in widths],
+        input_output_aliases={1 + number + n: n for n in range(kept)},
+    )(jnp.stack(places), *pieces, *before)
 
 
 def tie(*values):
@@ -443,35 +497,66 @@
         self.step = 0
         self.back = False
         self.done = False
-        self.held = weight_grads(net.bits[0], lefts, rights)
+        sent, kept = weight_grads(net.digits[0], lefts, rights)
+        self.held = [[sent], [kept]]
+        self.cuts = [[]]
 
     def go(self):
-        if self.back:
-            self.got = self.net.swap_step(self.held[0], self.step - 1)
-        else:
-            self.got = self.net.swap_step(self.held[0], self.step)
+        net = self.net
+        if not self.back:
+            self.got = [
+                net.send(v, self.step, r) for r, v in zip(net.peers(self.step), self.held[0])
+            ]
+            return
+        (piece,) = self.held
+        k = self.step - 1
+        self.got = [net.send(piece, k, r) for r in net.peers(k)]
+        self.whole = piece.shape[0] % 8 == 0
+        if self.whole:
+            widths = [piece.shape[1]] if k else self.widths
+            self.base = put([piece], [net.digits[k]], len(self.got) + 1, widths)
 
     def end(self):
-        bits = self.net.bits
+        net = self.net
         if self.back:
             self.step -= 1
-            self.done = self.step == 0
-            if self.done:
-                self.held = put_together(self.held[0], self.got, bits[0], self.widths)
+            k = self.step
+            self.done = k == 0
+            digit, peers = net.digits[k], net.peers(k)
+            if self.whole:
+                widths = self.widths if self.done else [self.held[0].shape[1]]
+                self.held = put(
+                    self.got, [digit ^ r for r in peers], len(peers) + 1, widths, self.base
+                )
             else:
-                self.held = [join(self.held[0], self.got, bits[self.step])]
+                self.held = [place([self.held[0], *self.got], digit)]
+                if self.done:
+                    ends = [sum(self.widths[: n + 1]) for n in range(len(self.widths))]
+                    self.held = [
+                        self.held[0][:, end - width : end] for end, width in zip(ends, self.widths)
+                    ]
             return
+        terms = [*self.held[1], *self.got]
+        self.cuts += [[] for _ in self.got]
         self.step += 1
-        self.back = self.step == len(bits)
-        kept, got = self.held[1], self.got
+        self.back = self.step == len(net.stages)
+
+        def total(more):
+            value = None
+            for term, cuts in zip(terms, self.cuts):
+                for which, count in cuts + more:
+                    term = part_of(term, which, count)
+                value = term if value is None else value + term
+            return value
+
         if self.back:
-            self.held = [kept + got]
-        else:
-            bit = bits[self.step]
-            self.held = [
-                half_of(kept, 1 - bit) + half_of(got, 1 - bit),
-                half_of(kept, bit) + half_of(got, bit),
-            ]
+            self.held = [total([])]
+            return
+        digit, peers = net.digits[self.step], net.peers(self.step)
+        count = len(peers) + 1
+        self.held = [[total([(digit ^ r, count)]) for r in peers], terms]
+        for cuts in self.cuts:
+            cuts.append((digit, count))
 
 
 def tie_all(sums, *values):
@@ -481,12 +566,11 @@
     return values
 
 
-def advance(sums, steps):
-    for s, count in zip(sums, steps):
-        for _ in range(count):
-            if not s.done:
-                s.go()
-                s.end()
+def advance(sums):
+    for s in sums:
+        s.go()
+    for s in sums:
+        s.end()
 
 
 def local(
@@ -519,8 +603,7 @@
     row_count = item_count * dp_count
     rows = micro_count * length
     net = Net()
-    bits = len(net.steps)
-    gather_order = (0, 4, 1, 2, 3) if bits == 5 else tuple(range(bits))
+    bits = net.count
 
     offset = jnp.arange(2 * length, dtype=jnp.int32) - length
     code = bucket_code(offset, bucket_count)
@@ -532,7 +615,7 @@
     segment = segment_ids[0]
 
     states_f = states[0].reshape(rows, model_width).astype(jnp.float32)
-    normed, back_attn = jax.vjp(rms_scale, states_f, gain_attn)
+    normed = rms_scale(states_f, gain_attn)
     normed_low = normed.astype(jnp.bfloat16)
     query_low = mm(normed_low, w_query).astype(jnp.bfloat16)
     key_low = mm(normed_low, w_key).astype(jnp.bfloat16)
@@ -560,16 +643,20 @@
     unit_embed, back_unit = jax.vjp(unit_rows, embed)
 
     every = unit_embed
-    for b in reversed(gather_order):
-        every = join(every, net.swap(every, b), net.bit(b))
-    every = every.reshape((2,) * bits + (micro_count, item_count, model_width))
-    place = [bits - 1 - b for b in gather_order]
-    every = jnp.transpose(
-        every,
-        [bits]
-        + [gather_order.index(b) for b in reversed(range(bits))]
-        + [bits + 1, bits + 2],
-    ).reshape(micro_count, 2, row_count, model_width)
+    if bits == 5:
+        for k in (3, 1, 2):
+            every = net.collect(every, net.stages[k])
+        every = every.reshape(2, 2, -1, model_width)
+        every = jnp.where(net.bit(0) == 0, jnp.swapaxes(every, 0, 1), every)
+        every = net.collect(every.reshape(-1, model_width), net.stages[0])
+        every = every.reshape(2, 2, 2, -1, micro_count, item_count, model_width)
+        every = jnp.transpose(every, (4, 1, 3, 2, 0, 5, 6))
+    else:
+        for b in range(bits):
+            every = net.collect(every, ((b,), (b,)))
+        every = every.reshape(2, net.dp, micro_count, item_count, model_width)
+        every = jnp.transpose(every, (2, 0, 1, 3, 4))
+    every = every.reshape(micro_count, 2, row_count, model_width)
     queries_all = every[:, 0]
     passages_all = every[:, 1]
     columns = jnp.arange(row_count, dtype=jnp.int32)[None, :]
@@ -615,7 +702,11 @@
         )
 
     grads = attention_part(0, query_low, ())
-    second = Sum(net, [normed_two_low], [grad_inner_low])
+    second = Sum(
+        net,
+        [normed_two_low, mixed_low, pooled_flat],
+        [grad_inner_low, grad_hidden_low, grad_e_low],
+    )
     first.end()
     query_low, grads = tie_all([first, second], query_low, grads)
     first.go()
@@ -627,47 +718,65 @@
     first.go()
     second.go()
     grads = attention_part(2, query_low, grads)
-    first.end()
-    (grads,) = tie_all([first], grads)
-    grad_query_h, grad_key_h, grad_value_h, grad_rows = grads
-    first.go()
-    third = Sum(
-        net,
-        [normed_low] * 3 + [mixed_low, pooled_flat],
-        [grad_query_h, grad_key_h, grad_value_h, grad_hidden_low, grad_e_low],
+    *grad_heads, grad_rows = grads
+    third = Sum(net, [normed_low] * 3, grad_heads)
+    grad_states, grad_gain_attn = project_backward(
+        grad_heads,
+        grad_hidden,
+        states[0].reshape(rows, model_width),
+        gain_attn,
+        (w_query, w_key, w_value),
     )
     first.end()
     second.end()
-    grad_query_h, grad_key_h, grad_value_h = tie_all(
-        [first, second, third], grad_query_h, grad_key_h, grad_value_h
-    )
-    sums = [first, second, third]
-    advance(sums, (1, 1, 1))
     grad_bias = jnp.einsum("hx,xb->bh", grad_rows[:, 0], code_back, precision=highest)
-    grad_normed = (
-        mm_t(grad_query_h, w_query) + mm_t(grad_key_h, w_key) + mm_t(grad_value_h, w_value)
-    )
-    grad_states_norm, grad_gain_attn = back_attn(grad_normed)
-    grad_states = grad_hidden + grad_states_norm
     small = jnp.concatenate(
-        [grad_gain_attn, grad_gain_ffn[0], grad_gain_final, grad_bias.reshape(-1)]
+        [grad_gain_attn[0], grad_gain_ffn[0], grad_gain_final, grad_bias.reshape(-1)]
     )
     lines = -(-small.shape[0] // (8 * LANES)) * 8
     small = jnp.pad(small, (0, lines * LANES - small.shape[0])).reshape(lines, LANES)
-    (grad_states,) = tie_all(sums, grad_states)
+    sums = [first, second, third]
+    small, grad_states = tie_all(sums, small, grad_states)
+    def swap_small(value, which):
+        for b in which:
+            value = value + net.swap(value, b)
+        return value
+
     if bits == 5:
-        plan = ((1, 1, 1), (1, 2, 1), (1, 1, 1), (1, 1, 1), (0, 1, 2), (0, 1, 1), (0, 0, 1), (0, 0, 1))
+        advance(sums)
+        (small,) = tie_all(sums, small)
+        advance(sums)
+        small = swap_small(small, (0, 1, 2))
+        (small,) = tie_all(sums, small)
+        advance(sums)
+        small = swap_small(small, (3, 4))
+        tie_all(sums)
+        first.go()
+        advance([second, third])
+        tie_all([second, third])
+        second.go()
+        third.go()
+        first.end()
+        third.end()
+        third.go()
+        first.held, second.base = tie(first.held, second.base)
+        second.end()
+        third.end()
+        tie_all([second, third])
+        third.go()
+        second.go()
+        second.end()
+        second.held, third.base = tie(second.held, third.base)
+        third.end()
+        tie_all([second, third])
+        advance([third])
     else:
-        plan = ((1, 1, 1),) * (2 * bits)
-    for turn, steps in enumerate(plan):
-        advance(sums, steps)
-        if turn < bits:
-            small = small + net.swap(small, turn)
-        if turn + 1 < len(plan):
-            (small,) = tie_all(sums, small)
+        while not all(s.done for s in sums):
+            advance([s for s in sums if not s.done])
+        small = swap_small(small, range(bits))
     (whole_ffout,) = first.held
-    (whole_in,) = second.held
-    whole_query, whole_key, whole_value, whole_out, whole_proj = third.held
+    whole_in, whole_out, whole_proj = second.held
+    whole_query, whole_key, whole_value = third.held
     small = small.reshape(-1)
     loss = loss_sum / (micro_count * row_count)
     width = model_width

time: 580 us -> 526 us (0.907)
  waiting for transfers between devices: 214 us -> 134 us
  Pallas kernels: 171 us -> 219 us
  other arithmetic: 89.3 us -> 47.4 us
  starting transfers between devices: 39.6 us -> 66.9 us
  matrix products: 39 us -> 32.6 us
    pallas_call x3 -> x25, Pallas kernels: 31.7 us -> 94.4 us  [the longest x24 84 us: put(): pl.pallas_call(kernel, name='put', grid_spec=pltpu.PrefetchScalarGridSpec...]
    ppermute x10 -> x5, waiting for transfers between devices: 79.4 us -> 26.8 us  [swap(): lax.ppermute(value, AXES, [(i, i ^ 1 << b) for i in range(self.size)])]
    ppermute x30 -> x42, starting transfers between devices: 26.2 us -> 58.6 us  [send_by(): lax.ppermute(value, AXES, [(i, i ^ masks[i & 1]) for i in range(self.size)])]
    select_n x19 -> x8, other arithmetic: 33.5 us -> 1.06 us  [the longest x6 0.69 us: place(): value = jnp.where(source == r, piece[None], value)]
    ppermute x30 -> x42, waiting for transfers between devices: 135 us -> 107 us  [send_by(): lax.ppermute(value, AXES, [(i, i ^ masks[i & 1]) for i in range(self.size)])]
    add x21 -> x17, other arithmetic: 44.3 us -> 35 us  [the longest x12 34.9 us: total(): value = term if value is None else value + term]
    dot_general x4 -> x1, matrix products: 8.57 us -> 0.42 us  [mm_t(): lax.dot_general(a, b, (((1,), (1,)), ((), ())), preferred_element_type=jn...]
    pallas_call x3, Pallas kernels: 41.4 us -> 34.4 us  [weight_grads(): pl.pallas_call(kernel, name='weight_grads', grid_spec=pltpu.PrefetchScala...]
  transfers between devices with their start and end apart: 40 -> 47, of which waited for: 20 -> 22; matrix products, arithmetic and copies ran while one was open for 8% -> 4% of each run, Pallas kernels for 17% -> 33%
where the time goes in v4:
time: 526 us; the launch traced here: 517 us
  Pallas kernels  219 us (42%)
  waiting for transfers between devices  134 us (25%)
  starting transfers between devices  66.9 us (13%)
  other arithmetic  47.4 us (9%)
  matrix products  32.6 us (6%)
  local copies, waits for them, and re-layouts  13.4 us (3%)
    ppermute x42, waiting for transfers between devices, send_by(): lax.ppermute(value, AXES, [(i, i ^ masks[i & 1]) for i in range(self.size)])  107 us
    pallas_call x24, Pallas kernels, put(): pl.pallas_call(kernel, name='put', grid_spec=pltpu.PrefetchScalarGridSpec...  84 us
    ppermute x42, starting transfers between devices, send_by(): lax.ppermute(value, AXES, [(i, i ^ masks[i & 1]) for i in range(self.size)])  58.6 us
    pallas_call x3, Pallas kernels, attention_grads(): pl.pallas_call(kernel, name='attention_backward', grid=(count, micro_coun...  44.9 us
    add x12, other arithmetic, total(): value = term if value is None else value + term  34.9 us
    pallas_call x3, Pallas kernels, weight_grads(): pl.pallas_call(kernel, name='weight_grads', grid_spec=pltpu.PrefetchScala...  34.4 us
    ppermute x5, waiting for transfers between devices, swap(): lax.ppermute(value, AXES, [(i, i ^ 1 << b) for i in range(self.size)])  26.8 us
    dot_general x7, matrix products, mm(): return jnp.dot(a, b, preferred_element_type=jnp.float32)  26.5 us
  transfers between devices with their start and end apart: 47, of which 22 were waited for; matrix products, arithmetic and copies ran while one was open for 4% of the time, Pallas kernels for 33%

profile of v4, /device:TPU:0, one launch (start us, length us, event | category | flops | bytes accessed | tf_op | source)
XLA Modules:
  0.0 517.2 jit_solution(1208213395418463471)
XLA Ops:
  3.8 2.5 convolution_convert_fusion.refs_2_
  6.4 2.5 convolution_convert_fusion.1.refs_1_
  8.9 2.5 convolution_convert_fusion.2.refs_0_
  14.2 23.0 %attention_forward.1.refs_1_.refs_4_ = bf16[1024,768]{1,0:T(8,128)(2,1)} custom-call(bf16[1024,768]{1,0:T(8,128)(2,1)} %convolution_convert_fusion.2.refs_0_, bf16[1024,768]{1,0:T(8,128)(2,1)} %convolution_convert_fusion.1.refs_1_, bf16[1024,768]{1,0:T(8,128)(2,1)} %convolution_convert_fusion.refs_2_, s32[1024,1]{1,0:T(8,128)} %bitcast.175, ...), custom_call_target="tpu_custom_call" | custom-call | tf_op jit(solution)/shard_map/attention_forward/pallas_call | solution.py:198
  37.3 3.3 multiply_reduce_fusion.2
  40.9 10.0 %maximum_convert_fusion.refs_0_.refs_1_.act_ref = bf16[1024,3072]{1,0:T(8,128)(2,1)S(1)} fusion(bf16[1024,768]{1,0:T(8,128)(2,1)S(1)} %multiply_convert_fusion.refs_0_.refs_3_, bf16[768,3072]{1,0:T(8,128)(2,1)} %win_ref.1), kind=kOutput, calls=%fused_computation | convolution fusion | flops 4838129664 | bytes 12582912 | tf_op jit(solution)/shard_map/dot_general | solution.py:46
  51.0 5.2 %multiply_reduce_fusion.1 = (f32[1024]{0:T(1024)S(1)}, f32[1024,768]{1,0:T(8,128)S(1)}) fusion(f32[1024,768]{1,0:T(8,128)S(1)} %get-tuple-element.301.hid_ref, bf16[1024,3072]{1,0:T(8,128)(2,1)S(1)} %maximum_convert_fusion.refs_0_.refs_1_.act_ref, bf16[3072,768]{1,0:T(8,128)(2,1)S(1)} %bitcast.184), kind=kOutput, calls=%fused_computation.11 | convolution fusion | flops 4834196480 | bytes 17305600 | tf_op jit(solution)/shard_map/dot_general | solution.py:46
  60.1 5.1 collective-permute-start
  67.4 2.9 collective-permute-done.1
  72.0 4.1 collective-permute-done.3
  77.9 6.1 %collective-permute-done.4 = f32[128,768]{1,0:T(8,128)S(1)} collective-permute-done((f32[128,768]{1,0:T(8,128)S(1)}, f32[128,768]{1,0:T(8,128)S(1)}, u32[]{:S(2)}, u32[]{:S(2)}) %collective-permute-start.4) | collective-permute-done | bytes 393248 | tf_op jit(solution)/shard_map/ppermute | solution.py:266
  93.7 2.9 fusion.59
  96.6 10.0 %weight_grads.3 = (f32[1536,768]{1,0:T(8,128)}, f32[1536,768]{1,0:T(8,128)}) custom-call(s32[1]{0:T(128)} %bitcast.43.bit_ref.places_ref, bf16[1024,3072]{1,0:T(8,128)(2,1)} %copy-done.3, bf16[1024,3072]{1,0:T(8,128)(2,1)} %copy-done.3, bf16[1024,768]{1,0:T(8,128)(2,1)} %get-tuple-element.280.refs_2_), custom_call_target="tpu_custom_call" | custom-call | tf_op jit(solution)/shard_map/weight_grads/pallas_call | solution.py:330
  107.3 22.2 %feed_backward.1 = (bf16[1024,3072]{1,0:T(8,128)(2,1)}, f32[1024,768]{1,0:T(8,128)}, bf16[1024,768]{1,0:T(8,128)(2,1)}, bf16[1024,768]{1,0:T(8,128)(2,1)}, f32[1,768]{1,0:T(1,128)}) custom-call(f32[1024,768]{1,0:T(8,128)} %get-tuple-element.139.go_ref, bf16[1024,3072]{1,0:T(8,128)(2,1)} %copy-done.3, f32[1024,768]{1,0:T(8,128)} %copy-done.11, ...), custom_call_target="tpu_custom_call" | custom-call | tf_op jit(solution)/shard_map/feed_backward/pallas_call | solution.py:424
  129.6 2.7 dynamic-slice_add_fusion.1
  135.0 14.1 %weight_grads.4 = (f32[384,4608]{1,0:T(8,128)}, f32[384,4608]{1,0:T(8,128)}) custom-call(s32[1]{0:T(128)} %bitcast.43.bit_ref.places_ref, bf16[1024,768]{1,0:T(8,128)(2,1)} %copy-done.10, bf16[1024,768]{1,0:T(8,128)(2,1)} %attention_forward.1.refs_1_.refs_4_, bf16[16,768]{1,0:T(8,128)(2,1)} %copy-done.24, bf16[1024,768]{1,0:T(8,128)(2,1)} %copy-done.10, ...), custom_call_target="tpu_custom_call" | custom-call | tf_op jit(solution)/shard_map/weight_grads/pallas_call | solution.py:330
  149.1 15.0 %attention_backward.3 = (bf16[1024,768]{1,0:T(8,128)(2,1)}, bf16[1024,768]{1,0:T(8,128)(2,1)}, bf16[1024,768]{1,0:T(8,128)(2,1)}, f32[12,1,1024]{2,1,0:T(1,128)}) custom-call(bf16[1024,768]{1,0:T(8,128)(2,1)} %convolution_convert_fusion.2.refs_0_, bf16[1024,768]{1,0:T(8,128)(2,1)} %convolution_convert_fusion.1.refs_1_, ...), custom_call_target="tpu_custom_call" | custom-call | tf_op jit(solution)/shard_map/attention_backward/pallas_call | solution.py:223
  168.1 14.9 %attention_backward.4 = (bf16[1024,768]{1,0:T(8,128)(2,1)}, bf16[1024,768]{1,0:T(8,128)(2,1)}, bf16[1024,768]{1,0:T(8,128)(2,1)}, f32[12,1,1024]{2,1,0:T(1,128)}) custom-call(bf16[1024,768]{1,0:T(8,128)(2,1)} %convolution_convert_fusion.2.refs_0_, ...), custom_call_target="tpu_custom_call", output_to_operand_aliasing={{0}: (7, {}), {1}: (8, {}), {2}: (9, {}), {3}: (10, {})} | custom-call | tf_op jit(solution)/shard_map/attention_backward/pallas_call | solution.py:223
  185.1 5.3 %dynamic-slice_add_fusion = f32[192,4608]{1,0:T(8,128)} fusion(f32[384,4608]{1,0:T(8,128)} %collective-permute-done.9, s32[]{:T(128)S(6)} %select_n.400, f32[384,4608]{1,0:T(8,128)} %get-tuple-element.208), kind=kLoop, calls=%fused_computation.4 | loop fusion | flops 884736 | bytes 10616836 | tf_op jit(solution)/shard_map/add | solution.py:549
  196.7 14.9 %attention_backward.5 = (bf16[1024,768]{1,0:T(8,128)(2,1)}, bf16[1024,768]{1,0:T(8,128)(2,1)}, bf16[1024,768]{1,0:T(8,128)(2,1)}, f32[12,1,1024]{2,1,0:T(1,128)}) custom-call(bf16[1024,768]{1,0:T(8,128)(2,1)} %convolution_convert_fusion.2.refs_0_, ...), custom_call_target="tpu_custom_call", output_to_operand_aliasing={{0}: (7, {}), {1}: (8, {}), {2}: (9, {}), {3}: (10, {})} | custom-call | tf_op jit(solution)/shard_map/attention_backward/pallas_call | solution.py:223
  211.6 10.3 %weight_grads.5 = (f32[384,2304]{1,0:T(8,128)}, f32[384,2304]{1,0:T(8,128)}) custom-call(s32[1]{0:T(128)} %bitcast.43.bit_ref.places_ref, bf16[1024,768]{1,0:T(8,128)(2,1)} %copy-done.2, bf16[1024,768]{1,0:T(8,128)(2,1)} %copy-done.2, bf16[1024,768]{1,0:T(8,128)(2,1)} %copy-done.2, bf16[1024,768]{1,0:T(8,128)(2,1)} %copy-done.2, ...), custom_call_target="tpu_custom_call" | custom-call | tf_op jit(solution)/shard_map/weight_grads/pallas_call | solution.py:330
  221.8 10.4 %project_backward.1 = (f32[1024,768]{1,0:T(8,128)}, f32[1,768]{1,0:T(1,128)}) custom-call(bf16[1024,768]{1,0:T(8,128)(2,1)} %get-tuple-element.177.gq_ref.refs_6_, bf16[1024,768]{1,0:T(8,128)(2,1)} %get-tuple-element.178.gk_ref.refs_7_, bf16[1024,768]{1,0:T(8,128)(2,1)} %get-tuple-element.179.gv_ref.refs_8_, f32[1024,768]{1,0:T(8,128)} %get-tuple-element.180.gh_ref, ...), custom_call_target="tpu_custom_call" | custom-call | tf_op jit(solution)/shard_map/project_backward/pallas_call | solution.py:391
  235.0 4.3 dynamic-slice_add_fusion.3
  240.1 2.7 collective-permute-start.15
  246.8 8.3 %collective-permute-done.14.refs_0_ = f32[96,768]{1,0:T(8,128)S(1)} collective-permute-done((f32[96,768]{1,0:T(8,128)S(1)}, f32[96,768]{1,0:T(8,128)S(1)}, u32[]{:S(2)}, u32[]{:S(2)}) %collective-permute-start.14) | collective-permute-done | bytes 294944 | tf_op jit(solution)/shard_map/ppermute | solution.py:266
  255.1 8.5 %collective-permute-done.15.refs_1_ = f32[96,768]{1,0:T(8,128)S(1)} collective-permute-done((f32[96,768]{1,0:T(8,128)S(1)}, f32[96,768]{1,0:T(8,128)S(1)}, u32[]{:S(2)}, u32[]{:S(2)}) %collective-permute-start.15) | collective-permute-done | bytes 294944 | tf_op jit(solution)/shard_map/ppermute | solution.py:266
  265.0 3.3 put.25.refs_0_
  268.3 4.0 dynamic-slice_add_fusion.6
  272.4 3.0 dynamic-slice_add_fusion.2
  276.6 5.4 %collective-permute-start.23 = (f32[24,4608]{1,0:T(8,128)}, f32[24,4608]{1,0:T(8,128)}, u32[]{:S(2)}, u32[]{:S(2)}) collective-permute-start(f32[24,4608]{1,0:T(8,128)} %get-tuple-element.212), channel_id=1, source_target_pairs={{0,4},{1,5},{2,6},{3,7},{4,0},{5,1},{6,2},{7,3},{8,12},{9,13},{10,... | collective-permute-start | bytes 1327112 | tf_op jit(solution)/shard_map/ppermute | solution.py:266
  286.4 3.2 collective-permute-done.20
  290.6 19.7 %collective-permute-done.21 = f32[24,128]{1,0:T(8,128)S(1)} collective-permute-done((f32[24,128]{1,0:T(8,128)S(1)}, f32[24,128]{1,0:T(8,128)S(1)}, u32[]{:S(2)}, u32[]{:S(2)}) %collective-permute-start.21) | collective-permute-done | bytes 12320 | tf_op jit(solution)/shard_map/ppermute | solution.py:256
  315.3 2.8 add_add_fusion.1.refs_0_
  318.0 8.5 %collective-permute-done.22.refs_0_ = f32[384,768]{1,0:T(8,128)} collective-permute-done((f32[384,768]{1,0:T(8,128)S(1)}, f32[384,768]{1,0:T(8,128)}, u32[]{:S(2)}, u32[]{:S(2)}) %collective-permute-start.22) | collective-permute-done | bytes 1179680 | tf_op jit(solution)/shard_map/ppermute | solution.py:266
  329.0 3.0 dynamic-slice_add_fusion.5
  333.8 2.5 collective-permute-start.28
  340.5 2.8 put.28.refs_1_
  343.2 7.3 %collective-permute-done.28.refs_0_ = f32[24,4608]{1,0:T(8,128)S(1)} collective-permute-done((f32[24,4608]{1,0:T(8,128)S(1)}, f32[24,4608]{1,0:T(8,128)S(1)}, u32[]{:S(2)}, u32[]{:S(2)}) %collective-permute-start.28) | collective-permute-done | bytes 442400 | tf_op jit(solution)/shard_map/ppermute | solution.py:266
  350.5 18.5 %collective-permute-done.29.refs_1_ = f32[24,4608]{1,0:T(8,128)} collective-permute-done((f32[24,4608]{1,0:T(8,128)S(1)}, f32[24,4608]{1,0:T(8,128)}, u32[]{:S(2)}, u32[]{:S(2)}) %collective-permute-start.29) | collective-permute-done | bytes 442400 | tf_op jit(solution)/shard_map/ppermute | solution.py:266
  369.0 3.5 put.31.refs_0_
  372.6 2.9 dynamic-slice_add_fusion.12
  375.5 2.9 put.29.refs_0_
  379.2 5.6 %collective-permute-start.33 = (f32[24,2304]{1,0:T(8,128)}, f32[24,2304]{1,0:T(8,128)S(1)}, u32[]{:S(2)}, u32[]{:S(2)}) collective-permute-start(f32[24,2304]{1,0:T(8,128)} %get-tuple-element.229), channel_id=1, source_target_pairs={{0,4},{1,5},{2,6},{3,7},{4,0},{5,1},{6,2},{7,3},{8,12},{9,13},{10,... | collective-permute-start | bytes 663560 | tf_op jit(solution)/shard_map/ppermute | solution.py:266
  387.3 2.4 put.32.refs_1_
  389.7 5.7 %collective-permute-done.33 = f32[24,2304]{1,0:T(8,128)S(1)} collective-permute-done((f32[24,2304]{1,0:T(8,128)}, f32[24,2304]{1,0:T(8,128)S(1)}, u32[]{:S(2)}, u32[]{:S(2)}) %collective-permute-start.33) | collective-permute-done | bytes 221216 | tf_op jit(solution)/shard_map/ppermute | solution.py:266
  395.4 8.2 %collective-permute-done.34 = f32[24,2304]{1,0:T(8,128)S(1)} collective-permute-done((f32[24,2304]{1,0:T(8,128)S(1)}, f32[24,2304]{1,0:T(8,128)S(1)}, u32[]{:S(2)}, u32[]{:S(2)}) %collective-permute-start.34) | collective-permute-done | bytes 221216 | tf_op jit(solution)/shard_map/ppermute | solution.py:266
  405.0 2.6 put.33.refs_0_
  408.9 4.6 collective-permute-start.38
  417.5 3.7 collective-permute-done.38.refs_0_
  421.1 10.9 %collective-permute-done.39.refs_1_ = f32[24,2304]{1,0:T(8,128)S(1)} collective-permute-done((f32[24,2304]{1,0:T(8,128)S(1)}, f32[24,2304]{1,0:T(8,128)S(1)}, u32[]{:S(2)}, u32[]{:S(2)}) %collective-permute-start.39) | collective-permute-done | bytes 221216 | tf_op jit(solution)/shard_map/ppermute | solution.py:266
  433.4 3.2 put.39.refs_0_
  437.1 5.0 put.34.refs_1_
  442.2 4.4 put.36.refs_1_
  448.7 7.6 %collective-permute-done.41.refs_0_ = f32[96,2304]{1,0:T(8,128)S(1)} collective-permute-done((f32[96,2304]{1,0:T(8,128)}, f32[96,2304]{1,0:T(8,128)S(1)}, u32[]{:S(2)}, u32[]{:S(2)}) %collective-permute-start.41) | collective-permute-done | bytes 884768 | tf_op jit(solution)/shard_map/ppermute | solution.py:266
  459.3 5.0 put.35
  464.4 4.5 put.37.refs_0_
  470.2 8.2 %put.42 = (f32[768,3072]{1,0:T(8,128)}, f32[768,768]{1,0:T(8,128)}, f32[768,768]{1,0:T(8,128)}) custom-call(s32[1]{0:T(128)} %bitcast.43.bit_ref.places_ref, f32[384,4608]{1,0:T(8,128)} %put.37.refs_0_), custom_call_target="tpu_custom_call" | custom-call | tf_op jit(solution)/shard_map/put/pallas_call | solution.py:474
  478.4 2.5 put.44.refs_1_
  480.9 8.2 %put.43 = (f32[768,3072]{1,0:T(8,128)}, f32[768,768]{1,0:T(8,128)}, f32[768,768]{1,0:T(8,128)}) custom-call(s32[1]{0:T(128)} %bitcast.47.places_ref, f32[384,4608]{1,0:T(8,128)} %collective-permute-done.42.refs_0_, f32[768,3072]{1,0:T(8,128)} %get-tuple-element.237.refs_1_, ...), custom_call_target="tpu_custom_call", output_to_operand_aliasing={{0}: (2, {}), {1}: (3, {}), {2}: (4, {})} | custom-call | tf_op jit(solution)/shard_map/put/pallas_call | solution.py:474
  489.1 2.4 collective-permute-done.43.refs_0_
  491.5 2.5 put.45.refs_0_
  494.0 6.0 %collective-permute-start.45 = (f32[24,128]{1,0:T(8,128)S(1)}, f32[24,128]{1,0:T(8,128)S(1)}, u32[]{:S(2)}, u32[]{:S(2)}) collective-permute-start(f32[24,128]{1,0:T(8,128)S(1)} %add.719), channel_id=1, source_target_pairs={{0,8},{1,9},{2,10},{3,11},{4,12},{5,13},{6,14},{7,15},{8,0},{9,1},... | collective-permute-start | bytes 36872 | tf_op jit(solution)/shard_map/ppermute | solution.py:256
  506.8 4.3 put.46
  511.1 4.5 put.47
  (261 shorter events, 93.8 us)
Async XLA Ops:
  0.6 59.0 %copy-start = (bf16[768,768]{1,0:T(8,128)(2,1)S(1)}, bf16[768,768]{1,0:T(8,128)(2,1)}, u32[]{:S(2)}) copy-start(bf16[768,768]{1,0:T(8,128)(2,1)} %param.25) | copy-start | bytes 3538948
  40.5 10.4 %copy-start.11 = (f32[1024,768]{1,0:T(8,128)}, f32[1024,768]{1,0:T(8,128)S(1)}, u32[]{:S(2)}) copy-start(f32[1024,768]{1,0:T(8,128)S(1)} %get-tuple-element.301.hid_ref) | copy-start | bytes 9437188
  40.6 10.4 %slice-start = ((s8[4718592]{0:T(1024)(128)(4,1)}), s8[4194304]{0:T(1024)(128)(4,1)S(1)}, s32[]{:S(2)}) async-start(s8[4718592]{0:T(1024)(128)(4,1)} %bitcast.183), calls=%async_computation | async-start | bytes 8388608
  40.9 10.0 %copy-start.10 = (bf16[1024,768]{1,0:T(8,128)(2,1)}, bf16[1024,768]{1,0:T(8,128)(2,1)S(1)}, u32[]{:S(2)}) copy-start(bf16[1024,768]{1,0:T(8,128)(2,1)S(1)} %multiply_convert_fusion.refs_0_.refs_3_) | copy-start | bytes 4718596
  40.9 10.0 %slice-start.1 = ((s8[4718592]{0:T(1024)(128)(4,1)}), s8[524288]{0:T(1024)(128)(4,1)S(1)}, s32[]{:S(2)}) async-start(s8[4718592]{0:T(1024)(128)(4,1)} %bitcast.183), calls=%async_computation.1 | async-start | bytes 1048576
  57.9 19.9 %copy-start.39 = (s32[2,128]{1,0:T(2,128)S(1)}, s32[2,128]{1,0:T(2,128)}, u32[]{:S(2)}) copy-start(s32[2,128]{1,0:T(2,128)} %param.18) | copy-start | bytes 3076
  60.0 30.2 %copy-start.14 = (f32[16,768]{1,0:T(8,128)}, f32[16,768]{1,0:T(8,128)S(1)}, u32[]{:S(2)}) copy-start(f32[16,768]{1,0:T(8,128)S(1)} %get-tuple-element.305) | copy-start | bytes 147460
  60.1 7.2 %collective-permute-start = (f32[16,768]{1,0:T(8,128)S(1)}, f32[16,768]{1,0:T(8,128)S(1)}, u32[]{:S(2)}, u32[]{:S(2)}) collective-permute-start(f32[16,768]{1,0:T(8,128)S(1)} %broadcast_multiply_fusion), channel_id=1, source_target_pairs={{0,12},{1,13},{2,14},{3,15},{4,8},{5,9},{6,10},{7,11},{8,4},{9,5},... | collective-permute-start | bytes 147464 | tf_op jit(solution)/shard_map/ppermute | solution.py:266
  65.2 5.0 collective-permute-start.1
  65.2 5.0 collective-permute-start.2
  70.3 5.7 %collective-permute-start.3 = (f32[64,768]{1,0:T(8,128)S(1)}, f32[64,768]{1,0:T(8,128)S(1)}, u32[]{:S(2)}, u32[]{:S(2)}) collective-permute-start(f32[64,768]{1,0:T(8,128)S(1)} %fusion.16), channel_id=1, source_target_pairs={{0,16},{1,3},{2,18},{3,1},{4,20},{5,7},{6,22},{7,5},{8,24},{9,11},... | collective-permute-start | bytes 589832 | tf_op jit(solution)/shard_map/ppermute | solution.py:266
  76.2 7.8 %collective-permute-start.4 = (f32[128,768]{1,0:T(8,128)S(1)}, f32[128,768]{1,0:T(8,128)S(1)}, u32[]{:S(2)}, u32[]{:S(2)}) collective-permute-start(f32[128,768]{1,0:T(8,128)S(1)} %bitcast_select_fusion.3), channel_id=1, source_target_pairs={{0,2},{1,17},{2,0},{3,19},{4,6},{5,21},{6,4},{7,23},{8,10},{9,25},... | collective-permute-start | bytes 1179656 | tf_op jit(solution)/shard_map/ppermute | solution.py:266
  84.2 2.4 collective-permute-start.5
  106.6 23.0 %collective-permute-start.6 = (f32[1536,768]{1,0:T(8,128)}, f32[1536,768]{1,0:T(8,128)}, u32[]{:S(2)}, u32[]{:S(2)}) collective-permute-start(f32[1536,768]{1,0:T(8,128)} %get-tuple-element.144), channel_id=1, source_target_pairs={{0,1},{1,0},{2,3},{3,2},{4,5},{5,4},{6,7},{7,6},{8,9},{9,8},{10,11... | collective-permute-start | bytes 14155784 | tf_op jit(solution)/shard_map/ppermute | solution.py:266
  132.3 31.9 %collective-permute-start.7 = (f32[768,768]{1,0:T(8,128)S(1)}, f32[768,768]{1,0:T(8,128)}, u32[]{:S(2)}, u32[]{:S(2)}) collective-permute-start(f32[768,768]{1,0:T(8,128)S(1)} %dynamic-slice_add_fusion.1), channel_id=1, source_target_pairs={{0,16},{1,3},{2,18},{3,1},{4,20},{5,7},{6,22},{7,5},{8,24},{9,11},... | collective-permute-start | bytes 7077896 | tf_op jit(solution)/shard_map/ppermute | solution.py:266
  166.4 18.6 %collective-permute-start.9 = (f32[384,4608]{1,0:T(8,128)}, f32[384,4608]{1,0:T(8,128)}, u32[]{:S(2)}, u32[]{:S(2)}) collective-permute-start(f32[384,4608]{1,0:T(8,128)} %get-tuple-element.171), channel_id=1, source_target_pairs={{0,1},{1,0},{2,3},{3,2},{4,5},{5,4},{6,7},{7,6},{8,9},{9,8},{10,11... | collective-permute-start | bytes 21233672 | tf_op jit(solution)/shard_map/ppermute | solution.py:266
  166.6 16.4 %collective-permute-start.8 = (f32[384,768]{1,0:T(8,128)S(1)}, f32[384,768]{1,0:T(8,128)S(1)}, u32[]{:S(2)}, u32[]{:S(2)}) collective-permute-start(f32[384,768]{1,0:T(8,128)S(1)} %dynamic-slice_add_fusion.4), channel_id=1, source_target_pairs={{0,2},{1,17},{2,0},{3,19},{4,6},{5,21},{6,4},{7,23},{8,10},{9,25},... | collective-permute-start | bytes 3538952 | tf_op jit(solution)/shard_map/ppermute | solution.py:266
  185.0 6.6 %copy-start.36 = (f32[768]{0:T(1024)S(1)}, f32[768]{0:T(1024)}, u32[]{:S(2)}) copy-start(f32[768]{0:T(1024)} %param.26) | copy-start | bytes 9220
  185.0 7.2 %copy-start.37 = (f32[1,768]{1,0:T(1,128)S(1)}, f32[1,768]{1,0:T(1,128)}, u32[]{:S(2)}) copy-start(f32[1,768]{1,0:T(1,128)} %get-tuple-element.182) | copy-start | bytes 9220
  190.4 44.7 %collective-permute-start.13 = (f32[192,4608]{1,0:T(8,128)}, f32[192,4608]{1,0:T(8,128)}, u32[]{:S(2)}, u32[]{:S(2)}) collective-permute-start(f32[192,4608]{1,0:T(8,128)} %dynamic-slice_add_fusion), channel_id=1, source_target_pairs={{0,16},{1,3},{2,18},{3,1},{4,20},{5,7},{6,22},{7,5},{8,24},{9,11},... | collective-permute-start | bytes 10616840 | tf_op jit(solution)/shard_map/ppermute | solution.py:266
  192.2 41.4 %collective-permute-start.10 = (f32[96,768]{1,0:T(8,128)S(1)}, f32[96,768]{1,0:T(8,128)S(1)}, u32[]{:S(2)}, u32[]{:S(2)}) collective-permute-start(f32[96,768]{1,0:T(8,128)S(1)} %get-tuple-element.189), channel_id=1, source_target_pairs={{0,4},{1,5},{2,6},{3,7},{4,0},{5,1},{6,2},{7,3},{8,12},{9,13},{10,... | collective-permute-start | bytes 884744 | tf_op jit(solution)/shard_map/ppermute | solution.py:266
  193.0 40.7 %collective-permute-start.11 = (f32[96,768]{1,0:T(8,128)S(1)}, f32[96,768]{1,0:T(8,128)S(1)}, u32[]{:S(2)}, u32[]{:S(2)}) collective-permute-start(f32[96,768]{1,0:T(8,128)S(1)} %get-tuple-element.190), channel_id=1, source_target_pairs={{0,8},{1,9},{2,10},{3,11},{4,12},{5,13},{6,14},{7,15},{8,0},{9,1},... | collective-permute-start | bytes 884744 | tf_op jit(solution)/shard_map/ppermute | solution.py:266
  195.0 38.7 %collective-permute-start.12 = (f32[96,768]{1,0:T(8,128)S(1)}, f32[96,768]{1,0:T(8,128)S(1)}, u32[]{:S(2)}, u32[]{:S(2)}) collective-permute-start(f32[96,768]{1,0:T(8,128)S(1)} %get-tuple-element.191), channel_id=1, source_target_pairs={{0,12},{1,13},{2,14},{3,15},{4,8},{5,9},{6,10},{7,11},{8,4},{9,5},... | collective-permute-start | bytes 884744 | tf_op jit(solution)/shard_map/ppermute | solution.py:266
  221.8 11.1 %copy-start.32 = (f32[12,1,1024]{2,1,0:T(1,128)S(1)}, f32[12,1,1024]{2,1,0:T(1,128)}, u32[]{:S(2)}) copy-start(f32[12,1,1024]{2,1,0:T(1,128)} %get-tuple-element.183) | copy-start | bytes 147460
  235.0 7.8 %copy-start.17 = (f32[96,768]{1,0:T(8,128)}, f32[96,768]{1,0:T(8,128)S(1)}, u32[]{:S(2)}) copy-start(f32[96,768]{1,0:T(8,128)S(1)} %add_add_fusion.2.refs_0_) | copy-start | bytes 884740
  239.4 33.0 %collective-permute-start.18 = (f32[384,2304]{1,0:T(8,128)}, f32[384,2304]{1,0:T(8,128)}, u32[]{:S(2)}, u32[]{:S(2)}) collective-permute-start(f32[384,2304]{1,0:T(8,128)} %get-tuple-element.205), channel_id=1, source_target_pairs={{0,1},{1,0},{2,3},{3,2},{4,5},{5,4},{6,7},{7,6},{8,9},{9,8},{10,11... | collective-permute-start | bytes 10616840 | tf_op jit(solution)/shard_map/ppermute | solution.py:266
  239.4 28.9 %collective-permute-start.17 = (f32[96,4608]{1,0:T(8,128)}, f32[96,4608]{1,0:T(8,128)S(1)}, u32[]{:S(2)}, u32[]{:S(2)}) collective-permute-start(f32[96,4608]{1,0:T(8,128)} %dynamic-slice_add_fusion.3), channel_id=1, source_target_pairs={{0,2},{1,17},{2,0},{3,19},{4,6},{5,21},{6,4},{7,23},{8,10},{9,25},... | collective-permute-start | bytes 5308424 | tf_op jit(solution)/shard_map/ppermute | solution.py:266
  240.1 14.9 %collective-permute-start.14 = (f32[96,768]{1,0:T(8,128)S(1)}, f32[96,768]{1,0:T(8,128)S(1)}, u32[]{:S(2)}, u32[]{:S(2)}) collective-permute-start(f32[96,768]{1,0:T(8,128)S(1)} %add_add_fusion.2.refs_0_), channel_id=1, source_target_pairs={{0,4},{1,5},{2,6},{3,7},{4,0},{5,1},{6,2},{7,3},{8,12},{9,13},{10,... | collective-permute-start | bytes 884744 | tf_op jit(solution)/shard_map/ppermute | solution.py:266
  240.1 23.5 %collective-permute-start.15 = (f32[96,768]{1,0:T(8,128)S(1)}, f32[96,768]{1,0:T(8,128)S(1)}, u32[]{:S(2)}, u32[]{:S(2)}) collective-permute-start(f32[96,768]{1,0:T(8,128)S(1)} %add_add_fusion.2.refs_0_), channel_id=1, source_target_pairs={{0,8},{1,9},{2,10},{3,11},{4,12},{5,13},{6,14},{7,15},{8,0},{9,1},... | collective-permute-start | bytes 884744 | tf_op jit(solution)/shard_map/ppermute | solution.py:266
  242.8 20.8 %collective-permute-start.16 = (f32[96,768]{1,0:T(8,128)S(1)}, f32[96,768]{1,0:T(8,128)S(1)}, u32[]{:S(2)}, u32[]{:S(2)}) collective-permute-start(f32[96,768]{1,0:T(8,128)S(1)} %add_add_fusion.2.refs_0_), channel_id=1, source_target_pairs={{0,12},{1,13},{2,14},{3,15},{4,8},{5,9},{6,10},{7,11},{8,4},{9,5},... | collective-permute-start | bytes 884744 | tf_op jit(solution)/shard_map/ppermute | solution.py:266
  255.1 8.5 %copy-start.25 = (f32[96,768]{1,0:T(8,128)}, f32[96,768]{1,0:T(8,128)S(1)}, u32[]{:S(2)}) copy-start(f32[96,768]{1,0:T(8,128)S(1)} %collective-permute-done.14.refs_0_) | copy-start | bytes 884740
  272.4 37.9 %copy-start.12 = (f32[384,768]{1,0:T(8,128)S(1)}, f32[384,768]{1,0:T(8,128)}, u32[]{:S(2)}) copy-start(f32[384,768]{1,0:T(8,128)} %put.25.refs_0_) | copy-start | bytes 3538948
  275.3 53.6 %collective-permute-start.26 = (f32[192,2304]{1,0:T(8,128)}, f32[192,2304]{1,0:T(8,128)}, u32[]{:S(2)}, u32[]{:S(2)}) collective-permute-start(f32[192,2304]{1,0:T(8,128)} %dynamic-slice_add_fusion.2), channel_id=1, source_target_pairs={{0,16},{1,3},{2,18},{3,1},{4,20},{5,7},{6,22},{7,5},{8,24},{9,11},... | collective-permute-start | bytes 5308424 | tf_op jit(solution)/shard_map/ppermute | solution.py:266
  276.6 36.5 %collective-permute-start.23 = (f32[24,4608]{1,0:T(8,128)}, f32[24,4608]{1,0:T(8,128)}, u32[]{:S(2)}, u32[]{:S(2)}) collective-permute-start(f32[24,4608]{1,0:T(8,128)} %get-tuple-element.212), channel_id=1, source_target_pairs={{0,4},{1,5},{2,6},{3,7},{4,0},{5,1},{6,2},{7,3},{8,12},{9,13},{10,... | collective-permute-start | bytes 1327112 | tf_op jit(solution)/shard_map/ppermute | solution.py:266
  282.1 33.2 %collective-permute-start.24 = (f32[24,4608]{1,0:T(8,128)}, f32[24,4608]{1,0:T(8,128)}, u32[]{:S(2)}, u32[]{:S(2)}) collective-permute-start(f32[24,4608]{1,0:T(8,128)} %get-tuple-element.213), channel_id=1, source_target_pairs={{0,8},{1,9},{2,10},{3,11},{4,12},{5,13},{6,14},{7,15},{8,0},{9,1},... | collective-permute-start | bytes 1327112 | tf_op jit(solution)/shard_map/ppermute | solution.py:266
  283.1 32.1 %collective-permute-start.25 = (f32[24,4608]{1,0:T(8,128)S(1)}, f32[24,4608]{1,0:T(8,128)}, u32[]{:S(2)}, u32[]{:S(2)}) collective-permute-start(f32[24,4608]{1,0:T(8,128)S(1)} %get-tuple-element.214), channel_id=1, source_target_pairs={{0,12},{1,13},{2,14},{3,15},{4,8},{5,9},{6,10},{7,11},{8,4},{9,5},... | collective-permute-start | bytes 1327112 | tf_op jit(solution)/shard_map/ppermute | solution.py:266
  284.6 1.2 collective-permute-start.19
  285.8 3.8 collective-permute-start.20
  289.6 20.7 %collective-permute-start.21 = (f32[24,128]{1,0:T(8,128)S(1)}, f32[24,128]{1,0:T(8,128)S(1)}, u32[]{:S(2)}, u32[]{:S(2)}) collective-permute-start(f32[24,128]{1,0:T(8,128)S(1)} %add.718), channel_id=1, source_target_pairs={{0,4},{1,5},{2,6},{3,7},{4,0},{5,1},{6,2},{7,3},{8,12},{9,13},{10,... | collective-permute-start | bytes 36872 | tf_op jit(solution)/shard_map/ppermute | solution.py:256
  310.3 16.3 %collective-permute-start.22 = (f32[384,768]{1,0:T(8,128)S(1)}, f32[384,768]{1,0:T(8,128)}, u32[]{:S(2)}, u32[]{:S(2)}) collective-permute-start(f32[384,768]{1,0:T(8,128)S(1)} %copy-done.12), channel_id=1, source_target_pairs={{0,2},{1,17},{2,0},{3,19},{4,6},{5,21},{6,4},{7,23},{8,10},{9,25},... | collective-permute-start | bytes 3538952 | tf_op jit(solution)/shard_map/ppermute | solution.py:266
  331.9 43.5 %collective-permute-start.27 = (f32[768,768]{1,0:T(8,128)S(1)}, f32[768,768]{1,0:T(8,128)}, u32[]{:S(2)}, u32[]{:S(2)}) collective-permute-start(f32[768,768]{1,0:T(8,128)S(1)} %copy-done.6), channel_id=1, source_target_pairs={{0,16},{1,3},{2,18},{3,1},{4,20},{5,7},{6,22},{7,5},{8,24},{9,11},... | collective-permute-start | bytes 7077896 | tf_op jit(solution)/shard_map/ppermute | solution.py:266
  332.6 40.0 %collective-permute-start.31 = (f32[96,2304]{1,0:T(8,128)}, f32[96,2304]{1,0:T(8,128)}, u32[]{:S(2)}, u32[]{:S(2)}) collective-permute-start(f32[96,2304]{1,0:T(8,128)} %dynamic-slice_add_fusion.5), channel_id=1, source_target_pairs={{0,2},{1,17},{2,0},{3,19},{4,6},{5,21},{6,4},{7,23},{8,10},{9,25},... | collective-permute-start | bytes 2654216 | tf_op jit(solution)/shard_map/ppermute | solution.py:266
  333.8 16.7 %collective-permute-start.28 = (f32[24,4608]{1,0:T(8,128)S(1)}, f32[24,4608]{1,0:T(8,128)S(1)}, u32[]{:S(2)}, u32[]{:S(2)}) collective-permute-start(f32[24,4608]{1,0:T(8,128)S(1)} %copy-done.16), channel_id=1, source_target_pairs={{0,4},{1,5},{2,6},{3,7},{4,0},{5,1},{6,2},{7,3},{8,12},{9,13},{10,... | collective-permute-start | bytes 1327112 | tf_op jit(solution)/shard_map/ppermute | solution.py:266
  336.3 32.7 %collective-permute-start.29 = (f32[24,4608]{1,0:T(8,128)S(1)}, f32[24,4608]{1,0:T(8,128)}, u32[]{:S(2)}, u32[]{:S(2)}) collective-permute-start(f32[24,4608]{1,0:T(8,128)S(1)} %copy-done.16), channel_id=1, source_target_pairs={{0,8},{1,9},{2,10},{3,11},{4,12},{5,13},{6,14},{7,15},{8,0},{9,1},... | collective-permute-start | bytes 1327112 | tf_op jit(solution)/shard_map/ppermute | solution.py:266
  337.2 31.9 %collective-permute-start.30 = (f32[24,4608]{1,0:T(8,128)S(1)}, f32[24,4608]{1,0:T(8,128)}, u32[]{:S(2)}, u32[]{:S(2)}) collective-permute-start(f32[24,4608]{1,0:T(8,128)S(1)} %copy-done.16), channel_id=1, source_target_pairs={{0,12},{1,13},{2,14},{3,15},{4,8},{5,9},{6,10},{7,11},{8,4},{9,5},... | collective-permute-start | bytes 1327112 | tf_op jit(solution)/shard_map/ppermute | solution.py:266
  350.5 18.5 %copy-start.23 = (f32[24,4608]{1,0:T(8,128)}, f32[24,4608]{1,0:T(8,128)S(1)}, u32[]{:S(2)}) copy-start(f32[24,4608]{1,0:T(8,128)S(1)} %collective-permute-done.28.refs_0_) | copy-start | bytes 1327108
  378.4 26.6 %collective-permute-start.32 = (f32[96,4608]{1,0:T(8,128)S(1)}, f32[96,4608]{1,0:T(8,128)}, u32[]{:S(2)}, u32[]{:S(2)}) collective-permute-start(f32[96,4608]{1,0:T(8,128)S(1)} %copy-done.7), channel_id=1, source_target_pairs={{0,2},{1,17},{2,0},{3,19},{4,6},{5,21},{6,4},{7,23},{8,10},{9,25},... | collective-permute-start | bytes 5308424 | tf_op jit(solution)/shard_map/ppermute | solution.py:266
  379.2 80.1 %collective-permute-start.37 = (f32[1536,768]{1,0:T(8,128)}, f32[1536,768]{1,0:T(8,128)}, u32[]{:S(2)}, u32[]{:S(2)}) collective-permute-start(f32[1536,768]{1,0:T(8,128)} %put.29.refs_0_), channel_id=1, source_target_pairs={{0,1},{1,0},{2,3},{3,2},{4,5},{5,4},{6,7},{7,6},{8,9},{9,8},{10,11... | collective-permute-start | bytes 14155784 | tf_op jit(solution)/shard_map/ppermute | solution.py:266
  379.2 16.1 %collective-permute-start.33 = (f32[24,2304]{1,0:T(8,128)}, f32[24,2304]{1,0:T(8,128)S(1)}, u32[]{:S(2)}, u32[]{:S(2)}) collective-permute-start(f32[24,2304]{1,0:T(8,128)} %get-tuple-element.229), channel_id=1, source_target_pairs={{0,4},{1,5},{2,6},{3,7},{4,0},{5,1},{6,2},{7,3},{8,12},{9,13},{10,... | collective-permute-start | bytes 663560 | tf_op jit(solution)/shard_map/ppermute | solution.py:266
  384.9 18.7 %collective-permute-start.34 = (f32[24,2304]{1,0:T(8,128)S(1)}, f32[24,2304]{1,0:T(8,128)S(1)}, u32[]{:S(2)}, u32[]{:S(2)}) collective-permute-start(f32[24,2304]{1,0:T(8,128)S(1)} %get-tuple-element.230), channel_id=1, source_target_pairs={{0,8},{1,9},{2,10},{3,11},{4,12},{5,13},{6,14},{7,15},{8,0},{9,1},... | collective-permute-start | bytes 663560 | tf_op jit(solution)/shard_map/ppermute | solution.py:266
  385.5 18.2 %collective-permute-start.35 = (f32[24,2304]{1,0:T(8,128)S(1)}, f32[24,2304]{1,0:T(8,128)S(1)}, u32[]{:S(2)}, u32[]{:S(2)}) collective-permute-start(f32[24,2304]{1,0:T(8,128)S(1)} %get-tuple-element.231), channel_id=1, source_target_pairs={{0,12},{1,13},{2,14},{3,15},{4,8},{5,9},{6,10},{7,11},{8,4},{9,5},... | collective-permute-start | bytes 663560 | tf_op jit(solution)/shard_map/ppermute | solution.py:266
  405.0 9.0 %copy-start.22 = (f32[24,2304]{1,0:T(8,128)}, f32[24,2304]{1,0:T(8,128)S(1)}, u32[]{:S(2)}) copy-start(f32[24,2304]{1,0:T(8,128)S(1)} %add_add_fusion.3.refs_0_) | copy-start | bytes 663556
  407.6 56.8 %collective-permute-start.36 = (f32[192,4608]{1,0:T(8,128)}, f32[192,4608]{1,0:T(8,128)}, u32[]{:S(2)}, u32[]{:S(2)}) collective-permute-start(f32[192,4608]{1,0:T(8,128)} %put.33.refs_0_), channel_id=1, source_target_pairs={{0,16},{1,3},{2,18},{3,1},{4,20},{5,7},{6,22},{7,5},{8,24},{9,11},... | collective-permute-start | bytes 10616840 | tf_op jit(solution)/shard_map/ppermute | solution.py:266
  408.9 12.2 %collective-permute-start.38 = (f32[24,2304]{1,0:T(8,128)S(1)}, f32[24,2304]{1,0:T(8,128)S(1)}, u32[]{:S(2)}, u32[]{:S(2)}) collective-permute-start(f32[24,2304]{1,0:T(8,128)S(1)} %add_add_fusion.3.refs_0_), channel_id=1, source_target_pairs={{0,4},{1,5},{2,6},{3,7},{4,0},{5,1},{6,2},{7,3},{8,12},{9,13},{10,... | collective-permute-start | bytes 663560 | tf_op jit(solution)/shard_map/ppermute | solution.py:266
  413.5 18.6 %collective-permute-start.39 = (f32[24,2304]{1,0:T(8,128)S(1)}, f32[24,2304]{1,0:T(8,128)S(1)}, u32[]{:S(2)}, u32[]{:S(2)}) collective-permute-start(f32[24,2304]{1,0:T(8,128)S(1)} %add_add_fusion.3.refs_0_), channel_id=1, source_target_pairs={{0,8},{1,9},{2,10},{3,11},{4,12},{5,13},{6,14},{7,15},{8,0},{9,1},... | collective-permute-start | bytes 663560 | tf_op jit(solution)/shard_map/ppermute | solution.py:266
  414.0 18.0 %collective-permute-start.40 = (f32[24,2304]{1,0:T(8,128)S(1)}, f32[24,2304]{1,0:T(8,128)S(1)}, u32[]{:S(2)}, u32[]{:S(2)}) collective-permute-start(f32[24,2304]{1,0:T(8,128)S(1)} %add_add_fusion.3.refs_0_), channel_id=1, source_target_pairs={{0,12},{1,13},{2,14},{3,15},{4,8},{5,9},{6,10},{7,11},{8,4},{9,5},... | collective-permute-start | bytes 663560 | tf_op jit(solution)/shard_map/ppermute | solution.py:266
  421.1 10.9 %copy-start.28 = (f32[24,2304]{1,0:T(8,128)}, f32[24,2304]{1,0:T(8,128)S(1)}, u32[]{:S(2)}) copy-start(f32[24,2304]{1,0:T(8,128)S(1)} %collective-permute-done.38.refs_0_) | copy-start | bytes 663556
  436.6 19.6 %collective-permute-start.41 = (f32[96,2304]{1,0:T(8,128)}, f32[96,2304]{1,0:T(8,128)S(1)}, u32[]{:S(2)}, u32[]{:S(2)}) collective-permute-start(f32[96,2304]{1,0:T(8,128)} %put.39.refs_0_), channel_id=1, source_target_pairs={{0,2},{1,17},{2,0},{3,19},{4,6},{5,21},{6,4},{7,23},{8,10},{9,25},... | collective-permute-start | bytes 2654216 | tf_op jit(solution)/shard_map/ppermute | solution.py:266
  468.9 12.0 %collective-permute-start.42 = (f32[384,4608]{1,0:T(8,128)}, f32[384,4608]{1,0:T(8,128)}, u32[]{:S(2)}, u32[]{:S(2)}) collective-permute-start(f32[384,4608]{1,0:T(8,128)} %put.37.refs_0_), channel_id=1, source_target_pairs={{0,1},{1,0},{2,3},{3,2},{4,5},{5,4},{6,7},{7,6},{8,9},{9,8},{10,11... | collective-permute-start | bytes 21233672 | tf_op jit(solution)/shard_map/ppermute | solution.py:266
  468.9 22.6 %collective-permute-start.43 = (f32[192,2304]{1,0:T(8,128)S(1)}, f32[192,2304]{1,0:T(8,128)}, u32[]{:S(2)}, u32[]{:S(2)}) collective-permute-start(f32[192,2304]{1,0:T(8,128)S(1)} %copy-done.8), channel_id=1, source_target_pairs={{0,16},{1,3},{2,18},{3,1},{4,20},{5,7},{6,22},{7,5},{8,24},{9,11},... | collective-permute-start | bytes 5308424 | tf_op jit(solution)/shard_map/ppermute | solution.py:266
  489.1 13.3 %copy-start.15 = (f32[16,768]{1,0:T(8,128)S(1)}, f32[16,768]{1,0:T(8,128)}, u32[]{:S(2)}) copy-start(f32[16,768]{1,0:T(8,128)} %copy-done.14) | copy-start | bytes 147460
  494.0 17.1 %collective-permute-start.44 = (f32[384,2304]{1,0:T(8,128)}, f32[384,2304]{1,0:T(8,128)}, u32[]{:S(2)}, u32[]{:S(2)}) collective-permute-start(f32[384,2304]{1,0:T(8,128)} %put.45.refs_0_), channel_id=1, source_target_pairs={{0,1},{1,0},{2,3},{3,2},{4,5},{5,4},{6,7},{7,6},{8,9},{9,8},{10,11... | collective-permute-start | bytes 10616840 | tf_op jit(solution)/shard_map/ppermute | solution.py:266
  494.0 7.7 %collective-permute-start.45 = (f32[24,128]{1,0:T(8,128)S(1)}, f32[24,128]{1,0:T(8,128)S(1)}, u32[]{:S(2)}, u32[]{:S(2)}) collective-permute-start(f32[24,128]{1,0:T(8,128)S(1)} %add.719), channel_id=1, source_target_pairs={{0,8},{1,9},{2,10},{3,11},{4,12},{5,13},{6,14},{7,15},{8,0},{9,1},... | collective-permute-start | bytes 36872 | tf_op jit(solution)/shard_map/ppermute | solution.py:256
  501.7 3.7 collective-permute-start.46
  (27 other events, 78.8 us)

commit v5 on v4

--- a/solution.py
+++ b/solution.py
@@ -12,6 +12,7 @@
 AXES = ("tower", "dp")
 LANES = 128
 TILE = 256
+BIAS_AT = 32
 
 
 def bucket_code(offset, bucket_count):
@@ -233,6 +234,32 @@
     )(query, key, value, grad, segment.reshape(-1, 1), segment[:, None, :], rows, *before)
 
 
+def pack_small(gains, grad_rows, code):
+    width = gains[0].shape[1]
+    heads = grad_rows.shape[0]
+    buckets = code.shape[0]
+
+    def kernel(*refs):
+        *gain_refs, rows_ref, code_ref, out_ref = refs
+        line = lax.broadcasted_iota(jnp.int32, (LANES, width), 0)
+        value = jnp.zeros((LANES, width), jnp.float32)
+        for n, ref in enumerate(gain_refs):
+            value = jnp.where(line == n, ref[...], value)
+        out_ref[...] = value.T
+        lane = lax.broadcasted_iota(jnp.int32, (buckets, LANES), 1)
+        value = out_ref[:buckets, :]
+        for h in range(heads):
+            part = jnp.sum(code_ref[...] * rows_ref[h], axis=1, keepdims=True)
+            value = jnp.where(lane == BIAS_AT + h, part, value)
+        out_ref[:buckets, :] = value
+
+    return pl.pallas_call(
+        kernel,
+        name="pack_small",
+        out_shape=jax.ShapeDtypeStruct((width, LANES), jnp.float32),
+    )(*gains, grad_rows, code)
+
+
 class Net:
     def __init__(self):
         self.dp = lax.axis_size("dp")
@@ -284,7 +311,7 @@
     return lax.dynamic_slice_in_dim(value, which * rows, rows, 0)
 
 
-def weight_grads(bit, lefts, rights):
+def weight_grads(bit, lefts, rights, extra=()):
     height = lefts[0].shape[1] // 2
     width = min(r.shape[1] for r in rights)
     rows = max(r for r in range(LANES, min(height, 512) + 1, LANES) if height % r == 0)
@@ -293,13 +320,16 @@
     starts = [end - r.shape[1] // width for end, r in zip(ends, rights)]
     columns = ends[-1]
     count = len(lefts)
+    narrow = len(extra)
+    total = columns * width + sum(v.shape[1] for v in extra)
     fresh = [n == 0 or lefts[n] is not lefts[n - 1] for n in range(count)]
     owners = [max(m for m in range(n + 1) if fresh[m]) for n in range(count)]
 
     def kernel(bit_ref, *refs):
         other_refs, own_refs, right_refs = (refs[n * count : (n + 1) * count] for n in range(3))
-        sent_ref, kept_ref = refs[3 * count : 3 * count + 2]
-        turned_refs = refs[3 * count + 2 :]
+        extra_refs, refs = refs[3 * count : 3 * count + 2 * narrow], refs[3 * count + 2 * narrow :]
+        sent_ref, kept_ref = refs[:2]
+        turned_refs = refs[2:]
         column = pl.program_id(1)
 
         def one(n):
@@ -317,12 +347,25 @@
         for n in range(count):
             pl.when((column >= starts[n]) & (column < ends[n]))(lambda n=n: one(n))
 
-    def left_place(side):
+        if narrow:
+
+            @pl.when(column == columns)
+            def _():
+                sent_ref[:, : extra[0].shape[1]] = extra_refs[0][...]
+                kept_ref[:, : extra[0].shape[1]] = extra_refs[1][...]
+
+    def row_place(side):
         def index(stack, column, bit_ref):
             half = jnp.where(side == 0, 1 - bit_ref[0], bit_ref[0])
-            return (0, half * stacks + stack)
+            return half * stacks + stack
 
         return index
+
+    def left_place(side):
+        return lambda *at: (0, row_place(side)(*at))
+
+    def extra_place(side):
+        return lambda *at: (row_place(side)(*at), 0)
 
     def right_place(start, end):
         return lambda stack, column, bit_ref: (0, jnp.clip(column - start, 0, end - start - 1))
@@ -332,20 +375,23 @@
         name="weight_grads",
         grid_spec=pltpu.PrefetchScalarGridSpec(
             num_scalar_prefetch=1,
-            grid=(stacks, columns),
+            grid=(stacks, columns + narrow),
             in_specs=[
                 pl.BlockSpec((v.shape[0], rows), left_place(side)) for side in (0, 1) for v in lefts
             ]
             + [
                 pl.BlockSpec((v.shape[0], width), right_place(start, end))
                 for v, start, end in zip(rights, starts, ends)
+            ]
+            + [
+                pl.BlockSpec((rows, v.shape[1]), extra_place(side)) for side in (0, 1) for v in extra
             ],
             out_specs=[pl.BlockSpec((rows, width), lambda stack, column, bit_ref: (stack, column))]
             * 2,
             scratch_shapes=[pltpu.VMEM((2 * rows, v.shape[0]), v.dtype) for v in lefts],
         ),
-        out_shape=[jax.ShapeDtypeStruct((height, columns * width), jnp.float32)] * 2,
-    )(bit.reshape(1), *lefts, *lefts, *rights)
+        out_shape=[jax.ShapeDtypeStruct((height, total), jnp.float32)] * 2,
+    )(bit.reshape(1), *lefts, *lefts, *rights, *extra, *extra)
 
 
 def row_tiles(rows):
@@ -491,13 +537,13 @@
 
 
 class Sum:
-    def __init__(self, net, lefts, rights):
+    def __init__(self, net, lefts, rights, extra=()):
         self.net = net
-        self.widths = [r.shape[1] for r in rights]
+        self.widths = [v.shape[1] for v in (*rights, *extra)]
         self.step = 0
         self.back = False
         self.done = False
-        sent, kept = weight_grads(net.digits[0], lefts, rights)
+        sent, kept = weight_grads(net.digits[0], lefts, rights, extra)
         self.held = [[sent], [kept]]
         self.cuts = [[]]
 
@@ -511,7 +557,7 @@
         (piece,) = self.held
         k = self.step - 1
         self.got = [net.send(piece, k, r) for r in net.peers(k)]
-        self.whole = piece.shape[0] % 8 == 0
+        self.whole = piece.shape[0] % 8 == 0 and len(self.got) == 1
         if self.whole:
             widths = [piece.shape[1]] if k else self.widths
             self.base = put([piece], [net.digits[k]], len(self.got) + 1, widths)
@@ -719,7 +765,6 @@
     second.go()
     grads = attention_part(2, query_low, grads)
     *grad_heads, grad_rows = grads
-    third = Sum(net, [normed_low] * 3, grad_heads)
     grad_states, grad_gain_attn = project_backward(
         grad_heads,
         grad_hidden,
@@ -727,39 +772,29 @@
         gain_attn,
         (w_query, w_key, w_value),
     )
+    small = pack_small(
+        (grad_gain_attn, grad_gain_ffn, grad_gain_final[None]), grad_rows, code_back.T
+    )
+    third = Sum(net, [normed_low] * 3, grad_heads, [small])
     first.end()
     second.end()
-    grad_bias = jnp.einsum("hx,xb->bh", grad_rows[:, 0], code_back, precision=highest)
-    small = jnp.concatenate(
-        [grad_gain_attn[0], grad_gain_ffn[0], grad_gain_final, grad_bias.reshape(-1)]
-    )
-    lines = -(-small.shape[0] // (8 * LANES)) * 8
-    small = jnp.pad(small, (0, lines * LANES - small.shape[0])).reshape(lines, LANES)
     sums = [first, second, third]
-    small, grad_states = tie_all(sums, small, grad_states)
-    def swap_small(value, which):
-        for b in which:
-            value = value + net.swap(value, b)
-        return value
-
+    (grad_states,) = tie_all(sums, grad_states)
     if bits == 5:
-        advance(sums)
-        (small,) = tie_all(sums, small)
-        advance(sums)
-        small = swap_small(small, (0, 1, 2))
-        (small,) = tie_all(sums, small)
-        advance(sums)
-        small = swap_small(small, (3, 4))
+        for _ in range(3):
+            advance(sums)
+            tie_all(sums)
+        for s in sums:
+            s.go()
+        first.end()
+        first.held, second.base = tie(first.held, second.base)
+        second.end()
+        third.end()
         tie_all(sums)
-        first.go()
-        advance([second, third])
-        tie_all([second, third])
         second.go()
         third.go()
-        first.end()
         third.end()
         third.go()
-        first.held, second.base = tie(first.held, second.base)
         second.end()
         third.end()
         tie_all([second, third])
@@ -773,11 +808,9 @@
     else:
         while not all(s.done for s in sums):
             advance([s for s in sums if not s.done])
-        small = swap_small(small, range(bits))
     (whole_ffout,) = first.held
     whole_in, whole_out, whole_proj = second.held
-    whole_query, whole_key, whole_value = third.held
-    small = small.reshape(-1)
+    whole_query, whole_key, whole_value, small = third.held
     loss = loss_sum / (micro_count * row_count)
     width = model_width
     return (
@@ -791,12 +824,10 @@
         whole_in,
         whole_ffout,
         whole_proj,
-        small[:width],
-        small[width : 2 * width],
-        small[2 * width : 3 * width],
-        small[3 * width : 3 * width + bucket_count * head_count].reshape(
-            bucket_count, head_count
-        ),
+        small[:, 0],
+        small[:, 1],
+        small[:, 2],
+        small[:bucket_count, BIAS_AT : BIAS_AT + head_count],
     )
 
 

time: 526 us -> 510 us (0.970)
  the two profiles are of different devices: /device:TPU:0 before, /device:TPU:9 now
where the time goes in v5:
time: 510 us; the launch traced here: 501 us
  Pallas kernels  206 us (40%)
  waiting for transfers between devices  147 us (29%)
  other arithmetic  51.1 us (10%)
  starting transfers between devices  44 us (9%)
  matrix products  32.1 us (6%)
  local copies, waits for them, and re-layouts  16.9 us (3%)
    ppermute x42, waiting for transfers between devices, send_by(): lax.ppermute(value, AXES, [(i, i ^ masks[i & 1]) for i in range(self.size)])  147 us
    pallas_call x18, Pallas kernels, put(): pl.pallas_call(kernel, name='put', grid_spec=pltpu.PrefetchScalarGridSpec...  69 us
    pallas_call x3, Pallas kernels, attention_grads(): pl.pallas_call(kernel, name='attention_backward', grid=(count, micro_coun...  44.8 us
    ppermute x42, starting transfers between devices, send_by(): lax.ppermute(value, AXES, [(i, i ^ masks[i & 1]) for i in range(self.size)])  44 us
    pallas_call x3, Pallas kernels, weight_grads(): pl.pallas_call(kernel, name='weight_grads', grid_spec=pltpu.PrefetchScala...  34.7 us
    add x12, other arithmetic, total(): value = term if value is None else value + term  34.7 us
    dot_general x7, matrix products, mm(): return jnp.dot(a, b, preferred_element_type=jnp.float32)  26.5 us
    pallas_call x1, Pallas kernels, attention(): pl.pallas_call(lambda *refs: forward_kernel(head_dim, *refs), name='atten...  23 us
  transfers between devices with their start and end apart: 42, of which 21 were waited for; matrix products, arithmetic and copies ran while one was open for 5% of the time, Pallas kernels for 31%

profile of v5, /device:TPU:9, one launch (start us, length us, event | category | flops | bytes accessed | tf_op | source)
XLA Modules:
  0.0 501.3 jit_solution(13189865981114598641)
XLA Ops:
  3.8 2.5 convolution_convert_fusion.refs_2_
  6.4 2.5 convolution_convert_fusion.1.refs_1_
  8.9 2.5 convolution_convert_fusion.2.refs_0_
  14.2 23.0 %attention_forward.1.refs_1_.refs_4_ = bf16[1024,768]{1,0:T(8,128)(2,1)} custom-call(bf16[1024,768]{1,0:T(8,128)(2,1)} %convolution_convert_fusion.2.refs_0_, bf16[1024,768]{1,0:T(8,128)(2,1)} %convolution_convert_fusion.1.refs_1_, bf16[1024,768]{1,0:T(8,128)(2,1)} %convolution_convert_fusion.refs_2_, s32[1024,1]{1,0:T(8,128)} %bitcast.196, ...), custom_call_target="tpu_custom_call" | custom-call | tf_op jit(solution)/shard_map/attention_forward/pallas_call | solution.py:199
  37.3 3.3 multiply_reduce_fusion.2
  40.9 10.0 %maximum_convert_fusion.refs_0_.refs_1_.act_ref = bf16[1024,3072]{1,0:T(8,128)(2,1)S(1)} fusion(bf16[1024,768]{1,0:T(8,128)(2,1)S(1)} %multiply_convert_fusion.refs_0_.refs_3_, bf16[768,3072]{1,0:T(8,128)(2,1)} %win_ref.1), kind=kOutput, calls=%fused_computation | convolution fusion | flops 4838129664 | bytes 12582912 | tf_op jit(solution)/shard_map/dot_general | solution.py:47
  51.0 5.2 %multiply_reduce_fusion.1 = (f32[1024]{0:T(1024)S(1)}, f32[1024,768]{1,0:T(8,128)S(1)}) fusion(f32[1024,768]{1,0:T(8,128)S(1)} %get-tuple-element.315.hid_ref, bf16[1024,3072]{1,0:T(8,128)(2,1)S(1)} %maximum_convert_fusion.refs_0_.refs_1_.act_ref, bf16[3072,768]{1,0:T(8,128)(2,1)S(1)} %bitcast.205), kind=kOutput, calls=%fused_computation.11 | convolution fusion | flops 4834196480 | bytes 17305600 | tf_op jit(solution)/shard_map/dot_general | solution.py:47
  68.5 3.5 collective-permute-done.3
  73.5 5.6 %collective-permute-done.4 = f32[128,768]{1,0:T(8,128)S(1)} collective-permute-done((f32[128,768]{1,0:T(8,128)S(1)}, f32[128,768]{1,0:T(8,128)S(1)}, u32[]{:S(2)}, u32[]{:S(2)}) %collective-permute-start.4) | collective-permute-done | bytes 393248 | tf_op jit(solution)/shard_map/ppermute | solution.py:293
  79.2 3.3 collective-permute-start.5
  91.6 2.9 fusion.59
  94.5 10.0 %weight_grads.3 = (f32[1536,768]{1,0:T(8,128)}, f32[1536,768]{1,0:T(8,128)}) custom-call(s32[1]{0:T(128)} %bitcast.43.bit_ref.places_ref, bf16[1024,3072]{1,0:T(8,128)(2,1)} %copy-done.3, bf16[1024,3072]{1,0:T(8,128)(2,1)} %copy-done.3, bf16[1024,768]{1,0:T(8,128)(2,1)} %get-tuple-element.297.refs_2_), custom_call_target="tpu_custom_call" | custom-call | tf_op jit(solution)/shard_map/weight_grads/pallas_call | solution.py:373
  105.4 22.2 %feed_backward.1 = (bf16[1024,3072]{1,0:T(8,128)(2,1)}, f32[1024,768]{1,0:T(8,128)}, bf16[1024,768]{1,0:T(8,128)(2,1)}, bf16[1024,768]{1,0:T(8,128)(2,1)}, f32[1,768]{1,0:T(1,128)}) custom-call(f32[1024,768]{1,0:T(8,128)} %get-tuple-element.139.go_ref, bf16[1024,3072]{1,0:T(8,128)(2,1)} %copy-done.3, f32[1024,768]{1,0:T(8,128)} %copy-done.10, ...), custom_call_target="tpu_custom_call" | custom-call | tf_op jit(solution)/shard_map/feed_backward/pallas_call | solution.py:470
  127.7 2.7 dynamic-slice_add_fusion.1
  132.8 14.1 %weight_grads.4 = (f32[384,4608]{1,0:T(8,128)}, f32[384,4608]{1,0:T(8,128)}) custom-call(s32[1]{0:T(128)} %bitcast.43.bit_ref.places_ref, bf16[1024,768]{1,0:T(8,128)(2,1)} %copy-done.9, bf16[1024,768]{1,0:T(8,128)(2,1)} %attention_forward.1.refs_1_.refs_4_, bf16[16,768]{1,0:T(8,128)(2,1)} %copy-done.22, bf16[1024,768]{1,0:T(8,128)(2,1)} %copy-done.9, ...), custom_call_target="tpu_custom_call" | custom-call | tf_op jit(solution)/shard_map/weight_grads/pallas_call | solution.py:373
  147.0 15.0 %attention_backward.3 = (bf16[1024,768]{1,0:T(8,128)(2,1)}, bf16[1024,768]{1,0:T(8,128)(2,1)}, bf16[1024,768]{1,0:T(8,128)(2,1)}, f32[12,1,1024]{2,1,0:T(1,128)}) custom-call(bf16[1024,768]{1,0:T(8,128)(2,1)} %convolution_convert_fusion.2.refs_0_, bf16[1024,768]{1,0:T(8,128)(2,1)} %convolution_convert_fusion.1.refs_1_, ...), custom_call_target="tpu_custom_call" | custom-call | tf_op jit(solution)/shard_map/attention_backward/pallas_call | solution.py:224
  162.0 2.2 dynamic-slice_add_fusion.4
  165.6 14.9 %attention_backward.4 = (bf16[1024,768]{1,0:T(8,128)(2,1)}, bf16[1024,768]{1,0:T(8,128)(2,1)}, bf16[1024,768]{1,0:T(8,128)(2,1)}, f32[12,1,1024]{2,1,0:T(1,128)}) custom-call(bf16[1024,768]{1,0:T(8,128)(2,1)} %convolution_convert_fusion.2.refs_0_, ...), custom_call_target="tpu_custom_call", output_to_operand_aliasing={{0}: (7, {}), {1}: (8, {}), {2}: (9, {}), {3}: (10, {})} | custom-call | tf_op jit(solution)/shard_map/attention_backward/pallas_call | solution.py:224
  182.5 5.3 %dynamic-slice_add_fusion = f32[192,4608]{1,0:T(8,128)} fusion(f32[384,4608]{1,0:T(8,128)} %collective-permute-done.9, s32[]{:T(128)S(6)} %select_n.442, f32[384,4608]{1,0:T(8,128)} %get-tuple-element.206), kind=kLoop, calls=%fused_computation.4 | loop fusion | flops 884736 | bytes 10616836 | tf_op jit(solution)/shard_map/add | solution.py:595
  193.6 14.9 %attention_backward.5 = (bf16[1024,768]{1,0:T(8,128)(2,1)}, bf16[1024,768]{1,0:T(8,128)(2,1)}, bf16[1024,768]{1,0:T(8,128)(2,1)}, f32[12,1,1024]{2,1,0:T(1,128)}) custom-call(bf16[1024,768]{1,0:T(8,128)(2,1)} %convolution_convert_fusion.2.refs_0_, ...), custom_call_target="tpu_custom_call", output_to_operand_aliasing={{0}: (7, {}), {1}: (8, {}), {2}: (9, {}), {3}: (10, {})} | custom-call | tf_op jit(solution)/shard_map/attention_backward/pallas_call | solution.py:224
  208.5 10.2 %project_backward.1 = (f32[1024,768]{1,0:T(8,128)}, f32[1,768]{1,0:T(1,128)}) custom-call(bf16[1024,768]{1,0:T(8,128)(2,1)} %get-tuple-element.177.gq_ref.refs_6_, bf16[1024,768]{1,0:T(8,128)(2,1)} %get-tuple-element.178.gk_ref.refs_7_, bf16[1024,768]{1,0:T(8,128)(2,1)} %get-tuple-element.179.gv_ref.refs_8_, f32[1024,768]{1,0:T(8,128)} %get-tuple-element.180.gh_ref, ...), custom_call_target="tpu_custom_call" | custom-call | tf_op jit(solution)/shard_map/project_backward/pallas_call | solution.py:437
  220.6 10.6 %weight_grads.5 = (f32[384,2432]{1,0:T(8,128)}, f32[384,2432]{1,0:T(8,128)}) custom-call(s32[1]{0:T(128)} %bitcast.43.bit_ref.places_ref, bf16[1024,768]{1,0:T(8,128)(2,1)} %copy-done.2, bf16[1024,768]{1,0:T(8,128)(2,1)} %copy-done.2, bf16[1024,768]{1,0:T(8,128)(2,1)} %copy-done.2, bf16[1024,768]{1,0:T(8,128)(2,1)} %copy-done.2, ...), custom_call_target="tpu_custom_call" | custom-call | tf_op jit(solution)/shard_map/weight_grads/pallas_call | solution.py:373
  232.6 4.2 dynamic-slice_add_fusion.3
  240.6 2.2 collective-permute-start.15
  244.8 15.6 %collective-permute-done.14 = f32[96,768]{1,0:T(8,128)S(1)} collective-permute-done((f32[96,768]{1,0:T(8,128)S(1)}, f32[96,768]{1,0:T(8,128)S(1)}, u32[]{:S(2)}, u32[]{:S(2)}) %collective-permute-start.14) | collective-permute-done | bytes 294944 | tf_op jit(solution)/shard_map/ppermute | solution.py:293
  260.4 5.2 %collective-permute-done.15 = f32[96,768]{1,0:T(8,128)S(1)} collective-permute-done((f32[96,768]{1,0:T(8,128)S(1)}, f32[96,768]{1,0:T(8,128)S(1)}, u32[]{:S(2)}, u32[]{:S(2)}) %collective-permute-start.15) | collective-permute-done | bytes 294944 | tf_op jit(solution)/shard_map/ppermute | solution.py:293
  267.7 4.4 dynamic-slice_add_fusion.6
  272.1 2.9 dynamic-slice_add_fusion.2
  276.2 2.2 collective-permute-start.20
  280.2 2.4 put.18.refs_1_
  282.5 13.6 %collective-permute-done.20 = f32[24,4608]{1,0:T(8,128)} collective-permute-done((f32[24,4608]{1,0:T(8,128)}, f32[24,4608]{1,0:T(8,128)}, u32[]{:S(2)}, u32[]{:S(2)}) %collective-permute-start.20) | collective-permute-done | bytes 442400 | tf_op jit(solution)/shard_map/ppermute | solution.py:293
  296.2 2.1 collective-permute-done.21
  298.3 19.0 %collective-permute-done.22 = f32[24,4608]{1,0:T(8,128)} collective-permute-done((f32[24,4608]{1,0:T(8,128)S(1)}, f32[24,4608]{1,0:T(8,128)}, u32[]{:S(2)}, u32[]{:S(2)}) %collective-permute-start.22) | collective-permute-done | bytes 442400 | tf_op jit(solution)/shard_map/ppermute | solution.py:293
  317.3 2.8 add_add_fusion.1
  320.1 2.4 put.19.refs_0_
  322.4 3.1 dynamic-slice_add_fusion.5
  330.2 2.8 put.20.refs_1_
  332.9 17.9 %collective-permute-done.25 = f32[24,4608]{1,0:T(8,128)S(1)} collective-permute-done((f32[24,4608]{1,0:T(8,128)S(1)}, f32[24,4608]{1,0:T(8,128)S(1)}, u32[]{:S(2)}, u32[]{:S(2)}) %collective-permute-start.25) | collective-permute-done | bytes 442400 | tf_op jit(solution)/shard_map/ppermute | solution.py:293
  350.8 8.2 %collective-permute-done.26 = f32[24,4608]{1,0:T(8,128)} collective-permute-done((f32[24,4608]{1,0:T(8,128)S(1)}, f32[24,4608]{1,0:T(8,128)}, u32[]{:S(2)}, u32[]{:S(2)}) %collective-permute-start.26) | collective-permute-done | bytes 442400 | tf_op jit(solution)/shard_map/ppermute | solution.py:293
  359.0 2.8 fusion.4.refs_0_
  361.9 2.3 dynamic-slice_add_fusion.12
  364.2 2.9 put.21.refs_0_
  371.6 5.0 %put.22.refs_1_ = f32[3072,768]{1,0:T(8,128)} custom-call(s32[1]{0:T(128)} %bitcast.43.bit_ref.places_ref, f32[1536,768]{1,0:T(8,128)} %put.21.refs_0_), custom_call_target="tpu_custom_call" | custom-call | tf_op jit(solution)/shard_map/put/pallas_call | solution.py:520
  376.7 2.5 put.24.refs_1_
  379.9 6.1 %collective-permute-done.32 = f32[24,2432]{1,0:T(8,128)S(1)} collective-permute-done((f32[24,2432]{1,0:T(8,128)S(1)}, f32[24,2432]{1,0:T(8,128)S(1)}, u32[]{:S(2)}, u32[]{:S(2)}) %collective-permute-start.32) | collective-permute-done | bytes 233504 | tf_op jit(solution)/shard_map/ppermute | solution.py:293
  386.1 6.3 %collective-permute-done.33 = f32[24,2432]{1,0:T(8,128)S(1)} collective-permute-done((f32[24,2432]{1,0:T(8,128)S(1)}, f32[24,2432]{1,0:T(8,128)S(1)}, u32[]{:S(2)}, u32[]{:S(2)}) %collective-permute-start.33) | collective-permute-done | bytes 233504 | tf_op jit(solution)/shard_map/ppermute | solution.py:293
  393.8 5.1 %put.23 = f32[3072,768]{1,0:T(8,128)} custom-call(s32[1]{0:T(128)} %bitcast.46.places_ref, f32[1536,768]{1,0:T(8,128)} %collective-permute-done.29.refs_0_, f32[3072,768]{1,0:T(8,128)} %put.22.refs_1_), custom_call_target="tpu_custom_call", output_to_operand_aliasing={{}: (2, {})} | custom-call | tf_op jit(solution)/shard_map/put/pallas_call | solution.py:520
  398.8 2.4 put.25.refs_0_
  404.8 12.0 %collective-permute-done.35 = f32[24,2432]{1,0:T(8,128)S(1)} collective-permute-done((f32[24,2432]{1,0:T(8,128)S(1)}, f32[24,2432]{1,0:T(8,128)S(1)}, u32[]{:S(2)}, u32[]{:S(2)}) %collective-permute-start.35) | collective-permute-done | bytes 233504 | tf_op jit(solution)/shard_map/ppermute | solution.py:293
  416.8 3.9 collective-permute-done.36
  421.5 4.4 put.26.refs_1_
  425.9 2.2 put.28.refs_1_
  428.1 16.0 %collective-permute-done.38.refs_0_ = f32[96,2432]{1,0:T(8,128)S(1)} collective-permute-done((f32[96,2432]{1,0:T(8,128)S(1)}, f32[96,2432]{1,0:T(8,128)S(1)}, u32[]{:S(2)}, u32[]{:S(2)}) %collective-permute-start.38) | collective-permute-done | bytes 933920 | tf_op jit(solution)/shard_map/ppermute | solution.py:293
  445.0 2.2 put.29.refs_0_
  447.2 5.0 %collective-permute-done.34.refs_0_ = f32[192,4608]{1,0:T(8,128)} collective-permute-done((f32[192,4608]{1,0:T(8,128)}, f32[192,4608]{1,0:T(8,128)}, u32[]{:S(2)}, u32[]{:S(2)}) %collective-permute-start.34) | collective-permute-done | bytes 3538976 | tf_op jit(solution)/shard_map/ppermute | solution.py:293
  452.2 4.4 put.27.refs_0_
  459.6 8.2 %put.30 = (f32[768,3072]{1,0:T(8,128)}, f32[768,768]{1,0:T(8,128)}, f32[768,768]{1,0:T(8,128)}) custom-call(s32[1]{0:T(128)} %bitcast.43.bit_ref.places_ref, f32[384,4608]{1,0:T(8,128)} %put.27.refs_0_), custom_call_target="tpu_custom_call" | custom-call | tf_op jit(solution)/shard_map/put/pallas_call | solution.py:520
  467.8 2.5 put.32.refs_1_
  470.3 8.2 %put.31 = (f32[768,3072]{1,0:T(8,128)}, f32[768,768]{1,0:T(8,128)}, f32[768,768]{1,0:T(8,128)}) custom-call(s32[1]{0:T(128)} %bitcast.46.places_ref, f32[384,4608]{1,0:T(8,128)} %collective-permute-done.39.refs_0_, f32[768,3072]{1,0:T(8,128)} %get-tuple-element.236.refs_1_, ...), custom_call_target="tpu_custom_call", output_to_operand_aliasing={{0}: (2, {}), {1}: (3, {}), {2}: (4, {})} | custom-call | tf_op jit(solution)/shard_map/put/pallas_call | solution.py:520
  478.5 2.8 collective-permute-done.40.refs_0_
  481.3 2.5 put.33.refs_0_
  486.6 4.5 put.34
  491.2 4.5 put.35
  496.5 2.5 slice_reduce_fusion
  (241 shorter events, 78.5 us)
Async XLA Ops:
  0.6 59.0 %copy-start = (bf16[768,768]{1,0:T(8,128)(2,1)S(1)}, bf16[768,768]{1,0:T(8,128)(2,1)}, u32[]{:S(2)}) copy-start(bf16[768,768]{1,0:T(8,128)(2,1)} %param.25) | copy-start | bytes 3538948
  3.8 5.1 %copy-start.2 = (bf16[1024,768]{1,0:T(8,128)(2,1)}, bf16[1024,768]{1,0:T(8,128)(2,1)S(1)}, u32[]{:S(2)}) copy-start(bf16[1024,768]{1,0:T(8,128)(2,1)S(1)} %fusion.1.refs_0_.refs_1_.refs_2_.refs_3_.refs_4_.refs_5_) | copy-start | bytes 4718596
  40.5 10.4 %copy-start.10 = (f32[1024,768]{1,0:T(8,128)}, f32[1024,768]{1,0:T(8,128)S(1)}, u32[]{:S(2)}) copy-start(f32[1024,768]{1,0:T(8,128)S(1)} %get-tuple-element.315.hid_ref) | copy-start | bytes 9437188
  40.6 10.4 %slice-start = ((s8[4718592]{0:T(1024)(128)(4,1)}), s8[4194304]{0:T(1024)(128)(4,1)S(1)}, s32[]{:S(2)}) async-start(s8[4718592]{0:T(1024)(128)(4,1)} %bitcast.204), calls=%async_computation | async-start | bytes 8388608
  40.9 10.0 %copy-start.9 = (bf16[1024,768]{1,0:T(8,128)(2,1)}, bf16[1024,768]{1,0:T(8,128)(2,1)S(1)}, u32[]{:S(2)}) copy-start(bf16[1024,768]{1,0:T(8,128)(2,1)S(1)} %multiply_convert_fusion.refs_0_.refs_3_) | copy-start | bytes 4718596
  40.9 10.0 %slice-start.1 = ((s8[4718592]{0:T(1024)(128)(4,1)}), s8[524288]{0:T(1024)(128)(4,1)S(1)}, s32[]{:S(2)}) async-start(s8[4718592]{0:T(1024)(128)(4,1)} %bitcast.204), calls=%async_computation.1 | async-start | bytes 1048576
  50.9 5.3 %copy-start.3 = (bf16[1024,3072]{1,0:T(8,128)(2,1)}, bf16[1024,3072]{1,0:T(8,128)(2,1)S(1)}, u32[]{:S(2)}) copy-start(bf16[1024,3072]{1,0:T(8,128)(2,1)S(1)} %maximum_convert_fusion.refs_0_.refs_1_.act_ref) | copy-start | bytes 18874372
  51.0 5.3 %copy-start.29 = (s32[1,2,8]{2,1,0:T(2,128)S(1)}, s32[1,2,8]{2,1,0:T(2,128)}, u32[]{:S(2)}) copy-start(s32[1,2,8]{2,1,0:T(2,128)} %param.17) | copy-start | bytes 196
  51.0 5.3 %copy-start.26 = (f32[768]{0:T(1024)S(1)}, f32[768]{0:T(1024)}, u32[]{:S(2)}) copy-start(f32[768]{0:T(1024)} %param.28) | copy-start | bytes 9220
  57.9 15.4 %copy-start.30 = (s32[2,128]{1,0:T(2,128)S(1)}, s32[2,128]{1,0:T(2,128)}, u32[]{:S(2)}) copy-start(s32[2,128]{1,0:T(2,128)} %param.18) | copy-start | bytes 3076
  60.0 28.1 %copy-start.15 = (f32[16,768]{1,0:T(8,128)}, f32[16,768]{1,0:T(8,128)S(1)}, u32[]{:S(2)}) copy-start(f32[16,768]{1,0:T(8,128)S(1)} %get-tuple-element.319) | copy-start | bytes 147460
  60.1 4.7 collective-permute-start
  61.4 3.9 collective-permute-start.1
  62.5 4.4 collective-permute-start.2
  63.6 19.0 %copy-start.31 = (pred[4]{0:T(512)(128)(4,1)}, pred[4]{0:T(512)(128)(4,1)S(1)}, u32[]{:S(2)}) copy-start(pred[4]{0:T(512)(128)(4,1)S(1)} %get-tuple-element.326) | copy-start | bytes 16
  63.6 19.0 %copy-start.33 = (pred[4]{0:T(512)(128)(4,1)}, pred[4]{0:T(512)(128)(4,1)S(1)}, u32[]{:S(2)}) copy-start(pred[4]{0:T(512)(128)(4,1)S(1)} %get-tuple-element.327) | copy-start | bytes 16
  67.0 4.9 collective-permute-start.3
  72.0 7.0 %collective-permute-start.4 = (f32[128,768]{1,0:T(8,128)S(1)}, f32[128,768]{1,0:T(8,128)S(1)}, u32[]{:S(2)}, u32[]{:S(2)}) collective-permute-start(f32[128,768]{1,0:T(8,128)S(1)} %bitcast_select_fusion.6), channel_id=1, source_target_pairs={{0,2},{1,17},{2,0},{3,19},{4,6},{5,21},{6,4},{7,23},{8,10},{9,25},... | collective-permute-start | bytes 1179656 | tf_op jit(solution)/shard_map/ppermute | solution.py:293
  79.2 5.2 %collective-permute-start.5 = (f32[256,768]{1,0:T(8,128)S(1)}, f32[256,768]{1,0:T(8,128)S(1)}, u32[]{:S(2)}, u32[]{:S(2)}) collective-permute-start(f32[256,768]{1,0:T(8,128)S(1)} %fusion.12), channel_id=1, source_target_pairs={{0,1},{1,0},{2,3},{3,2},{4,5},{5,4},{6,7},{7,6},{8,9},{9,8},{10,11... | collective-permute-start | bytes 2359304 | tf_op jit(solution)/shard_map/ppermute | solution.py:293
  104.5 23.2 %collective-permute-start.6 = (f32[1536,768]{1,0:T(8,128)}, f32[1536,768]{1,0:T(8,128)}, u32[]{:S(2)}, u32[]{:S(2)}) collective-permute-start(f32[1536,768]{1,0:T(8,128)} %get-tuple-element.144), channel_id=1, source_target_pairs={{0,1},{1,0},{2,3},{3,2},{4,5},{5,4},{6,7},{7,6},{8,9},{9,8},{10,11... | collective-permute-start | bytes 14155784 | tf_op jit(solution)/shard_map/ppermute | solution.py:293
  130.4 31.6 %collective-permute-start.7 = (f32[768,768]{1,0:T(8,128)S(1)}, f32[768,768]{1,0:T(8,128)}, u32[]{:S(2)}, u32[]{:S(2)}) collective-permute-start(f32[768,768]{1,0:T(8,128)S(1)} %dynamic-slice_add_fusion.1), channel_id=1, source_target_pairs={{0,16},{1,3},{2,18},{3,1},{4,20},{5,7},{6,22},{7,5},{8,24},{9,11},... | collective-permute-start | bytes 7077896 | tf_op jit(solution)/shard_map/ppermute | solution.py:293
  164.2 18.3 %collective-permute-start.9 = (f32[384,4608]{1,0:T(8,128)}, f32[384,4608]{1,0:T(8,128)}, u32[]{:S(2)}, u32[]{:S(2)}) collective-permute-start(f32[384,4608]{1,0:T(8,128)} %get-tuple-element.171), channel_id=1, source_target_pairs={{0,1},{1,0},{2,3},{3,2},{4,5},{5,4},{6,7},{7,6},{8,9},{9,8},{10,11... | collective-permute-start | bytes 21233672 | tf_op jit(solution)/shard_map/ppermute | solution.py:293
  164.7 15.8 %collective-permute-start.8 = (f32[384,768]{1,0:T(8,128)S(1)}, f32[384,768]{1,0:T(8,128)S(1)}, u32[]{:S(2)}, u32[]{:S(2)}) collective-permute-start(f32[384,768]{1,0:T(8,128)S(1)} %dynamic-slice_add_fusion.4), channel_id=1, source_target_pairs={{0,2},{1,17},{2,0},{3,19},{4,6},{5,21},{6,4},{7,23},{8,10},{9,25},... | collective-permute-start | bytes 3538952 | tf_op jit(solution)/shard_map/ppermute | solution.py:293
  182.5 9.2 %copy-start.28 = (f32[768]{0:T(1024)S(1)}, f32[768]{0:T(1024)}, u32[]{:S(2)}) copy-start(f32[768]{0:T(1024)} %param.26) | copy-start | bytes 9220
  187.9 44.7 %collective-permute-start.13 = (f32[192,4608]{1,0:T(8,128)}, f32[192,4608]{1,0:T(8,128)}, u32[]{:S(2)}, u32[]{:S(2)}) collective-permute-start(f32[192,4608]{1,0:T(8,128)} %dynamic-slice_add_fusion), channel_id=1, source_target_pairs={{0,16},{1,3},{2,18},{3,1},{4,20},{5,7},{6,22},{7,5},{8,24},{9,11},... | collective-permute-start | bytes 10616840 | tf_op jit(solution)/shard_map/ppermute | solution.py:293
  188.7 42.5 %collective-permute-start.10 = (f32[96,768]{1,0:T(8,128)S(1)}, f32[96,768]{1,0:T(8,128)S(1)}, u32[]{:S(2)}, u32[]{:S(2)}) collective-permute-start(f32[96,768]{1,0:T(8,128)S(1)} %get-tuple-element.186), channel_id=1, source_target_pairs={{0,4},{1,5},{2,6},{3,7},{4,0},{5,1},{6,2},{7,3},{8,12},{9,13},{10,... | collective-permute-start | bytes 884744 | tf_op jit(solution)/shard_map/ppermute | solution.py:293
  189.8 41.4 %collective-permute-start.11 = (f32[96,768]{1,0:T(8,128)S(1)}, f32[96,768]{1,0:T(8,128)S(1)}, u32[]{:S(2)}, u32[]{:S(2)}) collective-permute-start(f32[96,768]{1,0:T(8,128)S(1)} %get-tuple-element.187), channel_id=1, source_target_pairs={{0,8},{1,9},{2,10},{3,11},{4,12},{5,13},{6,14},{7,15},{8,0},{9,1},... | collective-permute-start | bytes 884744 | tf_op jit(solution)/shard_map/ppermute | solution.py:293
  191.8 39.5 %collective-permute-start.12 = (f32[96,768]{1,0:T(8,128)S(1)}, f32[96,768]{1,0:T(8,128)S(1)}, u32[]{:S(2)}, u32[]{:S(2)}) collective-permute-start(f32[96,768]{1,0:T(8,128)S(1)} %get-tuple-element.188), channel_id=1, source_target_pairs={{0,12},{1,13},{2,14},{3,15},{4,8},{5,9},{6,10},{7,11},{8,4},{9,5},... | collective-permute-start | bytes 884744 | tf_op jit(solution)/shard_map/ppermute | solution.py:293
  232.5 10.3 %copy-start.34 = (pred[4]{0:T(512)(128)(4,1)S(1)}, pred[4]{0:T(512)(128)(4,1)}, u32[]{:S(2)}) copy-start(pred[4]{0:T(512)(128)(4,1)} %copy-done.33) | copy-start | bytes 16
  232.5 10.9 %copy-start.32 = (pred[4]{0:T(512)(128)(4,1)S(1)}, pred[4]{0:T(512)(128)(4,1)}, u32[]{:S(2)}) copy-start(pred[4]{0:T(512)(128)(4,1)} %copy-done.31) | copy-start | bytes 16
  236.8 35.3 %collective-permute-start.18 = (f32[384,2432]{1,0:T(8,128)}, f32[384,2432]{1,0:T(8,128)}, u32[]{:S(2)}, u32[]{:S(2)}) collective-permute-start(f32[384,2432]{1,0:T(8,128)} %get-tuple-element.204), channel_id=1, source_target_pairs={{0,1},{1,0},{2,3},{3,2},{4,5},{5,4},{6,7},{7,6},{8,9},{9,8},{10,11... | collective-permute-start | bytes 11206664 | tf_op jit(solution)/shard_map/ppermute | solution.py:293
  238.6 29.2 %collective-permute-start.17 = (f32[96,4608]{1,0:T(8,128)}, f32[96,4608]{1,0:T(8,128)S(1)}, u32[]{:S(2)}, u32[]{:S(2)}) collective-permute-start(f32[96,4608]{1,0:T(8,128)} %dynamic-slice_add_fusion.3), channel_id=1, source_target_pairs={{0,2},{1,17},{2,0},{3,19},{4,6},{5,21},{6,4},{7,23},{8,10},{9,25},... | collective-permute-start | bytes 5308424 | tf_op jit(solution)/shard_map/ppermute | solution.py:293
  238.9 21.5 %collective-permute-start.14 = (f32[96,768]{1,0:T(8,128)S(1)}, f32[96,768]{1,0:T(8,128)S(1)}, u32[]{:S(2)}, u32[]{:S(2)}) collective-permute-start(f32[96,768]{1,0:T(8,128)S(1)} %add_add_fusion.2), channel_id=1, source_target_pairs={{0,12},{1,13},{2,14},{3,15},{4,8},{5,9},{6,10},{7,11},{8,4},{9,5},... | collective-permute-start | bytes 884744 | tf_op jit(solution)/shard_map/ppermute | solution.py:293
  240.6 25.0 %collective-permute-start.15 = (f32[96,768]{1,0:T(8,128)S(1)}, f32[96,768]{1,0:T(8,128)S(1)}, u32[]{:S(2)}, u32[]{:S(2)}) collective-permute-start(f32[96,768]{1,0:T(8,128)S(1)} %add_add_fusion.2), channel_id=1, source_target_pairs={{0,8},{1,9},{2,10},{3,11},{4,12},{5,13},{6,14},{7,15},{8,0},{9,1},... | collective-permute-start | bytes 884744 | tf_op jit(solution)/shard_map/ppermute | solution.py:293
  242.8 23.5 %collective-permute-start.16 = (f32[96,768]{1,0:T(8,128)S(1)}, f32[96,768]{1,0:T(8,128)}, u32[]{:S(2)}, u32[]{:S(2)}) collective-permute-start(f32[96,768]{1,0:T(8,128)S(1)} %add_add_fusion.2), channel_id=1, source_target_pairs={{0,4},{1,5},{2,6},{3,7},{4,0},{5,1},{6,2},{7,3},{8,12},{9,13},{10,... | collective-permute-start | bytes 884744 | tf_op jit(solution)/shard_map/ppermute | solution.py:293
  267.7 11.9 %copy-start.12 = (f32[384,768]{1,0:T(8,128)}, f32[384,768]{1,0:T(8,128)S(1)}, u32[]{:S(2)}) copy-start(f32[384,768]{1,0:T(8,128)S(1)} %fusion.6.refs_0_) | copy-start | bytes 3538948
  275.0 47.4 %collective-permute-start.23 = (f32[192,2432]{1,0:T(8,128)}, f32[192,2432]{1,0:T(8,128)}, u32[]{:S(2)}, u32[]{:S(2)}) collective-permute-start(f32[192,2432]{1,0:T(8,128)} %dynamic-slice_add_fusion.2), channel_id=1, source_target_pairs={{0,16},{1,3},{2,18},{3,1},{4,20},{5,7},{6,22},{7,5},{8,24},{9,11},... | collective-permute-start | bytes 5603336 | tf_op jit(solution)/shard_map/ppermute | solution.py:293
  276.2 19.9 %collective-permute-start.20 = (f32[24,4608]{1,0:T(8,128)}, f32[24,4608]{1,0:T(8,128)}, u32[]{:S(2)}, u32[]{:S(2)}) collective-permute-start(f32[24,4608]{1,0:T(8,128)} %get-tuple-element.210), channel_id=1, source_target_pairs={{0,4},{1,5},{2,6},{3,7},{4,0},{5,1},{6,2},{7,3},{8,12},{9,13},{10,... | collective-permute-start | bytes 1327112 | tf_op jit(solution)/shard_map/ppermute | solution.py:293
  278.4 19.8 %collective-permute-start.21 = (f32[24,4608]{1,0:T(8,128)}, f32[24,4608]{1,0:T(8,128)}, u32[]{:S(2)}, u32[]{:S(2)}) collective-permute-start(f32[24,4608]{1,0:T(8,128)} %get-tuple-element.211), channel_id=1, source_target_pairs={{0,8},{1,9},{2,10},{3,11},{4,12},{5,13},{6,14},{7,15},{8,0},{9,1},... | collective-permute-start | bytes 1327112 | tf_op jit(solution)/shard_map/ppermute | solution.py:293
  279.3 37.9 %collective-permute-start.22 = (f32[24,4608]{1,0:T(8,128)S(1)}, f32[24,4608]{1,0:T(8,128)}, u32[]{:S(2)}, u32[]{:S(2)}) collective-permute-start(f32[24,4608]{1,0:T(8,128)S(1)} %get-tuple-element.212), channel_id=1, source_target_pairs={{0,12},{1,13},{2,14},{3,15},{4,8},{5,9},{6,10},{7,11},{8,4},{9,5},... | collective-permute-start | bytes 1327112 | tf_op jit(solution)/shard_map/ppermute | solution.py:293
  279.6 40.4 %collective-permute-start.19 = (f32[384,768]{1,0:T(8,128)S(1)}, f32[384,768]{1,0:T(8,128)}, u32[]{:S(2)}, u32[]{:S(2)}) collective-permute-start(f32[384,768]{1,0:T(8,128)S(1)} %fusion.6.refs_0_), channel_id=1, source_target_pairs={{0,2},{1,17},{2,0},{3,19},{4,6},{5,21},{6,4},{7,23},{8,10},{9,25},... | collective-permute-start | bytes 3538952 | tf_op jit(solution)/shard_map/ppermute | solution.py:293
  322.4 4.6 copy-start.17
  325.5 38.7 %collective-permute-start.24 = (f32[768,768]{1,0:T(8,128)S(1)}, f32[768,768]{1,0:T(8,128)}, u32[]{:S(2)}, u32[]{:S(2)}) collective-permute-start(f32[768,768]{1,0:T(8,128)S(1)} %copy-done.6), channel_id=1, source_target_pairs={{0,16},{1,3},{2,18},{3,1},{4,20},{5,7},{6,22},{7,5},{8,24},{9,11},... | collective-permute-start | bytes 7077896 | tf_op jit(solution)/shard_map/ppermute | solution.py:293
  325.6 36.3 %collective-permute-start.28 = (f32[96,2432]{1,0:T(8,128)}, f32[96,2432]{1,0:T(8,128)}, u32[]{:S(2)}, u32[]{:S(2)}) collective-permute-start(f32[96,2432]{1,0:T(8,128)} %dynamic-slice_add_fusion.5), channel_id=1, source_target_pairs={{0,2},{1,17},{2,0},{3,19},{4,6},{5,21},{6,4},{7,23},{8,10},{9,25},... | collective-permute-start | bytes 2801672 | tf_op jit(solution)/shard_map/ppermute | solution.py:293
  327.0 23.8 %collective-permute-start.25 = (f32[24,4608]{1,0:T(8,128)S(1)}, f32[24,4608]{1,0:T(8,128)S(1)}, u32[]{:S(2)}, u32[]{:S(2)}) collective-permute-start(f32[24,4608]{1,0:T(8,128)S(1)} %copy-done.17), channel_id=1, source_target_pairs={{0,12},{1,13},{2,14},{3,15},{4,8},{5,9},{6,10},{7,11},{8,4},{9,5},... | collective-permute-start | bytes 1327112 | tf_op jit(solution)/shard_map/ppermute | solution.py:293
  328.2 30.8 %collective-permute-start.26 = (f32[24,4608]{1,0:T(8,128)S(1)}, f32[24,4608]{1,0:T(8,128)}, u32[]{:S(2)}, u32[]{:S(2)}) collective-permute-start(f32[24,4608]{1,0:T(8,128)S(1)} %copy-done.17), channel_id=1, source_target_pairs={{0,8},{1,9},{2,10},{3,11},{4,12},{5,13},{6,14},{7,15},{8,0},{9,1},... | collective-permute-start | bytes 1327112 | tf_op jit(solution)/shard_map/ppermute | solution.py:293
  328.2 30.8 %collective-permute-start.27 = (f32[24,4608]{1,0:T(8,128)S(1)}, f32[24,4608]{1,0:T(8,128)}, u32[]{:S(2)}, u32[]{:S(2)}) collective-permute-start(f32[24,4608]{1,0:T(8,128)S(1)} %copy-done.17), channel_id=1, source_target_pairs={{0,4},{1,5},{2,6},{3,7},{4,0},{5,1},{6,2},{7,3},{8,12},{9,13},{10,... | collective-permute-start | bytes 1327112 | tf_op jit(solution)/shard_map/ppermute | solution.py:293
  367.1 26.7 %collective-permute-start.29 = (f32[1536,768]{1,0:T(8,128)}, f32[1536,768]{1,0:T(8,128)}, u32[]{:S(2)}, u32[]{:S(2)}) collective-permute-start(f32[1536,768]{1,0:T(8,128)} %put.21.refs_0_), channel_id=1, source_target_pairs={{0,1},{1,0},{2,3},{3,2},{4,5},{5,4},{6,7},{7,6},{8,9},{9,8},{10,11... | collective-permute-start | bytes 14155784 | tf_op jit(solution)/shard_map/ppermute | solution.py:293
  367.6 31.3 %collective-permute-start.30 = (f32[96,4608]{1,0:T(8,128)S(1)}, f32[96,4608]{1,0:T(8,128)}, u32[]{:S(2)}, u32[]{:S(2)}) collective-permute-start(f32[96,4608]{1,0:T(8,128)S(1)} %copy-done.11), channel_id=1, source_target_pairs={{0,2},{1,17},{2,0},{3,19},{4,6},{5,21},{6,4},{7,23},{8,10},{9,25},... | collective-permute-start | bytes 5308424 | tf_op jit(solution)/shard_map/ppermute | solution.py:293
  368.6 11.3 %collective-permute-start.31 = (f32[24,2432]{1,0:T(8,128)S(1)}, f32[24,2432]{1,0:T(8,128)S(1)}, u32[]{:S(2)}, u32[]{:S(2)}) collective-permute-start(f32[24,2432]{1,0:T(8,128)S(1)} %get-tuple-element.230), channel_id=1, source_target_pairs={{0,4},{1,5},{2,6},{3,7},{4,0},{5,1},{6,2},{7,3},{8,12},{9,13},{10,... | collective-permute-start | bytes 700424 | tf_op jit(solution)/shard_map/ppermute | solution.py:293
  370.5 15.6 %collective-permute-start.32 = (f32[24,2432]{1,0:T(8,128)S(1)}, f32[24,2432]{1,0:T(8,128)S(1)}, u32[]{:S(2)}, u32[]{:S(2)}) collective-permute-start(f32[24,2432]{1,0:T(8,128)S(1)} %get-tuple-element.231), channel_id=1, source_target_pairs={{0,8},{1,9},{2,10},{3,11},{4,12},{5,13},{6,14},{7,15},{8,0},{9,1},... | collective-permute-start | bytes 700424 | tf_op jit(solution)/shard_map/ppermute | solution.py:293
  371.3 21.0 %collective-permute-start.33 = (f32[24,2432]{1,0:T(8,128)S(1)}, f32[24,2432]{1,0:T(8,128)S(1)}, u32[]{:S(2)}, u32[]{:S(2)}) collective-permute-start(f32[24,2432]{1,0:T(8,128)S(1)} %get-tuple-element.232), channel_id=1, source_target_pairs={{0,12},{1,13},{2,14},{3,15},{4,8},{5,9},{6,10},{7,11},{8,4},{9,5},... | collective-permute-start | bytes 700424 | tf_op jit(solution)/shard_map/ppermute | solution.py:293
  401.3 51.0 %collective-permute-start.34 = (f32[192,4608]{1,0:T(8,128)}, f32[192,4608]{1,0:T(8,128)}, u32[]{:S(2)}, u32[]{:S(2)}) collective-permute-start(f32[192,4608]{1,0:T(8,128)} %put.25.refs_0_), channel_id=1, source_target_pairs={{0,16},{1,3},{2,18},{3,1},{4,20},{5,7},{6,22},{7,5},{8,24},{9,11},... | collective-permute-start | bytes 10616840 | tf_op jit(solution)/shard_map/ppermute | solution.py:293
  402.2 14.7 %collective-permute-start.35 = (f32[24,2432]{1,0:T(8,128)S(1)}, f32[24,2432]{1,0:T(8,128)S(1)}, u32[]{:S(2)}, u32[]{:S(2)}) collective-permute-start(f32[24,2432]{1,0:T(8,128)S(1)} %add_add_fusion.3), channel_id=1, source_target_pairs={{0,12},{1,13},{2,14},{3,15},{4,8},{5,9},{6,10},{7,11},{8,4},{9,5},... | collective-permute-start | bytes 700424 | tf_op jit(solution)/shard_map/ppermute | solution.py:293
  403.5 17.2 %collective-permute-start.36 = (f32[24,2432]{1,0:T(8,128)S(1)}, f32[24,2432]{1,0:T(8,128)S(1)}, u32[]{:S(2)}, u32[]{:S(2)}) collective-permute-start(f32[24,2432]{1,0:T(8,128)S(1)} %add_add_fusion.3), channel_id=1, source_target_pairs={{0,8},{1,9},{2,10},{3,11},{4,12},{5,13},{6,14},{7,15},{8,0},{9,1},... | collective-permute-start | bytes 700424 | tf_op jit(solution)/shard_map/ppermute | solution.py:293
  403.5 17.2 %collective-permute-start.37 = (f32[24,2432]{1,0:T(8,128)S(1)}, f32[24,2432]{1,0:T(8,128)S(1)}, u32[]{:S(2)}, u32[]{:S(2)}) collective-permute-start(f32[24,2432]{1,0:T(8,128)S(1)} %add_add_fusion.3), channel_id=1, source_target_pairs={{0,4},{1,5},{2,6},{3,7},{4,0},{5,1},{6,2},{7,3},{8,12},{9,13},{10,... | collective-permute-start | bytes 700424 | tf_op jit(solution)/shard_map/ppermute | solution.py:293
  421.2 4.8 copy-start.14
  421.2 22.9 %collective-permute-start.38 = (f32[96,2432]{1,0:T(8,128)S(1)}, f32[96,2432]{1,0:T(8,128)S(1)}, u32[]{:S(2)}, u32[]{:S(2)}) collective-permute-start(f32[96,2432]{1,0:T(8,128)S(1)} %fusion.11.refs_0_), channel_id=1, source_target_pairs={{0,2},{1,17},{2,0},{3,19},{4,6},{5,21},{6,4},{7,23},{8,10},{9,25},... | collective-permute-start | bytes 2801672 | tf_op jit(solution)/shard_map/ppermute | solution.py:293
  447.2 11.3 %copy-start.7 = (f32[192,2432]{1,0:T(8,128)S(1)}, f32[192,2432]{1,0:T(8,128)}, u32[]{:S(2)}) copy-start(f32[192,2432]{1,0:T(8,128)} %put.29.refs_0_) | copy-start | bytes 5603332
  456.6 13.7 %collective-permute-start.39 = (f32[384,4608]{1,0:T(8,128)}, f32[384,4608]{1,0:T(8,128)}, u32[]{:S(2)}, u32[]{:S(2)}) collective-permute-start(f32[384,4608]{1,0:T(8,128)} %put.27.refs_0_), channel_id=1, source_target_pairs={{0,1},{1,0},{2,3},{3,2},{4,5},{5,4},{6,7},{7,6},{8,9},{9,8},{10,11... | collective-permute-start | bytes 21233672 | tf_op jit(solution)/shard_map/ppermute | solution.py:293
  458.5 22.8 %collective-permute-start.40 = (f32[192,2432]{1,0:T(8,128)S(1)}, f32[192,2432]{1,0:T(8,128)}, u32[]{:S(2)}, u32[]{:S(2)}) collective-permute-start(f32[192,2432]{1,0:T(8,128)S(1)} %copy-done.7), channel_id=1, source_target_pairs={{0,16},{1,3},{2,18},{3,1},{4,20},{5,7},{6,22},{7,5},{8,24},{9,11},... | collective-permute-start | bytes 5603336 | tf_op jit(solution)/shard_map/ppermute | solution.py:293
  478.5 6.2 %copy-start.16 = (f32[16,768]{1,0:T(8,128)S(1)}, f32[16,768]{1,0:T(8,128)}, u32[]{:S(2)}) copy-start(f32[16,768]{1,0:T(8,128)} %copy-done.15) | copy-start | bytes 147460
  483.8 7.3 %collective-permute-start.41 = (f32[384,2432]{1,0:T(8,128)}, f32[384,2432]{1,0:T(8,128)}, u32[]{:S(2)}, u32[]{:S(2)}) collective-permute-start(f32[384,2432]{1,0:T(8,128)} %put.33.refs_0_), channel_id=1, source_target_pairs={{0,1},{1,0},{2,3},{3,2},{4,5},{5,4},{6,7},{7,6},{8,9},{9,8},{10,11... | collective-permute-start | bytes 11206664 | tf_op jit(solution)/shard_map/ppermute | solution.py:293
  491.1 8.6 %copy-start.1 = (bf16[768,768]{1,0:T(8,128)(2,1)S(1)}, bf16[768,768]{1,0:T(8,128)(2,1)}, u32[]{:S(2)}) copy-start(bf16[768,768]{1,0:T(8,128)(2,1)} %param.25) | copy-start | bytes 3538948
  (17 other events, 42.4 us)

commit v6 on v5

--- a/solution.py
+++ b/solution.py
@@ -238,20 +238,21 @@
     width = gains[0].shape[1]
     heads = grad_rows.shape[0]
     buckets = code.shape[0]
+    lines = width // LANES
 
     def kernel(*refs):
         *gain_refs, rows_ref, code_ref, out_ref = refs
-        line = lax.broadcasted_iota(jnp.int32, (LANES, width), 0)
-        value = jnp.zeros((LANES, width), jnp.float32)
+        out_ref[...] = jnp.zeros_like(out_ref)
         for n, ref in enumerate(gain_refs):
-            value = jnp.where(line == n, ref[...], value)
-        out_ref[...] = value.T
+            for line in range(lines):
+                at = n * lines + line
+                out_ref[at : at + 1, :] = ref[:, line * LANES : (line + 1) * LANES]
         lane = lax.broadcasted_iota(jnp.int32, (buckets, LANES), 1)
-        value = out_ref[:buckets, :]
+        value = jnp.zeros((buckets, LANES), jnp.float32)
         for h in range(heads):
             part = jnp.sum(code_ref[...] * rows_ref[h], axis=1, keepdims=True)
-            value = jnp.where(lane == BIAS_AT + h, part, value)
-        out_ref[:buckets, :] = value
+            value = jnp.where(lane == h, part, value)
+        out_ref[BIAS_AT : BIAS_AT + buckets, :] = value
 
     return pl.pallas_call(
         kernel,
@@ -404,6 +405,69 @@
         return pl.BlockSpec(shape, lambda t: (0, 0))
 
     return tile, lines, whole
+
+
+def norm_low(values, gain):
+    scale = lax.rsqrt(jnp.mean(values * values, axis=1, keepdims=True) + norm_epsilon)
+    return (values * scale * gain).astype(jnp.bfloat16)
+
+
+def project_kernel(x_ref, gain_ref, wq_ref, wk_ref, wv_ref, n_ref, q_ref, k_ref, v_ref):
+    normed = norm_low(x_ref[...].astype(jnp.float32), gain_ref[...])
+    n_ref[...] = normed
+    for weight, out in ((wq_ref, q_ref), (wk_ref, k_ref), (wv_ref, v_ref)):
+        out[...] = dot_nn(normed, weight[...]).astype(jnp.bfloat16)
+
+
+def project(states, gain, weights):
+    rows, width = states.shape
+    tile, lines, whole = row_tiles(rows)
+    return pl.pallas_call(
+        project_kernel,
+        name="project",
+        grid=(rows // tile,),
+        in_specs=[lines(width), whole(1, width)] + [whole(width, width)] * 3,
+        out_specs=[lines(width)] * 4,
+        out_shape=[jax.ShapeDtypeStruct((rows, width), jnp.bfloat16)] * 4,
+    )(states, gain[None], *weights)
+
+
+def feed_kernel(
+    mix_ref, x_ref, gain_ref, wout_ref, win_ref, wff_ref, hid_ref, n_ref, act_ref, y_ref
+):
+    hidden = x_ref[...].astype(jnp.float32) + dot_nn(mix_ref[...], wout_ref[...])
+    hid_ref[...] = hidden
+    normed = norm_low(hidden, gain_ref[...])
+    n_ref[...] = normed
+    activ = jnp.maximum(dot_nn(normed, win_ref[...]), 0.0).astype(jnp.bfloat16)
+    act_ref[...] = activ
+    y_ref[...] = hidden + dot_nn(activ, wff_ref[...])
+
+
+def feed(mixed, states, gain, w_out, w_in, w_ffout):
+    rows, width = states.shape
+    inner = w_in.shape[1]
+    tile, lines, whole = row_tiles(rows)
+    return pl.pallas_call(
+        feed_kernel,
+        name="feed_forward",
+        grid=(rows // tile,),
+        in_specs=[
+            lines(width),
+            lines(width),
+            whole(1, width),
+            whole(width, width),
+            whole(width, inner),
+            whole(inner, width),
+        ],
+        out_specs=[lines(width), lines(width), lines(inner), lines(width)],
+        out_shape=[
+            jax.ShapeDtypeStruct((rows, width), jnp.float32),
+            jax.ShapeDtypeStruct((rows, width), jnp.bfloat16),
+            jax.ShapeDtypeStruct((rows, inner), jnp.bfloat16),
+            jax.ShapeDtypeStruct((rows, width), jnp.float32),
+        ],
+    )(mixed, states, gain[None], w_out, w_in, w_ffout)
 
 
 def norm_backward(values, grad, gain, sum_ref):
@@ -660,14 +724,12 @@
 
     segment = segment_ids[0]
 
-    states_f = states[0].reshape(rows, model_width).astype(jnp.float32)
-    normed = rms_scale(states_f, gain_attn)
-    normed_low = normed.astype(jnp.bfloat16)
-    query_low = mm(normed_low, w_query).astype(jnp.bfloat16)
-    key_low = mm(normed_low, w_key).astype(jnp.bfloat16)
-    value_low = mm(normed_low, w_value).astype(jnp.bfloat16)
+    states_low = states[0].reshape(rows, model_width)
+    normed_low, query_low, key_low, value_low = project(
+        states_low, gain_attn, (w_query, w_key, w_value)
+    )
     mixed_low = attention(query_low, key_low, value_low, segment, bias_rows(code), head_dim)
-    hidden = states_f + mm(mixed_low, w_out)
+    hidden = states_low.astype(jnp.float32) + mm(mixed_low, w_out)
     normed_two = rms_scale(hidden, gain_ffn)
     normed_two_low = normed_two.astype(jnp.bfloat16)
     activ_low = jnp.maximum(mm(normed_two_low, w_in), 0.0).astype(jnp.bfloat16)
@@ -768,7 +830,7 @@
     grad_states, grad_gain_attn = project_backward(
         grad_heads,
         grad_hidden,
-        states[0].reshape(rows, model_width),
+        states_low,
         gain_attn,
         (w_query, w_key, w_value),
     )
@@ -786,14 +848,14 @@
             tie_all(sums)
         for s in sums:
             s.go()
-        first.end()
-        first.held, second.base = tie(first.held, second.base)
         second.end()
         third.end()
-        tie_all(sums)
+        second.held, third.held, first.base = tie(second.held, third.held, first.base)
         second.go()
         third.go()
+        first.end()
         third.end()
+        first.held, third.held = tie(first.held, third.held)
         third.go()
         second.end()
         third.end()
@@ -811,8 +873,8 @@
     (whole_ffout,) = first.held
     whole_in, whole_out, whole_proj = second.held
     whole_query, whole_key, whole_value, small = third.held
+    lines = model_width // LANES
     loss = loss_sum / (micro_count * row_count)
-    width = model_width
     return (
         loss,
         unit_embed.reshape(1, micro_count, item_count, model_width),
@@ -824,10 +886,8 @@
         whole_in,
         whole_ffout,
         whole_proj,
-        small[:, 0],
-        small[:, 1],
-        small[:, 2],
-        small[:bucket_count, BIAS_AT : BIAS_AT + head_count],
+        *(small[n * lines : (n + 1) * lines].reshape(-1) for n in range(3)),
+        small[BIAS_AT : BIAS_AT + bucket_count, :head_count],
     )
 
 

time: 510 us -> 507 us (level)
  the two profiles are of different devices: /device:TPU:9 before, /device:TPU:0 now
where the time goes in v6:
time: 507 us; the launch traced here: 497 us
  Pallas kernels  214 us (42%)
  waiting for transfers between devices  132 us (26%)
  starting transfers between devices  54.2 us (11%)
  other arithmetic  48.1 us (9%)
  matrix products  25.1 us (5%)
  local copies, waits for them, and re-layouts  19.1 us (4%)
    ppermute x42, waiting for transfers between devices, send_by(): lax.ppermute(value, AXES, [(i, i ^ masks[i & 1]) for i in range(self.size)])  132 us
    pallas_call x18, Pallas kernels, put(): pl.pallas_call(kernel, name='put', grid_spec=pltpu.PrefetchScalarGridSpec...  69.3 us
    ppermute x42, starting transfers between devices, send_by(): lax.ppermute(value, AXES, [(i, i ^ masks[i & 1]) for i in range(self.size)])  54.2 us
    pallas_call x3, Pallas kernels, attention_grads(): pl.pallas_call(kernel, name='attention_backward', grid=(count, micro_coun...  44.8 us
    pallas_call x3, Pallas kernels, weight_grads(): pl.pallas_call(kernel, name='weight_grads', grid_spec=pltpu.PrefetchScala...  35 us
    add x12, other arithmetic, total(): value = term if value is None else value + term  34.7 us
    pallas_call x1, Pallas kernels, attention(): pl.pallas_call(lambda *refs: forward_kernel(head_dim, *refs), name='atten...  23.1 us
    pallas_call x1, Pallas kernels, feed_backward(): pl.pallas_call(feed_backward_kernel, name='feed_backward', grid=(rows //...  22.3 us
  transfers between devices with their start and end apart: 42, of which 19 were waited for; matrix products, arithmetic and copies ran while one was open for 5% of the time, Pallas kernels for 32%

profile of v6, /device:TPU:0, one launch (start us, length us, event | category | flops | bytes accessed | tf_op | source)
XLA Modules:
  0.0 497.3 jit_solution(3606429291886832749)
XLA Ops:
  6.9 7.6 %project.1 = (bf16[1024,768]{1,0:T(8,128)(2,1)}, bf16[1024,768]{1,0:T(8,128)(2,1)}, bf16[1024,768]{1,0:T(8,128)(2,1)}, bf16[1024,768]{1,0:T(8,128)(2,1)}) custom-call(bf16[1024,768]{1,0:T(8,128)(2,1)} %bitcast.198, f32[1,768]{1,0:T(1,128)} %broadcast_in_dim.327.gain_ref, bf16[768,768]{1,0:T(8,128)(2,1)} %wq_ref.3, bf16[768,768]{1,0:T(8,128)(2,1)} %wk_ref.3, ...), custom_call_target="tpu_custom_call" | custom-call | tf_op jit(solution)/shard_map/project/pallas_call | solution.py:425
  14.5 23.1 %attention_forward.1.refs_1_.refs_4_ = bf16[1024,768]{1,0:T(8,128)(2,1)} custom-call(bf16[1024,768]{1,0:T(8,128)(2,1)} %get-tuple-element.179.refs_0_, bf16[1024,768]{1,0:T(8,128)(2,1)} %get-tuple-element.142.refs_1_, bf16[1024,768]{1,0:T(8,128)(2,1)} %get-tuple-element.143.refs_2_, s32[1024,1]{1,0:T(8,128)} %bitcast.190, ...), custom_call_target="tpu_custom_call" | custom-call | tf_op jit(solution)/shard_map/attention_forward/pallas_call | solution.py:199
  37.6 3.3 multiply_reduce_fusion.2
  41.3 10.0 %maximum_convert_fusion.refs_0_.refs_1_.act_ref = bf16[1024,3072]{1,0:T(8,128)(2,1)S(1)} fusion(bf16[1024,768]{1,0:T(8,128)(2,1)S(1)} %multiply_convert_fusion.refs_0_.refs_3_, bf16[768,3072]{1,0:T(8,128)(2,1)} %win_ref.1), kind=kOutput, calls=%fused_computation | convolution fusion | flops 4838129664 | bytes 12582912 | tf_op jit(solution)/shard_map/dot_general | solution.py:47
  51.4 5.2 %multiply_reduce_fusion.1 = (f32[1024]{0:T(1024)S(1)}, f32[1024,768]{1,0:T(8,128)S(1)}) fusion(f32[1024,768]{1,0:T(8,128)S(1)} %get-tuple-element.323.hid_ref, bf16[1024,3072]{1,0:T(8,128)(2,1)S(1)} %maximum_convert_fusion.refs_0_.refs_1_.act_ref, bf16[3072,768]{1,0:T(8,128)(2,1)S(1)} %bitcast.202), kind=kOutput, calls=%fused_computation.7 | convolution fusion | flops 4834196480 | bytes 17305600 | tf_op jit(solution)/shard_map/dot_general | solution.py:47
  60.5 5.1 %collective-permute-start = (f32[16,768]{1,0:T(8,128)S(1)}, f32[16,768]{1,0:T(8,128)S(1)}, u32[]{:S(2)}, u32[]{:S(2)}) collective-permute-start(f32[16,768]{1,0:T(8,128)S(1)} %broadcast_multiply_fusion), channel_id=1, source_target_pairs={{0,12},{1,13},{2,14},{3,15},{4,8},{5,9},{6,10},{7,11},{8,4},{9,5},... | collective-permute-start | bytes 147464 | tf_op jit(solution)/shard_map/ppermute | solution.py:294
  67.7 2.9 collective-permute-done.1
  72.3 4.1 collective-permute-done.3
  78.3 6.2 %collective-permute-done.4 = f32[128,768]{1,0:T(8,128)S(1)} collective-permute-done((f32[128,768]{1,0:T(8,128)S(1)}, f32[128,768]{1,0:T(8,128)S(1)}, u32[]{:S(2)}, u32[]{:S(2)}) %collective-permute-start.4) | collective-permute-done | bytes 393248 | tf_op jit(solution)/shard_map/ppermute | solution.py:294
  94.1 2.9 fusion.57
  97.0 10.0 %weight_grads.3 = (f32[1536,768]{1,0:T(8,128)}, f32[1536,768]{1,0:T(8,128)}) custom-call(s32[1]{0:T(128)} %bitcast.43.bit_ref.places_ref, bf16[1024,3072]{1,0:T(8,128)(2,1)} %copy-done.2, bf16[1024,3072]{1,0:T(8,128)(2,1)} %copy-done.2, bf16[1024,768]{1,0:T(8,128)(2,1)} %get-tuple-element.302.refs_2_), custom_call_target="tpu_custom_call" | custom-call | tf_op jit(solution)/shard_map/weight_grads/pallas_call | solution.py:374
  107.8 22.3 %feed_backward.1 = (bf16[1024,3072]{1,0:T(8,128)(2,1)}, f32[1024,768]{1,0:T(8,128)}, bf16[1024,768]{1,0:T(8,128)(2,1)}, bf16[1024,768]{1,0:T(8,128)(2,1)}, f32[1,768]{1,0:T(1,128)}) custom-call(f32[1024,768]{1,0:T(8,128)} %get-tuple-element.146.go_ref, bf16[1024,3072]{1,0:T(8,128)(2,1)} %copy-done.2, f32[1024,768]{1,0:T(8,128)} %copy-done.7, ...), custom_call_target="tpu_custom_call" | custom-call | tf_op jit(solution)/shard_map/feed_backward/pallas_call | solution.py:534
  130.1 2.7 dynamic-slice_add_fusion.1
  135.4 14.2 %weight_grads.4 = (f32[384,4608]{1,0:T(8,128)}, f32[384,4608]{1,0:T(8,128)}) custom-call(s32[1]{0:T(128)} %bitcast.43.bit_ref.places_ref, bf16[1024,768]{1,0:T(8,128)(2,1)} %copy-done.6, bf16[1024,768]{1,0:T(8,128)(2,1)} %attention_forward.1.refs_1_.refs_4_, bf16[16,768]{1,0:T(8,128)(2,1)} %copy-done.18, bf16[1024,768]{1,0:T(8,128)(2,1)} %copy-done.6, ...), custom_call_target="tpu_custom_call" | custom-call | tf_op jit(solution)/shard_map/weight_grads/pallas_call | solution.py:374
  149.6 15.0 %attention_backward.3 = (bf16[1024,768]{1,0:T(8,128)(2,1)}, bf16[1024,768]{1,0:T(8,128)(2,1)}, bf16[1024,768]{1,0:T(8,128)(2,1)}, f32[12,1,1024]{2,1,0:T(1,128)}) custom-call(bf16[1024,768]{1,0:T(8,128)(2,1)} %get-tuple-element.179.refs_0_, bf16[1024,768]{1,0:T(8,128)(2,1)} %get-tuple-element.142.refs_1_, bf16[1024,768]{1,0:T(8,128)(2,1)} %get-tuple-element.143.refs_2_, ...), custom_call_target="tpu_custom_call" | custom-call | tf_op jit(solution)/shard_map/attention_backward/pallas_call | solution.py:224
  164.7 2.2 dynamic-slice_add_fusion.4
  168.6 14.9 %attention_backward.4 = (bf16[1024,768]{1,0:T(8,128)(2,1)}, bf16[1024,768]{1,0:T(8,128)(2,1)}, bf16[1024,768]{1,0:T(8,128)(2,1)}, f32[12,1,1024]{2,1,0:T(1,128)}) custom-call(bf16[1024,768]{1,0:T(8,128)(2,1)} %get-tuple-element.179.refs_0_, ...), custom_call_target="tpu_custom_call", output_to_operand_aliasing={{0}: (7, {}), {1}: (8, {}), {2}: (9, {}), {3}: (10, {})} | custom-call | tf_op jit(solution)/shard_map/attention_backward/pallas_call | solution.py:224
  185.5 5.4 %dynamic-slice_add_fusion = f32[192,4608]{1,0:T(8,128)} fusion(f32[384,4608]{1,0:T(8,128)} %collective-permute-done.9, s32[]{:T(128)S(6)} %select_n.442, f32[384,4608]{1,0:T(8,128)} %get-tuple-element.214), kind=kLoop, calls=%fused_computation.2 | loop fusion | flops 884736 | bytes 10616836 | tf_op jit(solution)/shard_map/add | solution.py:659
  197.8 14.9 %attention_backward.5 = (bf16[1024,768]{1,0:T(8,128)(2,1)}, bf16[1024,768]{1,0:T(8,128)(2,1)}, bf16[1024,768]{1,0:T(8,128)(2,1)}, f32[12,1,1024]{2,1,0:T(1,128)}) custom-call(bf16[1024,768]{1,0:T(8,128)(2,1)} %get-tuple-element.179.refs_0_, ...), custom_call_target="tpu_custom_call", output_to_operand_aliasing={{0}: (7, {}), {1}: (8, {}), {2}: (9, {}), {3}: (10, {})} | custom-call | tf_op jit(solution)/shard_map/attention_backward/pallas_call | solution.py:224
  212.7 10.2 %project_backward.1 = (f32[1024,768]{1,0:T(8,128)}, f32[1,768]{1,0:T(1,128)}) custom-call(bf16[1024,768]{1,0:T(8,128)(2,1)} %get-tuple-element.184.gq_ref.refs_6_, bf16[1024,768]{1,0:T(8,128)(2,1)} %get-tuple-element.185.gk_ref.refs_7_, bf16[1024,768]{1,0:T(8,128)(2,1)} %get-tuple-element.186.gv_ref.refs_8_, f32[1024,768]{1,0:T(8,128)} %get-tuple-element.187.gh_ref, ...), custom_call_target="tpu_custom_call" | custom-call | tf_op jit(solution)/shard_map/project_backward/pallas_call | solution.py:501
  224.8 10.8 %weight_grads.5 = (f32[384,2432]{1,0:T(8,128)}, f32[384,2432]{1,0:T(8,128)}) custom-call(s32[1]{0:T(128)} %bitcast.43.bit_ref.places_ref, bf16[1024,768]{1,0:T(8,128)(2,1)} %get-tuple-element.199.refs_0_.refs_1_.refs_2_.refs_3_.refs_4_.refs_5_, bf16[1024,768]{1,0:T(8,128)(2,1)} %get-tuple-element.199.refs_0_.refs_1_.refs_2_.refs_3_.refs_4_.refs_5_, ...), custom_call_target="tpu_custom_call" | custom-call | tf_op jit(solution)/shard_map/weight_grads/pallas_call | solution.py:374
  236.9 4.2 dynamic-slice_add_fusion.3
  241.9 2.1 collective-permute-start.14
  244.0 2.3 collective-permute-start.16
  248.3 5.4 %collective-permute-done.14 = f32[96,768]{1,0:T(8,128)S(1)} collective-permute-done((f32[96,768]{1,0:T(8,128)S(1)}, f32[96,768]{1,0:T(8,128)S(1)}, u32[]{:S(2)}, u32[]{:S(2)}) %collective-permute-start.14) | collective-permute-done | bytes 294944 | tf_op jit(solution)/shard_map/ppermute | solution.py:294
  253.7 15.8 %collective-permute-done.15 = f32[96,768]{1,0:T(8,128)S(1)} collective-permute-done((f32[96,768]{1,0:T(8,128)S(1)}, f32[96,768]{1,0:T(8,128)S(1)}, u32[]{:S(2)}, u32[]{:S(2)}) %collective-permute-start.15) | collective-permute-done | bytes 294944 | tf_op jit(solution)/shard_map/ppermute | solution.py:294
  271.6 4.4 dynamic-slice_add_fusion.6
  276.0 2.9 dynamic-slice_add_fusion.2
  280.3 3.2 collective-permute-start.21
  285.3 2.4 put.18.refs_1_
  287.6 12.9 %collective-permute-done.20 = f32[24,4608]{1,0:T(8,128)} collective-permute-done((f32[24,4608]{1,0:T(8,128)}, f32[24,4608]{1,0:T(8,128)}, u32[]{:S(2)}, u32[]{:S(2)}) %collective-permute-start.20) | collective-permute-done | bytes 442400 | tf_op jit(solution)/shard_map/ppermute | solution.py:294
  300.5 13.3 %collective-permute-done.21 = f32[24,4608]{1,0:T(8,128)} collective-permute-done((f32[24,4608]{1,0:T(8,128)}, f32[24,4608]{1,0:T(8,128)}, u32[]{:S(2)}, u32[]{:S(2)}) %collective-permute-start.21) | collective-permute-done | bytes 442400 | tf_op jit(solution)/shard_map/ppermute | solution.py:294
  313.8 2.8 add_add_fusion.1
  316.6 2.4 put.19.refs_0_
  319.0 3.1 dynamic-slice_add_fusion.5
  324.1 2.2 collective-permute-start.25
  326.3 7.5 %collective-permute-start.26 = (f32[24,4608]{1,0:T(8,128)S(1)}, f32[24,4608]{1,0:T(8,128)}, u32[]{:S(2)}, u32[]{:S(2)}) collective-permute-start(f32[24,4608]{1,0:T(8,128)S(1)} %copy-done.16), channel_id=1, source_target_pairs={{0,8},{1,9},{2,10},{3,11},{4,12},{5,13},{6,14},{7,15},{8,0},{9,1},... | collective-permute-start | bytes 1327112 | tf_op jit(solution)/shard_map/ppermute | solution.py:294
  334.2 2.8 put.20.refs_1_
  337.0 25.7 %collective-permute-done.26 = f32[24,4608]{1,0:T(8,128)} collective-permute-done((f32[24,4608]{1,0:T(8,128)S(1)}, f32[24,4608]{1,0:T(8,128)}, u32[]{:S(2)}, u32[]{:S(2)}) %collective-permute-start.26) | collective-permute-done | bytes 442400 | tf_op jit(solution)/shard_map/ppermute | solution.py:294
  362.7 2.8 fusion.2.refs_0_
  365.5 2.3 dynamic-slice_add_fusion.12
  367.8 2.9 put.21.refs_0_
  371.3 3.0 collective-permute-start.31
  375.7 5.0 %put.24.refs_1_ = f32[3072,768]{1,0:T(8,128)} custom-call(s32[1]{0:T(128)} %bitcast.43.bit_ref.places_ref, f32[1536,768]{1,0:T(8,128)} %put.21.refs_0_), custom_call_target="tpu_custom_call" | custom-call | tf_op jit(solution)/shard_map/put/pallas_call | solution.py:584
  380.7 2.5 put.22.refs_1_
  383.8 7.0 %collective-permute-done.31 = f32[24,2432]{1,0:T(8,128)S(1)} collective-permute-done((f32[24,2432]{1,0:T(8,128)S(1)}, f32[24,2432]{1,0:T(8,128)S(1)}, u32[]{:S(2)}, u32[]{:S(2)}) %collective-permute-start.31) | collective-permute-done | bytes 233504 | tf_op jit(solution)/shard_map/ppermute | solution.py:294
  393.4 2.4 put.23.refs_0_
  396.5 2.3 collective-permute-start.35
  398.8 3.6 collective-permute-start.36
  402.5 3.6 collective-permute-done.35
  406.1 14.1 %collective-permute-done.36 = f32[24,2432]{1,0:T(8,128)S(1)} collective-permute-done((f32[24,2432]{1,0:T(8,128)S(1)}, f32[24,2432]{1,0:T(8,128)S(1)}, u32[]{:S(2)}, u32[]{:S(2)}) %collective-permute-start.36) | collective-permute-done | bytes 233504 | tf_op jit(solution)/shard_map/ppermute | solution.py:294
  420.6 5.4 %put.27 = f32[3072,768]{1,0:T(8,128)} custom-call(s32[1]{0:T(128)} %bitcast.46.places_ref, f32[1536,768]{1,0:T(8,128)} %collective-permute-done.34.refs_0_, f32[3072,768]{1,0:T(8,128)} %put.24.refs_1_), custom_call_target="tpu_custom_call", output_to_operand_aliasing={{}: (2, {})} | custom-call | tf_op jit(solution)/shard_map/put/pallas_call | solution.py:584
  427.5 4.4 put.25.refs_1_
  431.8 2.2 put.28.refs_1_
  434.0 12.5 %collective-permute-done.33.refs_0_ = f32[192,4608]{1,0:T(8,128)} collective-permute-done((f32[192,4608]{1,0:T(8,128)}, f32[192,4608]{1,0:T(8,128)}, u32[]{:S(2)}, u32[]{:S(2)}) %collective-permute-start.33) | collective-permute-done | bytes 3538976 | tf_op jit(solution)/shard_map/ppermute | solution.py:294
  446.5 4.4 put.26.refs_0_
  451.8 2.2 put.29.refs_0_
  454.0 8.2 %put.30 = (f32[768,3072]{1,0:T(8,128)}, f32[768,768]{1,0:T(8,128)}, f32[768,768]{1,0:T(8,128)}) custom-call(s32[1]{0:T(128)} %bitcast.43.bit_ref.places_ref, f32[384,4608]{1,0:T(8,128)} %put.26.refs_0_), custom_call_target="tpu_custom_call" | custom-call | tf_op jit(solution)/shard_map/put/pallas_call | solution.py:584
  462.2 2.5 put.32.refs_1_
  465.6 8.2 %put.31 = (f32[768,3072]{1,0:T(8,128)}, f32[768,768]{1,0:T(8,128)}, f32[768,768]{1,0:T(8,128)}) custom-call(s32[1]{0:T(128)} %bitcast.46.places_ref, f32[384,4608]{1,0:T(8,128)} %collective-permute-done.39.refs_0_, f32[768,3072]{1,0:T(8,128)} %get-tuple-element.244.refs_1_, ...), custom_call_target="tpu_custom_call", output_to_operand_aliasing={{0}: (2, {}), {1}: (3, {}), {2}: (4, {})} | custom-call | tf_op jit(solution)/shard_map/put/pallas_call | solution.py:584
  473.8 4.0 collective-permute-done.40.refs_0_
  479.0 2.5 put.33.refs_0_
  483.5 4.5 put.34
  488.4 4.5 put.35
  (223 shorter events, 68.1 us)
Async XLA Ops:
  0.6 59.4 %copy-start = (bf16[768,768]{1,0:T(8,128)(2,1)S(1)}, bf16[768,768]{1,0:T(8,128)(2,1)}, u32[]{:S(2)}) copy-start(bf16[768,768]{1,0:T(8,128)(2,1)} %param.25) | copy-start | bytes 3538948
  14.5 23.1 %copy-start.9 = (bf16[1,2,512,768]{3,2,1,0:T(8,128)(2,1)S(1)}, bf16[1,2,512,768]{3,2,1,0:T(8,128)(2,1)}, u32[]{:S(2)}) copy-start(bf16[1,2,512,768]{3,2,1,0:T(8,128)(2,1)} %param.15) | copy-start | bytes 4718596
  40.9 10.4 %copy-start.7 = (f32[1024,768]{1,0:T(8,128)}, f32[1024,768]{1,0:T(8,128)S(1)}, u32[]{:S(2)}) copy-start(f32[1024,768]{1,0:T(8,128)S(1)} %get-tuple-element.323.hid_ref) | copy-start | bytes 9437188
  40.9 10.4 %slice-start = ((s8[4718592]{0:T(1024)(128)(4,1)}), s8[4194304]{0:T(1024)(128)(4,1)S(1)}, s32[]{:S(2)}) async-start(s8[4718592]{0:T(1024)(128)(4,1)} %bitcast.201), calls=%async_computation | async-start | bytes 8388608
  41.3 10.0 %copy-start.6 = (bf16[1024,768]{1,0:T(8,128)(2,1)}, bf16[1024,768]{1,0:T(8,128)(2,1)S(1)}, u32[]{:S(2)}) copy-start(bf16[1024,768]{1,0:T(8,128)(2,1)S(1)} %multiply_convert_fusion.refs_0_.refs_3_) | copy-start | bytes 4718596
  41.3 10.0 %slice-start.1 = ((s8[4718592]{0:T(1024)(128)(4,1)}), s8[524288]{0:T(1024)(128)(4,1)S(1)}, s32[]{:S(2)}) async-start(s8[4718592]{0:T(1024)(128)(4,1)} %bitcast.201), calls=%async_computation.1 | async-start | bytes 1048576
  51.3 5.3 %copy-start.2 = (bf16[1024,3072]{1,0:T(8,128)(2,1)}, bf16[1024,3072]{1,0:T(8,128)(2,1)S(1)}, u32[]{:S(2)}) copy-start(bf16[1024,3072]{1,0:T(8,128)(2,1)S(1)} %maximum_convert_fusion.refs_0_.refs_1_.act_ref) | copy-start | bytes 18874372
  51.3 5.3 %copy-start.24 = (s32[1,2,8]{2,1,0:T(2,128)S(1)}, s32[1,2,8]{2,1,0:T(2,128)}, u32[]{:S(2)}) copy-start(s32[1,2,8]{2,1,0:T(2,128)} %param.17) | copy-start | bytes 196
  51.3 5.3 %copy-start.22 = (f32[768]{0:T(1024)S(1)}, f32[768]{0:T(1024)}, u32[]{:S(2)}) copy-start(f32[768]{0:T(1024)} %param.28) | copy-start | bytes 9220
  58.3 19.9 %copy-start.25 = (s32[2,128]{1,0:T(2,128)S(1)}, s32[2,128]{1,0:T(2,128)}, u32[]{:S(2)}) copy-start(s32[2,128]{1,0:T(2,128)} %param.18) | copy-start | bytes 3076
  60.4 30.2 %copy-start.14 = (f32[16,768]{1,0:T(8,128)}, f32[16,768]{1,0:T(8,128)S(1)}, u32[]{:S(2)}) copy-start(f32[16,768]{1,0:T(8,128)S(1)} %get-tuple-element.327) | copy-start | bytes 147460
  60.5 7.2 %collective-permute-start = (f32[16,768]{1,0:T(8,128)S(1)}, f32[16,768]{1,0:T(8,128)S(1)}, u32[]{:S(2)}, u32[]{:S(2)}) collective-permute-start(f32[16,768]{1,0:T(8,128)S(1)} %broadcast_multiply_fusion), channel_id=1, source_target_pairs={{0,12},{1,13},{2,14},{3,15},{4,8},{5,9},{6,10},{7,11},{8,4},{9,5},... | collective-permute-start | bytes 147464 | tf_op jit(solution)/shard_map/ppermute | solution.py:294
  65.6 5.0 %collective-permute-start.1 = (f32[16,768]{1,0:T(8,128)S(1)}, f32[16,768]{1,0:T(8,128)S(1)}, u32[]{:S(2)}, u32[]{:S(2)}) collective-permute-start(f32[16,768]{1,0:T(8,128)S(1)} %broadcast_multiply_fusion), channel_id=1, source_target_pairs={{0,8},{1,9},{2,10},{3,11},{4,12},{5,13},{6,14},{7,15},{8,0},{9,1},... | collective-permute-start | bytes 147464 | tf_op jit(solution)/shard_map/ppermute | solution.py:294
  65.6 5.0 %collective-permute-start.2 = (f32[16,768]{1,0:T(8,128)S(1)}, f32[16,768]{1,0:T(8,128)S(1)}, u32[]{:S(2)}, u32[]{:S(2)}) collective-permute-start(f32[16,768]{1,0:T(8,128)S(1)} %broadcast_multiply_fusion), channel_id=1, source_target_pairs={{0,4},{1,5},{2,6},{3,7},{4,0},{5,1},{6,2},{7,3},{8,12},{9,13},{10,... | collective-permute-start | bytes 147464 | tf_op jit(solution)/shard_map/ppermute | solution.py:294
  66.3 18.5 %copy-start.26 = (pred[4]{0:T(512)(128)(4,1)}, pred[4]{0:T(512)(128)(4,1)S(1)}, u32[]{:S(2)}) copy-start(pred[4]{0:T(512)(128)(4,1)S(1)} %get-tuple-element.334) | copy-start | bytes 16
  66.3 18.5 %copy-start.28 = (pred[4]{0:T(512)(128)(4,1)}, pred[4]{0:T(512)(128)(4,1)S(1)}, u32[]{:S(2)}) copy-start(pred[4]{0:T(512)(128)(4,1)S(1)} %get-tuple-element.335) | copy-start | bytes 16
  70.7 5.7 %collective-permute-start.3 = (f32[64,768]{1,0:T(8,128)S(1)}, f32[64,768]{1,0:T(8,128)S(1)}, u32[]{:S(2)}, u32[]{:S(2)}) collective-permute-start(f32[64,768]{1,0:T(8,128)S(1)} %fusion.16), channel_id=1, source_target_pairs={{0,16},{1,3},{2,18},{3,1},{4,20},{5,7},{6,22},{7,5},{8,24},{9,11},... | collective-permute-start | bytes 589832 | tf_op jit(solution)/shard_map/ppermute | solution.py:294
  76.6 7.8 %collective-permute-start.4 = (f32[128,768]{1,0:T(8,128)S(1)}, f32[128,768]{1,0:T(8,128)S(1)}, u32[]{:S(2)}, u32[]{:S(2)}) collective-permute-start(f32[128,768]{1,0:T(8,128)S(1)} %bitcast_select_fusion.6), channel_id=1, source_target_pairs={{0,2},{1,17},{2,0},{3,19},{4,6},{5,21},{6,4},{7,23},{8,10},{9,25},... | collective-permute-start | bytes 1179656 | tf_op jit(solution)/shard_map/ppermute | solution.py:294
  84.6 2.4 collective-permute-start.5
  107.0 23.0 %collective-permute-start.6 = (f32[1536,768]{1,0:T(8,128)}, f32[1536,768]{1,0:T(8,128)}, u32[]{:S(2)}, u32[]{:S(2)}) collective-permute-start(f32[1536,768]{1,0:T(8,128)} %get-tuple-element.151), channel_id=1, source_target_pairs={{0,1},{1,0},{2,3},{3,2},{4,5},{5,4},{6,7},{7,6},{8,9},{9,8},{10,11... | collective-permute-start | bytes 14155784 | tf_op jit(solution)/shard_map/ppermute | solution.py:294
  130.0 4.2 copy-start.30
  132.7 32.0 %collective-permute-start.7 = (f32[768,768]{1,0:T(8,128)S(1)}, f32[768,768]{1,0:T(8,128)}, u32[]{:S(2)}, u32[]{:S(2)}) collective-permute-start(f32[768,768]{1,0:T(8,128)S(1)} %dynamic-slice_add_fusion.1), channel_id=1, source_target_pairs={{0,16},{1,3},{2,18},{3,1},{4,20},{5,7},{6,22},{7,5},{8,24},{9,11},... | collective-permute-start | bytes 7077896 | tf_op jit(solution)/shard_map/ppermute | solution.py:294
  166.9 18.6 %collective-permute-start.9 = (f32[384,4608]{1,0:T(8,128)}, f32[384,4608]{1,0:T(8,128)}, u32[]{:S(2)}, u32[]{:S(2)}) collective-permute-start(f32[384,4608]{1,0:T(8,128)} %get-tuple-element.178), channel_id=1, source_target_pairs={{0,1},{1,0},{2,3},{3,2},{4,5},{5,4},{6,7},{7,6},{8,9},{9,8},{10,11... | collective-permute-start | bytes 21233672 | tf_op jit(solution)/shard_map/ppermute | solution.py:294
  167.1 16.3 %collective-permute-start.8 = (f32[384,768]{1,0:T(8,128)S(1)}, f32[384,768]{1,0:T(8,128)S(1)}, u32[]{:S(2)}, u32[]{:S(2)}) collective-permute-start(f32[384,768]{1,0:T(8,128)S(1)} %dynamic-slice_add_fusion.4), channel_id=1, source_target_pairs={{0,2},{1,17},{2,0},{3,19},{4,6},{5,21},{6,4},{7,23},{8,10},{9,25},... | collective-permute-start | bytes 3538952 | tf_op jit(solution)/shard_map/ppermute | solution.py:294
  190.9 46.0 %collective-permute-start.13 = (f32[192,4608]{1,0:T(8,128)}, f32[192,4608]{1,0:T(8,128)}, u32[]{:S(2)}, u32[]{:S(2)}) collective-permute-start(f32[192,4608]{1,0:T(8,128)} %dynamic-slice_add_fusion), channel_id=1, source_target_pairs={{0,16},{1,3},{2,18},{3,1},{4,20},{5,7},{6,22},{7,5},{8,24},{9,11},... | collective-permute-start | bytes 10616840 | tf_op jit(solution)/shard_map/ppermute | solution.py:294
  192.2 43.4 %collective-permute-start.10 = (f32[96,768]{1,0:T(8,128)S(1)}, f32[96,768]{1,0:T(8,128)S(1)}, u32[]{:S(2)}, u32[]{:S(2)}) collective-permute-start(f32[96,768]{1,0:T(8,128)S(1)} %get-tuple-element.193), channel_id=1, source_target_pairs={{0,4},{1,5},{2,6},{3,7},{4,0},{5,1},{6,2},{7,3},{8,12},{9,13},{10,... | collective-permute-start | bytes 884744 | tf_op jit(solution)/shard_map/ppermute | solution.py:294
  192.9 42.7 %collective-permute-start.11 = (f32[96,768]{1,0:T(8,128)S(1)}, f32[96,768]{1,0:T(8,128)S(1)}, u32[]{:S(2)}, u32[]{:S(2)}) collective-permute-start(f32[96,768]{1,0:T(8,128)S(1)} %get-tuple-element.194), channel_id=1, source_target_pairs={{0,8},{1,9},{2,10},{3,11},{4,12},{5,13},{6,14},{7,15},{8,0},{9,1},... | collective-permute-start | bytes 884744 | tf_op jit(solution)/shard_map/ppermute | solution.py:294
  194.9 40.7 %collective-permute-start.12 = (f32[96,768]{1,0:T(8,128)S(1)}, f32[96,768]{1,0:T(8,128)S(1)}, u32[]{:S(2)}, u32[]{:S(2)}) collective-permute-start(f32[96,768]{1,0:T(8,128)S(1)} %get-tuple-element.195), channel_id=1, source_target_pairs={{0,12},{1,13},{2,14},{3,15},{4,8},{5,9},{6,10},{7,11},{8,4},{9,5},... | collective-permute-start | bytes 884744 | tf_op jit(solution)/shard_map/ppermute | solution.py:294
  236.9 9.4 %copy-start.29 = (pred[4]{0:T(512)(128)(4,1)S(1)}, pred[4]{0:T(512)(128)(4,1)}, u32[]{:S(2)}) copy-start(pred[4]{0:T(512)(128)(4,1)} %copy-done.28) | copy-start | bytes 16
  236.9 10.1 %copy-start.27 = (pred[4]{0:T(512)(128)(4,1)S(1)}, pred[4]{0:T(512)(128)(4,1)}, u32[]{:S(2)}) copy-start(pred[4]{0:T(512)(128)(4,1)} %copy-done.26) | copy-start | bytes 16
  241.1 34.8 %collective-permute-start.18 = (f32[384,2432]{1,0:T(8,128)}, f32[384,2432]{1,0:T(8,128)}, u32[]{:S(2)}, u32[]{:S(2)}) collective-permute-start(f32[384,2432]{1,0:T(8,128)} %get-tuple-element.212), channel_id=1, source_target_pairs={{0,1},{1,0},{2,3},{3,2},{4,5},{5,4},{6,7},{7,6},{8,9},{9,8},{10,11... | collective-permute-start | bytes 11206664 | tf_op jit(solution)/shard_map/ppermute | solution.py:294
  241.1 30.5 %collective-permute-start.17 = (f32[96,4608]{1,0:T(8,128)}, f32[96,4608]{1,0:T(8,128)S(1)}, u32[]{:S(2)}, u32[]{:S(2)}) collective-permute-start(f32[96,4608]{1,0:T(8,128)} %dynamic-slice_add_fusion.3), channel_id=1, source_target_pairs={{0,2},{1,17},{2,0},{3,19},{4,6},{5,21},{6,4},{7,23},{8,10},{9,25},... | collective-permute-start | bytes 5308424 | tf_op jit(solution)/shard_map/ppermute | solution.py:294
  241.9 11.8 %collective-permute-start.14 = (f32[96,768]{1,0:T(8,128)S(1)}, f32[96,768]{1,0:T(8,128)S(1)}, u32[]{:S(2)}, u32[]{:S(2)}) collective-permute-start(f32[96,768]{1,0:T(8,128)S(1)} %add_add_fusion.2), channel_id=1, source_target_pairs={{0,12},{1,13},{2,14},{3,15},{4,8},{5,9},{6,10},{7,11},{8,4},{9,5},... | collective-permute-start | bytes 884744 | tf_op jit(solution)/shard_map/ppermute | solution.py:294
  244.0 25.5 %collective-permute-start.15 = (f32[96,768]{1,0:T(8,128)S(1)}, f32[96,768]{1,0:T(8,128)S(1)}, u32[]{:S(2)}, u32[]{:S(2)}) collective-permute-start(f32[96,768]{1,0:T(8,128)S(1)} %add_add_fusion.2), channel_id=1, source_target_pairs={{0,8},{1,9},{2,10},{3,11},{4,12},{5,13},{6,14},{7,15},{8,0},{9,1},... | collective-permute-start | bytes 884744 | tf_op jit(solution)/shard_map/ppermute | solution.py:294
  244.0 26.2 %collective-permute-start.16 = (f32[96,768]{1,0:T(8,128)S(1)}, f32[96,768]{1,0:T(8,128)}, u32[]{:S(2)}, u32[]{:S(2)}) collective-permute-start(f32[96,768]{1,0:T(8,128)S(1)} %add_add_fusion.2), channel_id=1, source_target_pairs={{0,4},{1,5},{2,6},{3,7},{4,0},{5,1},{6,2},{7,3},{8,12},{9,13},{10,... | collective-permute-start | bytes 884744 | tf_op jit(solution)/shard_map/ppermute | solution.py:294
  271.6 13.1 %copy-start.10 = (f32[384,768]{1,0:T(8,128)}, f32[384,768]{1,0:T(8,128)S(1)}, u32[]{:S(2)}) copy-start(f32[384,768]{1,0:T(8,128)S(1)} %fusion.4.refs_0_) | copy-start | bytes 3538948
  271.6 4.4 copy-start.11
  278.9 40.0 %collective-permute-start.23 = (f32[192,2432]{1,0:T(8,128)}, f32[192,2432]{1,0:T(8,128)}, u32[]{:S(2)}, u32[]{:S(2)}) collective-permute-start(f32[192,2432]{1,0:T(8,128)} %dynamic-slice_add_fusion.2), channel_id=1, source_target_pairs={{0,16},{1,3},{2,18},{3,1},{4,20},{5,7},{6,22},{7,5},{8,24},{9,11},... | collective-permute-start | bytes 5603336 | tf_op jit(solution)/shard_map/ppermute | solution.py:294
  280.3 20.2 %collective-permute-start.20 = (f32[24,4608]{1,0:T(8,128)}, f32[24,4608]{1,0:T(8,128)}, u32[]{:S(2)}, u32[]{:S(2)}) collective-permute-start(f32[24,4608]{1,0:T(8,128)} %get-tuple-element.218), channel_id=1, source_target_pairs={{0,4},{1,5},{2,6},{3,7},{4,0},{5,1},{6,2},{7,3},{8,12},{9,13},{10,... | collective-permute-start | bytes 1327112 | tf_op jit(solution)/shard_map/ppermute | solution.py:294
  280.3 33.5 %collective-permute-start.21 = (f32[24,4608]{1,0:T(8,128)}, f32[24,4608]{1,0:T(8,128)}, u32[]{:S(2)}, u32[]{:S(2)}) collective-permute-start(f32[24,4608]{1,0:T(8,128)} %get-tuple-element.219), channel_id=1, source_target_pairs={{0,8},{1,9},{2,10},{3,11},{4,12},{5,13},{6,14},{7,15},{8,0},{9,1},... | collective-permute-start | bytes 1327112 | tf_op jit(solution)/shard_map/ppermute | solution.py:294
  283.5 30.3 %collective-permute-start.22 = (f32[24,4608]{1,0:T(8,128)S(1)}, f32[24,4608]{1,0:T(8,128)}, u32[]{:S(2)}, u32[]{:S(2)}) collective-permute-start(f32[24,4608]{1,0:T(8,128)S(1)} %get-tuple-element.220), channel_id=1, source_target_pairs={{0,12},{1,13},{2,14},{3,15},{4,8},{5,9},{6,10},{7,11},{8,4},{9,5},... | collective-permute-start | bytes 1327112 | tf_op jit(solution)/shard_map/ppermute | solution.py:294
  284.7 31.9 %collective-permute-start.19 = (f32[384,768]{1,0:T(8,128)S(1)}, f32[384,768]{1,0:T(8,128)}, u32[]{:S(2)}, u32[]{:S(2)}) collective-permute-start(f32[384,768]{1,0:T(8,128)S(1)} %fusion.4.refs_0_), channel_id=1, source_target_pairs={{0,2},{1,17},{2,0},{3,19},{4,6},{5,21},{6,4},{7,23},{8,10},{9,25},... | collective-permute-start | bytes 3538952 | tf_op jit(solution)/shard_map/ppermute | solution.py:294
  319.0 5.1 %copy-start.16 = (f32[24,4608]{1,0:T(8,128)S(1)}, f32[24,4608]{1,0:T(8,128)}, u32[]{:S(2)}) copy-start(f32[24,4608]{1,0:T(8,128)} %add_add_fusion.1) | copy-start | bytes 1327108
  322.0 45.8 %collective-permute-start.24 = (f32[768,768]{1,0:T(8,128)S(1)}, f32[768,768]{1,0:T(8,128)}, u32[]{:S(2)}, u32[]{:S(2)}) collective-permute-start(f32[768,768]{1,0:T(8,128)S(1)} %copy-done.5), channel_id=1, source_target_pairs={{0,16},{1,3},{2,18},{3,1},{4,20},{5,7},{6,22},{7,5},{8,24},{9,11},... | collective-permute-start | bytes 7077896 | tf_op jit(solution)/shard_map/ppermute | solution.py:294
  322.6 42.9 %collective-permute-start.28 = (f32[96,2432]{1,0:T(8,128)}, f32[96,2432]{1,0:T(8,128)}, u32[]{:S(2)}, u32[]{:S(2)}) collective-permute-start(f32[96,2432]{1,0:T(8,128)} %dynamic-slice_add_fusion.5), channel_id=1, source_target_pairs={{0,2},{1,17},{2,0},{3,19},{4,6},{5,21},{6,4},{7,23},{8,10},{9,25},... | collective-permute-start | bytes 2801672 | tf_op jit(solution)/shard_map/ppermute | solution.py:294
  324.1 12.9 %collective-permute-start.25 = (f32[24,4608]{1,0:T(8,128)S(1)}, f32[24,4608]{1,0:T(8,128)S(1)}, u32[]{:S(2)}, u32[]{:S(2)}) collective-permute-start(f32[24,4608]{1,0:T(8,128)S(1)} %copy-done.16), channel_id=1, source_target_pairs={{0,12},{1,13},{2,14},{3,15},{4,8},{5,9},{6,10},{7,11},{8,4},{9,5},... | collective-permute-start | bytes 1327112 | tf_op jit(solution)/shard_map/ppermute | solution.py:294
  326.3 36.4 %collective-permute-start.26 = (f32[24,4608]{1,0:T(8,128)S(1)}, f32[24,4608]{1,0:T(8,128)}, u32[]{:S(2)}, u32[]{:S(2)}) collective-permute-start(f32[24,4608]{1,0:T(8,128)S(1)} %copy-done.16), channel_id=1, source_target_pairs={{0,8},{1,9},{2,10},{3,11},{4,12},{5,13},{6,14},{7,15},{8,0},{9,1},... | collective-permute-start | bytes 1327112 | tf_op jit(solution)/shard_map/ppermute | solution.py:294
  333.7 29.0 %collective-permute-start.27 = (f32[24,4608]{1,0:T(8,128)S(1)}, f32[24,4608]{1,0:T(8,128)}, u32[]{:S(2)}, u32[]{:S(2)}) collective-permute-start(f32[24,4608]{1,0:T(8,128)S(1)} %copy-done.16), channel_id=1, source_target_pairs={{0,4},{1,5},{2,6},{3,7},{4,0},{5,1},{6,2},{7,3},{8,12},{9,13},{10,... | collective-permute-start | bytes 1327112 | tf_op jit(solution)/shard_map/ppermute | solution.py:294
  370.8 49.9 %collective-permute-start.34 = (f32[1536,768]{1,0:T(8,128)}, f32[1536,768]{1,0:T(8,128)}, u32[]{:S(2)}, u32[]{:S(2)}) collective-permute-start(f32[1536,768]{1,0:T(8,128)} %put.21.refs_0_), channel_id=1, source_target_pairs={{0,1},{1,0},{2,3},{3,2},{4,5},{5,4},{6,7},{7,6},{8,9},{9,8},{10,11... | collective-permute-start | bytes 14155784 | tf_op jit(solution)/shard_map/ppermute | solution.py:294
  370.8 22.6 %collective-permute-start.29 = (f32[96,4608]{1,0:T(8,128)S(1)}, f32[96,4608]{1,0:T(8,128)}, u32[]{:S(2)}, u32[]{:S(2)}) collective-permute-start(f32[96,4608]{1,0:T(8,128)S(1)} %copy-done.8), channel_id=1, source_target_pairs={{0,2},{1,17},{2,0},{3,19},{4,6},{5,21},{6,4},{7,23},{8,10},{9,25},... | collective-permute-start | bytes 5308424 | tf_op jit(solution)/shard_map/ppermute | solution.py:294
  371.3 12.5 %collective-permute-start.30 = (f32[24,2432]{1,0:T(8,128)S(1)}, f32[24,2432]{1,0:T(8,128)S(1)}, u32[]{:S(2)}, u32[]{:S(2)}) collective-permute-start(f32[24,2432]{1,0:T(8,128)S(1)} %get-tuple-element.235), channel_id=1, source_target_pairs={{0,4},{1,5},{2,6},{3,7},{4,0},{5,1},{6,2},{7,3},{8,12},{9,13},{10,... | collective-permute-start | bytes 700424 | tf_op jit(solution)/shard_map/ppermute | solution.py:294
  371.3 19.6 %collective-permute-start.31 = (f32[24,2432]{1,0:T(8,128)S(1)}, f32[24,2432]{1,0:T(8,128)S(1)}, u32[]{:S(2)}, u32[]{:S(2)}) collective-permute-start(f32[24,2432]{1,0:T(8,128)S(1)} %get-tuple-element.236), channel_id=1, source_target_pairs={{0,8},{1,9},{2,10},{3,11},{4,12},{5,13},{6,14},{7,15},{8,0},{9,1},... | collective-permute-start | bytes 700424 | tf_op jit(solution)/shard_map/ppermute | solution.py:294
  374.3 16.6 %collective-permute-start.32 = (f32[24,2432]{1,0:T(8,128)S(1)}, f32[24,2432]{1,0:T(8,128)S(1)}, u32[]{:S(2)}, u32[]{:S(2)}) collective-permute-start(f32[24,2432]{1,0:T(8,128)S(1)} %get-tuple-element.237), channel_id=1, source_target_pairs={{0,12},{1,13},{2,14},{3,15},{4,8},{5,9},{6,10},{7,11},{8,4},{9,5},... | collective-permute-start | bytes 700424 | tf_op jit(solution)/shard_map/ppermute | solution.py:294
  395.8 50.7 %collective-permute-start.33 = (f32[192,4608]{1,0:T(8,128)}, f32[192,4608]{1,0:T(8,128)}, u32[]{:S(2)}, u32[]{:S(2)}) collective-permute-start(f32[192,4608]{1,0:T(8,128)} %put.23.refs_0_), channel_id=1, source_target_pairs={{0,16},{1,3},{2,18},{3,1},{4,20},{5,7},{6,22},{7,5},{8,24},{9,11},... | collective-permute-start | bytes 10616840 | tf_op jit(solution)/shard_map/ppermute | solution.py:294
  396.5 9.5 %collective-permute-start.35 = (f32[24,2432]{1,0:T(8,128)S(1)}, f32[24,2432]{1,0:T(8,128)S(1)}, u32[]{:S(2)}, u32[]{:S(2)}) collective-permute-start(f32[24,2432]{1,0:T(8,128)S(1)} %add_add_fusion.3), channel_id=1, source_target_pairs={{0,12},{1,13},{2,14},{3,15},{4,8},{5,9},{6,10},{7,11},{8,4},{9,5},... | collective-permute-start | bytes 700424 | tf_op jit(solution)/shard_map/ppermute | solution.py:294
  398.8 21.3 %collective-permute-start.36 = (f32[24,2432]{1,0:T(8,128)S(1)}, f32[24,2432]{1,0:T(8,128)S(1)}, u32[]{:S(2)}, u32[]{:S(2)}) collective-permute-start(f32[24,2432]{1,0:T(8,128)S(1)} %add_add_fusion.3), channel_id=1, source_target_pairs={{0,8},{1,9},{2,10},{3,11},{4,12},{5,13},{6,14},{7,15},{8,0},{9,1},... | collective-permute-start | bytes 700424 | tf_op jit(solution)/shard_map/ppermute | solution.py:294
  402.5 17.7 %collective-permute-start.37 = (f32[24,2432]{1,0:T(8,128)S(1)}, f32[24,2432]{1,0:T(8,128)S(1)}, u32[]{:S(2)}, u32[]{:S(2)}) collective-permute-start(f32[24,2432]{1,0:T(8,128)S(1)} %add_add_fusion.3), channel_id=1, source_target_pairs={{0,4},{1,5},{2,6},{3,7},{4,0},{5,1},{6,2},{7,3},{8,12},{9,13},{10,... | collective-permute-start | bytes 700424 | tf_op jit(solution)/shard_map/ppermute | solution.py:294
  420.6 5.4 %copy-start.12 = (f32[96,2432]{1,0:T(8,128)}, f32[96,2432]{1,0:T(8,128)S(1)}, u32[]{:S(2)}) copy-start(f32[96,2432]{1,0:T(8,128)S(1)} %fusion.9.refs_0_) | copy-start | bytes 2801668
  426.0 24.9 %collective-permute-start.38 = (f32[96,2432]{1,0:T(8,128)S(1)}, f32[96,2432]{1,0:T(8,128)S(1)}, u32[]{:S(2)}, u32[]{:S(2)}) collective-permute-start(f32[96,2432]{1,0:T(8,128)S(1)} %fusion.9.refs_0_), channel_id=1, source_target_pairs={{0,2},{1,17},{2,0},{3,19},{4,6},{5,21},{6,4},{7,23},{8,10},{9,25},... | collective-permute-start | bytes 2801672 | tf_op jit(solution)/shard_map/ppermute | solution.py:294
  454.0 11.6 %collective-permute-start.39 = (f32[384,4608]{1,0:T(8,128)}, f32[384,4608]{1,0:T(8,128)}, u32[]{:S(2)}, u32[]{:S(2)}) collective-permute-start(f32[384,4608]{1,0:T(8,128)} %put.26.refs_0_), channel_id=1, source_target_pairs={{0,1},{1,0},{2,3},{3,2},{4,5},{5,4},{6,7},{7,6},{8,9},{9,8},{10,11... | collective-permute-start | bytes 21233672 | tf_op jit(solution)/shard_map/ppermute | solution.py:294
  454.0 23.8 %collective-permute-start.40 = (f32[192,2432]{1,0:T(8,128)}, f32[192,2432]{1,0:T(8,128)S(1)}, u32[]{:S(2)}, u32[]{:S(2)}) collective-permute-start(f32[192,2432]{1,0:T(8,128)} %put.29.refs_0_), channel_id=1, source_target_pairs={{0,16},{1,3},{2,18},{3,1},{4,20},{5,7},{6,22},{7,5},{8,24},{9,11},... | collective-permute-start | bytes 5603336 | tf_op jit(solution)/shard_map/ppermute | solution.py:294
  473.8 7.8 %copy-start.15 = (f32[16,768]{1,0:T(8,128)S(1)}, f32[16,768]{1,0:T(8,128)}, u32[]{:S(2)}) copy-start(f32[16,768]{1,0:T(8,128)} %copy-done.14) | copy-start | bytes 147460
  481.6 6.8 %collective-permute-start.41 = (f32[384,2432]{1,0:T(8,128)}, f32[384,2432]{1,0:T(8,128)}, u32[]{:S(2)}, u32[]{:S(2)}) collective-permute-start(f32[384,2432]{1,0:T(8,128)} %put.33.refs_0_), channel_id=1, source_target_pairs={{0,1},{1,0},{2,3},{3,2},{4,5},{5,4},{6,7},{7,6},{8,9},{9,8},{10,11... | collective-permute-start | bytes 11206664 | tf_op jit(solution)/shard_map/ppermute | solution.py:294
  488.4 7.3 %copy-start.1 = (bf16[768,768]{1,0:T(8,128)(2,1)S(1)}, bf16[768,768]{1,0:T(8,128)(2,1)}, u32[]{:S(2)}) copy-start(bf16[768,768]{1,0:T(8,128)(2,1)} %param.25) | copy-start | bytes 3538948
  (11 other events, 19.5 us)

commit v7 on v6

--- a/solution.py
+++ b/solution.py
@@ -558,7 +558,7 @@
 def put(pieces, places, count, widths, before=()):
     rows, wide = pieces[0].shape
     splits = 1
-    while rows % (16 * splits) == 0 and rows // splits * wide > 320 * 1024:
+    while splits < 4 and rows % (16 * splits) == 0 and rows // splits * wide > 320 * 1024:
         splits *= 2
     block = rows // splits
     number, kept = len(pieces), len(before)

time: 507 us -> 506 us (level)
  no operation moved by 1% of the time
where the time goes in v7:
time: 506 us; the launch traced here: 497 us
  Pallas kernels  211 us (42%)
  waiting for transfers between devices  136 us (27%)
  starting transfers between devices  54.2 us (11%)
  other arithmetic  48.1 us (10%)
  matrix products  25.1 us (5%)
  local copies, waits for them, and re-layouts  19.1 us (4%)
    ppermute x42, waiting for transfers between devices, send_by(): lax.ppermute(value, AXES, [(i, i ^ masks[i & 1]) for i in range(self.size)])  136 us
    pallas_call x18, Pallas kernels, put(): pl.pallas_call(kernel, name='put', grid_spec=pltpu.PrefetchScalarGridSpec...  65.6 us
    ppermute x42, starting transfers between devices, send_by(): lax.ppermute(value, AXES, [(i, i ^ masks[i & 1]) for i in range(self.size)])  54.2 us
    pallas_call x3, Pallas kernels, attention_grads(): pl.pallas_call(kernel, name='attention_backward', grid=(count, micro_coun...  44.8 us
    pallas_call x3, Pallas kernels, weight_grads(): pl.pallas_call(kernel, name='weight_grads', grid_spec=pltpu.PrefetchScala...  35 us
    add x12, other arithmetic, total(): value = term if value is None else value + term  34.7 us
    pallas_call x1, Pallas kernels, attention(): pl.pallas_call(lambda *refs: forward_kernel(head_dim, *refs), name='atten...  23.1 us
    pallas_call x1, Pallas kernels, feed_backward(): pl.pallas_call(feed_backward_kernel, name='feed_backward', grid=(rows //...  22.3 us
  transfers between devices with their start and end apart: 42, of which 19 were waited for; matrix products, arithmetic and copies ran while one was open for 5% of the time, Pallas kernels for 32%

profile of v7, /device:TPU:0, one launch (start us, length us, event | category | flops | bytes accessed | tf_op | source)
XLA Modules:
  0.0 497.3 jit_solution(11195051220821042151)
XLA Ops:
  6.9 7.6 %project.1 = (bf16[1024,768]{1,0:T(8,128)(2,1)}, bf16[1024,768]{1,0:T(8,128)(2,1)}, bf16[1024,768]{1,0:T(8,128)(2,1)}, bf16[1024,768]{1,0:T(8,128)(2,1)}) custom-call(bf16[1024,768]{1,0:T(8,128)(2,1)} %bitcast.198, f32[1,768]{1,0:T(1,128)} %broadcast_in_dim.327.gain_ref, bf16[768,768]{1,0:T(8,128)(2,1)} %wq_ref.3, bf16[768,768]{1,0:T(8,128)(2,1)} %wk_ref.3, ...), custom_call_target="tpu_custom_call" | custom-call | tf_op jit(solution)/shard_map/project/pallas_call | solution.py:425
  14.5 23.1 %attention_forward.1.refs_1_.refs_4_ = bf16[1024,768]{1,0:T(8,128)(2,1)} custom-call(bf16[1024,768]{1,0:T(8,128)(2,1)} %get-tuple-element.179.refs_0_, bf16[1024,768]{1,0:T(8,128)(2,1)} %get-tuple-element.142.refs_1_, bf16[1024,768]{1,0:T(8,128)(2,1)} %get-tuple-element.143.refs_2_, s32[1024,1]{1,0:T(8,128)} %bitcast.190, ...), custom_call_target="tpu_custom_call" | custom-call | tf_op jit(solution)/shard_map/attention_forward/pallas_call | solution.py:199
  37.6 3.3 multiply_reduce_fusion.2
  41.3 10.0 %maximum_convert_fusion.refs_0_.refs_1_.act_ref = bf16[1024,3072]{1,0:T(8,128)(2,1)S(1)} fusion(bf16[1024,768]{1,0:T(8,128)(2,1)S(1)} %multiply_convert_fusion.refs_0_.refs_3_, bf16[768,3072]{1,0:T(8,128)(2,1)} %win_ref.1), kind=kOutput, calls=%fused_computation | convolution fusion | flops 4838129664 | bytes 12582912 | tf_op jit(solution)/shard_map/dot_general | solution.py:47
  51.4 5.2 %multiply_reduce_fusion.1 = (f32[1024]{0:T(1024)S(1)}, f32[1024,768]{1,0:T(8,128)S(1)}) fusion(f32[1024,768]{1,0:T(8,128)S(1)} %get-tuple-element.323.hid_ref, bf16[1024,3072]{1,0:T(8,128)(2,1)S(1)} %maximum_convert_fusion.refs_0_.refs_1_.act_ref, bf16[3072,768]{1,0:T(8,128)(2,1)S(1)} %bitcast.202), kind=kOutput, calls=%fused_computation.7 | convolution fusion | flops 4834196480 | bytes 17305600 | tf_op jit(solution)/shard_map/dot_general | solution.py:47
  60.5 5.1 %collective-permute-start = (f32[16,768]{1,0:T(8,128)S(1)}, f32[16,768]{1,0:T(8,128)S(1)}, u32[]{:S(2)}, u32[]{:S(2)}) collective-permute-start(f32[16,768]{1,0:T(8,128)S(1)} %broadcast_multiply_fusion), channel_id=1, source_target_pairs={{0,12},{1,13},{2,14},{3,15},{4,8},{5,9},{6,10},{7,11},{8,4},{9,5},... | collective-permute-start | bytes 147464 | tf_op jit(solution)/shard_map/ppermute | solution.py:294
  67.7 2.9 collective-permute-done.1
  72.3 4.1 collective-permute-done.3
  78.3 6.2 %collective-permute-done.4 = f32[128,768]{1,0:T(8,128)S(1)} collective-permute-done((f32[128,768]{1,0:T(8,128)S(1)}, f32[128,768]{1,0:T(8,128)S(1)}, u32[]{:S(2)}, u32[]{:S(2)}) %collective-permute-start.4) | collective-permute-done | bytes 393248 | tf_op jit(solution)/shard_map/ppermute | solution.py:294
  94.1 2.9 fusion.57
  97.0 10.0 %weight_grads.3 = (f32[1536,768]{1,0:T(8,128)}, f32[1536,768]{1,0:T(8,128)}) custom-call(s32[1]{0:T(128)} %bitcast.43.bit_ref.places_ref, bf16[1024,3072]{1,0:T(8,128)(2,1)} %copy-done.2, bf16[1024,3072]{1,0:T(8,128)(2,1)} %copy-done.2, bf16[1024,768]{1,0:T(8,128)(2,1)} %get-tuple-element.302.refs_2_), custom_call_target="tpu_custom_call" | custom-call | tf_op jit(solution)/shard_map/weight_grads/pallas_call | solution.py:374
  107.8 22.3 %feed_backward.1 = (bf16[1024,3072]{1,0:T(8,128)(2,1)}, f32[1024,768]{1,0:T(8,128)}, bf16[1024,768]{1,0:T(8,128)(2,1)}, bf16[1024,768]{1,0:T(8,128)(2,1)}, f32[1,768]{1,0:T(1,128)}) custom-call(f32[1024,768]{1,0:T(8,128)} %get-tuple-element.146.go_ref, bf16[1024,3072]{1,0:T(8,128)(2,1)} %copy-done.2, f32[1024,768]{1,0:T(8,128)} %copy-done.7, ...), custom_call_target="tpu_custom_call" | custom-call | tf_op jit(solution)/shard_map/feed_backward/pallas_call | solution.py:534
  130.1 2.7 dynamic-slice_add_fusion.1
  135.4 14.2 %weight_grads.4 = (f32[384,4608]{1,0:T(8,128)}, f32[384,4608]{1,0:T(8,128)}) custom-call(s32[1]{0:T(128)} %bitcast.43.bit_ref.places_ref, bf16[1024,768]{1,0:T(8,128)(2,1)} %copy-done.6, bf16[1024,768]{1,0:T(8,128)(2,1)} %attention_forward.1.refs_1_.refs_4_, bf16[16,768]{1,0:T(8,128)(2,1)} %copy-done.18, bf16[1024,768]{1,0:T(8,128)(2,1)} %copy-done.6, ...), custom_call_target="tpu_custom_call" | custom-call | tf_op jit(solution)/shard_map/weight_grads/pallas_call | solution.py:374
  149.6 15.0 %attention_backward.3 = (bf16[1024,768]{1,0:T(8,128)(2,1)}, bf16[1024,768]{1,0:T(8,128)(2,1)}, bf16[1024,768]{1,0:T(8,128)(2,1)}, f32[12,1,1024]{2,1,0:T(1,128)}) custom-call(bf16[1024,768]{1,0:T(8,128)(2,1)} %get-tuple-element.179.refs_0_, bf16[1024,768]{1,0:T(8,128)(2,1)} %get-tuple-element.142.refs_1_, bf16[1024,768]{1,0:T(8,128)(2,1)} %get-tuple-element.143.refs_2_, ...), custom_call_target="tpu_custom_call" | custom-call | tf_op jit(solution)/shard_map/attention_backward/pallas_call | solution.py:224
  164.7 2.2 dynamic-slice_add_fusion.4
  168.6 14.9 %attention_backward.4 = (bf16[1024,768]{1,0:T(8,128)(2,1)}, bf16[1024,768]{1,0:T(8,128)(2,1)}, bf16[1024,768]{1,0:T(8,128)(2,1)}, f32[12,1,1024]{2,1,0:T(1,128)}) custom-call(bf16[1024,768]{1,0:T(8,128)(2,1)} %get-tuple-element.179.refs_0_, ...), custom_call_target="tpu_custom_call", output_to_operand_aliasing={{0}: (7, {}), {1}: (8, {}), {2}: (9, {}), {3}: (10, {})} | custom-call | tf_op jit(solution)/shard_map/attention_backward/pallas_call | solution.py:224
  185.5 5.4 %dynamic-slice_add_fusion = f32[192,4608]{1,0:T(8,128)} fusion(f32[384,4608]{1,0:T(8,128)} %collective-permute-done.9, s32[]{:T(128)S(6)} %select_n.442, f32[384,4608]{1,0:T(8,128)} %get-tuple-element.214), kind=kLoop, calls=%fused_computation.2 | loop fusion | flops 884736 | bytes 10616836 | tf_op jit(solution)/shard_map/add | solution.py:659
  197.8 14.9 %attention_backward.5 = (bf16[1024,768]{1,0:T(8,128)(2,1)}, bf16[1024,768]{1,0:T(8,128)(2,1)}, bf16[1024,768]{1,0:T(8,128)(2,1)}, f32[12,1,1024]{2,1,0:T(1,128)}) custom-call(bf16[1024,768]{1,0:T(8,128)(2,1)} %get-tuple-element.179.refs_0_, ...), custom_call_target="tpu_custom_call", output_to_operand_aliasing={{0}: (7, {}), {1}: (8, {}), {2}: (9, {}), {3}: (10, {})} | custom-call | tf_op jit(solution)/shard_map/attention_backward/pallas_call | solution.py:224
  212.7 10.2 %project_backward.1 = (f32[1024,768]{1,0:T(8,128)}, f32[1,768]{1,0:T(1,128)}) custom-call(bf16[1024,768]{1,0:T(8,128)(2,1)} %get-tuple-element.184.gq_ref.refs_6_, bf16[1024,768]{1,0:T(8,128)(2,1)} %get-tuple-element.185.gk_ref.refs_7_, bf16[1024,768]{1,0:T(8,128)(2,1)} %get-tuple-element.186.gv_ref.refs_8_, f32[1024,768]{1,0:T(8,128)} %get-tuple-element.187.gh_ref, ...), custom_call_target="tpu_custom_call" | custom-call | tf_op jit(solution)/shard_map/project_backward/pallas_call | solution.py:501
  224.8 10.8 %weight_grads.5 = (f32[384,2432]{1,0:T(8,128)}, f32[384,2432]{1,0:T(8,128)}) custom-call(s32[1]{0:T(128)} %bitcast.43.bit_ref.places_ref, bf16[1024,768]{1,0:T(8,128)(2,1)} %get-tuple-element.199.refs_0_.refs_1_.refs_2_.refs_3_.refs_4_.refs_5_, bf16[1024,768]{1,0:T(8,128)(2,1)} %get-tuple-element.199.refs_0_.refs_1_.refs_2_.refs_3_.refs_4_.refs_5_, ...), custom_call_target="tpu_custom_call" | custom-call | tf_op jit(solution)/shard_map/weight_grads/pallas_call | solution.py:374
  236.9 4.2 dynamic-slice_add_fusion.3
  244.0 2.3 collective-permute-start.16
  248.3 5.4 %collective-permute-done.14 = f32[96,768]{1,0:T(8,128)S(1)} collective-permute-done((f32[96,768]{1,0:T(8,128)S(1)}, f32[96,768]{1,0:T(8,128)S(1)}, u32[]{:S(2)}, u32[]{:S(2)}) %collective-permute-start.14) | collective-permute-done | bytes 294944 | tf_op jit(solution)/shard_map/ppermute | solution.py:294
  253.7 15.8 %collective-permute-done.15 = f32[96,768]{1,0:T(8,128)S(1)} collective-permute-done((f32[96,768]{1,0:T(8,128)S(1)}, f32[96,768]{1,0:T(8,128)S(1)}, u32[]{:S(2)}, u32[]{:S(2)}) %collective-permute-start.15) | collective-permute-done | bytes 294944 | tf_op jit(solution)/shard_map/ppermute | solution.py:294
  271.6 4.4 dynamic-slice_add_fusion.6
  276.0 2.9 dynamic-slice_add_fusion.2
  280.3 3.2 collective-permute-start.21
  285.3 2.4 put.18.refs_1_
  287.6 12.9 %collective-permute-done.20 = f32[24,4608]{1,0:T(8,128)} collective-permute-done((f32[24,4608]{1,0:T(8,128)}, f32[24,4608]{1,0:T(8,128)}, u32[]{:S(2)}, u32[]{:S(2)}) %collective-permute-start.20) | collective-permute-done | bytes 442400 | tf_op jit(solution)/shard_map/ppermute | solution.py:294
  300.5 13.3 %collective-permute-done.21 = f32[24,4608]{1,0:T(8,128)} collective-permute-done((f32[24,4608]{1,0:T(8,128)}, f32[24,4608]{1,0:T(8,128)}, u32[]{:S(2)}, u32[]{:S(2)}) %collective-permute-start.21) | collective-permute-done | bytes 442400 | tf_op jit(solution)/shard_map/ppermute | solution.py:294
  313.8 2.8 add_add_fusion.1
  316.6 2.4 put.19.refs_0_
  319.0 3.1 dynamic-slice_add_fusion.5
  324.1 2.2 collective-permute-start.25
  326.3 7.5 %collective-permute-start.26 = (f32[24,4608]{1,0:T(8,128)S(1)}, f32[24,4608]{1,0:T(8,128)}, u32[]{:S(2)}, u32[]{:S(2)}) collective-permute-start(f32[24,4608]{1,0:T(8,128)S(1)} %copy-done.16), channel_id=1, source_target_pairs={{0,8},{1,9},{2,10},{3,11},{4,12},{5,13},{6,14},{7,15},{8,0},{9,1},... | collective-permute-start | bytes 1327112 | tf_op jit(solution)/shard_map/ppermute | solution.py:294
  334.2 2.8 put.20.refs_1_
  337.0 25.7 %collective-permute-done.26 = f32[24,4608]{1,0:T(8,128)} collective-permute-done((f32[24,4608]{1,0:T(8,128)S(1)}, f32[24,4608]{1,0:T(8,128)}, u32[]{:S(2)}, u32[]{:S(2)}) %collective-permute-start.26) | collective-permute-done | bytes 442400 | tf_op jit(solution)/shard_map/ppermute | solution.py:294
  362.7 2.8 fusion.2.refs_0_
  365.5 2.3 dynamic-slice_add_fusion.12
  367.8 2.9 put.21.refs_0_
  371.3 3.0 collective-permute-start.31
  375.7 5.0 %put.24.refs_1_ = f32[3072,768]{1,0:T(8,128)} custom-call(s32[1]{0:T(128)} %bitcast.43.bit_ref.places_ref, f32[1536,768]{1,0:T(8,128)} %put.21.refs_0_), custom_call_target="tpu_custom_call" | custom-call | tf_op jit(solution)/shard_map/put/pallas_call | solution.py:584
  380.7 2.5 put.22.refs_1_
  383.8 7.0 %collective-permute-done.31 = f32[24,2432]{1,0:T(8,128)S(1)} collective-permute-done((f32[24,2432]{1,0:T(8,128)S(1)}, f32[24,2432]{1,0:T(8,128)S(1)}, u32[]{:S(2)}, u32[]{:S(2)}) %collective-permute-start.31) | collective-permute-done | bytes 233504 | tf_op jit(solution)/shard_map/ppermute | solution.py:294
  393.4 2.4 put.23.refs_0_
  396.5 2.3 collective-permute-start.35
  398.8 3.6 collective-permute-start.36
  402.5 3.6 collective-permute-done.35
  406.1 14.1 %collective-permute-done.36 = f32[24,2432]{1,0:T(8,128)S(1)} collective-permute-done((f32[24,2432]{1,0:T(8,128)S(1)}, f32[24,2432]{1,0:T(8,128)S(1)}, u32[]{:S(2)}, u32[]{:S(2)}) %collective-permute-start.36) | collective-permute-done | bytes 233504 | tf_op jit(solution)/shard_map/ppermute | solution.py:294
  420.6 5.4 %put.27 = f32[3072,768]{1,0:T(8,128)} custom-call(s32[1]{0:T(128)} %bitcast.46.places_ref, f32[1536,768]{1,0:T(8,128)} %collective-permute-done.34.refs_0_, f32[3072,768]{1,0:T(8,128)} %put.24.refs_1_), custom_call_target="tpu_custom_call", output_to_operand_aliasing={{}: (2, {})} | custom-call | tf_op jit(solution)/shard_map/put/pallas_call | solution.py:584
  427.5 4.4 put.25.refs_1_
  431.8 2.2 put.28.refs_1_
  434.0 12.5 %collective-permute-done.33.refs_0_ = f32[192,4608]{1,0:T(8,128)} collective-permute-done((f32[192,4608]{1,0:T(8,128)}, f32[192,4608]{1,0:T(8,128)}, u32[]{:S(2)}, u32[]{:S(2)}) %collective-permute-start.33) | collective-permute-done | bytes 3538976 | tf_op jit(solution)/shard_map/ppermute | solution.py:294
  446.5 4.4 put.26.refs_0_
  451.8 2.2 put.29.refs_0_
  454.0 6.4 %put.30 = (f32[768,3072]{1,0:T(8,128)}, f32[768,768]{1,0:T(8,128)}, f32[768,768]{1,0:T(8,128)}) custom-call(s32[1]{0:T(128)} %bitcast.43.bit_ref.places_ref, f32[384,4608]{1,0:T(8,128)} %put.26.refs_0_), custom_call_target="tpu_custom_call" | custom-call | tf_op jit(solution)/shard_map/put/pallas_call | solution.py:584
  460.4 2.5 put.32.refs_1_
  462.9 2.7 collective-permute-done.39.refs_0_
  465.6 6.4 %put.31 = (f32[768,3072]{1,0:T(8,128)}, f32[768,768]{1,0:T(8,128)}, f32[768,768]{1,0:T(8,128)}) custom-call(s32[1]{0:T(128)} %bitcast.46.places_ref, f32[384,4608]{1,0:T(8,128)} %collective-permute-done.39.refs_0_, f32[768,3072]{1,0:T(8,128)} %get-tuple-element.244.refs_1_, ...), custom_call_target="tpu_custom_call", output_to_operand_aliasing={{0}: (2, {}), {1}: (3, {}), {2}: (4, {})} | custom-call | tf_op jit(solution)/shard_map/put/pallas_call | solution.py:584
  472.0 5.8 %collective-permute-done.40.refs_0_ = f32[192,2432]{1,0:T(8,128)S(1)} collective-permute-done((f32[192,2432]{1,0:T(8,128)}, f32[192,2432]{1,0:T(8,128)S(1)}, u32[]{:S(2)}, u32[]{:S(2)}) %collective-permute-start.40) | collective-permute-done | bytes 1867808 | tf_op jit(solution)/shard_map/ppermute | solution.py:294
  479.0 2.5 put.33.refs_0_
  483.5 4.5 put.34
  488.4 4.5 put.35
  (223 shorter events, 69.2 us)
Async XLA Ops:
  0.6 59.4 %copy-start = (bf16[768,768]{1,0:T(8,128)(2,1)S(1)}, bf16[768,768]{1,0:T(8,128)(2,1)}, u32[]{:S(2)}) copy-start(bf16[768,768]{1,0:T(8,128)(2,1)} %param.25) | copy-start | bytes 3538948
  14.5 23.1 %copy-start.9 = (bf16[1,2,512,768]{3,2,1,0:T(8,128)(2,1)S(1)}, bf16[1,2,512,768]{3,2,1,0:T(8,128)(2,1)}, u32[]{:S(2)}) copy-start(bf16[1,2,512,768]{3,2,1,0:T(8,128)(2,1)} %param.15) | copy-start | bytes 4718596
  40.9 10.4 %copy-start.7 = (f32[1024,768]{1,0:T(8,128)}, f32[1024,768]{1,0:T(8,128)S(1)}, u32[]{:S(2)}) copy-start(f32[1024,768]{1,0:T(8,128)S(1)} %get-tuple-element.323.hid_ref) | copy-start | bytes 9437188
  40.9 10.4 %slice-start = ((s8[4718592]{0:T(1024)(128)(4,1)}), s8[4194304]{0:T(1024)(128)(4,1)S(1)}, s32[]{:S(2)}) async-start(s8[4718592]{0:T(1024)(128)(4,1)} %bitcast.201), calls=%async_computation | async-start | bytes 8388608
  41.3 10.0 %copy-start.6 = (bf16[1024,768]{1,0:T(8,128)(2,1)}, bf16[1024,768]{1,0:T(8,128)(2,1)S(1)}, u32[]{:S(2)}) copy-start(bf16[1024,768]{1,0:T(8,128)(2,1)S(1)} %multiply_convert_fusion.refs_0_.refs_3_) | copy-start | bytes 4718596
  41.3 10.0 %slice-start.1 = ((s8[4718592]{0:T(1024)(128)(4,1)}), s8[524288]{0:T(1024)(128)(4,1)S(1)}, s32[]{:S(2)}) async-start(s8[4718592]{0:T(1024)(128)(4,1)} %bitcast.201), calls=%async_computation.1 | async-start | bytes 1048576
  51.3 5.3 %copy-start.2 = (bf16[1024,3072]{1,0:T(8,128)(2,1)}, bf16[1024,3072]{1,0:T(8,128)(2,1)S(1)}, u32[]{:S(2)}) copy-start(bf16[1024,3072]{1,0:T(8,128)(2,1)S(1)} %maximum_convert_fusion.refs_0_.refs_1_.act_ref) | copy-start | bytes 18874372
  51.3 5.3 %copy-start.24 = (s32[1,2,8]{2,1,0:T(2,128)S(1)}, s32[1,2,8]{2,1,0:T(2,128)}, u32[]{:S(2)}) copy-start(s32[1,2,8]{2,1,0:T(2,128)} %param.17) | copy-start | bytes 196
  51.3 5.3 %copy-start.22 = (f32[768]{0:T(1024)S(1)}, f32[768]{0:T(1024)}, u32[]{:S(2)}) copy-start(f32[768]{0:T(1024)} %param.28) | copy-start | bytes 9220
  58.3 19.9 %copy-start.25 = (s32[2,128]{1,0:T(2,128)S(1)}, s32[2,128]{1,0:T(2,128)}, u32[]{:S(2)}) copy-start(s32[2,128]{1,0:T(2,128)} %param.18) | copy-start | bytes 3076
  60.4 30.2 %copy-start.14 = (f32[16,768]{1,0:T(8,128)}, f32[16,768]{1,0:T(8,128)S(1)}, u32[]{:S(2)}) copy-start(f32[16,768]{1,0:T(8,128)S(1)} %get-tuple-element.327) | copy-start | bytes 147460
  60.5 7.2 %collective-permute-start = (f32[16,768]{1,0:T(8,128)S(1)}, f32[16,768]{1,0:T(8,128)S(1)}, u32[]{:S(2)}, u32[]{:S(2)}) collective-permute-start(f32[16,768]{1,0:T(8,128)S(1)} %broadcast_multiply_fusion), channel_id=1, source_target_pairs={{0,12},{1,13},{2,14},{3,15},{4,8},{5,9},{6,10},{7,11},{8,4},{9,5},... | collective-permute-start | bytes 147464 | tf_op jit(solution)/shard_map/ppermute | solution.py:294
  65.6 5.0 %collective-permute-start.1 = (f32[16,768]{1,0:T(8,128)S(1)}, f32[16,768]{1,0:T(8,128)S(1)}, u32[]{:S(2)}, u32[]{:S(2)}) collective-permute-start(f32[16,768]{1,0:T(8,128)S(1)} %broadcast_multiply_fusion), channel_id=1, source_target_pairs={{0,8},{1,9},{2,10},{3,11},{4,12},{5,13},{6,14},{7,15},{8,0},{9,1},... | collective-permute-start | bytes 147464 | tf_op jit(solution)/shard_map/ppermute | solution.py:294
  65.6 5.0 %collective-permute-start.2 = (f32[16,768]{1,0:T(8,128)S(1)}, f32[16,768]{1,0:T(8,128)S(1)}, u32[]{:S(2)}, u32[]{:S(2)}) collective-permute-start(f32[16,768]{1,0:T(8,128)S(1)} %broadcast_multiply_fusion), channel_id=1, source_target_pairs={{0,4},{1,5},{2,6},{3,7},{4,0},{5,1},{6,2},{7,3},{8,12},{9,13},{10,... | collective-permute-start | bytes 147464 | tf_op jit(solution)/shard_map/ppermute | solution.py:294
  66.3 18.5 %copy-start.26 = (pred[4]{0:T(512)(128)(4,1)}, pred[4]{0:T(512)(128)(4,1)S(1)}, u32[]{:S(2)}) copy-start(pred[4]{0:T(512)(128)(4,1)S(1)} %get-tuple-element.334) | copy-start | bytes 16
  66.3 18.5 %copy-start.28 = (pred[4]{0:T(512)(128)(4,1)}, pred[4]{0:T(512)(128)(4,1)S(1)}, u32[]{:S(2)}) copy-start(pred[4]{0:T(512)(128)(4,1)S(1)} %get-tuple-element.335) | copy-start | bytes 16
  70.7 5.7 %collective-permute-start.3 = (f32[64,768]{1,0:T(8,128)S(1)}, f32[64,768]{1,0:T(8,128)S(1)}, u32[]{:S(2)}, u32[]{:S(2)}) collective-permute-start(f32[64,768]{1,0:T(8,128)S(1)} %fusion.16), channel_id=1, source_target_pairs={{0,16},{1,3},{2,18},{3,1},{4,20},{5,7},{6,22},{7,5},{8,24},{9,11},... | collective-permute-start | bytes 589832 | tf_op jit(solution)/shard_map/ppermute | solution.py:294
  76.6 7.8 %collective-permute-start.4 = (f32[128,768]{1,0:T(8,128)S(1)}, f32[128,768]{1,0:T(8,128)S(1)}, u32[]{:S(2)}, u32[]{:S(2)}) collective-permute-start(f32[128,768]{1,0:T(8,128)S(1)} %bitcast_select_fusion.6), channel_id=1, source_target_pairs={{0,2},{1,17},{2,0},{3,19},{4,6},{5,21},{6,4},{7,23},{8,10},{9,25},... | collective-permute-start | bytes 1179656 | tf_op jit(solution)/shard_map/ppermute | solution.py:294
  84.6 2.4 collective-permute-start.5
  107.0 23.0 %collective-permute-start.6 = (f32[1536,768]{1,0:T(8,128)}, f32[1536,768]{1,0:T(8,128)}, u32[]{:S(2)}, u32[]{:S(2)}) collective-permute-start(f32[1536,768]{1,0:T(8,128)} %get-tuple-element.151), channel_id=1, source_target_pairs={{0,1},{1,0},{2,3},{3,2},{4,5},{5,4},{6,7},{7,6},{8,9},{9,8},{10,11... | collective-permute-start | bytes 14155784 | tf_op jit(solution)/shard_map/ppermute | solution.py:294
  130.0 4.2 copy-start.30
  132.7 32.0 %collective-permute-start.7 = (f32[768,768]{1,0:T(8,128)S(1)}, f32[768,768]{1,0:T(8,128)}, u32[]{:S(2)}, u32[]{:S(2)}) collective-permute-start(f32[768,768]{1,0:T(8,128)S(1)} %dynamic-slice_add_fusion.1), channel_id=1, source_target_pairs={{0,16},{1,3},{2,18},{3,1},{4,20},{5,7},{6,22},{7,5},{8,24},{9,11},... | collective-permute-start | bytes 7077896 | tf_op jit(solution)/shard_map/ppermute | solution.py:294
  166.9 18.6 %collective-permute-start.9 = (f32[384,4608]{1,0:T(8,128)}, f32[384,4608]{1,0:T(8,128)}, u32[]{:S(2)}, u32[]{:S(2)}) collective-permute-start(f32[384,4608]{1,0:T(8,128)} %get-tuple-element.178), channel_id=1, source_target_pairs={{0,1},{1,0},{2,3},{3,2},{4,5},{5,4},{6,7},{7,6},{8,9},{9,8},{10,11... | collective-permute-start | bytes 21233672 | tf_op jit(solution)/shard_map/ppermute | solution.py:294
  167.1 16.3 %collective-permute-start.8 = (f32[384,768]{1,0:T(8,128)S(1)}, f32[384,768]{1,0:T(8,128)S(1)}, u32[]{:S(2)}, u32[]{:S(2)}) collective-permute-start(f32[384,768]{1,0:T(8,128)S(1)} %dynamic-slice_add_fusion.4), channel_id=1, source_target_pairs={{0,2},{1,17},{2,0},{3,19},{4,6},{5,21},{6,4},{7,23},{8,10},{9,25},... | collective-permute-start | bytes 3538952 | tf_op jit(solution)/shard_map/ppermute | solution.py:294
  190.9 46.0 %collective-permute-start.13 = (f32[192,4608]{1,0:T(8,128)}, f32[192,4608]{1,0:T(8,128)}, u32[]{:S(2)}, u32[]{:S(2)}) collective-permute-start(f32[192,4608]{1,0:T(8,128)} %dynamic-slice_add_fusion), channel_id=1, source_target_pairs={{0,16},{1,3},{2,18},{3,1},{4,20},{5,7},{6,22},{7,5},{8,24},{9,11},... | collective-permute-start | bytes 10616840 | tf_op jit(solution)/shard_map/ppermute | solution.py:294
  192.2 43.4 %collective-permute-start.10 = (f32[96,768]{1,0:T(8,128)S(1)}, f32[96,768]{1,0:T(8,128)S(1)}, u32[]{:S(2)}, u32[]{:S(2)}) collective-permute-start(f32[96,768]{1,0:T(8,128)S(1)} %get-tuple-element.193), channel_id=1, source_target_pairs={{0,4},{1,5},{2,6},{3,7},{4,0},{5,1},{6,2},{7,3},{8,12},{9,13},{10,... | collective-permute-start | bytes 884744 | tf_op jit(solution)/shard_map/ppermute | solution.py:294
  192.9 42.7 %collective-permute-start.11 = (f32[96,768]{1,0:T(8,128)S(1)}, f32[96,768]{1,0:T(8,128)S(1)}, u32[]{:S(2)}, u32[]{:S(2)}) collective-permute-start(f32[96,768]{1,0:T(8,128)S(1)} %get-tuple-element.194), channel_id=1, source_target_pairs={{0,8},{1,9},{2,10},{3,11},{4,12},{5,13},{6,14},{7,15},{8,0},{9,1},... | collective-permute-start | bytes 884744 | tf_op jit(solution)/shard_map/ppermute | solution.py:294
  194.9 40.7 %collective-permute-start.12 = (f32[96,768]{1,0:T(8,128)S(1)}, f32[96,768]{1,0:T(8,128)S(1)}, u32[]{:S(2)}, u32[]{:S(2)}) collective-permute-start(f32[96,768]{1,0:T(8,128)S(1)} %get-tuple-element.195), channel_id=1, source_target_pairs={{0,12},{1,13},{2,14},{3,15},{4,8},{5,9},{6,10},{7,11},{8,4},{9,5},... | collective-permute-start | bytes 884744 | tf_op jit(solution)/shard_map/ppermute | solution.py:294
  236.9 9.4 %copy-start.29 = (pred[4]{0:T(512)(128)(4,1)S(1)}, pred[4]{0:T(512)(128)(4,1)}, u32[]{:S(2)}) copy-start(pred[4]{0:T(512)(128)(4,1)} %copy-done.28) | copy-start | bytes 16
  236.9 10.1 %copy-start.27 = (pred[4]{0:T(512)(128)(4,1)S(1)}, pred[4]{0:T(512)(128)(4,1)}, u32[]{:S(2)}) copy-start(pred[4]{0:T(512)(128)(4,1)} %copy-done.26) | copy-start | bytes 16
  241.1 34.8 %collective-permute-start.18 = (f32[384,2432]{1,0:T(8,128)}, f32[384,2432]{1,0:T(8,128)}, u32[]{:S(2)}, u32[]{:S(2)}) collective-permute-start(f32[384,2432]{1,0:T(8,128)} %get-tuple-element.212), channel_id=1, source_target_pairs={{0,1},{1,0},{2,3},{3,2},{4,5},{5,4},{6,7},{7,6},{8,9},{9,8},{10,11... | collective-permute-start | bytes 11206664 | tf_op jit(solution)/shard_map/ppermute | solution.py:294
  241.1 30.5 %collective-permute-start.17 = (f32[96,4608]{1,0:T(8,128)}, f32[96,4608]{1,0:T(8,128)S(1)}, u32[]{:S(2)}, u32[]{:S(2)}) collective-permute-start(f32[96,4608]{1,0:T(8,128)} %dynamic-slice_add_fusion.3), channel_id=1, source_target_pairs={{0,2},{1,17},{2,0},{3,19},{4,6},{5,21},{6,4},{7,23},{8,10},{9,25},... | collective-permute-start | bytes 5308424 | tf_op jit(solution)/shard_map/ppermute | solution.py:294
  241.9 11.8 %collective-permute-start.14 = (f32[96,768]{1,0:T(8,128)S(1)}, f32[96,768]{1,0:T(8,128)S(1)}, u32[]{:S(2)}, u32[]{:S(2)}) collective-permute-start(f32[96,768]{1,0:T(8,128)S(1)} %add_add_fusion.2), channel_id=1, source_target_pairs={{0,12},{1,13},{2,14},{3,15},{4,8},{5,9},{6,10},{7,11},{8,4},{9,5},... | collective-permute-start | bytes 884744 | tf_op jit(solution)/shard_map/ppermute | solution.py:294
  244.0 25.5 %collective-permute-start.15 = (f32[96,768]{1,0:T(8,128)S(1)}, f32[96,768]{1,0:T(8,128)S(1)}, u32[]{:S(2)}, u32[]{:S(2)}) collective-permute-start(f32[96,768]{1,0:T(8,128)S(1)} %add_add_fusion.2), channel_id=1, source_target_pairs={{0,8},{1,9},{2,10},{3,11},{4,12},{5,13},{6,14},{7,15},{8,0},{9,1},... | collective-permute-start | bytes 884744 | tf_op jit(solution)/shard_map/ppermute | solution.py:294
  244.0 26.2 %collective-permute-start.16 = (f32[96,768]{1,0:T(8,128)S(1)}, f32[96,768]{1,0:T(8,128)}, u32[]{:S(2)}, u32[]{:S(2)}) collective-permute-start(f32[96,768]{1,0:T(8,128)S(1)} %add_add_fusion.2), channel_id=1, source_target_pairs={{0,4},{1,5},{2,6},{3,7},{4,0},{5,1},{6,2},{7,3},{8,12},{9,13},{10,... | collective-permute-start | bytes 884744 | tf_op jit(solution)/shard_map/ppermute | solution.py:294
  271.6 13.1 %copy-start.10 = (f32[384,768]{1,0:T(8,128)}, f32[384,768]{1,0:T(8,128)S(1)}, u32[]{:S(2)}) copy-start(f32[384,768]{1,0:T(8,128)S(1)} %fusion.4.refs_0_) | copy-start | bytes 3538948
  271.6 4.4 copy-start.11
  278.9 40.0 %collective-permute-start.23 = (f32[192,2432]{1,0:T(8,128)}, f32[192,2432]{1,0:T(8,128)}, u32[]{:S(2)}, u32[]{:S(2)}) collective-permute-start(f32[192,2432]{1,0:T(8,128)} %dynamic-slice_add_fusion.2), channel_id=1, source_target_pairs={{0,16},{1,3},{2,18},{3,1},{4,20},{5,7},{6,22},{7,5},{8,24},{9,11},... | collective-permute-start | bytes 5603336 | tf_op jit(solution)/shard_map/ppermute | solution.py:294
  280.3 20.2 %collective-permute-start.20 = (f32[24,4608]{1,0:T(8,128)}, f32[24,4608]{1,0:T(8,128)}, u32[]{:S(2)}, u32[]{:S(2)}) collective-permute-start(f32[24,4608]{1,0:T(8,128)} %get-tuple-element.218), channel_id=1, source_target_pairs={{0,4},{1,5},{2,6},{3,7},{4,0},{5,1},{6,2},{7,3},{8,12},{9,13},{10,... | collective-permute-start | bytes 1327112 | tf_op jit(solution)/shard_map/ppermute | solution.py:294
  280.3 33.5 %collective-permute-start.21 = (f32[24,4608]{1,0:T(8,128)}, f32[24,4608]{1,0:T(8,128)}, u32[]{:S(2)}, u32[]{:S(2)}) collective-permute-start(f32[24,4608]{1,0:T(8,128)} %get-tuple-element.219), channel_id=1, source_target_pairs={{0,8},{1,9},{2,10},{3,11},{4,12},{5,13},{6,14},{7,15},{8,0},{9,1},... | collective-permute-start | bytes 1327112 | tf_op jit(solution)/shard_map/ppermute | solution.py:294
  283.5 30.3 %collective-permute-start.22 = (f32[24,4608]{1,0:T(8,128)S(1)}, f32[24,4608]{1,0:T(8,128)}, u32[]{:S(2)}, u32[]{:S(2)}) collective-permute-start(f32[24,4608]{1,0:T(8,128)S(1)} %get-tuple-element.220), channel_id=1, source_target_pairs={{0,12},{1,13},{2,14},{3,15},{4,8},{5,9},{6,10},{7,11},{8,4},{9,5},... | collective-permute-start | bytes 1327112 | tf_op jit(solution)/shard_map/ppermute | solution.py:294
  284.7 31.9 %collective-permute-start.19 = (f32[384,768]{1,0:T(8,128)S(1)}, f32[384,768]{1,0:T(8,128)}, u32[]{:S(2)}, u32[]{:S(2)}) collective-permute-start(f32[384,768]{1,0:T(8,128)S(1)} %fusion.4.refs_0_), channel_id=1, source_target_pairs={{0,2},{1,17},{2,0},{3,19},{4,6},{5,21},{6,4},{7,23},{8,10},{9,25},... | collective-permute-start | bytes 3538952 | tf_op jit(solution)/shard_map/ppermute | solution.py:294
  319.0 5.1 %copy-start.16 = (f32[24,4608]{1,0:T(8,128)S(1)}, f32[24,4608]{1,0:T(8,128)}, u32[]{:S(2)}) copy-start(f32[24,4608]{1,0:T(8,128)} %add_add_fusion.1) | copy-start | bytes 1327108
  322.0 45.8 %collective-permute-start.24 = (f32[768,768]{1,0:T(8,128)S(1)}, f32[768,768]{1,0:T(8,128)}, u32[]{:S(2)}, u32[]{:S(2)}) collective-permute-start(f32[768,768]{1,0:T(8,128)S(1)} %copy-done.5), channel_id=1, source_target_pairs={{0,16},{1,3},{2,18},{3,1},{4,20},{5,7},{6,22},{7,5},{8,24},{9,11},... | collective-permute-start | bytes 7077896 | tf_op jit(solution)/shard_map/ppermute | solution.py:294
  322.6 42.9 %collective-permute-start.28 = (f32[96,2432]{1,0:T(8,128)}, f32[96,2432]{1,0:T(8,128)}, u32[]{:S(2)}, u32[]{:S(2)}) collective-permute-start(f32[96,2432]{1,0:T(8,128)} %dynamic-slice_add_fusion.5), channel_id=1, source_target_pairs={{0,2},{1,17},{2,0},{3,19},{4,6},{5,21},{6,4},{7,23},{8,10},{9,25},... | collective-permute-start | bytes 2801672 | tf_op jit(solution)/shard_map/ppermute | solution.py:294
  324.1 12.9 %collective-permute-start.25 = (f32[24,4608]{1,0:T(8,128)S(1)}, f32[24,4608]{1,0:T(8,128)S(1)}, u32[]{:S(2)}, u32[]{:S(2)}) collective-permute-start(f32[24,4608]{1,0:T(8,128)S(1)} %copy-done.16), channel_id=1, source_target_pairs={{0,12},{1,13},{2,14},{3,15},{4,8},{5,9},{6,10},{7,11},{8,4},{9,5},... | collective-permute-start | bytes 1327112 | tf_op jit(solution)/shard_map/ppermute | solution.py:294
  326.3 36.4 %collective-permute-start.26 = (f32[24,4608]{1,0:T(8,128)S(1)}, f32[24,4608]{1,0:T(8,128)}, u32[]{:S(2)}, u32[]{:S(2)}) collective-permute-start(f32[24,4608]{1,0:T(8,128)S(1)} %copy-done.16), channel_id=1, source_target_pairs={{0,8},{1,9},{2,10},{3,11},{4,12},{5,13},{6,14},{7,15},{8,0},{9,1},... | collective-permute-start | bytes 1327112 | tf_op jit(solution)/shard_map/ppermute | solution.py:294
  333.7 29.0 %collective-permute-start.27 = (f32[24,4608]{1,0:T(8,128)S(1)}, f32[24,4608]{1,0:T(8,128)}, u32[]{:S(2)}, u32[]{:S(2)}) collective-permute-start(f32[24,4608]{1,0:T(8,128)S(1)} %copy-done.16), channel_id=1, source_target_pairs={{0,4},{1,5},{2,6},{3,7},{4,0},{5,1},{6,2},{7,3},{8,12},{9,13},{10,... | collective-permute-start | bytes 1327112 | tf_op jit(solution)/shard_map/ppermute | solution.py:294
  370.8 49.9 %collective-permute-start.34 = (f32[1536,768]{1,0:T(8,128)}, f32[1536,768]{1,0:T(8,128)}, u32[]{:S(2)}, u32[]{:S(2)}) collective-permute-start(f32[1536,768]{1,0:T(8,128)} %put.21.refs_0_), channel_id=1, source_target_pairs={{0,1},{1,0},{2,3},{3,2},{4,5},{5,4},{6,7},{7,6},{8,9},{9,8},{10,11... | collective-permute-start | bytes 14155784 | tf_op jit(solution)/shard_map/ppermute | solution.py:294
  370.8 22.6 %collective-permute-start.29 = (f32[96,4608]{1,0:T(8,128)S(1)}, f32[96,4608]{1,0:T(8,128)}, u32[]{:S(2)}, u32[]{:S(2)}) collective-permute-start(f32[96,4608]{1,0:T(8,128)S(1)} %copy-done.8), channel_id=1, source_target_pairs={{0,2},{1,17},{2,0},{3,19},{4,6},{5,21},{6,4},{7,23},{8,10},{9,25},... | collective-permute-start | bytes 5308424 | tf_op jit(solution)/shard_map/ppermute | solution.py:294
  371.3 12.5 %collective-permute-start.30 = (f32[24,2432]{1,0:T(8,128)S(1)}, f32[24,2432]{1,0:T(8,128)S(1)}, u32[]{:S(2)}, u32[]{:S(2)}) collective-permute-start(f32[24,2432]{1,0:T(8,128)S(1)} %get-tuple-element.235), channel_id=1, source_target_pairs={{0,4},{1,5},{2,6},{3,7},{4,0},{5,1},{6,2},{7,3},{8,12},{9,13},{10,... | collective-permute-start | bytes 700424 | tf_op jit(solution)/shard_map/ppermute | solution.py:294
  371.3 19.6 %collective-permute-start.31 = (f32[24,2432]{1,0:T(8,128)S(1)}, f32[24,2432]{1,0:T(8,128)S(1)}, u32[]{:S(2)}, u32[]{:S(2)}) collective-permute-start(f32[24,2432]{1,0:T(8,128)S(1)} %get-tuple-element.236), channel_id=1, source_target_pairs={{0,8},{1,9},{2,10},{3,11},{4,12},{5,13},{6,14},{7,15},{8,0},{9,1},... | collective-permute-start | bytes 700424 | tf_op jit(solution)/shard_map/ppermute | solution.py:294
  374.3 16.6 %collective-permute-start.32 = (f32[24,2432]{1,0:T(8,128)S(1)}, f32[24,2432]{1,0:T(8,128)S(1)}, u32[]{:S(2)}, u32[]{:S(2)}) collective-permute-start(f32[24,2432]{1,0:T(8,128)S(1)} %get-tuple-element.237), channel_id=1, source_target_pairs={{0,12},{1,13},{2,14},{3,15},{4,8},{5,9},{6,10},{7,11},{8,4},{9,5},... | collective-permute-start | bytes 700424 | tf_op jit(solution)/shard_map/ppermute | solution.py:294
  395.8 50.7 %collective-permute-start.33 = (f32[192,4608]{1,0:T(8,128)}, f32[192,4608]{1,0:T(8,128)}, u32[]{:S(2)}, u32[]{:S(2)}) collective-permute-start(f32[192,4608]{1,0:T(8,128)} %put.23.refs_0_), channel_id=1, source_target_pairs={{0,16},{1,3},{2,18},{3,1},{4,20},{5,7},{6,22},{7,5},{8,24},{9,11},... | collective-permute-start | bytes 10616840 | tf_op jit(solution)/shard_map/ppermute | solution.py:294
  396.5 9.5 %collective-permute-start.35 = (f32[24,2432]{1,0:T(8,128)S(1)}, f32[24,2432]{1,0:T(8,128)S(1)}, u32[]{:S(2)}, u32[]{:S(2)}) collective-permute-start(f32[24,2432]{1,0:T(8,128)S(1)} %add_add_fusion.3), channel_id=1, source_target_pairs={{0,12},{1,13},{2,14},{3,15},{4,8},{5,9},{6,10},{7,11},{8,4},{9,5},... | collective-permute-start | bytes 700424 | tf_op jit(solution)/shard_map/ppermute | solution.py:294
  398.8 21.3 %collective-permute-start.36 = (f32[24,2432]{1,0:T(8,128)S(1)}, f32[24,2432]{1,0:T(8,128)S(1)}, u32[]{:S(2)}, u32[]{:S(2)}) collective-permute-start(f32[24,2432]{1,0:T(8,128)S(1)} %add_add_fusion.3), channel_id=1, source_target_pairs={{0,8},{1,9},{2,10},{3,11},{4,12},{5,13},{6,14},{7,15},{8,0},{9,1},... | collective-permute-start | bytes 700424 | tf_op jit(solution)/shard_map/ppermute | solution.py:294
  402.5 17.7 %collective-permute-start.37 = (f32[24,2432]{1,0:T(8,128)S(1)}, f32[24,2432]{1,0:T(8,128)S(1)}, u32[]{:S(2)}, u32[]{:S(2)}) collective-permute-start(f32[24,2432]{1,0:T(8,128)S(1)} %add_add_fusion.3), channel_id=1, source_target_pairs={{0,4},{1,5},{2,6},{3,7},{4,0},{5,1},{6,2},{7,3},{8,12},{9,13},{10,... | collective-permute-start | bytes 700424 | tf_op jit(solution)/shard_map/ppermute | solution.py:294
  420.6 5.4 %copy-start.12 = (f32[96,2432]{1,0:T(8,128)}, f32[96,2432]{1,0:T(8,128)S(1)}, u32[]{:S(2)}) copy-start(f32[96,2432]{1,0:T(8,128)S(1)} %fusion.9.refs_0_) | copy-start | bytes 2801668
  426.0 24.9 %collective-permute-start.38 = (f32[96,2432]{1,0:T(8,128)S(1)}, f32[96,2432]{1,0:T(8,128)S(1)}, u32[]{:S(2)}, u32[]{:S(2)}) collective-permute-start(f32[96,2432]{1,0:T(8,128)S(1)} %fusion.9.refs_0_), channel_id=1, source_target_pairs={{0,2},{1,17},{2,0},{3,19},{4,6},{5,21},{6,4},{7,23},{8,10},{9,25},... | collective-permute-start | bytes 2801672 | tf_op jit(solution)/shard_map/ppermute | solution.py:294
  454.0 11.6 %collective-permute-start.39 = (f32[384,4608]{1,0:T(8,128)}, f32[384,4608]{1,0:T(8,128)}, u32[]{:S(2)}, u32[]{:S(2)}) collective-permute-start(f32[384,4608]{1,0:T(8,128)} %put.26.refs_0_), channel_id=1, source_target_pairs={{0,1},{1,0},{2,3},{3,2},{4,5},{5,4},{6,7},{7,6},{8,9},{9,8},{10,11... | collective-permute-start | bytes 21233672 | tf_op jit(solution)/shard_map/ppermute | solution.py:294
  454.0 23.8 %collective-permute-start.40 = (f32[192,2432]{1,0:T(8,128)}, f32[192,2432]{1,0:T(8,128)S(1)}, u32[]{:S(2)}, u32[]{:S(2)}) collective-permute-start(f32[192,2432]{1,0:T(8,128)} %put.29.refs_0_), channel_id=1, source_target_pairs={{0,16},{1,3},{2,18},{3,1},{4,20},{5,7},{6,22},{7,5},{8,24},{9,11},... | collective-permute-start | bytes 5603336 | tf_op jit(solution)/shard_map/ppermute | solution.py:294
  472.0 9.6 %copy-start.15 = (f32[16,768]{1,0:T(8,128)S(1)}, f32[16,768]{1,0:T(8,128)}, u32[]{:S(2)}) copy-start(f32[16,768]{1,0:T(8,128)} %copy-done.14) | copy-start | bytes 147460
  481.6 6.8 %collective-permute-start.41 = (f32[384,2432]{1,0:T(8,128)}, f32[384,2432]{1,0:T(8,128)}, u32[]{:S(2)}, u32[]{:S(2)}) collective-permute-start(f32[384,2432]{1,0:T(8,128)} %put.33.refs_0_), channel_id=1, source_target_pairs={{0,1},{1,0},{2,3},{3,2},{4,5},{5,4},{6,7},{7,6},{8,9},{9,8},{10,11... | collective-permute-start | bytes 11206664 | tf_op jit(solution)/shard_map/ppermute | solution.py:294
  488.4 7.3 %copy-start.1 = (bf16[768,768]{1,0:T(8,128)(2,1)S(1)}, bf16[768,768]{1,0:T(8,128)(2,1)}, u32[]{:S(2)}) copy-start(bf16[768,768]{1,0:T(8,128)(2,1)} %param.25) | copy-start | bytes 3538948
  (11 other events, 19.5 us)
